TPU v7x, 32 devices: a whole 2x2x4 slice. The times are simulated.
32 devices in a mesh: seq: 8 (over z, y), head: 4 (over x, core).
Axes of the slice: x: 2, y: 2, z: 4, core: 2. Of those that a mesh axis runs over, the one named last changes fastest.
Arguments:
- tokens: bfloat16 [16384, 768], P(('seq', 'head')), may hold values from -6 to 6
- input_gain: float32 [768], replicated, may hold values from 0.25 to 1.75
- proj_gate: bfloat16 [768, 1536], P(None, 'head'), may hold values from -0.21875 to 0.21875
- proj_value: bfloat16 [768, 1536], P(None, 'head'), may hold values from -0.21875 to 0.21875
- proj_state: bfloat16 [768, 128], replicated, may hold values from -0.21875 to 0.21875
- proj_step: bfloat16 [2, 768, 24], P(None, None, 'head'), may hold values from -0.21875 to 0.21875
- step_bias: float32 [2, 24], P(None, 'head'), may hold values from -8.5 to -3
- decay_log: float32 [24], P('head'), may hold values from 0 to 2.3
- conv_value: float32 [4, 1536], P(None, 'head'), may hold values from -3 to 3
- conv_state: float32 [4, 128], replicated, may hold values from -3 to 3
- skip_gain: float32 [24], P('head'), may hold values from 0.5 to 1.5
- mixer_gain: float32 [1536], P('head'), may hold values from 0.25 to 1.75
- proj_out: bfloat16 [1536, 768], P('head'), may hold values from -0.15625 to 0.15625
- doc_lengths: int32 [64], replicated, may hold values from 1 to 4096, 16384 in all
- pad_mask: int32 [16384], P('seq'), may hold values 0 or 1
- cotangent: bfloat16 [16384, 768], P(('seq', 'head')), may hold values from -6 to 6
Outputs:
- layer_out: bfloat16 [16384, 768], P(('seq', 'head'))
- grad_tokens: bfloat16 [16384, 768], P(('seq', 'head'))
- grad_input_gain: float32 [768], replicated
- grad_proj_gate: float32 [768, 1536], P(None, 'head')
- grad_proj_value: float32 [768, 1536], P(None, 'head')
- grad_proj_state: float32 [768, 128], replicated
- grad_proj_step: float32 [2, 768, 24], P(None, None, 'head')
- grad_step_bias: float32 [2, 24], P(None, 'head')
- grad_decay_log: float32 [24], P('head')
- grad_conv_value: float32 [4, 1536], P(None, 'head')
- grad_conv_state: float32 [4, 128], replicated
- grad_skip_gain: float32 [24], P('head')
- grad_mixer_gain: float32 [1536], P('head')
- grad_proj_out: float32 [1536, 768], P('head')
Inputs may be any that keep to these rules, and one draw needn't show every extreme that they name: `doc_lengths`: they sum to 16384, and the longest is exactly 4096.
All inputs are finite; a program needn't handle non-finite values. No bound on the sum of `pad_mask` on one device may be relied on, other than what follows from the above.
Results may differ from a plain program's by a relative error of at most 0.0089.
Values may be sent and summed in bfloat16 or wider, within the bound.
No kernel may reach another device: no remote copies, remote signals or barrier semaphores. Data moves between devices by JAX's collectives and lax.ppermute only.
A program may use at most 256 MiB of HBM per device.

v0:
```python
from functools import partial

import jax
import jax.numpy as jnp
from jax import lax
from jax.sharding import PartitionSpec as P

SPAN = 128


PRECISE = lax.Precision.HIGHEST
EPSILON = 1e-05


def from_behind(array, axis, by):
    length = lax.axis_size(axis)
    pairs = [(i, i + by) for i in range(length) if 0 <= i + by < length]
    return lax.ppermute(array, axis, pairs)


def entering_2(array, axis, join, neutral):
    place = lax.axis_index(axis)
    gathered = jax.tree.map(
        lambda a, kind: lax.all_gather(a.astype(kind), axis), array, (jnp.bfloat16, jnp.bfloat16)
    )
    state = jax.tree.map(lambda a, e: jnp.zeros_like(a) + jnp.asarray(e, a.dtype), array, neutral)

    def one(lap, state):
        return join(
            state,
            jax.tree.map(
                lambda a, own: lax.dynamic_index_in_dim(a, lap, 0, False).astype(own.dtype),
                gathered,
                array,
            ),
        )

    return lax.fori_loop(0, place, one, state)


def carried_in(array, axis, combine, identity, reverse):
    length, mine = (lax.axis_size(axis), lax.axis_index(axis))
    everything = jax.tree.map(lambda part: lax.all_gather(part, axis), array)
    start = jax.tree.map(
        lambda part, zero: jnp.broadcast_to(jnp.asarray(zero, part.dtype), part.shape),
        array,
        identity,
    )

    def lap(k, before):
        at = length - 1 - k if reverse else k
        reached = at > mine if reverse else at < mine
        new = combine(before, jax.tree.map(lambda part: part[at], everything))
        return jax.tree.map(lambda a, b: jnp.where(reached, a, b), new, before)

    return lax.fori_loop(0, length, lap, start)


def prefix(array, axis, combine, identity):
    length, mine = (lax.axis_size(axis), lax.axis_index(axis))
    everything = jax.tree.map(
        lambda part, kind: lax.all_gather(part.astype(kind), axis),
        array,
        jax.tree.map(lambda a: jnp.bfloat16 if a.dtype == jnp.float32 else a.dtype, array),
    )
    start = jax.tree.map(
        lambda part, zero: jnp.broadcast_to(jnp.asarray(zero, part.dtype), part.shape),
        array,
        identity,
    )

    def lap(k, before):
        at = length - 1 - k
        reached = at > mine
        new = combine(
            before, jax.tree.map(lambda part, own: part[at].astype(own.dtype), everything, array)
        )
        return jax.tree.map(lambda a, b: jnp.where(reached, a, b), new, before)

    return lax.fori_loop(0, length, lap, start)


def link_states(earlier, later):
    first_gate, first_state = earlier
    second_gate, second_state = later
    return (first_gate * second_gate, second_gate[..., None, None] * first_state + second_state)


def conv_rows(extended, kernel, start_flags, margin):
    length = extended.shape[0] - margin
    result = kernel[0] * extended[margin:]
    within = jnp.ones((length, 1), extended.dtype)
    for offset in range(1, margin + 1):
        within = (
            within
            * (1.0 - start_flags[margin - offset + 1 : margin - offset + 1 + length])[:, None]
        )
        result = (
            result + kernel[offset] * extended[margin - offset : margin - offset + length] * within
        )
    return result


def block_parts(values, keys_in, queries, step_sizes, log_decay, starts, block_width):
    length, head_count, head_size = values.shape
    blocks = length // block_width
    values = values.reshape(blocks, block_width, head_count, head_size)
    keys_in = keys_in.reshape(blocks, block_width, -1)
    queries = queries.reshape(blocks, block_width, -1)
    step_sizes = step_sizes.reshape(blocks, block_width, head_count)
    running = jnp.cumsum(log_decay.reshape(blocks, block_width, head_count), axis=1)
    opened = jnp.cumsum(starts.reshape(blocks, block_width), axis=1)
    places = jnp.arange(block_width)
    paired = (places[:, None] > places[None, :])[None] & (opened[:, :, None] == opened[:, None, :])
    by_head = jnp.swapaxes(running, 1, 2)
    log_gaps = by_head[:, :, :, None] - by_head[:, :, None, :]
    decays = jnp.exp(jnp.where(paired[:, None], log_gaps, -1e30))
    scores = jnp.einsum("ctn,csn->cts", queries, keys_in, precision=PRECISE)
    weighted = values * step_sizes[..., None]
    inside = jnp.einsum("chts,cshp->cthp", decays * scores[:, None], weighted, precision=PRECISE)
    final_log = running[:, -1, :]
    final_open = opened[:, -1]
    to_end = jnp.exp(
        jnp.where(
            (opened == final_open[:, None])[:, :, None], final_log[:, None, :] - running, -1e30
        )
    )
    block_states = jnp.einsum(
        "csn,cshp->chnp", keys_in, weighted * to_end[..., None], precision=PRECISE
    )
    block_gates = jnp.exp(final_log) * (final_open == 0)[:, None].astype(final_log.dtype)
    joined_gates, joined_states = lax.associative_scan(
        link_states, (block_gates, block_states), axis=0
    )
    prior_states = jnp.concatenate([jnp.zeros_like(joined_states[:1]), joined_states[:-1]], axis=0)
    entries = jnp.exp(running) * (opened == 0)[:, :, None].astype(running.dtype)
    carried = (
        jnp.einsum("ctn,chnp->cthp", queries, prior_states, precision=PRECISE) * entries[..., None]
    )
    output = (inside + carried).reshape(length, head_count, head_size)
    return (output, joined_gates[-1], joined_states[-1])


def block_inflow(entering, queries, log_decay, starts, block_width):
    length, head_count = log_decay.shape
    blocks = length // block_width
    running = jnp.cumsum(log_decay.reshape(blocks, block_width, head_count), axis=1)
    opened = jnp.cumsum(starts.reshape(blocks, block_width), axis=1)
    totals = jnp.cumsum(running[:, -1, :], axis=0) - running[:, -1, :]
    before = jnp.cumsum(opened[:, -1]) - opened[:, -1]
    leading = jnp.exp(totals) * (before == 0)[:, None].astype(totals.dtype)
    entries = (
        jnp.exp(running) * (opened == 0)[:, :, None].astype(running.dtype) * leading[:, None, :]
    )
    drawn = jnp.einsum("ln,hnp->lhp", queries, entering, precision=PRECISE)
    return drawn * entries.reshape(length, head_count)[:, :, None]


def per_device(
    tokens,
    input_gain,
    proj_gate,
    proj_value,
    proj_state,
    proj_step,
    step_bias,
    decay_log,
    conv_value,
    conv_state,
    skip_gain,
    mixer_gain,
    proj_out,
    doc_lengths,
    pad_mask,
    cotangent,
):
    head_devices = lax.axis_size("head")
    length = pad_mask.shape[0]
    local_width = proj_gate.shape[1]
    head_count = proj_step.shape[2]
    head_size = local_width // head_count
    state_width = proj_state.shape[1] // 2
    margin = conv_value.shape[0] - 1
    first_place = lax.axis_index("seq") * length
    all_tokens = length * lax.axis_size("seq")
    offsets = jnp.cumsum(doc_lengths) - doc_lengths
    places = first_place - margin + jnp.arange(length + margin + 1, dtype=jnp.int32)
    start_flags = (
        jnp.any(places[:, None] == offsets[None, :], axis=1) | (places >= all_tokens)
    ).astype(jnp.float32)
    forward_starts = start_flags[margin : margin + length]
    backward_starts = start_flags[margin + 1 :][::-1]
    live = pad_mask.astype(jnp.float32)
    token_values = tokens.astype(jnp.float32)
    scale_rows = lax.rsqrt(jnp.mean(token_values * token_values, axis=1, keepdims=True) + EPSILON)
    normed = (token_values * scale_rows * input_gain).astype(jnp.bfloat16)
    gathered = lax.all_gather(normed, "head", axis=0, tiled=True)
    gate_in = jnp.dot(gathered, proj_gate, preferred_element_type=jnp.float32)
    value_in = jnp.dot(gathered, proj_value, preferred_element_type=jnp.float32)
    state_in = jnp.dot(gathered, proj_state, preferred_element_type=jnp.float32)
    step_raw = jnp.einsum("ld,kdh->lkh", gathered, proj_step, preferred_element_type=jnp.float32)
    mixed_in = jnp.concatenate([value_in, state_in], axis=1)
    received = from_behind(mixed_in[length - margin :], "seq", 1)
    extended = jnp.concatenate([received, mixed_in], axis=0)
    kernel = jnp.concatenate([conv_value, conv_state], axis=1)

    def front(ext_rows, raw_steps, taps, bias_steps, rate_log):
        activated = (
            jax.nn.silu(conv_rows(ext_rows, taps, start_flags[: length + margin], margin))
            * live[:, None]
        )
        sizes_out = jax.nn.softplus(raw_steps + bias_steps[None])
        decay_out = sizes_out * (-jnp.exp(rate_log))[None, None, :]
        return (activated, sizes_out, decay_out)

    (activated, step_sizes, log_decay), front_back = jax.vjp(
        front, extended, step_raw, kernel, step_bias, decay_log
    )
    values = activated[:, :local_width].reshape(length, head_count, head_size)
    keys_in = activated[:, local_width : local_width + state_width]
    queries = activated[:, local_width + state_width :]
    forward_parts = partial(block_parts, starts=forward_starts, block_width=SPAN)
    backward_parts = partial(block_parts, starts=backward_starts, block_width=SPAN)
    forward_inflow = partial(block_inflow, starts=forward_starts, block_width=SPAN)
    backward_inflow = partial(block_inflow, starts=backward_starts, block_width=SPAN)
    (ahead_base, ahead_gate, ahead_state), ahead_back = jax.vjp(
        forward_parts, values, keys_in, queries, step_sizes[:, 0], log_decay[:, 0]
    )
    (behind_base, behind_gate, behind_state), behind_back = jax.vjp(
        backward_parts,
        values[::-1],
        keys_in[::-1],
        queries[::-1],
        step_sizes[::-1, 1],
        log_decay[::-1, 1],
    )
    neutral = (jnp.ones_like(ahead_gate), jnp.zeros_like(ahead_state))
    ahead_enter = entering_2((ahead_gate, ahead_state), "seq", link_states, neutral)[1]
    behind_enter = carried_in((behind_gate, behind_state), "seq", link_states, neutral, True)[1]
    ahead_extra, ahead_inflow_back = jax.vjp(forward_inflow, ahead_enter, queries, log_decay[:, 0])
    behind_extra, behind_inflow_back = jax.vjp(
        backward_inflow, behind_enter, queries[::-1], log_decay[::-1, 1]
    )
    mixed = (
        ahead_base
        + ahead_extra
        + (behind_base + behind_extra)[::-1]
        + skip_gain[None, :, None] * values
    ).reshape(length, local_width)
    gate_act = jax.nn.silu(gate_in)
    gated = mixed * gate_act
    inner_width = local_width * head_devices
    energy = lax.psum(jnp.sum(gated * gated, axis=1), "head")
    factor = lax.rsqrt(energy / inner_width + EPSILON)[:, None]
    output_in = (gated * factor * mixer_gain).astype(jnp.bfloat16)
    picked = output_in
    mixer = lax.psum_scatter(
        jnp.dot(picked, proj_out, preferred_element_type=jnp.float32),
        "head",
        scatter_dimension=0,
        tiled=True,
    )
    layer_out = (token_values + mixer).astype(jnp.bfloat16)
    piece = lax.all_gather(cotangent, "head", axis=0, tiled=True)
    picked = output_in
    grad_weight = jnp.einsum("tc,td->cd", picked, piece, preferred_element_type=jnp.float32)
    product = jnp.einsum("td,cd->tc", piece, proj_out, preferred_element_type=jnp.float32)
    grad_output = product
    grad_proj_out, grad_output = (grad_weight, grad_output)
    scaled_grad = grad_output * mixer_gain
    cross = lax.psum(jnp.sum(scaled_grad * gated, axis=1), "head")
    grad_gated = scaled_grad * factor - gated * factor**3 * (cross / inner_width)[:, None]
    grad_mixer_gain = jnp.sum(grad_output * gated * factor, axis=0)
    sigmoid_gate = jax.nn.sigmoid(gate_in)
    grad_mixed = (grad_gated * gate_act).reshape(length, head_count, head_size)
    grad_gate = grad_gated * mixed * sigmoid_gate * (1.0 + gate_in * (1.0 - sigmoid_gate))
    grad_skip_gain = jnp.sum(grad_mixed * values, axis=(0, 2))
    ahead_hold, ahead_query_in, ahead_log_in = ahead_inflow_back(grad_mixed)
    ahead_adjoint = prefix((ahead_gate, ahead_hold), "seq", link_states, neutral)[1]
    ahead_gate_grad = jnp.sum(ahead_adjoint * ahead_enter, axis=(1, 2))
    ahead_values, ahead_keys, ahead_queries, ahead_steps, ahead_logs = ahead_back(
        (grad_mixed, ahead_gate_grad, ahead_adjoint)
    )
    flipped_grad = grad_mixed[::-1]
    behind_hold, behind_query_in, behind_log_in = behind_inflow_back(flipped_grad)
    behind_adjoint = carried_in((behind_gate, behind_hold), "seq", link_states, neutral, False)[1]
    behind_gate_grad = jnp.sum(behind_adjoint * behind_enter, axis=(1, 2))
    behind_values, behind_keys, behind_queries, behind_steps, behind_logs = behind_back(
        (flipped_grad, behind_gate_grad, behind_adjoint)
    )
    grad_values = ahead_values + behind_values[::-1] + grad_mixed * skip_gain[None, :, None]
    grad_keys = ahead_keys + behind_keys[::-1]
    grad_queries = ahead_queries + ahead_query_in + (behind_queries + behind_query_in)[::-1]
    grad_steps = jnp.stack([ahead_steps, behind_steps[::-1]], axis=1)
    grad_logs = jnp.stack([ahead_logs + ahead_log_in, (behind_logs + behind_log_in)[::-1]], axis=1)
    grad_act = jnp.concatenate(
        [grad_values.reshape(length, local_width), grad_keys, grad_queries], axis=1
    )
    grad_ext, grad_raw, grad_kernel, grad_step_bias, grad_decay_log = front_back(
        (grad_act, grad_steps, grad_logs)
    )
    returned = from_behind(grad_ext[:margin], "seq", -1)
    grad_rows = grad_ext[margin:].at[length - margin :].add(returned)
    grad_value_low = grad_rows[:, :local_width].astype(jnp.bfloat16)
    grad_gate_low = grad_gate.astype(jnp.bfloat16)
    grad_raw_low = grad_raw.astype(jnp.bfloat16)
    partial_in = jnp.einsum(
        "lc,dc->ld", grad_gate_low, proj_gate, preferred_element_type=jnp.float32
    )
    partial_in = partial_in + jnp.einsum(
        "lc,dc->ld", grad_value_low, proj_value, preferred_element_type=jnp.float32
    )
    partial_in = partial_in + jnp.einsum(
        "lkh,kdh->ld", grad_raw_low, proj_step, preferred_element_type=jnp.float32
    )
    own_in, own_state = (
        lax.psum_scatter(partial_in, "head", scatter_dimension=0, tiled=True),
        lax.psum_scatter(grad_rows[:, local_width:], "head", scatter_dimension=0, tiled=True),
    )
    own_state_low = own_state.astype(jnp.bfloat16)
    grad_normed = own_in + jnp.einsum(
        "lc,dc->ld", own_state_low, proj_state, preferred_element_type=jnp.float32
    )
    grad_proj_state = jnp.einsum(
        "ld,lc->dc", normed, own_state_low, preferred_element_type=jnp.float32
    )
    grad_proj_gate = jnp.einsum(
        "ld,lc->dc", gathered, grad_gate_low, preferred_element_type=jnp.float32
    )
    grad_proj_value = jnp.einsum(
        "ld,lc->dc", gathered, grad_value_low, preferred_element_type=jnp.float32
    )
    grad_proj_step = jnp.einsum(
        "ld,lkh->kdh", gathered, grad_raw_low, preferred_element_type=jnp.float32
    )
    scaled_normed = grad_normed * input_gain
    grad_tokens = (
        cotangent.astype(jnp.float32)
        + scale_rows * scaled_normed
        - token_values
        * scale_rows**3
        * jnp.mean(scaled_normed * token_values, axis=1, keepdims=True)
    )
    grad_input_gain = jnp.sum(grad_normed * token_values * scale_rows, axis=0)
    seq_sums = lax.psum(
        (
            grad_proj_gate,
            grad_proj_value,
            grad_proj_step,
            grad_proj_out,
            grad_kernel[:, :local_width],
            grad_step_bias,
            grad_decay_log,
            grad_skip_gain,
            grad_mixer_gain,
        ),
        "seq",
    )
    shared_sums = lax.psum(
        (grad_proj_state, grad_kernel[:, local_width:], grad_input_gain), ("seq", "head")
    )
    return (
        layer_out,
        grad_tokens.astype(jnp.bfloat16),
        shared_sums[2],
        seq_sums[0],
        seq_sums[1],
        shared_sums[0],
        seq_sums[2],
        seq_sums[5],
        seq_sums[6],
        seq_sums[4],
        shared_sums[1],
        seq_sums[7],
        seq_sums[8],
        seq_sums[3],
    )


def solution(mesh):
    return jax.shard_map(
        per_device,
        mesh=mesh,
        in_specs=(
            P(("seq", "head"), None),
            P(),
            P(None, "head"),
            P(None, "head"),
            P(),
            P(None, None, "head"),
            P(None, "head"),
            P("head"),
            P(None, "head"),
            P(),
            P("head"),
            P("head"),
            P("head", None),
            P(),
            P("seq"),
            P(("seq", "head"), None),
        ),
        out_specs=(
            P(("seq", "head"), None),
            P(("seq", "head"), None),
            P(),
            P(None, "head"),
            P(None, "head"),
            P(),
            P(None, None, "head"),
            P(None, "head"),
            P("head"),
            P(None, "head"),
            P(),
            P("head"),
            P("head"),
            P("head", None),
        ),
        check_vma=False,
    )
```

profile of v0, /device:TPU:0, one launch (start us, length us, event | category | flops | bytes accessed | tf_op | source)
XLA Modules:
  0.0 1669.4 jit_solution(14035806070159851844)
XLA Ops:
  17.2 26.3 %all-gather.7.cloned.1.call-done = bf16[2048,768]{1,0:T(8,128)(2,1)} async-done(((bf16[512,768]{1,0:T(8,128)(2,1)}), bf16[2048,768]{1,0:T(8,128)(2,1)}) %all-gather.7.cloned.1.call-update) | async-done | bytes 3145744 | tf_op jit(solution)/shard_map/all_gather | solution.py:197
  77.2 18.3 %all-gather.2 = bf16[8,1,6]{2,1,0:T(2,128)(2,1)S(1)} all-gather(bf16[1,1,6]{2,1,0:T(2,128)(2,1)S(1)} %get-tuple-element.871), channel_id=1, replica_groups=mesh['seq'=8,'head'=4] {'seq'}, dimensions={0}, use_global_device_ids=true | all-gather | bytes 108 | tf_op jit(solution)/shard_map/all_gather | solution.py:24
  103.7 17.0 %all-gather.3 = f32[8,1,6]{2,1,0:T(1,128)} all-gather(f32[1,1,6]{2,1,0:T(1,128)S(1)} %get-tuple-element.872), channel_id=1, replica_groups=mesh['seq'=8,'head'=4] {'seq'}, dimensions={0}, use_global_device_ids=true | all-gather | bytes 216 | tf_op jit(solution)/shard_map/all_gather | solution.py:43
  124.0 6.4 multiply_multiply_fusion
  137.2 10.8 rev.41
  164.2 7.2 pad.518
  175.7 9.3 pad.520
  185.0 13.0 pad.521
  202.6 24.4 %pad.989 = f32[15,6,64,64]{2,3,1,0:T(8,128)} pad(f32[8,6,64,64]{2,3,1,0:T(8,128)} %add.667, f32[]{:T(128)} %constant.231.clone.1), padding=0_0_1x0_0_0x0_0_0x0_0_0 | pad | bytes 2260996
  227.0 16.8 %pad.523 = f32[16,6,64,64]{2,3,1,0:T(8,128)} pad(f32[8,6,64,64]{2,3,1,0:T(8,128)S(1)} %copy-done.56, f32[]{:T(128)} %constant.231.clone.1), padding=1_0_1x0_0_0x0_0_0x0_0_0 | pad | bytes 2359300 | tf_op jit(solution)/shard_map/jvp()/pad | solution.py:132
  261.2 7.3 pad.502
  272.7 9.3 pad.504
  282.0 13.0 pad.505
  299.6 24.3 %pad.993 = f32[15,6,64,64]{2,3,1,0:T(8,128)} pad(f32[8,6,64,64]{2,3,1,0:T(8,128)} %add.650, f32[]{:T(128)} %constant.231.clone.1), padding=0_0_1x0_0_0x0_0_0x0_0_0 | pad | bytes 2260996
  323.9 16.5 pad.507
  340.4 6.7 rev.45
  352.7 24.4 %pad.522 = f32[16,6,64,64]{2,3,1,0:T(8,128)} pad(f32[8,6,64,64]{2,3,1,0:T(8,128)} %pad_maximum_fusion.2, f32[]{:T(128)} %constant.231.clone.1), padding=0_1_1x0_0_0x0_0_0x0_0_0 | pad | bytes 2359300 | tf_op jit(solution)/shard_map/jvp()/pad | solution.py:132
  377.2 37.6 %all_gather.39 = f32[8,6,64,64]{3,2,1,0:T(8,128)} all-gather(f32[1,6,64,64]{3,2,1,0:T(8,128)S(1)} %copy.611), channel_id=1, replica_groups=mesh['seq'=8,'head'=4] {'seq'}, dimensions={0}, use_global_device_ids=true | all-gather | bytes 884736 | tf_op jit(solution)/shard_map/all_gather | solution.py:43
  414.8 13.9 while.60
  434.6 16.4 pad.506
  452.0 31.6 %all_gather.37 = bf16[8,6,64,64]{3,2,1,0:T(8,128)(2,1)S(1)} all-gather(bf16[1,6,64,64]{3,2,1,0:T(8,128)(2,1)S(1)} %copy.591), channel_id=1, replica_groups=mesh['seq'=8,'head'=4] {'seq'}, dimensions={0}, use_global_device_ids=true | all-gather | bytes 442368 | tf_op jit(solution)/shard_map/all_gather | solution.py:24
  497.5 12.9 fusion.39
  512.5 10.5 rev.47
  533.4 13.3 fusion.40
  561.1 6.8 multiply_reduce_fusion.6
  567.9 7.6 psum.99
  576.2 8.3 multiply_reduce_fusion.7
  592.1 37.3 %all-gather = bf16[48,64,64]{2,1,0:T(8,128)(2,1)} all-gather(bf16[6,64,64]{2,1,0:T(8,128)(2,1)} %copy.615), channel_id=2, replica_groups=mesh['seq'=8,'head'=4] {'seq'}, dimensions={0}, use_global_device_ids=true | all-gather | bytes 442368 | tf_op jit(solution)/shard_map/all_gather | solution.py:62
  629.4 19.6 %while.61 = (s32[]{:T(128)}, f32[6,64,64]{2,1,0:T(8,128)}, s32[]{:T(128)}, bf16[8,6]{1,0:T(8,128)(2,1)}, bf16[8,6,64,64]{3,2,1,0:T(8,128)(2,1)}, /*index=5*/s32[]{:T(128)}, s32[]{:T(128)}, s32[]{:T(128)}, s32[]{:T(128)}) while((s32[]{:T(128)}, f32[6,64,64]{2,1,0:T(8,128)}, s32[]{:T(128)}, bf16[8,6]{1,0:T(8,128)(2,1)}, ...), condition=%wide.region_21.22_spmd.clone, body=%wide.region_20.21_spmd.clone.sunk | while | flops 122894 | bytes 245995 | solution.py:80
  652.4 10.5 rev.48
  678.7 15.6 fusion.18
  696.0 40.3 %all-gather.1 = f32[48,64,64]{2,1,0:T(8,128)} all-gather(f32[6,64,64]{2,1,0:T(8,128)} %copy.622), channel_id=3, replica_groups=mesh['seq'=8,'head'=4] {'seq'}, dimensions={0}, use_global_device_ids=true | all-gather | bytes 884736 | tf_op jit(solution)/shard_map/all_gather | solution.py:43
  736.3 19.7 %while.62 = (s32[]{:T(128)}, f32[6,64,64]{2,1,0:T(8,128)}, s32[]{:T(128)}, f32[8,6]{1,0:T(8,128)}, f32[8,6,64,64]{3,2,1,0:T(8,128)}, /*index=5*/s32[]{:T(128)}, s32[]{:T(128)}) while((s32[]{:T(128)}, f32[6,64,64]{2,1,0:T(8,128)}, s32[]{:T(128)}, f32[8,6]{1,0:T(8,128)}, f32[8,6,64,64]{3,2,1,0:T(8,128)}, /*index=5*/s32[]{:T(128)}, ...), condition=%wide.region_23.24_spmd.clone, body=%wide.region_22.23_spmd.clone.sunk | while | flops 98308 | bytes 295097 | solution.py:56
  779.7 7.0 fusion.169
  786.8 16.5 fusion.16
  834.7 7.3 pad.554
  845.4 8.5 pad.555
  860.9 8.6 pad.582
  869.4 6.7 pad.568
  876.1 8.6 pad.583
  889.8 16.4 pad.584
  906.2 21.6 %pad.563 = f32[16,6,64,64]{2,3,1,0:T(8,128)} pad(f32[7,6,64,64]{2,3,1,0:T(8,128)} %get-tuple-element.750, f32[]{:T(128)} %constant.231.clone.1), padding=2_1_1x0_0_0x0_0_0x0_0_0 | pad | bytes 2260996 | tf_op jit(solution)/shard_map/transpose(jvp())/pad | solution.py:132
  927.8 16.4 pad.585
  959.4 8.6 pad.556
  967.9 6.7 pad.541
  979.8 16.4 pad.557
  996.2 24.4 %pad.558 = f32[16,6,64,64]{2,3,1,0:T(8,128)} pad(f32[8,6,64,64]{2,3,1,0:T(8,128)} %broadcast_multiply_fusion.2, f32[]{:T(128)} %constant.231.clone.1), padding=0_1_1x0_0_0x0_0_0x0_0_0 | pad | bytes 2359300 | tf_op jit(solution)/shard_map/transpose(jvp())/pad | solution.py:132
  1020.6 14.7 pad.536
  1040.4 7.0 fusion.173
  1063.5 11.6 multiply_reduce_fusion.9
  1076.0 8.7 rev.50
  1090.6 12.0 multiply_reduce_fusion.11
  1104.7 10.8 rev.49
  1128.7 7.6 multiply_reduce_fusion.5
  1145.6 9.1 pad_add_fusion
  1166.2 23.5 %fusion.333 = f32[16,128,6]{2,0,1:T(8,128)S(1)} fusion(f32[16,128,6]{2,0,1:T(8,128)S(1)} %copy.673), kind=kOutput, calls=%fused_computation.583 | output fusion | flops 1560576 | bytes 98304 | tf_op jit(solution)/shard_map/transpose(jvp(jit(cumsum)))/reduce_window_sum | solution.py:147
  1226.7 23.6 %fusion.328 = f32[16,128,6]{2,0,1:T(8,128)S(1)} fusion(f32[16,128,6]{2,0,1:T(8,128)S(1)} %copy.651), kind=kOutput, calls=%fused_computation.578 | output fusion | flops 1560576 | bytes 98304 | tf_op jit(solution)/shard_map/transpose(jvp(jit(cumsum)))/reduce_window_sum | solution.py:111
  1260.6 6.5 fusion.289
  1278.2 6.7 fusion.199
  1288.3 36.1 %all-reduce.121 = (f32[2,768,6]{1,2,0:T(8,128)S(1)}, f32[2,6]{1,0:T(2,128)}, f32[6]{0:T(128)}, f32[4,384]{1,0:T(4,128)}, f32[6]{0:T(128)}, /*index=5*/f32[384]{0:T(512)}) all-reduce(f32[2,768,6]{1,2,0:T(8,128)S(1)} %fusion.192, f32[2,6]{1,0:T(2,128)S(1)} %get-tuple-element.693, ...), channel_id=1, replica_groups=mesh['seq'=8,'head'=4] {'seq'}, use_global_device_ids=true, to_apply=%region_72.73 | all-reduce | flops 11160 | bytes 89280 | tf_op jit(solution)/shard_map/psum | solution.py:345
  1328.5 37.3 %all-reduce.120 = (f32[768]{0:T(1024)}, f32[4,128]{1,0:T(4,128)}) all-reduce(f32[768]{0:T(1024)S(1)} %get-tuple-element.622, f32[4,128]{1,0:T(4,128)S(1)} %pad_add_fusion.19), channel_id=1, replica_groups=mesh['seq'=8,'head'=4] {'seq','head'}, use_global_device_ids=true, to_apply=%region_68.69 | all-reduce | flops 1280 | bytes 10240 | tf_op jit(solution)/shard_map/psum | solution.py:359
  1365.8 13.0 reduce-scatter.4.cloned.1.call-done
  1382.7 130.2 %all-reduce.126.cloned.1.call-done = f32[768,128]{1,0:T(8,128)} async-done(((f32[768,128]{1,0:T(8,128)}), f32[768,128]{1,0:T(8,128)}) %all-reduce.126.cloned.1.call-update) | async-done | bytes 393232 | tf_op jit(solution)/shard_map/psum | solution.py:359
  1512.8 144.3 %all-reduce.128.cloned.1.call-done = (f32[768,384]{1,0:T(8,128)}, f32[768,384]{1,0:T(8,128)}, f32[384,768]{1,0:T(8,128)}) async-done(((f32[768,384]{1,0:T(8,128)}, f32[768,384]{1,0:T(8,128)}, f32[384,768]{1,0:T(8,128)}), (f32[768,384]{1,0:T(8,128)}, f32[768,384]{1,0:T(8,128)}, f32[384,768]{1,0:T(8,128)})) %all-reduce.128.cloned.1.call-update) | async-done | bytes 3538960 | tf_op jit(solution)/shard_map/psum | solution.py:345
  (1151 shorter events, 474.4 us)
Async XLA Ops:
  7.2 541.1 %copy-start = (bf16[768,384]{1,0:T(8,128)(2,1)S(1)}, bf16[768,384]{1,0:T(8,128)(2,1)}, u32[]{:S(2)}) copy-start(bf16[768,384]{1,0:T(8,128)(2,1)} %param.28) | copy-start | bytes 1769476
  7.2 36.3 %copy-start.258 = (bf16[2,768,6]{1,0,2:T(2,128)(2,1)S(1)}, bf16[2,768,6]{1,0,2:T(2,128)(2,1)}, u32[]{:S(2)}) copy-start(bf16[2,768,6]{1,0,2:T(2,128)(2,1)} %param.31) | copy-start | bytes 55300
  7.3 36.3 %copy-start.335 = (f32[2,6]{1,0:T(2,128)S(1)}, f32[2,6]{1,0:T(2,128)}, u32[]{:S(2)}) copy-start(f32[2,6]{1,0:T(2,128)} %param.32) | copy-start | bytes 148
  7.3 36.3 %all-gather.7.cloned.1.call-start = ((), (), s32[]{:S(2)}) async-start(), calls=%async_computation.3 | async-start | bytes 3932160 | tf_op jit(solution)/shard_map/all_gather | solution.py:197
  12.2 548.9 %all-gather.9.cloned.1.call-start = ((), (), s32[]{:S(2)}) async-start(), calls=%async_computation.5 | async-start | bytes 3932160 | tf_op jit(solution)/shard_map/all_gather | solution.py:264
  13.0 1262.6 %reduce-scatter.8.cloned.1.call-start = ((), (), s32[]{:S(2)}) async-start(), calls=%async_computation.7 | async-start | bytes 1310720 | tf_op jit(solution)/shard_map/reduce_scatter | solution.py:318
  13.1 33.9 %copy-start.331 = (f32[6]{0:T(128)}, f32[6]{0:T(128)S(1)}, u32[]{:S(2)}) copy-start(f32[6]{0:T(128)S(1)} %exponential_negate_fusion) | copy-start | bytes 76
  13.1 110.8 %copy-start.208 = (f32[2048]{0:T(1024)}, f32[2048]{0:T(1024)S(1)}, u32[]{:S(2)}) copy-start(f32[2048]{0:T(1024)S(1)} %convert_element_type.146) | copy-start | bytes 24580
  14.4 109.6 %copy-start.194 = (f32[2048]{0:T(1024)}, f32[2048]{0:T(1024)S(1)}, u32[]{:S(2)}) copy-start(f32[2048]{0:T(1024)S(1)} %get-tuple-element.808) | copy-start | bytes 24580
  14.4 109.6 %copy-start.196 = (f32[2048]{0:T(1024)}, f32[2048]{0:T(1024)S(1)}, u32[]{:S(2)}) copy-start(f32[2048]{0:T(1024)S(1)} %get-tuple-element.809) | copy-start | bytes 24580
  14.4 109.6 %copy-start.198 = (f32[2048]{0:T(1024)}, f32[2048]{0:T(1024)S(1)}, u32[]{:S(2)}) copy-start(f32[2048]{0:T(1024)S(1)} %get-tuple-element.810) | copy-start | bytes 24580
  15.0 43.2 %copy-start.314 = (f32[16]{0:T(128)}, f32[16]{0:T(128)S(1)}, u32[]{:S(2)}) copy-start(f32[16]{0:T(128)S(1)} %get-tuple-element.634) | copy-start | bytes 196
  15.0 46.3 %copy-start.320 = (f32[16]{0:T(128)}, f32[16]{0:T(128)S(1)}, u32[]{:S(2)}) copy-start(f32[16]{0:T(128)S(1)} %get-tuple-element.636) | copy-start | bytes 196
  15.7 42.5 %copy-start.315 = (f32[16]{0:T(128)}, f32[16]{0:T(128)S(1)}, u32[]{:S(2)}) copy-start(f32[16]{0:T(128)S(1)} %get-tuple-element.637) | copy-start | bytes 196
  15.7 42.9 %copy-start.322 = (f32[16]{0:T(128)}, f32[16]{0:T(128)S(1)}, u32[]{:S(2)}) copy-start(f32[16]{0:T(128)S(1)} %get-tuple-element.639) | copy-start | bytes 196
  15.7 59.3 %copy-start.212 = (f32[16,128]{1,0:T(8,128)}, f32[16,128]{1,0:T(8,128)S(1)}, u32[]{:S(2)}) copy-start(f32[16,128]{1,0:T(8,128)S(1)} %get-tuple-element.818) | copy-start | bytes 24580
  15.8 59.3 %copy-start.262 = (pred[16,128]{1,0:T(8,128)(4,1)}, pred[16,128]{1,0:T(8,128)(4,1)S(1)}, u32[]{:S(2)}) copy-start(pred[16,128]{1,0:T(8,128)(4,1)S(1)} %get-tuple-element.817) | copy-start | bytes 6148
  15.8 59.3 %copy-start.210 = (f32[16,128]{1,0:T(8,128)}, f32[16,128]{1,0:T(8,128)S(1)}, u32[]{:S(2)}) copy-start(f32[16,128]{1,0:T(8,128)S(1)} %get-tuple-element.815) | copy-start | bytes 24580
  15.8 59.4 %copy-start.260 = (pred[16,128]{1,0:T(8,128)(4,1)}, pred[16,128]{1,0:T(8,128)(4,1)S(1)}, u32[]{:S(2)}) copy-start(pred[16,128]{1,0:T(8,128)(4,1)S(1)} %get-tuple-element.814) | copy-start | bytes 6148
  58.6 94.6 %copy-start.206 = (f32[8,6]{1,0:T(8,128)}, f32[8,6]{1,0:T(8,128)S(1)}, u32[]{:S(2)}) copy-start(f32[8,6]{1,0:T(8,128)S(1)} %slice.535) | copy-start | bytes 580
  58.7 95.8 %copy-start.230 = (f32[4,6]{1,0:T(4,128)}, f32[4,6]{1,0:T(4,128)S(1)}, u32[]{:S(2)}) copy-start(f32[4,6]{1,0:T(4,128)S(1)} %slice.541) | copy-start | bytes 292
  61.4 189.5 %copy-start.204 = (f32[8,6]{1,0:T(8,128)}, f32[8,6]{1,0:T(8,128)S(1)}, u32[]{:S(2)}) copy-start(f32[8,6]{1,0:T(8,128)S(1)} %slice.492) | copy-start | bytes 580
  68.2 55.8 %copy-start.35 = (f32[2048,128]{0,1:T(8,128)}, f32[2048,128]{0,1:T(8,128)S(1)}, u32[]{:S(2)}) copy-start(f32[2048,128]{0,1:T(8,128)S(1)} %fusion.335) | copy-start | bytes 3145732
  71.5 49.1 %collective-permute-start = (f32[3,512]{0,1:T(8,128)S(1)}, f32[3,512]{0,1:T(8,128)S(1)}, u32[]{:S(2)}, u32[]{:S(2)}) collective-permute-start(f32[3,512]{0,1:T(8,128)S(1)} %fusion.234), channel_id=1, source_target_pairs={{0,4},{4,8},{8,12},{12,16},{16,20},{20,24},{24,28},{1,5},{5,9},{9,... | collective-permute-start | bytes 18440 | tf_op jit(solution)/shard_map/ppermute | solution.py:18
  75.2 48.8 %copy-start.177 = (f32[16,128,6]{1,0,2:T(8,128)}, f32[16,128,6]{1,0,2:T(8,128)S(1)}, u32[]{:S(2)}) copy-start(f32[16,128,6]{1,0,2:T(8,128)S(1)} %get-tuple-element.802) | copy-start | bytes 147460
  75.3 48.6 %copy-start.175 = (f32[16,128,6]{1,0,2:T(8,128)}, f32[16,128,6]{1,0,2:T(8,128)S(1)}, u32[]{:S(2)}) copy-start(f32[16,128,6]{1,0,2:T(8,128)S(1)} %get-tuple-element.799) | copy-start | bytes 147460
  96.6 51.4 %copy-start.161 = (f32[2048,1,6]{0,2,1:T(8,128)}, f32[2048,1,6]{0,2,1:T(8,128)S(1)}, u32[]{:S(2)}) copy-start(f32[2048,1,6]{0,2,1:T(8,128)S(1)} %rev.42) | copy-start | bytes 147460
  101.8 46.3 %copy-start.155 = (f32[16,128,6]{1,2,0:T(8,128)}, f32[16,128,6]{1,2,0:T(8,128)S(1)}, u32[]{:S(2)}) copy-start(f32[16,128,6]{1,2,0:T(8,128)S(1)} %copy.604) | copy-start | bytes 147460
  323.9 26.0 %slice-start.2 = ((f32[16,6,64,64]{2,3,1,0:T(8,128)}), f32[1,6,64,64]{2,3,1,0:T(8,128)S(1)}, s32[]{:S(2)}) async-start(f32[16,6,64,64]{2,3,1,0:T(8,128)} %copy-done.26), calls=%async_computation.12 | async-start | bytes 393216 | tf_op jit(solution)/shard_map/jvp()/slice | solution.py:132
  347.2 81.7 %copy-start.37 = (f32[2048,64]{0,1:T(8,128)}, f32[2048,64]{0,1:T(8,128)S(1)}, u32[]{:S(2)}) copy-start(f32[2048,64]{0,1:T(8,128)S(1)} %rev.45) | copy-start | bytes 1572868
  352.7 24.4 %slice-start.6 = ((f32[15,6,64,64]{2,3,1,0:T(8,128)}), f32[1,6,64,64]{2,3,1,0:T(8,128)S(1)}, s32[]{:S(2)}) async-start(f32[15,6,64,64]{2,3,1,0:T(8,128)} %pad.989), calls=%async_computation.16 | async-start | bytes 393216 | tf_op jit(solution)/shard_map/jvp()/slice | solution.py:141
  775.8 27.6 %copy-start.13 = (f32[48,8,16,128]{3,2,1,0:T(8,128)}, f32[48,8,16,128]{3,2,1,0:T(8,128)S(1)}, u32[]{:S(2)}) copy-start(f32[48,8,16,128]{3,2,1,0:T(8,128)S(1)} %copy.739) | copy-start | bytes 9437188
  996.2 24.4 %copy-start.95 = (f32[7,6,64,64]{2,3,1,0:T(8,128)S(1)}, f32[7,6,64,64]{2,3,1,0:T(8,128)}, u32[]{:S(2)}) copy-start(f32[7,6,64,64]{2,3,1,0:T(8,128)} %get-tuple-element.745) | copy-start | bytes 2064388
  1165.4 29.0 %copy-start.249 = (f32[8,6]{1,0:T(8,128)S(1)}, f32[8,6]{1,0:T(8,128)}, u32[]{:S(2)}) copy-start(f32[8,6]{1,0:T(8,128)} %copy-done.248) | copy-start | bytes 580
  1165.5 29.0 %copy-start.282 = (f32[8,6]{1,0:T(8,128)S(1)}, f32[8,6]{1,0:T(8,128)}, u32[]{:S(2)}) copy-start(f32[8,6]{1,0:T(8,128)} %get-tuple-element.700) | copy-start | bytes 580
  1165.5 29.0 %copy-start.287 = (f32[8,6]{1,0:T(8,128)S(1)}, f32[8,6]{1,0:T(8,128)}, u32[]{:S(2)}) copy-start(f32[8,6]{1,0:T(8,128)} %pad.596) | copy-start | bytes 580
  1165.5 29.0 %copy-start.288 = (f32[8,6]{1,0:T(8,128)S(1)}, f32[8,6]{1,0:T(8,128)}, u32[]{:S(2)}) copy-start(f32[8,6]{1,0:T(8,128)} %pad.611) | copy-start | bytes 580
  1165.5 29.1 %copy-start.121 = (f32[16,128,6]{1,0,2:T(8,128)S(1)}, f32[16,128,6]{1,0,2:T(8,128)}, u32[]{:S(2)}) copy-start(f32[16,128,6]{1,0,2:T(8,128)} %copy-done.120) | copy-start | bytes 147460
  1165.5 29.1 %copy-start.201 = (f32[16,6]{0,1:T(8,128)S(1)}, f32[16,6]{0,1:T(8,128)}, u32[]{:S(2)}) copy-start(f32[16,6]{0,1:T(8,128)} %copy-done.200) | copy-start | bytes 1156
  1165.5 29.1 %copy-start.261 = (pred[16,128]{1,0:T(8,128)(4,1)S(1)}, pred[16,128]{1,0:T(8,128)(4,1)}, u32[]{:S(2)}) copy-start(pred[16,128]{1,0:T(8,128)(4,1)} %copy-done.260) | copy-start | bytes 6148
  1165.5 29.4 %copy-start.215 = (f32[16,6]{1,0:T(8,128)S(1)}, f32[16,6]{1,0:T(8,128)}, u32[]{:S(2)}) copy-start(f32[16,6]{1,0:T(8,128)} %copy-done.214) | copy-start | bytes 1156
  1165.5 29.3 %copy-start.264 = (f32[16,6]{1,0:T(8,128)S(1)}, f32[16,6]{1,0:T(8,128)}, u32[]{:S(2)}) copy-start(f32[16,6]{1,0:T(8,128)} %pad.590) | copy-start | bytes 1156
  1165.5 29.3 %copy-start.321 = (f32[16]{0:T(128)S(1)}, f32[16]{0:T(128)}, u32[]{:S(2)}) copy-start(f32[16]{0:T(128)} %copy-done.320) | copy-start | bytes 196
  1165.6 29.6 %copy-start.176 = (f32[16,128,6]{1,0,2:T(8,128)S(1)}, f32[16,128,6]{1,0,2:T(8,128)}, u32[]{:S(2)}) copy-start(f32[16,128,6]{1,0,2:T(8,128)} %copy-done.175) | copy-start | bytes 147460
  1166.1 28.4 %slice-start.9 = ((f32[4,6]{1,0:T(4,128)}), f32[1,6]{1,0:T(1,128)S(1)}, s32[]{:S(2)}) async-start(f32[4,6]{1,0:T(4,128)} %copy-done.310), calls=%async_computation.19 | async-start | bytes 1024 | tf_op jit(solution)/shard_map/transpose(jvp())/split | solution.py:132
  1166.1 29.5 %copy-start.180 = (f32[16,1,6]{1,0,2:T(8,128)S(1)}, f32[16,1,6]{1,0,2:T(8,128)}, u32[]{:S(2)}) copy-start(f32[16,1,6]{1,0,2:T(8,128)} %copy-done.179) | copy-start | bytes 1156
  1166.1 30.7 %copy-start.185 = (f32[16,128,6]{1,2,0:T(8,128)S(1)}, f32[16,128,6]{1,2,0:T(8,128)}, u32[]{:S(2)}) copy-start(f32[16,128,6]{1,2,0:T(8,128)} %multiply_reduce_fusion.12) | copy-start | bytes 147460
  1166.1 30.7 %copy-start.211 = (f32[16,128]{1,0:T(8,128)S(1)}, f32[16,128]{1,0:T(8,128)}, u32[]{:S(2)}) copy-start(f32[16,128]{1,0:T(8,128)} %copy-done.210) | copy-start | bytes 24580
  1166.1 30.6 %copy-start.226 = (f32[16,6,128]{2,1,0:T(8,128)S(1)}, f32[16,6,128]{2,1,0:T(8,128)}, u32[]{:S(2)}) copy-start(f32[16,6,128]{2,1,0:T(8,128)} %get-tuple-element.613) | copy-start | bytes 147460
  1166.2 30.6 %copy-start.253 = (f32[16,6]{0,1:T(8,128)S(1)}, f32[16,6]{0,1:T(8,128)}, u32[]{:S(2)}) copy-start(f32[16,6]{0,1:T(8,128)} %copy-done.252) | copy-start | bytes 1156
  1199.2 21.7 %collective-permute-start.1 = (f32[3,512]{0,1:T(8,128)S(1)}, f32[3,512]{0,1:T(8,128)S(1)}, u32[]{:S(2)}, u32[]{:S(2)}) collective-permute-start(f32[3,512]{0,1:T(8,128)S(1)} %pad_add_fusion.15), channel_id=1, source_target_pairs={{4,0},{8,4},{12,8},{16,12},{20,16},{24,20},{28,24},{5,1},{9,5},{13... | collective-permute-start | bytes 18440 | tf_op jit(solution)/shard_map/ppermute | solution.py:18
  1222.2 28.0 %copy-start.101 = (f32[16,128,6]{2,0,1:T(8,128)S(1)}, f32[16,128,6]{2,0,1:T(8,128)}, u32[]{:S(2)}) copy-start(f32[16,128,6]{2,0,1:T(8,128)} %fusion.330) | copy-start | bytes 147460
  1226.6 24.5 %copy-start.259 = (bf16[2,768,6]{1,0,2:T(2,128)(2,1)S(1)}, bf16[2,768,6]{1,0,2:T(2,128)(2,1)}, u32[]{:S(2)}) copy-start(bf16[2,768,6]{1,0,2:T(2,128)(2,1)} %param.31) | copy-start | bytes 55300
  1226.6 98.4 %reduce-scatter.6.cloned.1.call-start = ((), (), s32[]{:S(2)}) async-start(), calls=%async_computation.6 | async-start | bytes 7864320 | tf_op jit(solution)/shard_map/reduce_scatter | solution.py:317
  1259.6 119.2 %reduce-scatter.4.cloned.1.call-start = ((), (), s32[]{:S(2)}) async-start(), calls=%async_computation.4 | async-start | bytes 7864320 | tf_op jit(solution)/shard_map/reduce_scatter | solution.py:257
  1267.2 245.6 %all-reduce.126.cloned.1.call-start = ((), (), s32[]{:S(2)}) async-start(), calls=%async_computation.8 | async-start | bytes 786432 | tf_op jit(solution)/shard_map/psum | solution.py:359
  1277.7 379.4 %all-reduce.128.cloned.1.call-start = ((), (), s32[]{:S(2)}) async-start(), calls=%async_computation.9 | async-start | bytes 7077888 | tf_op jit(solution)/shard_map/psum | solution.py:345
  1285.0 40.1 %copy-start.62 = (bf16[512,768]{1,0:T(8,128)(2,1)S(1)}, bf16[512,768]{1,0:T(8,128)(2,1)}, u32[]{:S(2)}) copy-start(bf16[512,768]{1,0:T(8,128)(2,1)} %param.26) | copy-start | bytes 2359300
  1285.0 40.1 %copy-start.146 = (f32[512,128]{0,1:T(8,128)S(1)}, f32[512,128]{0,1:T(8,128)}, u32[]{:S(2)}) copy-start(f32[512,128]{0,1:T(8,128)} %reduce-scatter.8.cloned.1.call-done) | copy-start | bytes 786436
  1285.0 40.1 %copy-start.148 = (bf16[768,128]{1,0:T(8,128)(2,1)S(1)}, bf16[768,128]{1,0:T(8,128)(2,1)}, u32[]{:S(2)}) copy-start(bf16[768,128]{1,0:T(8,128)(2,1)} %param.30) | copy-start | bytes 589828
  1285.0 40.1 %copy-start.243 = (f32[768]{0:T(1024)S(1)}, f32[768]{0:T(1024)}, u32[]{:S(2)}) copy-start(f32[768]{0:T(1024)} %param.27) | copy-start | bytes 9220
  1285.0 40.1 %copy-start.257 = (f32[512]{0:T(512)S(1)}, f32[512]{0:T(512)}, u32[]{:S(2)}) copy-start(f32[512]{0:T(512)} %copy-done.256) | copy-start | bytes 6148
  1288.3 90.5 %copy-start.305 = (f32[512]{0:T(512)S(1)}, f32[512]{0:T(512)}, u32[]{:S(2)}) copy-start(f32[512]{0:T(512)} %get-tuple-element.835) | copy-start | bytes 6148
  1325.1 53.7 %copy-start.91 = (f32[512,768]{1,0:T(8,128)S(1)}, f32[512,768]{1,0:T(8,128)}, u32[]{:S(2)}) copy-start(f32[512,768]{1,0:T(8,128)} %reduce-scatter.6.cloned.1.call-done) | copy-start | bytes 4718596
  (293 other events, 2386.6 us)
Sparse Core Ops, SparseCore 0:
  12.3 31.2 all-gather.6
  45.1 28.5 all-gather.8
  1226.7 24.0 reduce-scatter.7
  1259.7 57.5 reduce-scatter.5
  1319.7 59.0 reduce-scatter.3
  1385.4 127.4 all-reduce.125
  1517.8 139.2 all-reduce.127
where the time goes:
time: 1700 us; the launch traced here: 1670 us
  local copies, waits for them, and re-layouts  558 us (33%)
  waiting for transfers between devices  315 us (19%)
  blocking collectives  269 us (16%)
  other arithmetic  268 us (16%)
  matrix products  235 us (14%)
  between operations  18.8 us (1%)
    pad x62, local copies, waits for them, and re-layouts, block_parts(): lax.associative_scan(link_states, (block_gates, block_states), axis=0)  327 us
    psum x1, waiting for transfers between devices, per_device(): lax.psum((grad_proj_gate, grad_proj_value, grad_proj_step, grad_proj_out,...  144 us
    psum x1, waiting for transfers between devices, per_device(): lax.psum((grad_proj_state, grad_kernel[:, local_width:], grad_input_gain)...  130 us
    unnamed x709, local copies, waits for them, and re-layouts  96.2 us
    all_gather x3, blocking collectives, carried_in(): everything = jax.tree.map(lambda part: lax.all_gather(part, axis), array)  94.9 us
    dot_general x6, matrix products, block_parts(): jnp.einsum('chts,cshp->cthp', decays * scores[:, None], weighted, precisi...  81.9 us
    all_gather x2, blocking collectives, entering_2(): lax.all_gather(a.astype(kind), axis)  49.9 us
    all_gather x1, blocking collectives, prefix(): lax.all_gather(part.astype(kind), axis)  37.3 us
  transfers between devices with their start and end apart: 9, of which 4 were waited for; matrix products, arithmetic and copies ran while one was open for 29% of the time, Pallas kernels for 0%

commit v1 on v0

v1 whole, which is shorter than its diff:
```python
from functools import partial

import jax
import jax.numpy as jnp
from jax import lax
from jax.experimental import pallas as pl
from jax.experimental.pallas import tpu as pltpu
from jax.sharding import PartitionSpec as P

SPAN = 128
HDIM = 64
LANES = 128
LONGEST = 4096
EPSILON = 1e-05
TINY = 1e-30
F32 = jnp.float32
BF16 = jnp.bfloat16
BLOCK = 256


def mm(a, b):
    return jnp.dot(a, b, preferred_element_type=F32)


def mm_nt(a, b):
    return lax.dot_general(a, b, (((1,), (1,)), ((), ())), preferred_element_type=F32)


def mm_tn(a, b):
    return lax.dot_general(a, b, (((0,), (0,)), ((), ())), preferred_element_type=F32)


def exact(a, b):
    return jnp.dot(a, b, precision=lax.Precision.HIGHEST, preferred_element_type=F32)


def exact_tn(a, b):
    return lax.dot_general(
        a, b, (((0,), (0,)), ((), ())), precision=lax.Precision.HIGHEST, preferred_element_type=F32
    )


def halves(v):
    high = v.astype(BF16)
    return high, (v - high.astype(F32)).astype(BF16)


def spread(v, ex):
    high, low = halves(v)
    return mm(high, ex) + mm(low, ex)


def gather_heads(v, ex):
    high, low = halves(v)
    return mm_nt(high, ex) + mm_nt(low, ex)


def sigmoid(v):
    return 1.0 / (1.0 + jnp.exp(-v))


def softplus(v):
    return jnp.maximum(v, 0.0) + jnp.log1p(jnp.exp(-jnp.abs(v)))


def iota(shape, dim):
    return lax.broadcasted_iota(jnp.int32, shape, dim)


def groups(width):
    found = []
    for at in range(0, width, LANES):
        wide = min(LANES, width - at)
        found.append((at, wide, [(at + k) // HDIM for k in range(0, wide, HDIM)]))
    return found


def stacked(v, wide):
    if wide == HDIM:
        return v
    first = iota(v.shape, 1) < HDIM
    zero = jnp.zeros_like(v)
    return jnp.concatenate([jnp.where(first, v, zero), jnp.where(first, zero, v)], axis=0)


def activated(conv, live):
    return conv * sigmoid(conv) * live


def front_kernel(
    nh,
    x_ref,
    halo_ref,
    gain_ref,
    wg_ref,
    wsv_ref,
    wst_ref,
    wstr_ref,
    pcol_ref,
    prow_ref,
    taps_ref,
    cols_ref,
    gm_ref,
    exf_ref,
    exb_ref,
    tril_ref,
    triu_ref,
    normed_ref,
    gate_ref,
    conv_ref,
    uv_ref,
    uvh_ref,
    z_ref,
    cc_ref,
    rowa_ref,
    rowp_ref,
    tot_ref,
    sf_ref,
    rb_ref,
    gf_ref,
    gb_ref,
    gfpre_ref,
    gbsuf_ref,
    gfsuf_ref,
    gbpre_ref,
    fmsg_ref,
    rmsg_ref,
    ubuf,
    state,
    incb,
):
    i = pl.program_id(0)
    tb = x_ref.shape[0]
    per = tb // SPAN
    nc = rb_ref.shape[0]

    def norm(x):
        xf = x.astype(F32)
        s = lax.rsqrt(jnp.mean(xf * xf, axis=1, keepdims=True) + EPSILON)
        return (xf * s * gain_ref[0:1, :]).astype(BF16)

    @pl.when(i == 0)
    def _():
        before = mm(norm(halo_ref[...]), wsv_ref[...])
        ubuf[0:8, :] = before
        uvh_ref[...] = before
        state[...] = jnp.zeros_like(state)

    @pl.when(i > 0)
    def _():
        ubuf[0:8, :] = ubuf[tb : tb + 8, :]

    nb = norm(x_ref[...])
    normed_ref[...] = nb
    gate_ref[...] = mm(nb, wg_ref[...])
    uv = mm(nb, wsv_ref[...])
    ubuf[8 : 8 + tb, :] = uv
    uv_ref[...] = uv.astype(BF16)
    conv = taps_ref[0:1, :] * uv
    for k in (1, 2, 3):
        conv = conv + taps_ref[k : k + 1, :] * ubuf[8 - k : 8 - k + tb, :] * cols_ref[:, k - 1 : k]
    conv_ref[...] = conv
    act = activated(conv, cols_ref[:, 3:4])
    z_all = mm(nb, wst_ref[...]) + pcol_ref[0:1, :]
    z_ref[...] = z_all
    zr_all = mm_nt(wstr_ref[...], nb)
    forward = iota((SPAN, LANES), 1) < nh
    forward_row = iota((16, SPAN), 0) < nh
    for j in range(per):
        rows = slice(j * SPAN, (j + 1) * SPAN)
        dt = softplus(z_all[rows])
        a = -dt * pcol_ref[1:2, :]
        total = exact(tril_ref[...], a)
        tot = total[SPAN - 1 : SPAN, :]
        cc = jnp.where(forward, total, total - a)
        cc_ref[rows, :] = cc
        tot8 = jnp.broadcast_to(tot, (8, LANES))
        tot_ref[j * 8 : j * 8 + 8, :] = tot8
        dtr = softplus(zr_all[:, rows] + prow_ref[:, :SPAN])
        ar = -dtr * prow_ref[:, SPAN:]
        run = exact(ar, triu_ref[...])
        rowa = jnp.where(forward_row, run, run - ar)
        ldt = jnp.log(jnp.maximum(dtr, TINY))
        rowa_ref[:, rows] = rowa
        rowp_ref[:, rows] = jnp.where(forward_row, rowa - ldt, rowa + ldt)
        gate8 = jnp.exp(tot8) * gm_ref[j * 8 : j * 8 + 8, :]
        gf = spread(gate8, exf_ref[...])
        gb = spread(gate8, exb_ref[...])
        keep = cols_ref[rows, :]
        w = (
            jnp.exp(jnp.where(forward, tot - cc, cc))
            * jnp.where(forward, keep[:, 6:7], keep[:, 8:9])
            * dt
        )
        x = act[rows, LANES:]
        b = act[rows, :HDIM].astype(BF16)
        c = i * per + j
        sf_ref[j] = state[...]
        state[...] = state[...] * gf[0:1, :] + mm_tn(b, (x * spread(w, exf_ref[...])).astype(BF16))
        incb[c] = mm_tn(b, (x * spread(w, exb_ref[...])).astype(BF16))
        gf_ref[c] = gf
        gb_ref[c] = gb

    @pl.when(i == pl.num_programs(0) - 1)
    def _():
        fmsg_ref[0:HDIM, :] = state[...]

        def up(c, carry):
            pf, pb = carry
            gfpre_ref[c] = pf
            gbpre_ref[c] = pb
            return pf * gf_ref[c], pb * gb_ref[c]

        one = jnp.ones(gf_ref.shape[1:], F32)
        pf, pb = lax.fori_loop(0, nc, up, (one, one))
        fmsg_ref[HDIM:, :] = pf
        rmsg_ref[HDIM:, :] = pb
        state[...] = jnp.zeros_like(state)

        def down(k, carry):
            c = nc - 1 - k
            pf, pb = carry
            gfsuf_ref[c] = pf
            gbsuf_ref[c] = pb
            rb_ref[c] = state[...]
            gb = gb_ref[c]
            state[...] = state[...] * gb[0:1, :] + incb[c]
            return pf * gf_ref[c], pb * gb

        lax.fori_loop(0, nc, down, (one, one))
        rmsg_ref[0:HDIM, :] = state[...]


def inner_kernel(
    nh,
    conv_ref,
    cols_ref,
    segrow_ref,
    cc_ref,
    rowp_ref,
    skip_ref,
    cot_ref,
    wo_ref,
    y_ref,
    dout_ref,
):
    tb, width = y_ref.shape
    dout_ref[...] = mm_nt(cot_ref[...], wo_ref[...])
    act = activated(conv_ref[...], cols_ref[:, 3:4])
    t_at = iota((SPAN, SPAN), 0)
    s_at = iota((SPAN, SPAN), 1)
    lower = t_at > s_at
    for j in range(tb // SPAN):
        rows = slice(j * SPAN, (j + 1) * SPAN)
        x = act[rows, LANES:]
        bc = act[rows, :LANES]
        b = bc[:, :HDIM].astype(BF16)
        c = pltpu.roll(bc, HDIM, 1)[:, :HDIM].astype(BF16)
        same = cols_ref[rows, 4:5] == segrow_ref[0:1, rows]
        score = jnp.where(same & (t_at != s_at), mm_nt(c, b), 0.0)
        cc = cc_ref[rows, :]
        for at, wide, heads in groups(width):
            xp = x[:, at : at + wide]
            mats = []
            for h in heads:
                gap = jnp.where(
                    lower,
                    cc[:, h : h + 1] - rowp_ref[h : h + 1, rows],
                    rowp_ref[nh + h : nh + h + 1, rows] - cc[:, nh + h : nh + h + 1],
                )
                mats.append((score * jnp.exp(gap)).astype(BF16))
            mats = jnp.concatenate(mats, axis=1) if len(mats) > 1 else mats[0]
            y_ref[rows, at : at + wide] = (
                mm(mats, stacked(xp.astype(BF16), wide)) + skip_ref[0:1, at : at + wide] * xp
            )


def merge_kernel(
    nh,
    conv_ref,
    cols_ref,
    cc_ref,
    tot_ref,
    sf_ref,
    rb_ref,
    gfpre_ref,
    gbsuf_ref,
    sent_ref,
    rent_ref,
    yin_ref,
    gate_ref,
    dout_ref,
    mg_ref,
    exf_ref,
    exb_ref,
    y_ref,
    stat_ref,
    sfull_ref,
    rfull_ref,
):
    tb, width = y_ref.shape
    forward = iota((SPAN, LANES), 1) < nh
    which = iota((8, width), 0)
    sel0 = jnp.where(which == 0, 1.0, 0.0).astype(BF16)
    sel1 = jnp.where(which == 1, 1.0, 0.0).astype(BF16)
    for j in range(tb // SPAN):
        rows = slice(j * SPAN, (j + 1) * SPAN)
        keep = cols_ref[rows, :]
        bc = activated(conv_ref[rows, :LANES], keep[:, 3:4])
        c = pltpu.roll(bc, HDIM, 1)[:, :HDIM].astype(BF16)
        cc = cc_ref[rows, :]
        tot = tot_ref[j * 8 : j * 8 + 1, :]
        w = jnp.exp(jnp.where(forward, cc, tot - cc)) * jnp.where(
            forward, keep[:, 5:6], keep[:, 7:8]
        )
        sfull = (sf_ref[j] + gfpre_ref[j][0:1, :] * sent_ref[...]).astype(BF16)
        rfull = (rb_ref[j] + gbsuf_ref[j][0:1, :] * rent_ref[...]).astype(BF16)
        sfull_ref[j] = sfull
        rfull_ref[j] = rfull
        y = (
            yin_ref[rows, :]
            + mm(c, sfull) * spread(w, exf_ref[...])
            + mm(c, rfull) * spread(w, exb_ref[...])
        )
        y_ref[rows, :] = y
        gate = gate_ref[rows, :]
        g = y * gate * sigmoid(gate)
        high, low = halves(g * g)
        stat = mm_nt(sel0, high) + mm_nt(sel0, low)
        high, low = halves(dout_ref[rows, :] * mg_ref[0:1, :] * g)
        stat_ref[:, rows] = stat + mm_nt(sel1, high) + mm_nt(sel1, low)


def turn_kernel(
    nh,
    inner,
    y_ref,
    gate_ref,
    dout_ref,
    mg_ref,
    stat_ref,
    conv_ref,
    cols_ref,
    cc_ref,
    tot_ref,
    gf_ref,
    gb_ref,
    gtf_ref,
    gtb_ref,
    exf_ref,
    exb_ref,
    eye_ref,
    dy_ref,
    dgate_ref,
    outin_ref,
    gmix_ref,
    gskip_ref,
    dso_ref,
    dro_ref,
    amsg_ref,
    bmsg_ref,
    state,
    incf,
):
    i = pl.program_id(0)
    tb, width = y_ref.shape
    per = tb // SPAN
    nc = dso_ref.shape[0]
    forward = iota((SPAN, LANES), 1) < nh

    @pl.when(i == 0)
    def _():
        gmix_ref[...] = jnp.zeros_like(gmix_ref)
        gskip_ref[...] = jnp.zeros_like(gskip_ref)
        state[...] = jnp.zeros_like(state)

    for j in range(per):
        rows = slice(j * SPAN, (j + 1) * SPAN)
        stats = exact_tn(stat_ref[:, rows], eye_ref[0:8, :])
        q = lax.rsqrt(stats[:, 0:1] * (1.0 / inner) + EPSILON)
        k3 = q * q * q * stats[:, 1:2] * (1.0 / inner)
        y = y_ref[rows, :]
        gate = gate_ref[rows, :]
        sig = sigmoid(gate)
        sg = gate * sig
        g = y * sg
        gq = g * q
        dout = dout_ref[rows, :]
        outin_ref[rows, :] = (gq * mg_ref[0:1, :]).astype(BF16)
        gmix_ref[0:1, :] += jnp.sum(dout * gq, axis=0, keepdims=True)
        dg = dout * mg_ref[0:1, :] * q - g * k3
        dy = dg * sg
        dyb = dy.astype(BF16)
        dy_ref[rows, :] = dyb
        dgate_ref[rows, :] = (dg * y * sig * (1.0 + gate * (1.0 - sig))).astype(BF16)
        keep = cols_ref[rows, :]
        act = activated(conv_ref[rows, :], keep[:, 3:4])
        gskip_ref[0:1, :] += jnp.sum(dy * act[:, LANES:], axis=0, keepdims=True)
        c = pltpu.roll(act[:, :LANES], HDIM, 1)[:, :HDIM].astype(BF16)
        cc = cc_ref[rows, :]
        tot = tot_ref[j * 8 : j * 8 + 1, :]
        w = jnp.exp(jnp.where(forward, cc, tot - cc)) * jnp.where(
            forward, keep[:, 5:6], keep[:, 7:8]
        )
        dyf = dyb.astype(F32)
        at = i * per + j
        incf[at] = mm_tn(c, (dyf * spread(w, exf_ref[...])).astype(BF16))
        dro_ref[j] = state[...]
        state[...] = state[...] * gb_ref[at][0:1, :] + mm_tn(
            c, (dyf * spread(w, exb_ref[...])).astype(BF16)
        )

    @pl.when(i == pl.num_programs(0) - 1)
    def _():
        bmsg_ref[0:HDIM, :] = state[...]
        bmsg_ref[HDIM:, :] = gtb_ref[...]
        amsg_ref[HDIM:, :] = gtf_ref[...]
        state[...] = jnp.zeros_like(state)

        def down(k, _):
            c = nc - 1 - k
            dso_ref[c] = state[...]
            state[...] = state[...] * gf_ref[c][0:1, :] + incf[c]
            return 0

        lax.fori_loop(0, nc, down, 0)
        amsg_ref[0:HDIM, :] = state[...]


def back_kernel(
    nh,
    conv_ref,
    cols_ref,
    halocols_ref,
    segrow_ref,
    cc_ref,
    z_ref,
    rowa_ref,
    tot_ref,
    dy_ref,
    sfull_ref,
    rfull_ref,
    dso_ref,
    dro_ref,
    gfsuf_ref,
    gbpre_ref,
    dsent_ref,
    drent_ref,
    gf_ref,
    gb_ref,
    uv_ref,
    uvh_ref,
    taps_ref,
    skip_ref,
    pcol_ref,
    exf_ref,
    exb_ref,
    tril_ref,
    triu_ref,
    eye_ref,
    dvs_ref,
    dst_ref,
    duh_ref,
    gconv_ref,
    gsmall_ref,
    dbuf,
    hbuf,
):
    i = pl.program_id(0)
    last = pl.num_programs(0) - 1
    tb = conv_ref.shape[0]
    width = conv_ref.shape[1] - LANES
    exf = exf_ref[...]
    exb = exb_ref[...]

    @pl.when(i == 0)
    def _():
        dbuf[tb : tb + 8, :] = jnp.zeros((8, LANES + width), F32)
        gconv_ref[...] = jnp.zeros_like(gconv_ref)
        gsmall_ref[...] = jnp.zeros_like(gsmall_ref)

    s_at = iota((SPAN, SPAN), 0)
    t_at = iota((SPAN, SPAN), 1)
    lower = t_at > s_at
    lane = iota((SPAN, LANES), 1)
    forward = lane < nh
    row16 = iota((16, SPAN), 0)
    front_half = lane < HDIM
    for j in reversed(range(tb // SPAN)):
        rows = slice(j * SPAN, (j + 1) * SPAN)
        keep = cols_ref[rows, :]
        conv = conv_ref[rows, :]
        sig = sigmoid(conv)
        act = conv * sig * keep[:, 3:4]
        xb = act[:, LANES:].astype(BF16)
        x = xb.astype(F32)
        dyb = dy_ref[rows, :]
        dy = dyb.astype(F32)
        bc = act[:, :LANES]
        cb = pltpu.roll(bc, HDIM, 1)
        b = bc[:, :HDIM].astype(BF16)
        c = cb[:, :HDIM].astype(BF16)
        cpad = jnp.where(front_half, cb, 0.0).astype(BF16)
        bpad = jnp.where(front_half, 0.0, cb).astype(BF16)
        within = (keep[:, 4:5] == segrow_ref[0:1, rows]) & (t_at != s_at)
        score = jnp.where(within, mm_nt(b, c), 0.0)
        cc = cc_ref[rows, :]
        z = z_ref[rows, :]
        dt = softplus(z)
        ldt = jnp.log(jnp.maximum(dt, TINY))
        pc = jnp.where(forward, cc - ldt, cc + ldt)
        dscore = jnp.zeros((SPAN, SPAN), F32)
        kc = jnp.zeros((SPAN, LANES), F32)
        qr = jnp.zeros((16, SPAN), F32)
        dx_parts = []
        for at, wide, heads in groups(width):
            dyp = dyb[:, at : at + wide]
            dmats = mm_nt(stacked(xb[:, at : at + wide], wide), dyp)
            mats = []
            for n, h in enumerate(heads):
                dmat = dmats[n * SPAN : (n + 1) * SPAN, :]
                decay = jnp.exp(
                    jnp.where(
                        lower,
                        rowa_ref[h : h + 1, rows] - pc[:, h : h + 1],
                        pc[:, nh + h : nh + h + 1] - rowa_ref[nh + h : nh + h + 1, rows],
                    )
                )
                spot = dmat * decay
                dscore = dscore + spot
                mats.append((score * decay).astype(BF16))
                pull = spot * score
                pull_low = jnp.where(lower, pull, 0.0)
                pull_up = pull - pull_low
                qr = jnp.where(row16 == h, jnp.sum(pull_low, axis=0, keepdims=True), qr)
                qr = jnp.where(row16 == nh + h, jnp.sum(pull_up, axis=0, keepdims=True), qr)
                kc = jnp.where(lane == h, jnp.sum(pull_low, axis=1, keepdims=True), kc)
                kc = jnp.where(lane == nh + h, jnp.sum(pull_up, axis=1, keepdims=True), kc)
            mats = jnp.concatenate(mats, axis=1) if len(mats) > 1 else mats[0]
            dx_parts.append(mm(mats, stacked(dyp, wide)))
        dscore = jnp.where(within, dscore, 0.0).astype(BF16)
        dbc = mm(dscore, cpad) + mm_tn(dscore, bpad)
        dx = jnp.concatenate(dx_parts, axis=1) if len(dx_parts) > 1 else dx_parts[0]

        tot = tot_ref[j * 8 : j * 8 + 1, :]
        to = jnp.exp(jnp.where(forward, tot - cc, cc)) * dt
        to = to * jnp.where(forward, keep[:, 6:7], keep[:, 8:9])
        fro = jnp.exp(jnp.where(forward, cc, tot - cc)) * jnp.where(
            forward, keep[:, 5:6], keep[:, 7:8]
        )
        dsfull = dso_ref[j] + gfsuf_ref[j][0:1, :] * dsent_ref[...]
        drfull = dro_ref[j] + gbpre_ref[j][0:1, :] * drent_ref[...]
        carried = jnp.zeros((SPAN, LANES), F32)
        leaving = jnp.zeros((SPAN, LANES), F32)
        through = jnp.zeros((8, LANES), F32)
        for ex, held, dheld, gates in (
            (exf, sfull_ref[j], dsfull, gf_ref[j]),
            (exb, rfull_ref[j], drfull, gb_ref[j]),
        ):
            to_wide = spread(to, ex)
            fro_wide = spread(fro, ex)
            dheld_low = dheld.astype(BF16)
            nothing = jnp.zeros_like(held)
            dbc = dbc + mm_nt(
                (x * to_wide).astype(BF16), jnp.concatenate([dheld_low, nothing], axis=0)
            )
            dbc = dbc + mm_nt(
                (dy * fro_wide).astype(BF16), jnp.concatenate([nothing, held], axis=0)
            )
            flow = mm(b, dheld_low) * to_wide
            dx = dx + flow
            carried = carried + gather_heads(dy * (mm(c, held) * fro_wide), ex)
            leaving = leaving + gather_heads(x * flow, ex)
            product = jnp.sum(dheld * held.astype(F32), axis=0, keepdims=True) * gates
            through = through + gather_heads(product, ex)
        moved = exact_tn(qr, eye_ref[...]) + carried - kc
        before = exact(tril_ref[...], jnp.where(forward, leaving, moved))
        after = exact(triu_ref[...], jnp.where(forward, moved, leaving))
        dlog = before + after - leaving + through[0:1, :]
        sigz = sigmoid(z)
        rate = pcol_ref[1:2, :]
        dstep = (kc + leaving) * (sigz / jnp.maximum(dt, TINY)) - dlog * rate * sigz
        dst_ref[rows, :] = dstep.astype(BF16)
        gsmall_ref[0:1, :] += jnp.sum(dstep, axis=0, keepdims=True)
        gsmall_ref[1:2, :] += jnp.sum(-dlog * dt * rate, axis=0, keepdims=True)
        dact = jnp.concatenate([dbc, dx + skip_ref[0:1, :] * dy], axis=1)
        dbuf[rows, :] = dact * keep[:, 3:4] * sig * (1.0 + conv * (1.0 - sig))

    dconv = dbuf[0:tb, :]
    uv = uv_ref[...].astype(F32)
    du = taps_ref[0:1, :] * dconv
    gconv_ref[0:1, :] += jnp.sum(uv * dconv, axis=0, keepdims=True)
    for k in (1, 2, 3):
        shifted = dbuf[k : k + tb, :] * cols_ref[:, 8 + k : 9 + k]
        du = du + taps_ref[k : k + 1, :] * shifted
        gconv_ref[k : k + 1, :] += jnp.sum(uv * shifted, axis=0, keepdims=True)
    dvs_ref[...] = du.astype(BF16)
    edge = dbuf[0:8, :]
    dbuf[tb : tb + 8, :] = edge

    @pl.when(i == last)
    def _():
        hbuf[0:8, :] = jnp.zeros_like(edge)
        hbuf[8:16, :] = edge
        duh = jnp.zeros_like(edge)
        for k in (1, 2, 3):
            shifted = hbuf[k : k + 8, :] * halocols_ref[:, k - 1 : k]
            duh = duh + taps_ref[k : k + 1, :] * shifted
            gconv_ref[k : k + 1, :] += jnp.sum(uvh_ref[...] * shifted, axis=0, keepdims=True)
        duh_ref[...] = duh


def whole(shape):
    return pl.BlockSpec(shape, lambda i: (0,) * len(shape))


def row_block(rows, width):
    return pl.BlockSpec((rows, width), lambda i: (i, 0))


def lane_block(rows, width):
    return pl.BlockSpec((rows, width), lambda i: (0, i))


def chunk_block(per, rows, width):
    return pl.BlockSpec((per, rows, width), lambda i: (i, 0, 0))


def sds(shape, dtype):
    return jax.ShapeDtypeStruct(shape, dtype)


def call(kernel, name, grid, ins, outs, scratch, flops, operands):
    moved = sum(o.size * o.dtype.itemsize for o in operands)
    moved += sum(s.size * s.dtype.itemsize for _, s in outs)
    return pl.pallas_call(
        kernel,
        name=name,
        grid=(grid,),
        in_specs=ins,
        out_specs=[spec for spec, _ in outs],
        out_shape=[shape for _, shape in outs],
        scratch_shapes=scratch,
        compiler_params=pltpu.CompilerParams(
            dimension_semantics=("arbitrary",), vmem_limit_bytes=56 * 1024 * 1024
        ),
        cost_estimate=pl.CostEstimate(
            flops=int(flops), bytes_accessed=int(moved), transcendentals=0
        ),
    )(*operands)


def shifted_in(array, axis, by):
    length = lax.axis_size(axis)
    pairs = [(i, i + by) for i in range(length) if 0 <= i + by < length]
    return lax.ppermute(array, axis, pairs)


def entering(message, hops, sign):
    parts = [shifted_in(message, "seq", sign * d) for d in range(1, hops + 1)]
    state = parts[-1][:HDIM]
    for part in reversed(parts[:-1]):
        state = part[:HDIM] + part[HDIM : HDIM + 1] * state
    return state


def sum_over(array, axis):
    size = lax.axis_size(axis)
    result = array
    for k in range(1, size):
        result = result + lax.ppermute(array, axis, [(i, i ^ k) for i in range(size)])
    return result


def per_device(
    tokens,
    input_gain,
    proj_gate,
    proj_value,
    proj_state,
    proj_step,
    step_bias,
    decay_log,
    conv_value,
    conv_state,
    skip_gain,
    mixer_gain,
    proj_out,
    doc_lengths,
    pad_mask,
    cotangent,
):
    head_devices = lax.axis_size("head")
    length = pad_mask.shape[0]
    model = tokens.shape[1]
    width = proj_gate.shape[1]
    nh = proj_step.shape[2]
    inner = width * head_devices
    nc = length // SPAN
    tb = BLOCK
    per = tb // SPAN
    grid = length // tb
    wide = LANES + width
    hops = -(-(LONGEST - 1) // length)
    seq_index = lax.axis_index("seq")
    first_place = seq_index * length
    all_tokens = length * lax.axis_size("seq")

    gathered = lax.all_gather(tokens, "head", axis=0, tiled=True)
    cot_all = lax.all_gather(cotangent, "head", axis=0, tiled=True)
    halo = shifted_in(gathered[length - 8 :], "seq", 1)

    offsets = jnp.cumsum(doc_lengths) - doc_lengths
    offsets = jnp.concatenate([offsets, jnp.full((1,), all_tokens, offsets.dtype)])
    places = first_place - 8 + jnp.arange(length + 16, dtype=jnp.int32)
    segs = jnp.sum((offsets[None, :] <= places[:, None]).astype(jnp.int32), axis=1).astype(F32)
    seg = segs[8 : 8 + length]
    by_chunk = seg.reshape(nc, SPAN)
    chunk_first = by_chunk[:, 0]
    chunk_last = by_chunk[:, -1]
    prev_last = jnp.concatenate([segs[7:8], chunk_last[:-1]])
    next_first = jnp.concatenate([chunk_first[1:], segs[8 + length : 9 + length]])
    live = pad_mask.astype(F32)

    def tap_mask(at, k):
        return (seg == segs[8 + at : 8 + at + length]).astype(F32)

    def edge_mask(edge):
        return (by_chunk == edge[:, None]).astype(F32).reshape(length)

    zeros = jnp.zeros((length,), F32)
    cols = jnp.stack(
        [tap_mask(-k, k) for k in (1, 2, 3)]
        + [live, seg]
        + [edge_mask(prev_last), edge_mask(chunk_last), edge_mask(next_first), edge_mask(chunk_first)]
        + [tap_mask(k, k) for k in (1, 2, 3)]
        + [zeros] * 4,
        axis=1,
    )
    halo_cols = jnp.stack(
        [(segs[:8] == segs[k : 8 + k]).astype(F32) for k in (1, 2, 3)] + [jnp.zeros((8,), F32)] * 13,
        axis=1,
    )
    seg_row = jnp.broadcast_to(seg[None, :], (8, length))
    lanes = jnp.arange(LANES)
    gate_mask = jnp.where(
        lanes[None, :] < nh,
        (chunk_last == prev_last).astype(F32)[:, None],
        (chunk_first == next_first).astype(F32)[:, None],
    )
    gate_mask = jnp.broadcast_to(gate_mask[:, None, :], (nc, 8, LANES)).reshape(nc * 8, LANES)
    head_of = jnp.arange(width)[None, :] // HDIM
    exf = (lanes[:, None] == head_of).astype(BF16)
    exb = (lanes[:, None] == head_of + nh).astype(BF16)
    at = jnp.arange(SPAN)
    tril = (at[:, None] >= at[None, :]).astype(F32)
    triu = (at[:, None] <= at[None, :]).astype(F32)
    eye = (jnp.arange(16)[:, None] == lanes[None, :]).astype(F32)

    rate = jnp.exp(decay_log)
    bias_line = jnp.concatenate([step_bias[0], step_bias[1]])
    rate_line = jnp.concatenate([rate, rate])
    pcol = jnp.zeros((8, LANES), F32)
    pcol = pcol.at[0, : 2 * nh].set(bias_line).at[1, : 2 * nh].set(rate_line)
    pad16 = jnp.zeros((16 - 2 * nh,), F32)
    prow = jnp.concatenate(
        [
            jnp.broadcast_to(jnp.concatenate([bias_line, pad16])[:, None], (16, SPAN)),
            jnp.broadcast_to(jnp.concatenate([rate_line, pad16])[:, None], (16, SPAN)),
        ],
        axis=1,
    )
    steps = jnp.concatenate([proj_step[0], proj_step[1]], axis=1)
    wst = jnp.pad(steps, ((0, 0), (0, LANES - 2 * nh)))
    wstr = jnp.pad(steps.T, ((0, 16 - 2 * nh), (0, 0)))
    wsv = jnp.concatenate([proj_state, proj_value], axis=1)
    taps = jnp.pad(jnp.concatenate([conv_state, conv_value], axis=1), ((0, 4), (0, 0)))
    gain = jnp.broadcast_to(input_gain[None, :], (8, model))
    mg = jnp.broadcast_to(mixer_gain[None, :], (8, width))
    skip = jnp.broadcast_to(jnp.repeat(skip_gain, HDIM)[None, :], (8, width))

    rows = partial(row_block, tb)
    states = sds((nc, HDIM, width), F32)
    gates = sds((nc, 8, width), F32)
    message = sds((HDIM + 8, width), F32)
    state_block = chunk_block(per, HDIM, width)
    gate_block = chunk_block(per, 8, width)
    tot_block = row_block(per * 8, LANES)

    (
        normed,
        gate_in,
        conv,
        uv,
        uvh,
        z,
        cc,
        rowa,
        rowp,
        tot,
        sf,
        rb,
        gf,
        gb,
        gfpre,
        gbsuf,
        gfsuf,
        gbpre,
        fmsg,
        rmsg,
    ) = call(
        partial(front_kernel, nh),
        "front",
        grid,
        [
            rows(model),
            whole((8, model)),
            whole((8, model)),
            whole((model, width)),
            whole((model, wide)),
            whole((model, LANES)),
            whole((16, model)),
            whole((8, LANES)),
            whole((16, 2 * SPAN)),
            whole((8, wide)),
            rows(16),
            tot_block,
            whole((LANES, width)),
            whole((LANES, width)),
            whole((SPAN, SPAN)),
            whole((SPAN, SPAN)),
        ],
        [
            (rows(model), sds((length, model), BF16)),
            (rows(width), sds((length, width), F32)),
            (rows(wide), sds((length, wide), F32)),
            (rows(wide), sds((length, wide), BF16)),
            (whole((8, wide)), sds((8, wide), F32)),
            (rows(LANES), sds((length, LANES), F32)),
            (rows(LANES), sds((length, LANES), F32)),
            (lane_block(16, tb), sds((16, length), F32)),
            (lane_block(16, tb), sds((16, length), F32)),
            (tot_block, sds((nc * 8, LANES), F32)),
            (state_block, states),
            (whole(states.shape), states),
            (whole(gates.shape), gates),
            (whole(gates.shape), gates),
            (whole(gates.shape), gates),
            (whole(gates.shape), gates),
            (whole(gates.shape), gates),
            (whole(gates.shape), gates),
            (whole(message.shape), message),
            (whole(message.shape), message),
        ],
        [
            pltpu.VMEM((tb + 8, wide), F32),
            pltpu.VMEM((HDIM, width), F32),
            pltpu.VMEM((nc, HDIM, width), F32),
        ],
        2 * length * model * (2 * width + 3 * LANES),
        [
            gathered,
            halo,
            gain,
            proj_gate,
            wsv,
            wst,
            wstr,
            pcol,
            prow,
            taps,
            cols,
            gate_mask,
            exf,
            exb,
            tril,
            triu,
        ],
    )

    sent = entering(fmsg, hops, 1)
    rent = entering(rmsg, hops, -1)

    yin, dout = call(
        partial(inner_kernel, nh),
        "inner",
        grid,
        [
            rows(wide),
            rows(16),
            lane_block(8, tb),
            rows(LANES),
            lane_block(16, tb),
            whole((8, width)),
            rows(model),
            whole((width, model)),
        ],
        [
            (rows(width), sds((length, width), F32)),
            (rows(width), sds((length, width), F32)),
        ],
        [],
        2 * length * width * (model + 2 * SPAN),
        [conv, cols, seg_row, cc, rowp, skip, cot_all, proj_out],
    )

    y, stat, sfull, rfull = call(
        partial(merge_kernel, nh),
        "merge",
        grid,
        [
            row_block(tb, LANES),
            rows(16),
            rows(LANES),
            tot_block,
            state_block,
            state_block,
            gate_block,
            gate_block,
            whole((HDIM, width)),
            whole((HDIM, width)),
            rows(width),
            rows(width),
            rows(width),
            whole((8, width)),
            whole((LANES, width)),
            whole((LANES, width)),
        ],
        [
            (rows(width), sds((length, width), F32)),
            (lane_block(8, tb), sds((8, length), F32)),
            (state_block, sds((nc, HDIM, width), BF16)),
            (state_block, sds((nc, HDIM, width), BF16)),
        ],
        [],
        2 * length * width * 2 * (HDIM + LANES),
        [conv, cols, cc, tot, sf, rb, gfpre, gbsuf, sent, rent, yin, gate_in, dout, mg, exf, exb],
    )

    stat = sum_over(stat, "head")

    dy, dgate, outin, gmix, gskip, dso, dro, amsg, bmsg = call(
        partial(turn_kernel, nh, inner),
        "turn",
        grid,
        [
            rows(width),
            rows(width),
            rows(width),
            whole((8, width)),
            lane_block(8, tb),
            rows(wide),
            rows(16),
            rows(LANES),
            tot_block,
            whole(gates.shape),
            whole(gates.shape),
            whole((8, width)),
            whole((8, width)),
            whole((LANES, width)),
            whole((LANES, width)),
            whole((16, LANES)),
        ],
        [
            (rows(width), sds((length, width), BF16)),
            (rows(width), sds((length, width), BF16)),
            (rows(width), sds((length, width), BF16)),
            (whole((8, width)), sds((8, width), F32)),
            (whole((8, width)), sds((8, width), F32)),
            (whole(states.shape), states),
            (state_block, states),
            (whole(message.shape), message),
            (whole(message.shape), message),
        ],
        [pltpu.VMEM((HDIM, width), F32), pltpu.VMEM((nc, HDIM, width), F32)],
        2 * length * width * 2 * (HDIM + LANES),
        [
            y,
            gate_in,
            dout,
            mg,
            stat,
            conv,
            cols,
            cc,
            tot,
            gf,
            gb,
            fmsg[HDIM:],
            rmsg[HDIM:],
            exf,
            exb,
            eye,
        ],
    )

    dsent = entering(amsg, hops, -1)
    drent = entering(bmsg, hops, 1)

    back = lambda i: grid - 1 - i

    def rev(spec):
        return pl.BlockSpec(spec.block_shape, lambda i: spec.index_map(back(i)))

    dvs, dst, duh, gconv, gsmall = call(
        partial(back_kernel, nh),
        "back",
        grid,
        [
            rev(rows(wide)),
            rev(rows(16)),
            whole((8, 16)),
            rev(lane_block(8, tb)),
            rev(rows(LANES)),
            rev(rows(LANES)),
            rev(lane_block(16, tb)),
            rev(tot_block),
            rev(rows(width)),
            rev(state_block),
            rev(state_block),
            rev(state_block),
            rev(state_block),
            rev(gate_block),
            rev(gate_block),
            whole((HDIM, width)),
            whole((HDIM, width)),
            rev(gate_block),
            rev(gate_block),
            rev(rows(wide)),
            whole((8, wide)),
            whole((8, wide)),
            whole((8, width)),
            whole((8, LANES)),
            whole((LANES, width)),
            whole((LANES, width)),
            whole((SPAN, SPAN)),
            whole((SPAN, SPAN)),
            whole((16, LANES)),
        ],
        [
            (rev(rows(wide)), sds((length, wide), BF16)),
            (rev(rows(LANES)), sds((length, LANES), BF16)),
            (whole((8, wide)), sds((8, wide), F32)),
            (whole((8, wide)), sds((8, wide), F32)),
            (whole((8, LANES)), sds((8, LANES), F32)),
        ],
        [pltpu.VMEM((tb + 8, wide), F32), pltpu.VMEM((16, wide), F32)],
        2 * length * width * (4 * SPAN + 6 * HDIM + 8 * LANES),
        [
            conv,
            cols,
            halo_cols,
            seg_row,
            cc,
            z,
            rowa,
            tot,
            dy,
            sfull,
            rfull,
            dso,
            dro,
            gfsuf,
            gbpre,
            dsent,
            drent,
            gf,
            gb,
            uv,
            uvh,
            taps,
            skip,
            pcol,
            exf,
            exb,
            tril,
            triu,
            eye,
        ],
    )

    returned = shifted_in(duh, "seq", -1)
    dvs = dvs.at[length - 8 :].add(returned.astype(BF16))

    mixer = lax.psum_scatter(
        jnp.dot(outin, proj_out, preferred_element_type=F32).astype(BF16),
        "head",
        scatter_dimension=0,
        tiled=True,
    )
    layer_out = (tokens.astype(F32) + mixer.astype(F32)).astype(BF16)

    def weight_grad(a, b):
        return lax.dot_general(a, b, (((0,), (0,)), ((), ())), preferred_element_type=F32)

    grad_proj_out = weight_grad(outin, cot_all)
    grad_proj_gate = weight_grad(normed, dgate)
    grad_vs = weight_grad(normed, dvs)
    grad_st = weight_grad(normed, dst)

    def back_dot(a, w):
        return lax.dot_general(a, w, (((1,), (1,)), ((), ())), preferred_element_type=F32)

    partial_in = back_dot(dgate, proj_gate) + back_dot(dvs, wsv) + back_dot(dst, wst)
    grad_gain = jnp.sum(partial_in * normed.astype(F32), axis=0) / input_gain
    own_in = lax.psum_scatter(
        partial_in.astype(BF16), "head", scatter_dimension=0, tiled=True
    ).astype(F32)
    token_values = tokens.astype(F32)
    scale_rows = lax.rsqrt(jnp.mean(token_values * token_values, axis=1, keepdims=True) + EPSILON)
    scaled = own_in * input_gain
    grad_tokens = (
        cotangent.astype(F32)
        + scale_rows * scaled
        - token_values * scale_rows**3 * jnp.mean(scaled * token_values, axis=1, keepdims=True)
    ).astype(BF16)

    grad_bias = gsmall[0, : 2 * nh].reshape(2, nh)
    grad_decay = gsmall[1, :nh] + gsmall[1, nh : 2 * nh]
    seq_sums = lax.psum(
        (
            grad_proj_gate,
            grad_vs[:, LANES:],
            grad_st[:, : 2 * nh],
            grad_proj_out,
            gconv[:4, LANES:],
            grad_bias,
            grad_decay,
            gskip[0],
            gmix[0],
        ),
        "seq",
    )
    shared = lax.psum((grad_vs[:, :LANES], gconv[:4, :LANES], grad_gain), ("seq", "head"))
    grad_step = jnp.stack([seq_sums[2][:, :nh], seq_sums[2][:, nh:]], axis=0)
    return (
        layer_out,
        grad_tokens,
        shared[2],
        seq_sums[0],
        seq_sums[1],
        shared[0],
        grad_step,
        seq_sums[5],
        seq_sums[6],
        seq_sums[4],
        shared[1],
        jnp.sum(seq_sums[7].reshape(nh, HDIM), axis=1),
        seq_sums[8],
        seq_sums[3],
    )


def solution(mesh):
    return jax.shard_map(
        per_device,
        mesh=mesh,
        in_specs=(
            P(("seq", "head"), None),
            P(),
            P(None, "head"),
            P(None, "head"),
            P(),
            P(None, None, "head"),
            P(None, "head"),
            P("head"),
            P(None, "head"),
            P(),
            P("head"),
            P("head"),
            P("head", None),
            P(),
            P("seq"),
            P(("seq", "head"), None),
        ),
        out_specs=(
            P(("seq", "head"), None),
            P(("seq", "head"), None),
            P(),
            P(None, "head"),
            P(None, "head"),
            P(),
            P(None, None, "head"),
            P(None, "head"),
            P("head"),
            P(None, "head"),
            P(),
            P("head"),
            P("head"),
            P("head", None),
        ),
        check_vma=False,
    )
```

time: 1700 us -> 585 us (0.34); the launches traced: 1670 us -> 583 us
  local copies, waits for them, and re-layouts: 558 us -> 24.4 us
  other arithmetic: 268 us -> 18.4 us
  matrix products: 235 us -> 24.7 us
  blocking collectives: 269 us -> 75.7 us
  Pallas kernels: 0 us -> 112 us
  waiting for transfers between devices: 315 us -> 284 us
  starting transfers between devices: 5.49 us -> 29.7 us
    pad x62 -> x2, local copies, waits for them, and re-layouts: 327 us -> 1.33 us  [the longest x1 0.72 us: per_device(): wst = jnp.pad(steps, ((0, 0), (0, LANES - 2 * nh)))]
    dot_general x41 -> x8, matrix products: 221 us -> 24.7 us  [the longest x4 12.7 us: weight_grad(): lax.dot_general(a, b, (((0,), (0,)), ((), ())), preferred_element_type=F32)]
    all_gather x6 -> x0, blocking collectives: 182 us -> none  [the longest x3 94.9 us: carried_in(): everything = jax.tree.map(lambda part: lax.all_gather(part, axis), array)]
    pallas_call x0 -> x5, Pallas kernels: none -> 112 us  [call(): pl.pallas_call(kernel, name=name, grid=(grid,), in_specs=ins, out_specs=[...]
    unnamed x709 -> x69, local copies, waits for them, and re-layouts: 96.2 us -> 8.43 us
    rev x13 -> x0, local copies, waits for them, and re-layouts: 74.6 us -> none  [the longest x1 10.8 us: per_device(): behind_values[::-1]]
    another operation x17 -> x8, other arithmetic: 60.5 us -> 0.6 us  [the longest x4 30.7 us: block_parts(): jnp.cumsum(log_decay.reshape(blocks, block_width, head_count), axis=1)]
    reduce_sum x26 -> x2, other arithmetic: 53.3 us -> 0.78 us  [the longest x1 0.63 us: per_device(): jnp.sum(seq_sums[7].reshape(nh, HDIM), axis=1)]
  transfers between devices with their start and end apart: 9 -> 19, of which waited for: 4 -> 6; matrix products, arithmetic and copies ran while one was open for 29% -> 9% of each run, Pallas kernels for 0% -> 6%
where the time goes in v1:
time: 585 us; the launch traced here: 583 us
  waiting for transfers between devices  284 us (49%)
  Pallas kernels  112 us (19%)
  blocking collectives  75.7 us (13%)
  starting transfers between devices  29.7 us (5%)
  matrix products  24.7 us (4%)
  local copies, waits for them, and re-layouts  24.4 us (4%)
  other arithmetic  18.4 us (3%)
  between operations  14.8 us (3%)
    psum x1, waiting for transfers between devices, per_device(): lax.psum((grad_proj_gate, grad_vs[:, LANES:], grad_st[:, :2 * nh], grad_p...  145 us
    pallas_call x5, Pallas kernels, call(): pl.pallas_call(kernel, name=name, grid=(grid,), in_specs=ins, out_specs=[...  112 us
    psum x1, waiting for transfers between devices, per_device(): lax.psum((grad_vs[:, :LANES], gconv[:4, :LANES], grad_gain), ('seq', 'hea...  109 us
    psum x1, blocking collectives, per_device(): lax.psum((grad_proj_gate, grad_vs[:, LANES:], grad_st[:, :2 * nh], grad_p...  38.3 us
    psum x1, blocking collectives, per_device(): lax.psum((grad_vs[:, :LANES], gconv[:4, :LANES], grad_gain), ('seq', 'hea...  37.3 us
    ppermute x10, starting transfers between devices, shifted_in(): return lax.ppermute(array, axis, pairs)  27.4 us
    all_gather x1, waiting for transfers between devices, per_device(): gathered = lax.all_gather(tokens, 'head', axis=0, tiled=True)  23.6 us
    dot_general x4, matrix products, weight_grad(): lax.dot_general(a, b, (((0,), (0,)), ((), ())), preferred_element_type=F32)  12.7 us
  transfers between devices with their start and end apart: 19, of which 6 were waited for; matrix products, arithmetic and copies ran while one was open for 9% of the time, Pallas kernels for 6%

profile of v1, /device:TPU:0, one launch (start us, length us, event | category | flops | bytes accessed | tf_op | source)
XLA Modules:
  0.0 582.8 jit_solution(17727167097042256721)
XLA Ops:
  7.3 0.7 all-gather.3.cloned.1.call-update
  8.0 0.7 all-gather.5.cloned.1.call-update
  10.4 1.4 pad_maximum_fusion.5
  13.2 1.5 convert_reduce_fusion.2
  14.8 0.7 fusion.14
  15.8 0.7 broadcast_bitcast_fusion.gm_ref
  16.6 0.7 fusion.8
  17.3 23.6 %all-gather.3.cloned.1.call-done.x_ref = bf16[2048,768]{1,0:T(8,128)(2,1)} async-done(((bf16[512,768]{1,0:T(8,128)(2,1)}), bf16[2048,768]{1,0:T(8,128)(2,1)}) %all-gather.3.cloned.1.call-update) | async-done | bytes 3145744 | tf_op jit(solution)/shard_map/all_gather | solution.py:709
  40.9 0.7 slice.260
  41.6 3.4 collective-permute-start
  46.0 0.7 pad.22.clone.wst_ref
  46.9 1.3 copy.99.cols_ref
  49.0 24.9 %front.1 = (bf16[2048,768]{1,0:T(8,128)(2,1)}, f32[2048,384]{1,0:T(8,128)}, f32[2048,512]{1,0:T(8,128)}, bf16[2048,512]{1,0:T(8,128)(2,1)}, f32[8,512]{1,0:T(8,1...) custom-call(bf16[2048,768]{1,0:T(8,128)(2,1)} %all-gather.3.cloned.1, ...), custom_call_target="tpu_custom_call" | custom-call | flops 3623878656 | bytes 24911872 | tf_op jit(solution)/shard_map/front/pallas_call | solution.py:636
  73.9 3.4 collective-permute-start.2
  77.3 3.4 collective-permute-start.1
  80.7 1.3 collective-permute-start.4
  82.0 1.3 collective-permute-start.3
  84.6 11.3 %inner.1 = (f32[2048,384]{1,0:T(8,128)}, f32[2048,384]{1,0:T(8,128)}) custom-call(f32[2048,512]{1,0:T(8,128)} %get-tuple-element.90.conv_ref, f32[2048,16]{1,0:T(8,128)} %copy.99.cols_ref, f32[8,2048]{1,0:T(8,128)} %broadcast_in_dim.61.segrow_ref, f32[2048,128]{1,0:T(8,128)} %get-tuple-element.91.cc_ref, f32[16,2048]{1,0:T(8,128)} %get-tuple-element.99.rowp_ref, ...), custom_call_target="tpu_custom_call" | custom-call | flops 1610612736 | bytes 15609856 | tf_op jit(solution)/shard_map/inner/pallas_call | solution.py:636
  95.9 0.7 fusion.13.sent_ref
  96.6 0.7 fusion.12.rent_ref
  97.8 14.0 %merge.1 = (f32[2048,384]{1,0:T(8,128)}, f32[8,2048]{1,0:T(8,128)}, bf16[16,64,384]{2,1,0:T(8,128)(2,1)}, bf16[16,64,384]{2,1,0:T(8,128)(2,1)}) custom-call(f32[2048,512]{1,0:T(8,128)} %get-tuple-element.90.conv_ref, f32[2048,16]{1,0:T(8,128)} %copy.99.cols_ref, f32[2048,128]{1,0:T(8,128)} %get-tuple-element.91.cc_ref, ...), custom_call_target="tpu_custom_call" | custom-call | flops 603979776 | bytes 23605248 | tf_op jit(solution)/shard_map/merge/pallas_call | solution.py:636
  112.0 1.0 collective-permute-start.6
  113.0 0.8 collective-permute-start.5
  114.4 1.3 slice.234.gtf_ref
  115.7 1.3 slice.235.gtb_ref
  117.2 1.5 add_add_fusion.1.stat_ref
  118.7 16.8 %turn.1 = (bf16[2048,384]{1,0:T(8,128)(2,1)}, bf16[2048,384]{1,0:T(8,128)(2,1)}, bf16[2048,384]{1,0:T(8,128)(2,1)}, f32[8,384]{1,0:T(8,128)}, f32[8,384]{1,0:T(8...) custom-call(f32[2048,384]{1,0:T(8,128)} %get-tuple-element.103.y_ref, ...), custom_call_target="tpu_custom_call" | custom-call | flops 603979776 | bytes 23687168 | tf_op jit(solution)/shard_map/turn/pallas_call | solution.py:636
  135.5 1.3 collective-permute-start.8
  137.1 0.7 stack.108.halocols_ref
  137.8 1.3 collective-permute-start.9
  139.1 7.2 %collective-permute-start.11 = (f32[72,384]{1,0:T(8,128)}, f32[72,384]{1,0:T(8,128)S(1)}, u32[]{:S(2)}, u32[]{:S(2)}) collective-permute-start(f32[72,384]{1,0:T(8,128)} %get-tuple-element.119), channel_id=1, source_target_pairs={{0,8},{4,12},{8,16},{12,20},{16,24},{20,28},{1,9},{5,13},{9,17},{1... | collective-permute-start | bytes 331784 | tf_op jit(solution)/shard_map/ppermute | solution.py:656
  146.2 3.6 collective-permute-start.10
  150.5 1.7 collective-permute-done.10
  152.3 0.7 fusion.10.drent_ref
  153.0 44.7 %back.1 = (bf16[2048,512]{1,0:T(8,128)(2,1)}, bf16[2048,128]{1,0:T(8,128)(2,1)}, f32[8,512]{1,0:T(8,128)}, f32[8,512]{1,0:T(8,128)}, f32[8,128]{1,0:T(8,128)}) custom-call(f32[2048,512]{1,0:T(8,128)} %get-tuple-element.90.conv_ref, f32[2048,16]{1,0:T(8,128)} %copy.99.cols_ref, f32[8,16]{1,0:T(8,128)} %stack.108.halocols_ref, ...), custom_call_target="tpu_custom_call" | custom-call | flops 3019898880 | bytes 19100160 | tf_op jit(solution)/shard_map/back/pallas_call | solution.py:636
  197.7 0.7 convert.15
  198.4 1.3 collective-permute-start.12
  199.7 1.8 fusion.41
  201.6 3.0 collective-permute-done.12
  204.6 1.9 fusion.42
  206.5 0.8 copy-done
  207.3 3.3 multiply_reduce_fusion
  210.7 5.0 convolution_convert_fusion
  216.0 4.4 fusion.43
  220.4 1.8 fusion.44
  222.2 1.2 copy-done.6
  223.4 0.8 slice.291
  224.3 4.9 fusion.45
  229.2 1.1 slice.290
  230.3 0.7 slice_reduce_fusion.7
  231.1 0.7 slice_reduce_fusion.6
  231.9 0.7 slice_reduce_fusion.8
  232.7 0.8 add_bitcast_fusion
  233.5 1.6 fusion.6
  235.1 38.3 %all-reduce.5 = (f32[768,12]{0,1:T(8,128)S(1)}, f32[2,6]{1,0:T(2,128)}, f32[6]{0:T(128)}, f32[4,384]{1,0:T(4,128)}, f32[6,64]{1,0:T(8,128)S(1)}, /*index=5*/f32[384]{0:T(512)}) all-reduce(f32[768,12]{0,1:T(8,128)S(1)} %fusion.6, f32[2,6]{1,0:T(2,128)S(1)} %reshape_squeeze.3, ...), channel_id=1, replica_groups=mesh['seq'=8,'head'=4] {'seq'}, use_global_device_ids=true, to_apply=%region_11.12 | all-reduce | flops 11538 | bytes 92304 | tf_op jit(solution)/shard_map/psum | solution.py:1120
  274.7 37.3 %all-reduce.4 = (f32[768]{0:T(1024)}, f32[4,128]{1,0:T(4,128)}) all-reduce(f32[768]{0:T(1024)S(1)} %div.35, f32[4,128]{1,0:T(4,128)S(1)} %slice.256), channel_id=1, replica_groups=mesh['seq'=8,'head'=4] {'seq','head'}, use_global_device_ids=true, to_apply=%region_7.8 | all-reduce | flops 1280 | bytes 10240 | tf_op jit(solution)/shard_map/psum | solution.py:1134
  312.1 1.8 fusion.1
  313.9 3.2 fusion.4
  317.1 108.8 %all-reduce.10.cloned.1.call-done = f32[768,128]{1,0:T(8,128)} async-done(((f32[768,128]{1,0:T(8,128)}), f32[768,128]{1,0:T(8,128)}) %all-reduce.10.cloned.1.call-update) | async-done | bytes 393232 | tf_op jit(solution)/shard_map/psum | solution.py:1134
  425.9 144.6 %all-reduce.12.cloned.1.call-done = (f32[768,384]{1,0:T(8,128)}, f32[768,384]{1,0:T(8,128)}, f32[384,768]{1,0:T(8,128)}) async-done(((f32[768,384]{1,0:T(8,128)}, f32[768,384]{1,0:T(8,128)}, f32[384,768]{1,0:T(8,128)}), (f32[768,384]{1,0:T(8,128)}, f32[768,384]{1,0:T(8,128)}, f32[384,768]{1,0:T(8,128)})) %all-reduce.12.cloned.1.call-update) | async-done | bytes 3538960 | tf_op jit(solution)/shard_map/psum | solution.py:1120
  570.5 2.5 copy.120
  573.0 1.0 copy.121
  574.2 0.7 copy.122
  575.0 1.0 copy.123
  (155 shorter events, 11.5 us)
Async XLA Ops:
  7.2 1.6 copy-start.30
  7.2 1.6 copy-start.27
  7.2 2.3 copy-start.26
  7.2 5.4 copy-start.24
  7.2 5.4 copy-start.22
  7.2 7.5 %copy-start.18 = (bf16[2,768,6]{1,0,2:T(2,128)(2,1)S(1)}, bf16[2,768,6]{1,0,2:T(2,128)(2,1)}, u32[]{:S(2)}) copy-start(bf16[2,768,6]{1,0,2:T(2,128)(2,1)} %param.27) | copy-start | bytes 55300
  7.2 8.2 %copy-start.17 = (bf16[768,128]{1,0:T(8,128)(2,1)S(1)}, bf16[768,128]{1,0:T(8,128)(2,1)}, u32[]{:S(2)}) copy-start(bf16[768,128]{1,0:T(8,128)(2,1)} %param.26) | copy-start | bytes 589828
  7.3 8.2 %copy-start.15 = (bf16[768,384]{1,0:T(8,128)(2,1)S(1)}, bf16[768,384]{1,0:T(8,128)(2,1)}, u32[]{:S(2)}) copy-start(bf16[768,384]{1,0:T(8,128)(2,1)} %param.25) | copy-start | bytes 1769476
  7.3 33.7 %all-gather.3.cloned.1.call-start = ((), (), s32[]{:S(2)}) async-start(), calls=%async_computation.2 | async-start | bytes 3932160 | tf_op jit(solution)/shard_map/all_gather | solution.py:709
  8.0 75.3 %all-gather.5.cloned.1.call-start = ((), (), s32[]{:S(2)}) async-start(), calls=%async_computation.3 | async-start | bytes 3932160 | tf_op jit(solution)/shard_map/all_gather | solution.py:710
  8.7 36.3 %copy-start.28 = (f32[6]{0:T(128)S(1)}, f32[6]{0:T(128)}, u32[]{:S(2)}) copy-start(f32[6]{0:T(128)} %param.32) | copy-start | bytes 76
  8.8 36.5 %copy-start.21 = (s32[2048]{0:T(1024)S(1)}, s32[2048]{0:T(1024)}, u32[]{:S(2)}) copy-start(s32[2048]{0:T(1024)} %param.36) | copy-start | bytes 24580
  8.8 303.3 %reduce-scatter.5.cloned.1.call-start = ((), (), s32[]{:S(2)}) async-start(), calls=%async_computation.5 | async-start | bytes 3932160 | tf_op jit(solution)/shard_map/reduce_scatter | solution.py:1106
  15.6 33.4 %copy-start.10 = (bf16[768,512]{1,0:T(8,128)(2,1)}, bf16[768,512]{1,0:T(8,128)(2,1)S(1)}, u32[]{:S(2)}) copy-start(bf16[768,512]{1,0:T(8,128)(2,1)S(1)} %constant_dynamic-update-slice_fusion.wsv_ref) | copy-start | bytes 2359300
  15.6 32.8 %copy-start.19 = (f32[768]{0:T(1024)S(1)}, f32[768]{0:T(1024)}, u32[]{:S(2)}) copy-start(f32[768]{0:T(1024)} %param.23) | copy-start | bytes 9220
  41.6 6.7 %collective-permute-start = (bf16[8,768]{1,0:T(8,128)(2,1)S(1)}, bf16[8,768]{1,0:T(8,128)(2,1)S(1)}, u32[]{:S(2)}, u32[]{:S(2)}) collective-permute-start(bf16[8,768]{1,0:T(8,128)(2,1)S(1)} %slice.260), channel_id=1, source_target_pairs={{0,4},{4,8},{8,12},{12,16},{16,20},{20,24},{24,28},{1,5},{5,9},{9,... | collective-permute-start | bytes 36872 | tf_op jit(solution)/shard_map/ppermute | solution.py:656
  48.3 0.7 copy-start.20
  48.4 0.6 copy-start.29
  73.9 22.0 %collective-permute-start.2 = (f32[72,384]{1,0:T(8,128)}, f32[72,384]{1,0:T(8,128)S(1)}, u32[]{:S(2)}, u32[]{:S(2)}) collective-permute-start(f32[72,384]{1,0:T(8,128)} %get-tuple-element.97), channel_id=1, source_target_pairs={{0,8},{4,12},{8,16},{12,20},{16,24},{20,28},{1,9},{5,13},{9,17},{1... | collective-permute-start | bytes 331784 | tf_op jit(solution)/shard_map/ppermute | solution.py:656
  77.3 18.5 %collective-permute-start.1 = (f32[72,384]{1,0:T(8,128)}, f32[72,384]{1,0:T(8,128)S(1)}, u32[]{:S(2)}, u32[]{:S(2)}) collective-permute-start(f32[72,384]{1,0:T(8,128)} %get-tuple-element.97), channel_id=1, source_target_pairs={{0,4},{4,8},{8,12},{12,16},{16,20},{20,24},{24,28},{1,5},{5,9},{9,... | collective-permute-start | bytes 331784 | tf_op jit(solution)/shard_map/ppermute | solution.py:656
  80.7 15.8 %collective-permute-start.4 = (f32[72,384]{1,0:T(8,128)}, f32[72,384]{1,0:T(8,128)S(1)}, u32[]{:S(2)}, u32[]{:S(2)}) collective-permute-start(f32[72,384]{1,0:T(8,128)} %get-tuple-element.98), channel_id=1, source_target_pairs={{8,0},{12,4},{16,8},{20,12},{24,16},{28,20},{9,1},{13,5},{17,9},{2... | collective-permute-start | bytes 331784 | tf_op jit(solution)/shard_map/ppermute | solution.py:656
  82.0 14.5 %collective-permute-start.3 = (f32[72,384]{1,0:T(8,128)}, f32[72,384]{1,0:T(8,128)S(1)}, u32[]{:S(2)}, u32[]{:S(2)}) collective-permute-start(f32[72,384]{1,0:T(8,128)} %get-tuple-element.98), channel_id=1, source_target_pairs={{4,0},{8,4},{12,8},{16,12},{20,16},{24,20},{28,24},{5,1},{9,5},{13... | collective-permute-start | bytes 331784 | tf_op jit(solution)/shard_map/ppermute | solution.py:656
  84.6 12.7 %copy-start.25 = (f32[384]{0:T(512)S(1)}, f32[384]{0:T(512)}, u32[]{:S(2)}) copy-start(f32[384]{0:T(512)} %param.33) | copy-start | bytes 4612
  111.9 5.1 collective-permute-start.7
  112.0 5.3 collective-permute-start.6
  113.0 4.2 collective-permute-start.5
  135.5 14.3 %collective-permute-start.8 = (f32[72,384]{1,0:T(8,128)}, f32[72,384]{1,0:T(8,128)S(1)}, u32[]{:S(2)}, u32[]{:S(2)}) collective-permute-start(f32[72,384]{1,0:T(8,128)} %get-tuple-element.118), channel_id=1, source_target_pairs={{4,0},{8,4},{12,8},{16,12},{20,16},{24,20},{28,24},{5,1},{9,5},{13... | collective-permute-start | bytes 331784 | tf_op jit(solution)/shard_map/ppermute | solution.py:656
  137.8 12.1 %collective-permute-start.9 = (f32[72,384]{1,0:T(8,128)}, f32[72,384]{1,0:T(8,128)S(1)}, u32[]{:S(2)}, u32[]{:S(2)}) collective-permute-start(f32[72,384]{1,0:T(8,128)} %get-tuple-element.118), channel_id=1, source_target_pairs={{8,0},{12,4},{16,8},{20,12},{24,16},{28,20},{9,1},{13,5},{17,9},{2... | collective-permute-start | bytes 331784 | tf_op jit(solution)/shard_map/ppermute | solution.py:656
  139.1 13.2 %collective-permute-start.11 = (f32[72,384]{1,0:T(8,128)}, f32[72,384]{1,0:T(8,128)S(1)}, u32[]{:S(2)}, u32[]{:S(2)}) collective-permute-start(f32[72,384]{1,0:T(8,128)} %get-tuple-element.119), channel_id=1, source_target_pairs={{0,8},{4,12},{8,16},{12,20},{16,24},{20,28},{1,9},{5,13},{9,17},{1... | collective-permute-start | bytes 331784 | tf_op jit(solution)/shard_map/ppermute | solution.py:656
  146.2 6.0 %collective-permute-start.10 = (f32[72,384]{1,0:T(8,128)}, f32[72,384]{1,0:T(8,128)S(1)}, u32[]{:S(2)}, u32[]{:S(2)}) collective-permute-start(f32[72,384]{1,0:T(8,128)} %get-tuple-element.119), channel_id=1, source_target_pairs={{0,4},{4,8},{8,12},{12,16},{16,20},{20,24},{24,28},{1,5},{5,9},{9,... | collective-permute-start | bytes 331784 | tf_op jit(solution)/shard_map/ppermute | solution.py:656
  153.0 46.7 %copy-start.4 = (bf16[2048,384]{1,0:T(8,128)(2,1)S(1)}, bf16[2048,384]{1,0:T(8,128)(2,1)}, u32[]{:S(2)}) copy-start(bf16[2048,384]{1,0:T(8,128)(2,1)} %get-tuple-element.108) | copy-start | bytes 4718596
  153.0 46.8 %copy-start.14 = (bf16[768,384]{1,0:T(8,128)(2,1)S(1)}, bf16[768,384]{1,0:T(8,128)(2,1)}, u32[]{:S(2)}) copy-start(bf16[768,384]{1,0:T(8,128)(2,1)} %wg_ref.1) | copy-start | bytes 1769476
  198.4 6.1 %collective-permute-start.12 = (bf16[8,512]{1,0:T(8,128)(2,1)S(1)}, bf16[8,512]{1,0:T(8,128)(2,1)S(1)}, u32[]{:S(2)}, u32[]{:S(2)}) collective-permute-start(bf16[8,512]{1,0:T(8,128)(2,1)S(1)} %convert.15), channel_id=1, source_target_pairs={{4,0},{8,4},{12,8},{16,12},{20,16},{24,20},{28,24},{5,1},{9,5},{13... | collective-permute-start | bytes 24584 | tf_op jit(solution)/shard_map/ppermute | solution.py:656
  199.7 4.8 copy-start.1
  199.7 4.8 copy-start.11
  204.6 1.9 copy-start.2
  204.6 2.6 copy-start
  204.6 2.7 copy-start.9
  210.6 103.3 %reduce-scatter.3.cloned.1.call-start = ((), (), s32[]{:S(2)}) async-start(), calls=%async_computation.4 | async-start | bytes 3932160 | tf_op jit(solution)/shard_map/reduce_scatter | solution.py:1085
  215.7 210.2 %all-reduce.10.cloned.1.call-start = ((), (), s32[]{:S(2)}) async-start(), calls=%async_computation.6 | async-start | bytes 786432 | tf_op jit(solution)/shard_map/psum | solution.py:1134
  216.0 4.4 copy-start.3
  222.2 1.2 copy-start.6
  224.2 346.3 %all-reduce.12.cloned.1.call-start = ((), (), s32[]{:S(2)}) async-start(), calls=%async_computation.7 | async-start | bytes 7077888 | tf_op jit(solution)/shard_map/psum | solution.py:1120
  224.2 4.9 copy-start.7
  230.3 1.6 copy-start.23
  235.1 78.8 %copy-start.5 = (bf16[512,768]{1,0:T(8,128)(2,1)S(1)}, bf16[512,768]{1,0:T(8,128)(2,1)}, u32[]{:S(2)}) copy-start(bf16[512,768]{1,0:T(8,128)(2,1)} %param.22) | copy-start | bytes 2359300
  235.1 78.9 %copy-start.8 = (bf16[512,768]{1,0:T(8,128)(2,1)S(1)}, bf16[512,768]{1,0:T(8,128)(2,1)}, u32[]{:S(2)}) copy-start(bf16[512,768]{1,0:T(8,128)(2,1)} %param.37) | copy-start | bytes 2359300
  570.5 2.5 copy-start.13
  573.0 1.2 copy-start.16
  573.0 2.0 copy-start.12
Sparse Core Ops, SparseCore 0:
  9.7 31.2 all-gather.2
  42.5 28.6 all-gather.4
  210.7 40.6 reduce-scatter.4
  253.9 38.7 reduce-scatter.2
  298.5 127.4 all-reduce.9
  431.3 139.2 all-reduce.11

commit v2 on v1

--- a/solution.py
+++ b/solution.py
@@ -106,6 +106,7 @@
     tril_ref,
     triu_ref,
     normed_ref,
+    normh_ref,
     gate_ref,
     conv_ref,
     uv_ref,
@@ -141,7 +142,9 @@
 
     @pl.when(i == 0)
     def _():
-        before = mm(norm(halo_ref[...]), wsv_ref[...])
+        edge = norm(halo_ref[...])
+        normh_ref[...] = edge
+        before = mm(edge, wsv_ref[...])
         ubuf[0:8, :] = before
         uvh_ref[...] = before
         state[...] = jnp.zeros_like(state)
@@ -429,6 +432,8 @@
 
 def back_kernel(
     nh,
+    peers,
+    at_ref,
     conv_ref,
     cols_ref,
     halocols_ref,
@@ -458,16 +463,22 @@
     tril_ref,
     triu_ref,
     eye_ref,
-    dvs_ref,
-    dst_ref,
-    duh_ref,
-    gconv_ref,
-    gsmall_ref,
-    dbuf,
-    hbuf,
+    normed_ref,
+    normh_ref,
+    dgate_ref,
+    wg_ref,
+    wcat_ref,
+    gmix_ref,
+    gskip_ref,
+    part_ref,
+    parth_ref,
+    *rest,
 ):
+    chunks = rest[:peers]
+    dbuf, hbuf, dcat, acc, lines = rest[peers:]
     i = pl.program_id(0)
     last = pl.num_programs(0) - 1
+    model = normed_ref.shape[1]
     tb = conv_ref.shape[0]
     width = conv_ref.shape[1] - LANES
     exf = exf_ref[...]
@@ -476,8 +487,8 @@
     @pl.when(i == 0)
     def _():
         dbuf[tb : tb + 8, :] = jnp.zeros((8, LANES + width), F32)
-        gconv_ref[...] = jnp.zeros_like(gconv_ref)
-        gsmall_ref[...] = jnp.zeros_like(gsmall_ref)
+        acc[...] = jnp.zeros_like(acc)
+        lines[...] = jnp.zeros_like(lines)
 
     s_at = iota((SPAN, SPAN), 0)
     t_at = iota((SPAN, SPAN), 1)
@@ -580,23 +591,30 @@
         sigz = sigmoid(z)
         rate = pcol_ref[1:2, :]
         dstep = (kc + leaving) * (sigz / jnp.maximum(dt, TINY)) - dlog * rate * sigz
-        dst_ref[rows, :] = dstep.astype(BF16)
-        gsmall_ref[0:1, :] += jnp.sum(dstep, axis=0, keepdims=True)
-        gsmall_ref[1:2, :] += jnp.sum(-dlog * dt * rate, axis=0, keepdims=True)
+        dcat[rows, :LANES] = dstep.astype(BF16)
+        lines[7:8, :LANES] += jnp.sum(dstep, axis=0, keepdims=True)
+        lines[8:9, :LANES] += jnp.sum(-dlog * dt * rate, axis=0, keepdims=True)
         dact = jnp.concatenate([dbc, dx + skip_ref[0:1, :] * dy], axis=1)
         dbuf[rows, :] = dact * keep[:, 3:4] * sig * (1.0 + conv * (1.0 - sig))
 
     dconv = dbuf[0:tb, :]
     uv = uv_ref[...].astype(F32)
     du = taps_ref[0:1, :] * dconv
-    gconv_ref[0:1, :] += jnp.sum(uv * dconv, axis=0, keepdims=True)
+    taps_at = slice(0, LANES + width)
+    lines[1:2, taps_at] += jnp.sum(uv * dconv, axis=0, keepdims=True)
     for k in (1, 2, 3):
         shifted = dbuf[k : k + tb, :] * cols_ref[:, 8 + k : 9 + k]
         du = du + taps_ref[k : k + 1, :] * shifted
-        gconv_ref[k : k + 1, :] += jnp.sum(uv * shifted, axis=0, keepdims=True)
-    dvs_ref[...] = du.astype(BF16)
+        lines[1 + k : 2 + k, taps_at] += jnp.sum(uv * shifted, axis=0, keepdims=True)
+    dcat[:, LANES:] = du.astype(BF16)
     edge = dbuf[0:8, :]
     dbuf[tb : tb + 8, :] = edge
+    normed = normed_ref[...]
+    d_all = dcat[...]
+    part = mm_nt(dgate_ref[...], wg_ref[...]) + mm_nt(d_all, wcat_ref[...])
+    part_ref[0] = part.astype(BF16)
+    lines[0:1, :] += jnp.sum(part * normed.astype(F32), axis=0, keepdims=True)
+    acc[...] += mm_tn(normed, d_all)
 
     @pl.when(i == last)
     def _():
@@ -606,48 +624,89 @@
         for k in (1, 2, 3):
             shifted = hbuf[k : k + 8, :] * halocols_ref[:, k - 1 : k]
             duh = duh + taps_ref[k : k + 1, :] * shifted
-            gconv_ref[k : k + 1, :] += jnp.sum(uvh_ref[...] * shifted, axis=0, keepdims=True)
-        duh_ref[...] = duh
+            lines[1 + k : 2 + k, taps_at] += jnp.sum(uvh_ref[...] * shifted, axis=0, keepdims=True)
+        duh = duh.astype(BF16)
+        normh = normh_ref[...]
+        parth = mm_nt(duh, wcat_ref[:, LANES:])
+        parth_ref[...] = parth
+        lines[0:1, :] += jnp.sum(parth * normh.astype(F32), axis=0, keepdims=True)
+        lines[5:6, :width] = gskip_ref[0:1, :]
+        lines[6:7, :width] = gmix_ref[0:1, :]
+        acc[:, LANES:] += mm_tn(normh, duh)
+        placed = jnp.where(iota((16, LANES), 1) == iota((16, LANES), 0) + 16, 1.0, 0.0)
+        acc[:, :LANES] += exact_tn(lines[...], placed)
+        size = model // peers
+        for k in range(peers):
+            start = pl.multiple_of((at_ref[0] ^ k) * size, 8)
+            chunks[k][...] = acc[pl.ds(start, size), :].astype(BF16)
+
+
+def finish_kernel(nh, peers, at_ref, *refs):
+    chunks = refs[:peers]
+    eye_ref = refs[peers]
+    gain_ref, value_ref, state_ref, step_ref, bias_ref, decay_ref = refs[peers + 1 : peers + 7]
+    convv_ref, convs_ref, skip_ref, mixer_ref, extra = refs[peers + 7 :]
+    size = chunks[0].shape[0]
+    width = value_ref.shape[1]
+    for k in range(peers):
+        rows = pl.ds(pl.multiple_of((at_ref[0] ^ k) * size, 8), size)
+        extra[rows, :] = chunks[k][:, :LANES].astype(F32)
+        state_ref[rows, :] = chunks[k][:, LANES : 2 * LANES].astype(F32)
+        value_ref[rows, :] = chunks[k][:, 2 * LANES :].astype(F32)
+    found = extra[...]
+    step_ref[0] = found[:, :nh]
+    step_ref[1] = found[:, nh : 2 * nh]
+    lines = mm_nt(eye_ref[...], found.astype(BF16))
+    gain_ref[...] = lines[0:1, :]
+    convs_ref[...] = lines[1:5, :LANES]
+    convv_ref[...] = lines[1:5, LANES : LANES + width]
+    skip_ref[...] = lines[5:6, :width]
+    mixer_ref[...] = lines[6:7, :width]
+    bias_ref[...] = lines[7:8, : 2 * nh]
+    decay_ref[...] = lines[8:9, :nh] + lines[8:9, nh : 2 * nh]
 
 
 def whole(shape):
-    return pl.BlockSpec(shape, lambda i: (0,) * len(shape))
+    return pl.BlockSpec(shape, lambda i, *_: (0,) * len(shape))
 
 
 def row_block(rows, width):
-    return pl.BlockSpec((rows, width), lambda i: (i, 0))
+    return pl.BlockSpec((rows, width), lambda i, *_: (i, 0))
 
 
 def lane_block(rows, width):
-    return pl.BlockSpec((rows, width), lambda i: (0, i))
+    return pl.BlockSpec((rows, width), lambda i, *_: (0, i))
 
 
 def chunk_block(per, rows, width):
-    return pl.BlockSpec((per, rows, width), lambda i: (i, 0, 0))
+    return pl.BlockSpec((per, rows, width), lambda i, *_: (i, 0, 0))
 
 
 def sds(shape, dtype):
     return jax.ShapeDtypeStruct(shape, dtype)
 
 
-def call(kernel, name, grid, ins, outs, scratch, flops, operands):
+def call(kernel, name, grid, ins, outs, scratch, flops, operands, scalars=()):
     moved = sum(o.size * o.dtype.itemsize for o in operands)
     moved += sum(s.size * s.dtype.itemsize for _, s in outs)
     return pl.pallas_call(
         kernel,
         name=name,
-        grid=(grid,),
-        in_specs=ins,
-        out_specs=[spec for spec, _ in outs],
+        grid_spec=pltpu.PrefetchScalarGridSpec(
+            num_scalar_prefetch=len(scalars),
+            grid=(grid,),
+            in_specs=ins,
+            out_specs=[spec for spec, _ in outs],
+            scratch_shapes=scratch,
+        ),
         out_shape=[shape for _, shape in outs],
-        scratch_shapes=scratch,
         compiler_params=pltpu.CompilerParams(
             dimension_semantics=("arbitrary",), vmem_limit_bytes=56 * 1024 * 1024
         ),
         cost_estimate=pl.CostEstimate(
             flops=int(flops), bytes_accessed=int(moved), transcendentals=0
         ),
-    )(*operands)
+    )(*scalars, *operands)
 
 
 def shifted_in(array, axis, by):
@@ -789,6 +848,7 @@
 
     (
         normed,
+        normh,
         gate_in,
         conv,
         uv,
@@ -832,6 +892,7 @@
         ],
         [
             (rows(model), sds((length, model), BF16)),
+            (whole((8, model)), sds((8, model), BF16)),
             (rows(width), sds((length, width), F32)),
             (rows(wide), sds((length, wide), F32)),
             (rows(wide), sds((length, wide), BF16)),
@@ -1000,10 +1061,24 @@
     back = lambda i: grid - 1 - i
 
     def rev(spec):
-        return pl.BlockSpec(spec.block_shape, lambda i: spec.index_map(back(i)))
-
-    dvs, dst, duh, gconv, gsmall = call(
-        partial(back_kernel, nh),
+        return pl.BlockSpec(spec.block_shape, lambda i, *_: spec.index_map(back(i)))
+
+    peers = lax.axis_size("seq")
+    own = length // head_devices
+    bits = head_devices.bit_length() - 1
+    here = lax.axis_index("head")
+    scalars = [jnp.stack([seq_index, here]).astype(jnp.int32)]
+    wcat = jnp.concatenate([wst, wsv], axis=1)
+    size = model // peers
+
+    def part_at(i, at):
+        row = back(i) * tb
+        slot = (row // own) ^ at[1]
+        place = sum(((slot >> b) & 1) << (bits - 1 - b) for b in range(bits))
+        return place, (row % own) // tb, 0
+
+    part, parth, *chunks = call(
+        partial(back_kernel, nh, peers),
         "back",
         grid,
         [
@@ -1036,16 +1111,27 @@
             whole((SPAN, SPAN)),
             whole((SPAN, SPAN)),
             whole((16, LANES)),
-        ],
-        [
-            (rev(rows(wide)), sds((length, wide), BF16)),
-            (rev(rows(LANES)), sds((length, LANES), BF16)),
-            (whole((8, wide)), sds((8, wide), F32)),
-            (whole((8, wide)), sds((8, wide), F32)),
-            (whole((8, LANES)), sds((8, LANES), F32)),
-        ],
-        [pltpu.VMEM((tb + 8, wide), F32), pltpu.VMEM((16, wide), F32)],
-        2 * length * width * (4 * SPAN + 6 * HDIM + 8 * LANES),
+            rev(rows(model)),
+            whole((8, model)),
+            rev(rows(width)),
+            whole((model, width)),
+            whole((model, LANES + wide)),
+            whole((8, width)),
+            whole((8, width)),
+        ],
+        [
+            (pl.BlockSpec((1, tb, model), part_at), sds((head_devices, own, model), BF16)),
+            (whole((8, model)), sds((8, model), F32)),
+        ]
+        + [(whole((size, LANES + wide)), sds((size, LANES + wide), BF16))] * peers,
+        [
+            pltpu.VMEM((tb + 8, wide), F32),
+            pltpu.VMEM((16, wide), F32),
+            pltpu.VMEM((tb, LANES + wide), BF16),
+            pltpu.VMEM((model, LANES + wide), F32),
+            pltpu.VMEM((16, model), F32),
+        ],
+        2 * length * (width * (4 * SPAN + 6 * HDIM + 8 * LANES) + model * (3 * width + 4 * LANES)),
         [
             conv,
             cols,
@@ -1076,11 +1162,46 @@
             tril,
             triu,
             eye,
-        ],
+            normed,
+            normh,
+            dgate,
+            proj_gate,
+            wcat,
+            gmix,
+            gskip,
+        ],
+        scalars,
     )
 
-    returned = shifted_in(duh, "seq", -1)
-    dvs = dvs.at[length - 8 :].add(returned.astype(BF16))
+    def swap(array, axis, k):
+        n = lax.axis_size(axis)
+        return lax.ppermute(array, axis, [(i, i ^ k) for i in range(n)])
+
+    summed = chunks[0].astype(F32)
+    for k in range(1, peers):
+        summed = summed + swap(chunks[k], "seq", k).astype(F32)
+    shared = summed[:, : 2 * LANES]
+    row_at = seq_index * size + jnp.arange(size)[:, None]
+    lane_at = jnp.arange(2 * LANES)[None, :]
+    common = (lane_at >= LANES) | (lane_at == 16)
+    common = common | ((lane_at > 16) & (lane_at < 21) & (row_at < LANES))
+    shared = jnp.where(common, sum_over(shared, "head"), shared)
+    reduced = jnp.concatenate([shared, summed[:, 2 * LANES :]], axis=1).astype(BF16)
+    spread_out = [reduced] + [swap(reduced, "seq", k) for k in range(1, peers)]
+
+    returned = shifted_in(parth, "seq", -1)
+    last_slot = (head_devices - 1) ^ here
+    last_slot = sum(((last_slot >> b) & 1) << (bits - 1 - b) for b in range(bits))
+    tail = lax.dynamic_slice(part, (last_slot, own - 8, 0), (1, 8, model))
+    tail = (tail.astype(F32) + returned[None]).astype(BF16)
+    own_in = lax.dynamic_update_slice(part, tail, (last_slot, own - 8, 0))
+    for b in range(bits):
+        half = own_in.shape[0] // 2
+        got = swap(own_in[half:], "head", 1 << b)
+        own_in = own_in[:half].astype(F32) + got.astype(F32)
+        if b < bits - 1:
+            own_in = own_in.astype(BF16)
+    own_in = own_in[0]
 
     mixer = lax.psum_scatter(
         jnp.dot(outin, proj_out, preferred_element_type=F32).astype(BF16),
@@ -1093,19 +1214,10 @@
     def weight_grad(a, b):
         return lax.dot_general(a, b, (((0,), (0,)), ((), ())), preferred_element_type=F32)
 
-    grad_proj_out = weight_grad(outin, cot_all)
-    grad_proj_gate = weight_grad(normed, dgate)
-    grad_vs = weight_grad(normed, dvs)
-    grad_st = weight_grad(normed, dst)
-
-    def back_dot(a, w):
-        return lax.dot_general(a, w, (((1,), (1,)), ((), ())), preferred_element_type=F32)
-
-    partial_in = back_dot(dgate, proj_gate) + back_dot(dvs, wsv) + back_dot(dst, wst)
-    grad_gain = jnp.sum(partial_in * normed.astype(F32), axis=0) / input_gain
-    own_in = lax.psum_scatter(
-        partial_in.astype(BF16), "head", scatter_dimension=0, tiled=True
-    ).astype(F32)
+    grad_proj_out = weight_grad(outin, cot_all).astype(BF16)
+    grad_proj_gate = weight_grad(normed, dgate).astype(BF16)
+    grad_proj_out, grad_proj_gate = lax.psum((grad_proj_out, grad_proj_gate), "seq")
+
     token_values = tokens.astype(F32)
     scale_rows = lax.rsqrt(jnp.mean(token_values * token_values, axis=1, keepdims=True) + EPSILON)
     scaled = own_in * input_gain
@@ -1115,39 +1227,45 @@
         - token_values * scale_rows**3 * jnp.mean(scaled * token_values, axis=1, keepdims=True)
     ).astype(BF16)
 
-    grad_bias = gsmall[0, : 2 * nh].reshape(2, nh)
-    grad_decay = gsmall[1, :nh] + gsmall[1, nh : 2 * nh]
-    seq_sums = lax.psum(
-        (
-            grad_proj_gate,
-            grad_vs[:, LANES:],
-            grad_st[:, : 2 * nh],
-            grad_proj_out,
-            gconv[:4, LANES:],
-            grad_bias,
-            grad_decay,
-            gskip[0],
-            gmix[0],
-        ),
-        "seq",
+    finals = [
+        sds((1, model), F32),
+        sds((model, width), F32),
+        sds((model, LANES), F32),
+        sds((2, model, nh), F32),
+        sds((1, 2 * nh), F32),
+        sds((1, nh), F32),
+        sds((4, width), F32),
+        sds((4, LANES), F32),
+        sds((1, width), F32),
+        sds((1, width), F32),
+    ]
+    picked = (jnp.arange(16)[:, None] + 16 == lanes[None, :]).astype(BF16)
+    ggain, gvalue, gstate, gstep, gbias, gdecay, gconvv, gconvs, gskips, gmixer = call(
+        partial(finish_kernel, nh, peers),
+        "finish",
+        1,
+        [whole((size, LANES + wide))] * peers + [whole((16, LANES))],
+        [(whole(f.shape), f) for f in finals],
+        [pltpu.VMEM((model, LANES), F32)],
+        0,
+        spread_out + [picked],
+        scalars,
     )
-    shared = lax.psum((grad_vs[:, :LANES], gconv[:4, :LANES], grad_gain), ("seq", "head"))
-    grad_step = jnp.stack([seq_sums[2][:, :nh], seq_sums[2][:, nh:]], axis=0)
     return (
         layer_out,
         grad_tokens,
-        shared[2],
-        seq_sums[0],
-        seq_sums[1],
-        shared[0],
-        grad_step,
-        seq_sums[5],
-        seq_sums[6],
-        seq_sums[4],
-        shared[1],
-        jnp.sum(seq_sums[7].reshape(nh, HDIM), axis=1),
-        seq_sums[8],
-        seq_sums[3],
+        ggain[0] / input_gain,
+        grad_proj_gate.astype(F32),
+        gvalue,
+        gstate,
+        gstep,
+        gbias.reshape(2, nh),
+        gdecay[0],
+        gconvv,
+        gconvs,
+        jnp.sum(gskips.reshape(nh, HDIM), axis=1),
+        gmixer[0],
+        grad_proj_out.astype(F32),
     )
 
 

time: 585 us -> 328 us (0.56)
  waiting for transfers between devices: 284 us -> 55.2 us
  blocking collectives: 75.7 us -> 0 us
  starting transfers between devices: 29.7 us -> 69.2 us
  matrix products: 24.7 us -> 9.9 us
  other arithmetic: 18.4 us -> 32.5 us
  Pallas kernels: 112 us -> 125 us
    psum x2 -> x1, waiting for transfers between devices: 253 us -> 0.01 us  [per_device(): lax.psum((grad_proj_out, grad_proj_gate), 'seq')]
    psum x2 -> x0, blocking collectives: 75.7 us -> none  [the longest x1 38.3 us: per_device(): lax.psum((grad_proj_gate, grad_vs[:, LANES:], grad_st[:, :2 * nh], grad_p...]
    ppermute x0 -> x16, starting transfers between devices: none -> 37.7 us  [swap(): return lax.ppermute(array, axis, [(i, i ^ k) for i in range(n)])]
    ppermute x0 -> x16, waiting for transfers between devices: none -> 18 us  [swap(): return lax.ppermute(array, axis, [(i, i ^ k) for i in range(n)])]
    pallas_call x5 -> x6, Pallas kernels: 112 us -> 125 us  [call(): pl.pallas_call(kernel, name=name, grid_spec=pltpu.PrefetchScalarGridSpec(...]
    dot_general x3 -> x0, matrix products: 6.93 us -> none  [back_dot(): lax.dot_general(a, w, (((1,), (1,)), ((), ())), preferred_element_type=F32)]
    ppermute x10, waiting for transfers between devices: 4.76 us -> 11.5 us  [shifted_in(): return lax.ppermute(array, axis, pairs)]
    dot_general x4 -> x2, matrix products: 12.7 us -> 6.45 us  [weight_grad(): lax.dot_general(a, b, (((0,), (0,)), ((), ())), preferred_element_type=F32)]
  transfers between devices with their start and end apart: 19 -> 36, of which waited for: 6 -> 13; matrix products, arithmetic and copies ran while one was open for 9% -> 15% of each run, Pallas kernels for 6% -> 29%
where the time goes in v2:
time: 328 us; the launch traced here: 325 us
  Pallas kernels  125 us (38%)
  starting transfers between devices  69.2 us (21%)
  waiting for transfers between devices  55.2 us (17%)
  other arithmetic  32.5 us (10%)
  local copies, waits for them, and re-layouts  19 us (6%)
  between operations  14.4 us (4%)
  matrix products  9.9 us (3%)
    pallas_call x6, Pallas kernels, call(): pl.pallas_call(kernel, name=name, grid_spec=pltpu.PrefetchScalarGridSpec(...  125 us
    ppermute x16, starting transfers between devices, swap(): return lax.ppermute(array, axis, [(i, i ^ k) for i in range(n)])  37.7 us
    ppermute x10, starting transfers between devices, shifted_in(): return lax.ppermute(array, axis, pairs)  27.3 us
    all_gather x1, waiting for transfers between devices, per_device(): gathered = lax.all_gather(tokens, 'head', axis=0, tiled=True)  23 us
    ppermute x16, waiting for transfers between devices, swap(): return lax.ppermute(array, axis, [(i, i ^ k) for i in range(n)])  18 us
    ppermute x10, waiting for transfers between devices, shifted_in(): return lax.ppermute(array, axis, pairs)  11.5 us
  transfers between devices with their start and end apart: 36, of which 13 were waited for; matrix products, arithmetic and copies ran while one was open for 15% of the time, Pallas kernels for 29%

profile of v2, /device:TPU:0, one launch (start us, length us, event | category | flops | bytes accessed | tf_op | source)
XLA Modules:
  0.0 324.7 jit_solution(13008711012262010378)
XLA Ops:
  10.4 1.4 pad_maximum_fusion.7
  13.2 1.5 convert_reduce_fusion.2
  15.4 1.0 pad_maximum_fusion.1.wsv_ref
  18.0 23.0 %all-gather.3.cloned.1.call-done.x_ref = bf16[2048,768]{1,0:T(8,128)(2,1)} async-done(((bf16[512,768]{1,0:T(8,128)(2,1)}), bf16[2048,768]{1,0:T(8,128)(2,1)}) %all-gather.3.cloned.1.call-update) | async-done | bytes 3145744 | tf_op jit(solution)/shard_map/all_gather | solution.py:768
  41.7 3.3 %collective-permute-start = (bf16[8,768]{1,0:T(8,128)(2,1)S(1)}, bf16[8,768]{1,0:T(8,128)(2,1)S(1)}, u32[]{:S(2)}, u32[]{:S(2)}) collective-permute-start(bf16[8,768]{1,0:T(8,128)(2,1)S(1)} %slice.216), channel_id=1, source_target_pairs={{0,4},{4,8},{8,12},{12,16},{16,20},{20,24},{24,28},{1,5},{5,9},{9,... | collective-permute-start | bytes 36872 | tf_op jit(solution)/shard_map/ppermute | solution.py:715
  46.8 1.3 copy.99.cols_ref
  49.0 24.8 %front.1 = (bf16[2048,768]{1,0:T(8,128)(2,1)}, bf16[8,768]{1,0:T(8,128)(2,1)}, f32[2048,384]{1,0:T(8,128)}, f32[2048,512]{1,0:T(8,128)}, bf16[2048,512]{1,0:T(8,...) custom-call(bf16[2048,768]{1,0:T(8,128)(2,1)} %all-gather.3.cloned.1, ...), custom_call_target="tpu_custom_call" | custom-call | flops 3623878656 | bytes 24924160 | tf_op jit(solution)/shard_map/front/pallas_call | solution.py:692
  73.9 3.4 %collective-permute-start.2 = (f32[72,384]{1,0:T(8,128)}, f32[72,384]{1,0:T(8,128)S(1)}, u32[]{:S(2)}, u32[]{:S(2)}) collective-permute-start(f32[72,384]{1,0:T(8,128)} %get-tuple-element.101), channel_id=1, source_target_pairs={{0,8},{4,12},{8,16},{12,20},{16,24},{20,28},{1,9},{5,13},{9,17},{1... | collective-permute-start | bytes 331784 | tf_op jit(solution)/shard_map/ppermute | solution.py:715
  77.3 3.4 %collective-permute-start.1 = (f32[72,384]{1,0:T(8,128)}, f32[72,384]{1,0:T(8,128)S(1)}, u32[]{:S(2)}, u32[]{:S(2)}) collective-permute-start(f32[72,384]{1,0:T(8,128)} %get-tuple-element.101), channel_id=1, source_target_pairs={{0,4},{4,8},{8,12},{12,16},{16,20},{20,24},{24,28},{1,5},{5,9},{9,... | collective-permute-start | bytes 331784 | tf_op jit(solution)/shard_map/ppermute | solution.py:715
  80.7 1.3 collective-permute-start.4
  82.0 1.3 collective-permute-start.3
  84.5 11.3 %inner.1 = (f32[2048,384]{1,0:T(8,128)}, f32[2048,384]{1,0:T(8,128)}) custom-call(f32[2048,512]{1,0:T(8,128)} %get-tuple-element.94.conv_ref, f32[2048,16]{1,0:T(8,128)} %copy.99.cols_ref, f32[8,2048]{1,0:T(8,128)} %broadcast_in_dim.63.segrow_ref, f32[2048,128]{1,0:T(8,128)} %get-tuple-element.95.cc_ref, f32[16,2048]{1,0:T(8,128)} %get-tuple-element.103.rowp_ref, ...), custom_call_target="tpu_custom_call" | custom-call | flops 1610612736 | bytes 15609856 | tf_op jit(solution)/shard_map/inner/pallas_call | solution.py:692
  97.8 14.0 %merge.1 = (f32[2048,384]{1,0:T(8,128)}, f32[8,2048]{1,0:T(8,128)}, bf16[16,64,384]{2,1,0:T(8,128)(2,1)}, bf16[16,64,384]{2,1,0:T(8,128)(2,1)}) custom-call(f32[2048,512]{1,0:T(8,128)} %get-tuple-element.94.conv_ref, f32[2048,16]{1,0:T(8,128)} %copy.99.cols_ref, f32[2048,128]{1,0:T(8,128)} %get-tuple-element.95.cc_ref, ...), custom_call_target="tpu_custom_call" | custom-call | flops 603979776 | bytes 23605248 | tf_op jit(solution)/shard_map/merge/pallas_call | solution.py:692
  111.9 1.0 collective-permute-start.6
  114.4 1.3 slice.198.gtf_ref
  115.7 1.3 slice.199.gtb_ref
  117.2 1.5 add_add_fusion.stat_ref
  118.7 16.9 %turn.1 = (bf16[2048,384]{1,0:T(8,128)(2,1)}, bf16[2048,384]{1,0:T(8,128)(2,1)}, bf16[2048,384]{1,0:T(8,128)(2,1)}, f32[8,384]{1,0:T(8,128)}, f32[8,384]{1,0:T(8...) custom-call(f32[2048,384]{1,0:T(8,128)} %get-tuple-element.107.y_ref, ...), custom_call_target="tpu_custom_call" | custom-call | flops 603979776 | bytes 23687168 | tf_op jit(solution)/shard_map/turn/pallas_call | solution.py:692
  135.6 4.2 %convolution_convert_fusion.2 = bf16[768,384]{1,0:T(8,128)(2,1)} fusion(bf16[2048,768]{1,0:T(8,128)(2,1)S(1)} %copy-done.3, bf16[2048,384]{1,0:T(8,128)(2,1)} %get-tuple-element.127.dgate_ref), kind=kOutput, calls=%fused_computation.14 | convolution fusion | flops 1208254464 | bytes 5308416 | tf_op jit(solution)/shard_map/dot_general | solution.py:1215
  139.8 2.3 convolution_convert_fusion.1
  142.3 3.4 %convolution_convert_fusion = bf16[2048,768]{1,0:T(8,128)(2,1)} fusion(bf16[2048,384]{1,0:T(8,128)(2,1)S(1)} %copy-done.29, bf16[384,768]{1,0:T(8,128)(2,1)S(1)} %copy-done.9), kind=kOutput, calls=%fused_computation | convolution fusion | flops 1209532416 | bytes 5308416 | tf_op jit(solution)/shard_map/dot_general | solution.py:1207
  146.9 1.1 pad_maximum_fusion.wcat_ref
  148.0 1.3 collective-permute-start.8
  149.8 1.3 collective-permute-start.9
  151.1 7.2 %collective-permute-start.11 = (f32[72,384]{1,0:T(8,128)S(1)}, f32[72,384]{1,0:T(8,128)S(1)}, u32[]{:S(2)}, u32[]{:S(2)}) collective-permute-start(f32[72,384]{1,0:T(8,128)S(1)} %copy-done.33), channel_id=1, source_target_pairs={{0,8},{4,12},{8,16},{12,20},{16,24},{20,28},{1,9},{5,13},{9,17},{1... | collective-permute-start | bytes 331784 | tf_op jit(solution)/shard_map/ppermute | solution.py:715
  158.3 3.4 %collective-permute-start.10 = (f32[72,384]{1,0:T(8,128)S(1)}, f32[72,384]{1,0:T(8,128)S(1)}, u32[]{:S(2)}, u32[]{:S(2)}) collective-permute-start(f32[72,384]{1,0:T(8,128)S(1)} %copy-done.33), channel_id=1, source_target_pairs={{0,4},{4,8},{8,12},{12,16},{16,20},{20,24},{24,28},{1,5},{5,9},{9,... | collective-permute-start | bytes 331784 | tf_op jit(solution)/shard_map/ppermute | solution.py:715
  161.7 7.1 %collective-permute-done.9 = f32[72,384]{1,0:T(8,128)S(1)} collective-permute-done((f32[72,384]{1,0:T(8,128)S(1)}, f32[72,384]{1,0:T(8,128)S(1)}, u32[]{:S(2)}, u32[]{:S(2)}) %collective-permute-start.9) | collective-permute-done | bytes 110624 | tf_op jit(solution)/shard_map/ppermute | solution.py:715
  170.2 53.8 %back.1 = (bf16[4,512,768]{2,1,0:T(8,128)(2,1)}, f32[8,768]{1,0:T(8,128)}, bf16[96,640]{1,0:T(8,128)(2,1)}, bf16[96,640]{1,0:T(8,128)(2,1)}, bf16[96,640]{1,0:T(...) custom-call(s32[2]{0:T(128)} %pad_add_fusion.1.at_ref, ...), custom_call_target="tpu_custom_call" | custom-call | flops 8254390272 | bytes 26923520 | tf_op jit(solution)/shard_map/back/pallas_call | solution.py:692
  224.0 1.5 collective-permute-start.12
  225.5 4.4 %collective-permute-done.12 = f32[8,768]{1,0:T(8,128)S(1)} collective-permute-done((f32[8,768]{1,0:T(8,128)}, f32[8,768]{1,0:T(8,128)S(1)}, u32[]{:S(2)}, u32[]{:S(2)}) %collective-permute-start.12) | collective-permute-done | bytes 24608 | tf_op jit(solution)/shard_map/ppermute | solution.py:715
  229.9 1.3 fusion.15
  231.2 1.6 slice.247
  232.9 3.2 collective-permute-start.21
  236.1 1.4 collective-permute-start.20
  237.4 1.6 collective-permute-start.19
  239.0 1.8 collective-permute-start.18
  241.4 11.7 %collective-permute-start.17 = (bf16[96,640]{1,0:T(8,128)(2,1)}, bf16[96,640]{1,0:T(8,128)(2,1)}, u32[]{:S(2)}, u32[]{:S(2)}) collective-permute-start(bf16[96,640]{1,0:T(8,128)(2,1)} %get-tuple-element.135), channel_id=1, source_target_pairs={{0,12},{4,8},{8,4},{12,0},{16,28},{20,24},{24,20},{28,16},{1,13},{... | collective-permute-start | bytes 368648 | tf_op jit(solution)/shard_map/ppermute | solution.py:1178
  253.1 1.7 collective-permute-start.16
  254.8 2.4 collective-permute-done.19
  257.2 1.4 collective-permute-start.15
  259.3 2.8 collective-permute-done.17
  262.1 1.1 collective-permute-done.16
  263.9 1.3 convert_add_fusion.1
  265.2 1.2 collective-permute-start.24
  267.1 1.8 add_convert_fusion
  269.8 1.6 collective-permute-start.14
  271.4 1.0 collective-permute-done.23
  272.6 1.0 collective-permute-start.25
  273.6 1.5 collective-permute-start.26
  275.1 1.1 collective-permute-start.27
  276.1 1.9 collective-permute-start.28
  278.0 2.7 collective-permute-start.29
  280.7 2.2 collective-permute-done.26.refs_2_
  283.0 2.5 collective-permute-start.30
  285.5 2.6 collective-permute-start.31
  288.7 7.5 %collective-permute-done.29.refs_5_ = bf16[96,640]{1,0:T(8,128)(2,1)S(1)} collective-permute-done((bf16[96,640]{1,0:T(8,128)(2,1)S(1)}, bf16[96,640]{1,0:T(8,128)(2,1)S(1)}, u32[]{:S(2)}, u32[]{:S(2)}) %collective-permute-start.29) | collective-permute-done | bytes 122912 | tf_op jit(solution)/shard_map/ppermute | solution.py:1178
  297.6 3.6 %finish.1 = (f32[1,768]{1,0:T(1,128)}, f32[768,384]{1,0:T(8,128)}, f32[768,128]{1,0:T(8,128)}, f32[2,768,6]{2,1,0:T(8,128)}, f32[1,12]{1,0:T(1,128)}, /*index=5*...) custom-call(s32[2]{0:T(128)} %pad_add_fusion.1.at_ref, ...), custom_call_target="tpu_custom_call" | custom-call | bytes 2611272 | tf_op jit(solution)/shard_map/finish/pallas_call | solution.py:692
  302.6 2.0 copy.107
  305.1 1.3 reduce.31
  308.5 1.2 reduce.18
  309.7 2.3 convert_element_type.208
  312.0 1.1 convert_element_type.210
  313.1 1.8 fusion.1
  314.9 3.3 %fusion.4 = (bf16[512,768]{1,0:T(8,128)(2,1)}, bf16[512,768]{1,0:T(8,128)(2,1)}) fusion(bf16[512,768]{1,0:T(8,128)(2,1)S(1)} %copy-done, bf16[512,768]{1,0:T(8,128)(2,1)S(1)} %copy-done.1, bf16[1,512,768]{2,1,0:T(8,128)(2,1)} %collective-permute-done.14, f32[512]{0:T(512)S(1)} %broadcast_multiply_fusion, f32[512]{0:T(512)S(1)} %get-tuple-element.255, ...), kind=kLoop, calls=%fused_computation.10 | loop fusion | flops 5898240 | bytes 5514240 | tf_op jit(solution)/shard_map/convert_element_type | solution.py:1228
  (198 shorter events, 28.0 us)
Async XLA Ops:
  7.2 2.2 copy-start.26
  7.2 5.4 %copy-start.22 = (f32[4,384]{1,0:T(4,128)S(1)}, f32[4,384]{1,0:T(4,128)}, u32[]{:S(2)}) copy-start(f32[4,384]{1,0:T(4,128)} %param.28) | copy-start | bytes 18436
  7.2 5.4 %copy-start.24 = (f32[4,128]{1,0:T(4,128)S(1)}, f32[4,128]{1,0:T(4,128)}, u32[]{:S(2)}) copy-start(f32[4,128]{1,0:T(4,128)} %param.29) | copy-start | bytes 6148
  7.2 7.5 %copy-start.19 = (bf16[2,768,6]{1,0,2:T(2,128)(2,1)S(1)}, bf16[2,768,6]{1,0,2:T(2,128)(2,1)}, u32[]{:S(2)}) copy-start(bf16[2,768,6]{1,0,2:T(2,128)(2,1)} %param.25) | copy-start | bytes 55300
  7.2 8.2 %copy-start.4 = (bf16[768,384]{1,0:T(8,128)(2,1)S(1)}, bf16[768,384]{1,0:T(8,128)(2,1)}, u32[]{:S(2)}) copy-start(bf16[768,384]{1,0:T(8,128)(2,1)} %param.23) | copy-start | bytes 1769476
  7.3 8.2 %copy-start.6 = (bf16[768,128]{1,0:T(8,128)(2,1)S(1)}, bf16[768,128]{1,0:T(8,128)(2,1)}, u32[]{:S(2)}) copy-start(bf16[768,128]{1,0:T(8,128)(2,1)} %param.24) | copy-start | bytes 589828
  7.3 33.7 %all-gather.3.cloned.1.call-start = ((), (), s32[]{:S(2)}) async-start(), calls=%async_computation.1 | async-start | bytes 3932160 | tf_op jit(solution)/shard_map/all_gather | solution.py:768
  8.0 75.3 %all-gather.5.cloned.1.call-start = ((), (), s32[]{:S(2)}) async-start(), calls=%async_computation.2 | async-start | bytes 3932160 | tf_op jit(solution)/shard_map/all_gather | solution.py:769
  8.7 301.0 %all-reduce.7.cloned.1.call-start = ((), (), s32[]{:S(2)}) async-start(), calls=%async_computation.4 | async-start | bytes 2359296 | tf_op jit(solution)/shard_map/psum | solution.py:1219
  12.6 34.0 %copy-start.21 = (s32[2048]{0:T(1024)S(1)}, s32[2048]{0:T(1024)}, u32[]{:S(2)}) copy-start(s32[2048]{0:T(1024)} %param.34) | copy-start | bytes 24580
  16.4 31.7 %copy-start.28 = (f32[6]{0:T(128)S(1)}, f32[6]{0:T(128)}, u32[]{:S(2)}) copy-start(f32[6]{0:T(128)} %param.30) | copy-start | bytes 76
  16.4 32.0 %copy-start.20 = (f32[768]{0:T(1024)S(1)}, f32[768]{0:T(1024)}, u32[]{:S(2)}) copy-start(f32[768]{0:T(1024)} %param.21) | copy-start | bytes 9220
  41.7 6.7 %collective-permute-start = (bf16[8,768]{1,0:T(8,128)(2,1)S(1)}, bf16[8,768]{1,0:T(8,128)(2,1)S(1)}, u32[]{:S(2)}, u32[]{:S(2)}) collective-permute-start(bf16[8,768]{1,0:T(8,128)(2,1)S(1)} %slice.216), channel_id=1, source_target_pairs={{0,4},{4,8},{8,12},{12,16},{16,20},{20,24},{24,28},{1,5},{5,9},{9,... | collective-permute-start | bytes 36872 | tf_op jit(solution)/shard_map/ppermute | solution.py:715
  73.9 22.0 %collective-permute-start.2 = (f32[72,384]{1,0:T(8,128)}, f32[72,384]{1,0:T(8,128)S(1)}, u32[]{:S(2)}, u32[]{:S(2)}) collective-permute-start(f32[72,384]{1,0:T(8,128)} %get-tuple-element.101), channel_id=1, source_target_pairs={{0,8},{4,12},{8,16},{12,20},{16,24},{20,28},{1,9},{5,13},{9,17},{1... | collective-permute-start | bytes 331784 | tf_op jit(solution)/shard_map/ppermute | solution.py:715
  77.3 18.6 %collective-permute-start.1 = (f32[72,384]{1,0:T(8,128)}, f32[72,384]{1,0:T(8,128)S(1)}, u32[]{:S(2)}, u32[]{:S(2)}) collective-permute-start(f32[72,384]{1,0:T(8,128)} %get-tuple-element.101), channel_id=1, source_target_pairs={{0,4},{4,8},{8,12},{12,16},{16,20},{20,24},{24,28},{1,5},{5,9},{9,... | collective-permute-start | bytes 331784 | tf_op jit(solution)/shard_map/ppermute | solution.py:715
  80.7 15.9 %collective-permute-start.4 = (f32[72,384]{1,0:T(8,128)}, f32[72,384]{1,0:T(8,128)S(1)}, u32[]{:S(2)}, u32[]{:S(2)}) collective-permute-start(f32[72,384]{1,0:T(8,128)} %get-tuple-element.102), channel_id=1, source_target_pairs={{8,0},{12,4},{16,8},{20,12},{24,16},{28,20},{9,1},{13,5},{17,9},{2... | collective-permute-start | bytes 331784 | tf_op jit(solution)/shard_map/ppermute | solution.py:715
  82.0 14.5 %collective-permute-start.3 = (f32[72,384]{1,0:T(8,128)}, f32[72,384]{1,0:T(8,128)S(1)}, u32[]{:S(2)}, u32[]{:S(2)}) collective-permute-start(f32[72,384]{1,0:T(8,128)} %get-tuple-element.102), channel_id=1, source_target_pairs={{4,0},{8,4},{12,8},{16,12},{20,16},{24,20},{28,24},{5,1},{9,5},{13... | collective-permute-start | bytes 331784 | tf_op jit(solution)/shard_map/ppermute | solution.py:715
  84.5 12.7 %copy-start.25 = (f32[384]{0:T(512)S(1)}, f32[384]{0:T(512)}, u32[]{:S(2)}) copy-start(f32[384]{0:T(512)} %param.31) | copy-start | bytes 4612
  111.8 5.1 %collective-permute-start.7 = (f32[8,2048]{1,0:T(8,128)}, f32[8,2048]{1,0:T(8,128)S(1)}, u32[]{:S(2)}, u32[]{:S(2)}) collective-permute-start(f32[8,2048]{1,0:T(8,128)} %get-tuple-element.108), channel_id=1, source_target_pairs={{0,3},{1,2},{2,1},{3,0},{4,7},{5,6},{6,5},{7,4},{8,11},{9,10},{10,... | collective-permute-start | bytes 196616 | tf_op jit(solution)/shard_map/ppermute | solution.py:730
  111.9 5.3 %collective-permute-start.6 = (f32[8,2048]{1,0:T(8,128)}, f32[8,2048]{1,0:T(8,128)S(1)}, u32[]{:S(2)}, u32[]{:S(2)}) collective-permute-start(f32[8,2048]{1,0:T(8,128)} %get-tuple-element.108), channel_id=1, source_target_pairs={{0,2},{1,3},{2,0},{3,1},{4,6},{5,7},{6,4},{7,5},{8,10},{9,11},{10,... | collective-permute-start | bytes 196616 | tf_op jit(solution)/shard_map/ppermute | solution.py:730
  113.0 4.2 %collective-permute-start.5 = (f32[8,2048]{1,0:T(8,128)}, f32[8,2048]{1,0:T(8,128)S(1)}, u32[]{:S(2)}, u32[]{:S(2)}) collective-permute-start(f32[8,2048]{1,0:T(8,128)} %get-tuple-element.108), channel_id=1, source_target_pairs={{0,1},{1,0},{2,3},{3,2},{4,5},{5,4},{6,7},{7,6},{8,9},{9,8},{10,11... | collective-permute-start | bytes 196616 | tf_op jit(solution)/shard_map/ppermute | solution.py:730
  118.7 16.9 %copy-start.3 = (bf16[2048,768]{1,0:T(8,128)(2,1)S(1)}, bf16[2048,768]{1,0:T(8,128)(2,1)}, u32[]{:S(2)}) copy-start(bf16[2048,768]{1,0:T(8,128)(2,1)} %get-tuple-element.125.normed_ref) | copy-start | bytes 9437188
  135.6 4.2 %copy-start.2 = (bf16[2048,768]{1,0:T(8,128)(2,1)S(1)}, bf16[2048,768]{1,0:T(8,128)(2,1)}, u32[]{:S(2)}) copy-start(bf16[2048,768]{1,0:T(8,128)(2,1)} %all-gather.5.cloned.1.call-done.cot_ref) | copy-start | bytes 9437188
  135.6 4.2 %copy-start.29 = (bf16[2048,384]{1,0:T(8,128)(2,1)S(1)}, bf16[2048,384]{1,0:T(8,128)(2,1)}, u32[]{:S(2)}) copy-start(bf16[2048,384]{1,0:T(8,128)(2,1)} %get-tuple-element.111) | copy-start | bytes 4718596
  139.8 2.5 copy-start.9
  142.1 172.8 %reduce-scatter.2.cloned.1.call-start = ((), (), s32[]{:S(2)}) async-start(), calls=%async_computation.3 | async-start | bytes 3932160 | tf_op jit(solution)/shard_map/reduce_scatter | solution.py:1206
  145.8 2.1 copy-start.34
  145.8 5.3 %copy-start.33 = (f32[72,384]{1,0:T(8,128)S(1)}, f32[72,384]{1,0:T(8,128)}, u32[]{:S(2)}) copy-start(f32[72,384]{1,0:T(8,128)} %get-tuple-element.122) | copy-start | bytes 331780
  148.0 13.7 %collective-permute-start.8 = (f32[72,384]{1,0:T(8,128)S(1)}, f32[72,384]{1,0:T(8,128)S(1)}, u32[]{:S(2)}, u32[]{:S(2)}) collective-permute-start(f32[72,384]{1,0:T(8,128)S(1)} %copy-done.34), channel_id=1, source_target_pairs={{4,0},{8,4},{12,8},{16,12},{20,16},{24,20},{28,24},{5,1},{9,5},{13... | collective-permute-start | bytes 331784 | tf_op jit(solution)/shard_map/ppermute | solution.py:715
  149.8 19.0 %collective-permute-start.9 = (f32[72,384]{1,0:T(8,128)S(1)}, f32[72,384]{1,0:T(8,128)S(1)}, u32[]{:S(2)}, u32[]{:S(2)}) collective-permute-start(f32[72,384]{1,0:T(8,128)S(1)} %copy-done.34), channel_id=1, source_target_pairs={{8,0},{12,4},{16,8},{20,12},{24,16},{28,20},{9,1},{13,5},{17,9},{2... | collective-permute-start | bytes 331784 | tf_op jit(solution)/shard_map/ppermute | solution.py:715
  151.1 18.4 %collective-permute-start.11 = (f32[72,384]{1,0:T(8,128)S(1)}, f32[72,384]{1,0:T(8,128)S(1)}, u32[]{:S(2)}, u32[]{:S(2)}) collective-permute-start(f32[72,384]{1,0:T(8,128)S(1)} %copy-done.33), channel_id=1, source_target_pairs={{0,8},{4,12},{8,16},{12,20},{16,24},{20,28},{1,9},{5,13},{9,17},{1... | collective-permute-start | bytes 331784 | tf_op jit(solution)/shard_map/ppermute | solution.py:715
  158.3 11.2 %collective-permute-start.10 = (f32[72,384]{1,0:T(8,128)S(1)}, f32[72,384]{1,0:T(8,128)S(1)}, u32[]{:S(2)}, u32[]{:S(2)}) collective-permute-start(f32[72,384]{1,0:T(8,128)S(1)} %copy-done.33), channel_id=1, source_target_pairs={{0,4},{4,8},{8,12},{12,16},{16,20},{20,24},{24,28},{1,5},{5,9},{9,... | collective-permute-start | bytes 331784 | tf_op jit(solution)/shard_map/ppermute | solution.py:715
  224.0 5.9 %collective-permute-start.12 = (f32[8,768]{1,0:T(8,128)}, f32[8,768]{1,0:T(8,128)S(1)}, u32[]{:S(2)}, u32[]{:S(2)}) collective-permute-start(f32[8,768]{1,0:T(8,128)} %get-tuple-element.131), channel_id=1, source_target_pairs={{4,0},{8,4},{12,8},{16,12},{20,16},{24,20},{28,24},{5,1},{9,5},{13... | collective-permute-start | bytes 73736 | tf_op jit(solution)/shard_map/ppermute | solution.py:715
  231.2 1.7 copy-start.32
  231.2 4.9 %copy-start.31 = (bf16[96,640]{1,0:T(8,128)(2,1)S(1)}, bf16[96,640]{1,0:T(8,128)(2,1)}, u32[]{:S(2)}) copy-start(bf16[96,640]{1,0:T(8,128)(2,1)} %get-tuple-element.138) | copy-start | bytes 368644
  231.2 6.2 %copy-start.30 = (bf16[96,640]{1,0:T(8,128)(2,1)S(1)}, bf16[96,640]{1,0:T(8,128)(2,1)}, u32[]{:S(2)}) copy-start(bf16[96,640]{1,0:T(8,128)(2,1)} %get-tuple-element.137) | copy-start | bytes 368644
  231.2 32.7 %copy-start.11 = (bf16[96,640]{1,0:T(8,128)(2,1)S(1)}, bf16[96,640]{1,0:T(8,128)(2,1)}, u32[]{:S(2)}) copy-start(bf16[96,640]{1,0:T(8,128)(2,1)} %get-tuple-element.132) | copy-start | bytes 368644
  232.8 34.3 %collective-permute-start.13 = (bf16[2,512,768]{2,1,0:T(8,128)(2,1)S(1)}, bf16[2,512,768]{2,1,0:T(8,128)(2,1)S(1)}, u32[]{:S(2)}, u32[]{:S(2)}) collective-permute-start(bf16[2,512,768]{2,1,0:T(8,128)(2,1)S(1)} %slice.247), channel_id=1, source_target_pairs={{0,1},{1,0},{2,3},{3,2},{4,5},{5,4},{6,7},{7,6},{8,9},{9,8},{10,11... | collective-permute-start | bytes 4718600 | tf_op jit(solution)/shard_map/ppermute | solution.py:1178
  232.9 8.5 %collective-permute-start.21 = (bf16[96,640]{1,0:T(8,128)(2,1)S(1)}, bf16[96,640]{1,0:T(8,128)(2,1)S(1)}, u32[]{:S(2)}, u32[]{:S(2)}) collective-permute-start(bf16[96,640]{1,0:T(8,128)(2,1)S(1)} %copy-done.32), channel_id=1, source_target_pairs={{0,28},{4,24},{8,20},{12,16},{16,12},{20,8},{24,4},{28,0},{1,29},{... | collective-permute-start | bytes 368648 | tf_op jit(solution)/shard_map/ppermute | solution.py:1178
  236.1 17.0 %collective-permute-start.20 = (bf16[96,640]{1,0:T(8,128)(2,1)S(1)}, bf16[96,640]{1,0:T(8,128)(2,1)S(1)}, u32[]{:S(2)}, u32[]{:S(2)}) collective-permute-start(bf16[96,640]{1,0:T(8,128)(2,1)S(1)} %copy-done.31), channel_id=1, source_target_pairs={{0,24},{4,28},{8,16},{12,20},{16,8},{20,12},{24,0},{28,4},{1,25},{... | collective-permute-start | bytes 368648 | tf_op jit(solution)/shard_map/ppermute | solution.py:1178
  237.4 19.8 %collective-permute-start.19 = (bf16[96,640]{1,0:T(8,128)(2,1)S(1)}, bf16[96,640]{1,0:T(8,128)(2,1)}, u32[]{:S(2)}, u32[]{:S(2)}) collective-permute-start(bf16[96,640]{1,0:T(8,128)(2,1)S(1)} %copy-done.30), channel_id=1, source_target_pairs={{0,20},{4,16},{8,28},{12,24},{16,4},{20,0},{24,12},{28,8},{1,21},{... | collective-permute-start | bytes 368648 | tf_op jit(solution)/shard_map/ppermute | solution.py:1178
  239.0 20.3 %collective-permute-start.18 = (bf16[96,640]{1,0:T(8,128)(2,1)}, bf16[96,640]{1,0:T(8,128)(2,1)}, u32[]{:S(2)}, u32[]{:S(2)}) collective-permute-start(bf16[96,640]{1,0:T(8,128)(2,1)} %get-tuple-element.136), channel_id=1, source_target_pairs={{0,16},{4,20},{8,24},{12,28},{16,0},{20,4},{24,8},{28,12},{1,17},{... | collective-permute-start | bytes 368648 | tf_op jit(solution)/shard_map/ppermute | solution.py:1178
  241.4 20.7 %collective-permute-start.17 = (bf16[96,640]{1,0:T(8,128)(2,1)}, bf16[96,640]{1,0:T(8,128)(2,1)}, u32[]{:S(2)}, u32[]{:S(2)}) collective-permute-start(bf16[96,640]{1,0:T(8,128)(2,1)} %get-tuple-element.135), channel_id=1, source_target_pairs={{0,12},{4,8},{8,4},{12,0},{16,28},{20,24},{24,20},{28,16},{1,13},{... | collective-permute-start | bytes 368648 | tf_op jit(solution)/shard_map/ppermute | solution.py:1178
  253.1 10.1 %collective-permute-start.16 = (bf16[96,640]{1,0:T(8,128)(2,1)}, bf16[96,640]{1,0:T(8,128)(2,1)}, u32[]{:S(2)}, u32[]{:S(2)}) collective-permute-start(bf16[96,640]{1,0:T(8,128)(2,1)} %get-tuple-element.134), channel_id=1, source_target_pairs={{0,8},{4,12},{8,0},{12,4},{16,24},{20,28},{24,16},{28,20},{1,9},{5... | collective-permute-start | bytes 368648 | tf_op jit(solution)/shard_map/ppermute | solution.py:1178
  257.2 6.7 %collective-permute-start.15 = (bf16[96,640]{1,0:T(8,128)(2,1)}, bf16[96,640]{1,0:T(8,128)(2,1)}, u32[]{:S(2)}, u32[]{:S(2)}) collective-permute-start(bf16[96,640]{1,0:T(8,128)(2,1)} %get-tuple-element.133), channel_id=1, source_target_pairs={{0,4},{4,0},{8,12},{12,8},{16,20},{20,16},{24,28},{28,24},{1,5},{5... | collective-permute-start | bytes 368648 | tf_op jit(solution)/shard_map/ppermute | solution.py:1178
  265.2 6.3 %collective-permute-start.24 = (f32[96,256]{1,0:T(8,128)S(1)}, f32[96,256]{1,0:T(8,128)S(1)}, u32[]{:S(2)}, u32[]{:S(2)}) collective-permute-start(f32[96,256]{1,0:T(8,128)S(1)} %slice.250), channel_id=1, source_target_pairs={{0,3},{1,2},{2,1},{3,0},{4,7},{5,6},{6,5},{7,4},{8,11},{9,10},{10,... | collective-permute-start | bytes 294920 | tf_op jit(solution)/shard_map/ppermute | solution.py:730
  266.3 6.1 %collective-permute-start.23 = (f32[96,256]{1,0:T(8,128)S(1)}, f32[96,256]{1,0:T(8,128)S(1)}, u32[]{:S(2)}, u32[]{:S(2)}) collective-permute-start(f32[96,256]{1,0:T(8,128)S(1)} %slice.250), channel_id=1, source_target_pairs={{0,2},{1,3},{2,0},{3,1},{4,6},{5,7},{6,4},{7,5},{8,10},{9,11},{10,... | collective-permute-start | bytes 294920 | tf_op jit(solution)/shard_map/ppermute | solution.py:730
  266.9 5.6 %collective-permute-start.22 = (f32[96,256]{1,0:T(8,128)S(1)}, f32[96,256]{1,0:T(8,128)S(1)}, u32[]{:S(2)}, u32[]{:S(2)}) collective-permute-start(f32[96,256]{1,0:T(8,128)S(1)} %slice.250), channel_id=1, source_target_pairs={{0,1},{1,0},{2,3},{3,2},{4,5},{5,4},{6,7},{7,6},{8,9},{9,8},{10,11... | collective-permute-start | bytes 294920 | tf_op jit(solution)/shard_map/ppermute | solution.py:730
  269.8 43.3 %collective-permute-start.14 = (bf16[1,512,768]{2,1,0:T(8,128)(2,1)}, bf16[1,512,768]{2,1,0:T(8,128)(2,1)}, u32[]{:S(2)}, u32[]{:S(2)}) collective-permute-start(bf16[1,512,768]{2,1,0:T(8,128)(2,1)} %slice.249), channel_id=1, source_target_pairs={{0,2},{1,3},{2,0},{3,1},{4,6},{5,7},{6,4},{7,5},{8,10},{9,11},{10,... | collective-permute-start | bytes 2359304 | tf_op jit(solution)/shard_map/ppermute | solution.py:1178
  272.6 23.7 %copy-start.10 = (bf16[96,640]{1,0:T(8,128)(2,1)}, bf16[96,640]{1,0:T(8,128)(2,1)S(1)}, u32[]{:S(2)}) copy-start(bf16[96,640]{1,0:T(8,128)(2,1)S(1)} %pad_maximum_fusion.2.refs_0_) | copy-start | bytes 368644
  272.6 5.4 %collective-permute-start.25 = (bf16[96,640]{1,0:T(8,128)(2,1)S(1)}, bf16[96,640]{1,0:T(8,128)(2,1)S(1)}, u32[]{:S(2)}, u32[]{:S(2)}) collective-permute-start(bf16[96,640]{1,0:T(8,128)(2,1)S(1)} %pad_maximum_fusion.2.refs_0_), channel_id=1, source_target_pairs={{0,4},{4,0},{8,12},{12,8},{16,20},{20,16},{24,28},{28,24},{1,5},{5... | collective-permute-start | bytes 368648 | tf_op jit(solution)/shard_map/ppermute | solution.py:1178
  273.6 9.4 %collective-permute-start.26 = (bf16[96,640]{1,0:T(8,128)(2,1)S(1)}, bf16[96,640]{1,0:T(8,128)(2,1)S(1)}, u32[]{:S(2)}, u32[]{:S(2)}) collective-permute-start(bf16[96,640]{1,0:T(8,128)(2,1)S(1)} %pad_maximum_fusion.2.refs_0_), channel_id=1, source_target_pairs={{0,8},{4,12},{8,0},{12,4},{16,24},{20,28},{24,16},{28,20},{1,9},{5... | collective-permute-start | bytes 368648 | tf_op jit(solution)/shard_map/ppermute | solution.py:1178
  275.1 10.4 %collective-permute-start.27 = (bf16[96,640]{1,0:T(8,128)(2,1)S(1)}, bf16[96,640]{1,0:T(8,128)(2,1)S(1)}, u32[]{:S(2)}, u32[]{:S(2)}) collective-permute-start(bf16[96,640]{1,0:T(8,128)(2,1)S(1)} %pad_maximum_fusion.2.refs_0_), channel_id=1, source_target_pairs={{0,12},{4,8},{8,4},{12,0},{16,28},{20,24},{24,20},{28,16},{1,13},{... | collective-permute-start | bytes 368648 | tf_op jit(solution)/shard_map/ppermute | solution.py:1178
  276.1 12.6 %collective-permute-start.28 = (bf16[96,640]{1,0:T(8,128)(2,1)S(1)}, bf16[96,640]{1,0:T(8,128)(2,1)S(1)}, u32[]{:S(2)}, u32[]{:S(2)}) collective-permute-start(bf16[96,640]{1,0:T(8,128)(2,1)S(1)} %pad_maximum_fusion.2.refs_0_), channel_id=1, source_target_pairs={{0,16},{4,20},{8,24},{12,28},{16,0},{20,4},{24,8},{28,12},{1,17},{... | collective-permute-start | bytes 368648 | tf_op jit(solution)/shard_map/ppermute | solution.py:1178
  278.0 18.3 %copy-start.12 = (bf16[96,640]{1,0:T(8,128)(2,1)}, bf16[96,640]{1,0:T(8,128)(2,1)S(1)}, u32[]{:S(2)}) copy-start(bf16[96,640]{1,0:T(8,128)(2,1)S(1)} %collective-permute-done.25.refs_1_) | copy-start | bytes 368644
  278.0 18.3 %collective-permute-start.29 = (bf16[96,640]{1,0:T(8,128)(2,1)S(1)}, bf16[96,640]{1,0:T(8,128)(2,1)S(1)}, u32[]{:S(2)}, u32[]{:S(2)}) collective-permute-start(bf16[96,640]{1,0:T(8,128)(2,1)S(1)} %pad_maximum_fusion.2.refs_0_), channel_id=1, source_target_pairs={{0,20},{4,16},{8,28},{12,24},{16,4},{20,0},{24,12},{28,8},{1,21},{... | collective-permute-start | bytes 368648 | tf_op jit(solution)/shard_map/ppermute | solution.py:1178
  283.0 13.4 %copy-start.13 = (bf16[96,640]{1,0:T(8,128)(2,1)}, bf16[96,640]{1,0:T(8,128)(2,1)S(1)}, u32[]{:S(2)}) copy-start(bf16[96,640]{1,0:T(8,128)(2,1)S(1)} %collective-permute-done.26.refs_2_) | copy-start | bytes 368644
  283.0 13.3 %collective-permute-start.30 = (bf16[96,640]{1,0:T(8,128)(2,1)S(1)}, bf16[96,640]{1,0:T(8,128)(2,1)S(1)}, u32[]{:S(2)}, u32[]{:S(2)}) collective-permute-start(bf16[96,640]{1,0:T(8,128)(2,1)S(1)} %pad_maximum_fusion.2.refs_0_), channel_id=1, source_target_pairs={{0,24},{4,28},{8,16},{12,20},{16,8},{20,12},{24,0},{28,4},{1,25},{... | collective-permute-start | bytes 368648 | tf_op jit(solution)/shard_map/ppermute | solution.py:1178
  285.5 10.9 %copy-start.14 = (bf16[96,640]{1,0:T(8,128)(2,1)}, bf16[96,640]{1,0:T(8,128)(2,1)S(1)}, u32[]{:S(2)}) copy-start(bf16[96,640]{1,0:T(8,128)(2,1)S(1)} %collective-permute-done.27.refs_3_) | copy-start | bytes 368644
  285.5 10.8 %collective-permute-start.31 = (bf16[96,640]{1,0:T(8,128)(2,1)S(1)}, bf16[96,640]{1,0:T(8,128)(2,1)S(1)}, u32[]{:S(2)}, u32[]{:S(2)}) collective-permute-start(bf16[96,640]{1,0:T(8,128)(2,1)S(1)} %pad_maximum_fusion.2.refs_0_), channel_id=1, source_target_pairs={{0,28},{4,24},{8,20},{12,16},{16,12},{20,8},{24,4},{28,0},{1,29},{... | collective-permute-start | bytes 368648 | tf_op jit(solution)/shard_map/ppermute | solution.py:1178
  288.7 7.6 %copy-start.15 = (bf16[96,640]{1,0:T(8,128)(2,1)}, bf16[96,640]{1,0:T(8,128)(2,1)S(1)}, u32[]{:S(2)}) copy-start(bf16[96,640]{1,0:T(8,128)(2,1)S(1)} %collective-permute-done.28.refs_4_) | copy-start | bytes 368644
  309.7 2.3 copy-start.8
  309.7 3.4 %copy-start = (bf16[512,768]{1,0:T(8,128)(2,1)S(1)}, bf16[512,768]{1,0:T(8,128)(2,1)}, u32[]{:S(2)}) copy-start(bf16[512,768]{1,0:T(8,128)(2,1)} %param.20) | copy-start | bytes 2359300
  313.1 1.8 copy-start.1
  (9 other events, 8.7 us)
Sparse Core Ops, SparseCore 0:
  9.7 31.2 all-gather.2
  42.5 28.6 all-gather.4
  142.2 87.0 all-reduce.6
  231.9 37.0 reduce-scatter.1

commit v3 on v2

v3 whole, which is shorter than its diff:
```python
from functools import partial

import jax
import jax.numpy as jnp
import numpy as np
from jax import lax
from jax.experimental import pallas as pl
from jax.experimental.pallas import tpu as pltpu
from jax.sharding import PartitionSpec as P

SPAN = 128
HDIM = 64
LANES = 128
LONGEST = 4096
EPSILON = 1e-05
TINY = 1e-30
F32 = jnp.float32
BF16 = jnp.bfloat16
BLOCK = 256


def mm(a, b):
    return jnp.dot(a, b, preferred_element_type=F32)


def mm_nt(a, b):
    return lax.dot_general(a, b, (((1,), (1,)), ((), ())), preferred_element_type=F32)


def mm_tn(a, b):
    return lax.dot_general(a, b, (((0,), (0,)), ((), ())), preferred_element_type=F32)


def pieces(v):
    high = v.astype(BF16)
    rest = v - high.astype(F32)
    mid = rest.astype(BF16)
    return high, mid, (rest - mid.astype(F32)).astype(BF16)


def exact_tn(a, b):
    return lax.dot_general(
        a, b, (((0,), (0,)), ((), ())), precision=lax.Precision.HIGHEST, preferred_element_type=F32
    )


def split(v, axis):
    high = v.astype(BF16)
    return jnp.concatenate([high, (v - high.astype(F32)).astype(BF16)], axis=axis)


def sigmoid(v):
    return 1.0 / (1.0 + jnp.exp(-v))


def softplus(v):
    return jnp.maximum(v, 0.0) + jnp.log1p(jnp.exp(-jnp.abs(v)))


def iota(shape, dim):
    return lax.broadcasted_iota(jnp.int32, shape, dim)


def groups(width):
    return [(n, n * LANES, (2 * n, 2 * n + 1)) for n in range(width // LANES)]


def sides(v, width):
    tiles = [v[:, at : at + LANES] for at in range(0, 2 * width, LANES)]
    return jnp.concatenate(tiles[::2], axis=1), jnp.concatenate(tiles[1::2], axis=1)


def stacked(v):
    first = iota(v.shape, 1) < HDIM
    zero = jnp.zeros_like(v)
    return jnp.concatenate([jnp.where(first, v, zero), jnp.where(first, zero, v)], axis=0)


def source_weights(pack, tot, dt, lane, nh):
    forward = lane < nh
    gap = jnp.where(forward, tot - pack, pack)
    kept = jnp.where(forward, pack[:, 38:39], pack[:, 40:41])
    return jnp.where(lane < 16, jnp.exp(jnp.where(lane < 16, gap, 0.0)) * kept * dt, 0.0)


def target_weights(pack, tot, lane, nh):
    forward = lane < nh
    gap = jnp.where(forward, pack, tot - pack)
    kept = jnp.where(forward, pack[:, 37:38], pack[:, 39:40])
    return jnp.where(lane < 16, jnp.exp(jnp.where(lane < 16, gap, 0.0)) * kept, 0.0)


def send_sides(at_ref, hops, up, down, refs):
    for d in range(1, hops + 1):
        low = (at_ref[0] // d) % 2 == 0
        refs[2 * d - 2][...] = jnp.where(low, up, down)
        refs[2 * d - 1][...] = jnp.where(low, down, up)


def land_sides(at_ref, hops, refs, from_earlier, from_later):
    for d in range(hops, 0, -1):
        low = (at_ref[0] // d) % 2 == 0
        first, second = refs[2 * d - 2][...], refs[2 * d - 1][...]
        for state, part in (
            (from_earlier, jnp.where(low, second, first)),
            (from_later, jnp.where(low, first, second)),
        ):
            if d == hops:
                state[...] = part[:HDIM]
            else:
                state[...] = part[:HDIM] + part[HDIM : HDIM + 1] * state[...]


def documents(off_ref, places):
    count = jnp.zeros(places.shape, F32)
    for at in range(0, off_ref.shape[1], LANES):
        begun = off_ref[0:1, at : at + LANES] <= places
        count = count + jnp.sum(jnp.where(begun, 1.0, 0.0), axis=1, keepdims=True)
    return count


def front_kernel(
    nh,
    hops,
    shares,
    own,
    at_ref,
    *refs,
):
    front_body(nh, hops, own, at_ref, refs[:shares], *refs[shares:])


def front_body(
    nh,
    hops,
    own,
    at_ref,
    x_refs,
    halo_ref,
    gain_ref,
    wg_ref,
    wsv_ref,
    wst_ref,
    wstr_ref,
    pcol_ref,
    prow_ref,
    taps_ref,
    off_ref,
    live_ref,
    ex_ref,
    tril_ref,
    triu_ref,
    normed_ref,
    normh_ref,
    gate_ref,
    act_ref,
    slope_ref,
    uv_ref,
    uvh_ref,
    pack_ref,
    rowa_ref,
    rowp_ref,
    segrow_ref,
    halocols_ref,
    tot_ref,
    sf_ref,
    rb_ref,
    gates_ref,
    gpre_ref,
    gsuf_ref,
    gtot_ref,
    *rest,
):
    messages = rest[: 2 * hops]
    ubuf, state, incb, marks, ends, docs = rest[2 * hops :]
    i = pl.program_id(0)
    tb = normed_ref.shape[0]
    per = tb // SPAN
    nc = rb_ref.shape[0]
    width = gate_ref.shape[1]
    piece = i * tb // own ^ at_ref[1]

    def norm(x):
        xf = x.astype(F32)
        s = lax.rsqrt(jnp.mean(xf * xf, axis=1, keepdims=True) + EPSILON)
        return (xf * s * gain_ref[0:1, :]).astype(BF16)

    @pl.when(i == 0)
    def _():
        edge = norm(halo_ref[...])
        normh_ref[...] = edge
        before = mm(edge, wsv_ref[...])
        ubuf[0:8, :] = before
        uvh_ref[...] = before
        state[...] = jnp.zeros_like(state)
        place = at_ref[2] - 8 + iota((8, 1), 0)
        here = documents(off_ref, place)
        lane8 = iota((8, LANES), 1)
        halo = jnp.zeros((8, LANES), F32)
        for k in (1, 2, 3):
            same = jnp.where(documents(off_ref, place + k) == here, 1.0, 0.0)
            halo = jnp.where(lane8 == k - 1, same, halo)
        halocols_ref[...] = halo

    @pl.when(i > 0)
    def _():
        ubuf[0:8, :] = ubuf[tb : tb + 8, :]

    for at in range(0, tb, 64):
        x = x_refs[0][at : at + 64, :]
        for k in range(1, len(x_refs)):
            x = jnp.where(piece == k, x_refs[k][at : at + 64, :], x)
        normed_ref[at : at + 64, :] = norm(x)
    nb = normed_ref[...]
    for at in range(0, width, LANES):
        tile = slice(at, at + LANES)
        gate_ref[:, tile] = mm(nb, wg_ref[:, tile]).astype(BF16)
    zr_all = mm_nt(wstr_ref[...], nb)
    lane = iota((SPAN, LANES), 1)
    forward = lane < nh
    forward_row = iota((16, SPAN), 0) < nh
    gate_lane = iota((8, LANES), 1) < nh
    for j in range(per):
        rows = slice(j * SPAN, (j + 1) * SPAN)
        base = at_ref[2] + (i * per + j) * SPAN
        around = documents(off_ref, base - 8 + iota((SPAN + 16, 1), 0))
        docs[...] = jnp.broadcast_to(around, docs.shape)
        seg = docs[8 : 8 + SPAN, :]
        prev_last, first = docs[7:8, :], docs[8:9, :]
        last, next_first = docs[7 + SPAN : 8 + SPAN, :], docs[8 + SPAN : 9 + SPAN, :]
        live = jnp.transpose(jnp.broadcast_to(live_ref[0:1, rows], (SPAN, SPAN)).astype(F32))
        mark = jnp.where(lane == 35, live, jnp.where(lane == 36, seg, 0.0))
        for k in (1, 2, 3):
            same = jnp.where(docs[8 - k : 8 - k + SPAN, :] == seg, 1.0, 0.0)
            mark = jnp.where(lane == 31 + k, same, mark)
            same = jnp.where(docs[8 + k : 8 + k + SPAN, :] == seg, 1.0, 0.0)
            mark = jnp.where(lane == 40 + k, same, mark)
        for k, bound in enumerate((prev_last, last, next_first, first)):
            mark = jnp.where(lane == 37 + k, jnp.where(seg == bound, 1.0, 0.0), mark)
        marks[rows, :] = mark
        opened = jnp.where(gate_lane, last - prev_last, next_first - first)
        ends[j * 8 : j * 8 + 8, :] = jnp.where(opened == 0.0, 1.0, 0.0)
        segrow_ref[:, rows] = jnp.transpose(seg)[:8]
    for at in range(0, LANES + width, LANES):
        tile = slice(at, at + LANES)
        uv = mm(nb, wsv_ref[:, tile])
        ubuf[8 : 8 + tb, tile] = uv
        uv_ref[:, tile] = uv.astype(BF16)
        for j in range(per):
            rows = slice(j * SPAN, (j + 1) * SPAN)
            keep = marks[rows, :]
            conv = taps_ref[0:1, tile] * ubuf[8 + j * SPAN : 8 + (j + 1) * SPAN, tile]
            for k in (1, 2, 3):
                moved = ubuf[8 - k + j * SPAN : 8 - k + (j + 1) * SPAN, tile]
                conv = conv + taps_ref[k : k + 1, tile] * moved * keep[:, 31 + k : 32 + k]
            sig = sigmoid(conv)
            live = keep[:, 35:36]
            act_ref[rows, tile] = (conv * sig * live).astype(BF16)
            slope_ref[rows, tile] = (live * sig * (1.0 + conv * (1.0 - sig))).astype(BF16)
    z_all = mm(nb, wst_ref[...])
    for j in range(per):
        rows = slice(j * SPAN, (j + 1) * SPAN)
        z = z_all[rows] + pcol_ref[0:1, :]
        dt = softplus(z)
        a = -dt * pcol_ref[1:2, :]
        total = mm(tril_ref[...], jnp.concatenate(pieces(a), axis=0))
        tot = total[SPAN - 1 : SPAN, :]
        cc = jnp.where(forward, total, total - a)
        pack = jnp.where(lane < 16, cc, jnp.where(lane < 32, z, marks[rows, :]))
        pack_ref[rows, :] = pack
        tot8 = jnp.broadcast_to(tot, (8, LANES))
        tot_ref[j * 8 : j * 8 + 8, :] = tot8
        dtr = softplus(zr_all[:, rows] + prow_ref[:, :SPAN])
        ar = -dtr * prow_ref[:, SPAN:]
        run = mm(jnp.concatenate(pieces(ar), axis=1), triu_ref[...])
        rowa = jnp.where(forward_row, run, run - ar)
        ldt = jnp.log(jnp.maximum(dtr, TINY))
        rowa_ref[:, rows] = rowa
        rowp_ref[:, rows] = jnp.where(forward_row, rowa - ldt, rowa + ldt)
        gates = split(jnp.exp(tot8) * ends[j * 8 : j * 8 + 8, :], 1)
        w = split(source_weights(pack, tot, dt, lane, nh), 1)
        bt = jnp.transpose(act_ref[rows, :LANES].astype(F32))[:HDIM].astype(BF16)
        c = i * per + j
        for n, at, _ in groups(width):
            tile = slice(at, at + LANES)
            both = slice(2 * at, 2 * at + 2 * LANES)
            x = act_ref[rows, LANES + at : 2 * LANES + at].astype(F32)
            wide = mm(w, ex_ref[:, both])
            fed = jnp.concatenate(
                [(x * wide[:, :LANES]).astype(BF16), (x * wide[:, LANES:]).astype(BF16)], axis=1
            )
            inc = mm(bt, fed)
            gate = mm(gates, ex_ref[:, both])
            gates_ref[c, :, both] = gate
            sf_ref[j, :, tile] = state[:, tile]
            state[:, tile] = state[:, tile] * gate[0:1, :LANES] + inc[:, :LANES]
            incb[c, :, tile] = inc[:, LANES:]

    @pl.when(i == pl.num_programs(0) - 1)
    def _():
        last_state = state[...]
        one = jnp.ones(gates_ref.shape[1:], F32)

        def up(c, p):
            gpre_ref[c] = p
            return p * gates_ref[c]

        p = lax.fori_loop(0, nc, up, one)
        tot_f, tot_b = sides(p, width)
        gtot_ref[:, :width] = tot_f
        gtot_ref[:, width:] = tot_b
        state[...] = jnp.zeros_like(state)

        def down(k, p):
            c = nc - 1 - k
            gsuf_ref[c] = p
            rb_ref[c] = state[...]
            gate = gates_ref[c]
            for n, at, _ in groups(width):
                tile = slice(at, at + LANES)
                second = slice(2 * at + LANES, 2 * at + 2 * LANES)
                state[:, tile] = state[:, tile] * gate[0:1, second] + incb[c, :, tile]
            return p * gate

        lax.fori_loop(0, nc, down, one)
        send_sides(
            at_ref,
            hops,
            jnp.concatenate([last_state, tot_f], axis=0),
            jnp.concatenate([state[...], tot_b], axis=0),
            messages,
        )


def inner_kernel(
    nh,
    act_ref,
    pack_ref,
    segrow_ref,
    rowp_ref,
    skip_ref,
    cot_ref,
    wo_ref,
    y_ref,
    dout_ref,
):
    tb, width = y_ref.shape
    for at in range(0, width, LANES):
        tile = slice(at, at + LANES)
        dout_ref[:, tile] = mm_nt(cot_ref[...], wo_ref[tile, :]).astype(BF16)
    t_at = iota((SPAN, SPAN), 0)
    s_at = iota((SPAN, SPAN), 1)
    lower = t_at > s_at
    for j in range(tb // SPAN):
        rows = slice(j * SPAN, (j + 1) * SPAN)
        bc = act_ref[rows, :LANES].astype(F32)
        b = bc[:, :HDIM].astype(BF16)
        c = pltpu.roll(bc, HDIM, 1)[:, :HDIM].astype(BF16)
        pack = pack_ref[rows, :]
        within = (pack[:, 36:37] == segrow_ref[0:1, rows]) & (t_at != s_at)
        score = jnp.where(within, mm_nt(c, b), 0.0)
        for n, at, heads in groups(width):
            tile = slice(at, at + LANES)
            mats = []
            for h in heads:
                gap = jnp.where(
                    lower,
                    pack[:, h : h + 1] - rowp_ref[h : h + 1, rows],
                    rowp_ref[nh + h : nh + h + 1, rows] - pack[:, nh + h : nh + h + 1],
                )
                mats.append((score * jnp.exp(gap)).astype(BF16))
            xp = act_ref[rows, LANES + at : 2 * LANES + at]
            y = mm(jnp.concatenate(mats, axis=1), stacked(xp))
            y_ref[rows, tile] = (y + skip_ref[0:1, tile] * xp.astype(F32)).astype(BF16)


def merge_kernel(
    nh,
    hops,
    at_ref,
    bc_ref,
    pack_ref,
    tot_ref,
    sf_ref,
    rb_ref,
    gpre_ref,
    gsuf_ref,
    yin_ref,
    gate_ref,
    dout_ref,
    mg_ref,
    ex_ref,
    *rest,
):
    arrived = rest[: 2 * hops]
    y_ref, stat_ref, full_ref, sent_ref, rent_ref = rest[2 * hops :]
    tb, width = y_ref.shape

    @pl.when(pl.program_id(0) == 0)
    def _():
        land_sides(at_ref, hops, arrived, sent_ref, rent_ref)

    lane = iota((SPAN, LANES), 1)
    row8 = iota((8, SPAN), 0)
    for j in range(tb // SPAN):
        rows = slice(j * SPAN, (j + 1) * SPAN)
        pack = pack_ref[rows, :]
        bc = bc_ref[rows, :].astype(F32)
        c = pltpu.roll(bc, HDIM, 1)[:, :HDIM].astype(BF16)
        w = split(target_weights(pack, tot_ref[j * 8 : j * 8 + 1, :], lane, nh), 1)
        energy = jnp.zeros((SPAN, LANES), F32)
        cross = jnp.zeros((SPAN, LANES), F32)
        for n, at, _ in groups(width):
            tile = slice(at, at + LANES)
            both = slice(2 * at, 2 * at + 2 * LANES)
            second = slice(2 * at + LANES, 2 * at + 2 * LANES)
            first = slice(2 * at, 2 * at + LANES)
            sfull = sf_ref[j, :, tile] + gpre_ref[j, 0:1, first] * sent_ref[:, tile]
            rfull = rb_ref[j, :, tile] + gsuf_ref[j, 0:1, second] * rent_ref[:, tile]
            held = jnp.concatenate([sfull.astype(BF16), rfull.astype(BF16)], axis=1)
            full_ref[j, :, both] = held
            seen = mm(c, held) * mm(w, ex_ref[:, both])
            y = (yin_ref[rows, tile].astype(F32) + seen[:, :LANES] + seen[:, LANES:]).astype(BF16)
            y_ref[rows, tile] = y
            gate = gate_ref[rows, tile].astype(F32)
            g = y.astype(F32) * gate * sigmoid(gate)
            energy = energy + g * g
            cross = cross + dout_ref[rows, tile].astype(F32) * mg_ref[0:1, tile] * g
        energy = jnp.sum(jnp.transpose(energy), axis=0, keepdims=True)
        cross = jnp.sum(jnp.transpose(cross), axis=0, keepdims=True)
        stat_ref[:, rows] = jnp.where(row8 == 0, energy, jnp.where(row8 == 1, cross, 0.0))


def turn_kernel(
    nh,
    inner,
    shares,
    hops,
    at_ref,
    y_ref,
    gate_ref,
    dout_ref,
    mg_ref,
    act_ref,
    pack_ref,
    tot_ref,
    gates_ref,
    gtot_ref,
    ex_ref,
    eye_ref,
    normed_ref,
    cot_ref,
    wo_ref,
    *rest,
):
    stats_in = rest[:shares]
    (
        mixer_ref,
        dy_ref,
        dgate_ref,
        gmix_ref,
        gskip_ref,
        gout_ref,
        ggate_ref,
        dso_ref,
        dro_ref,
        *messages,
        state,
        incf,
        outin,
        gout,
        ggate,
    ) = rest[shares:]
    i = pl.program_id(0)
    tb, width = y_ref.shape
    model = normed_ref.shape[1]
    per = tb // SPAN
    nc = dso_ref.shape[0]
    lane = iota((SPAN, LANES), 1)

    @pl.when(i == 0)
    def _():
        gmix_ref[...] = jnp.zeros_like(gmix_ref)
        gskip_ref[...] = jnp.zeros_like(gskip_ref)
        state[...] = jnp.zeros_like(state)
        gout[...] = jnp.zeros_like(gout)
        ggate[...] = jnp.zeros_like(ggate)

    for j in range(per):
        rows = slice(j * SPAN, (j + 1) * SPAN)
        stat = stats_in[0][:, rows]
        for more in stats_in[1:]:
            stat = stat + more[:, rows]
        stat = exact_tn(stat, eye_ref[0:8, :])
        q = lax.rsqrt(stat[:, 0:1] * (1.0 / inner) + EPSILON)
        k3 = q * q * q * stat[:, 1:2] * (1.0 / inner)
        pack = pack_ref[rows, :]
        w = split(target_weights(pack, tot_ref[j * 8 : j * 8 + 1, :], lane, nh), 1)
        ct = jnp.transpose(act_ref[rows, :LANES].astype(F32))[HDIM:].astype(BF16)
        c = i * per + j
        for n, at, _ in groups(width):
            tile = slice(at, at + LANES)
            both = slice(2 * at, 2 * at + 2 * LANES)
            second = slice(2 * at + LANES, 2 * at + 2 * LANES)
            y = y_ref[rows, tile].astype(F32)
            gate = gate_ref[rows, tile].astype(F32)
            sig = sigmoid(gate)
            sg = gate * sig
            g = y * sg
            gq = g * q
            dout = dout_ref[rows, tile].astype(F32)
            mg = mg_ref[0:1, tile]
            outin[rows, tile] = (gq * mg).astype(BF16)
            gmix_ref[0:1, tile] += jnp.sum(dout * gq, axis=0, keepdims=True)
            dg = dout * mg * q - g * k3
            dyb = (dg * sg).astype(BF16)
            dy_ref[rows, tile] = dyb
            dgate_ref[rows, tile] = (dg * y * (sig + sg * (1.0 - sig))).astype(BF16)
            dy = dyb.astype(F32)
            x = act_ref[rows, LANES + at : 2 * LANES + at].astype(F32)
            gskip_ref[0:1, tile] += jnp.sum(dy * x, axis=0, keepdims=True)
            wide = mm(w, ex_ref[:, both])
            fed = jnp.concatenate(
                [(dy * wide[:, :LANES]).astype(BF16), (dy * wide[:, LANES:]).astype(BF16)], axis=1
            )
            inc = mm(ct, fed)
            incf[c, :, tile] = inc[:, :LANES]
            dro_ref[j, :, tile] = state[:, tile]
            state[:, tile] = state[:, tile] * gates_ref[c, 0:1, second] + inc[:, LANES:]

    for at in range(0, model, 2 * LANES):
        tile = slice(at, at + 2 * LANES)
        mixer_ref[:, tile] = mm(outin[...], wo_ref[:, tile]).astype(BF16)
    for at in range(0, width, LANES):
        tile = slice(at, at + LANES)
        gout[tile, :] += mm_tn(outin[:, tile], cot_ref[...])
    for at in range(0, model, LANES):
        tile = slice(at, at + LANES)
        ggate[tile, :] += mm_tn(normed_ref[:, tile], dgate_ref[...])

    @pl.when(i == pl.num_programs(0) - 1)
    def _():
        gout_ref[...] = gout[...].astype(BF16)
        ggate_ref[...] = ggate[...].astype(BF16)
        last_state = state[...]
        state[...] = jnp.zeros_like(state)

        def down(k, _):
            c = nc - 1 - k
            dso_ref[c] = state[...]
            for n, at, _ in groups(width):
                tile = slice(at, at + LANES)
                first = slice(2 * at, 2 * at + LANES)
                state[:, tile] = state[:, tile] * gates_ref[c, 0:1, first] + incf[c, :, tile]
            return 0

        lax.fori_loop(0, nc, down, 0)
        send_sides(
            at_ref,
            hops,
            jnp.concatenate([last_state, gtot_ref[:, width:]], axis=0),
            jnp.concatenate([state[...], gtot_ref[:, :width]], axis=0),
            messages,
        )


def mid_kernel(
    nh,
    act_ref,
    pack_ref,
    segrow_ref,
    rowa_ref,
    dy_ref,
    eye_ref,
    dx_ref,
    dbc_ref,
    pulls_ref,
):
    tb, width = dx_ref.shape
    s_at = iota((SPAN, SPAN), 0)
    t_at = iota((SPAN, SPAN), 1)
    lower = t_at > s_at
    lane = iota((SPAN, LANES), 1)
    row16 = iota((16, SPAN), 0)
    front_half = lane < HDIM
    for j in range(tb // SPAN):
        rows = slice(j * SPAN, (j + 1) * SPAN)
        pack = pack_ref[rows, :]
        bc = act_ref[rows, :LANES].astype(F32)
        cb = pltpu.roll(bc, HDIM, 1)
        within = (pack[:, 36:37] == segrow_ref[0:1, rows]) & (t_at != s_at)
        score = mm_nt(bc[:, :HDIM].astype(BF16), cb[:, :HDIM].astype(BF16))
        score = jnp.where(within, score, 0.0)
        ldt = jnp.log(jnp.maximum(softplus(pltpu.roll(pack, LANES - 16, 1)), TINY))
        pc = jnp.where(lane < nh, pack - ldt, pack + ldt)
        dscore = jnp.zeros((SPAN, SPAN), F32)
        kc = jnp.zeros((SPAN, LANES), F32)
        qr = jnp.zeros((16, SPAN), F32)
        for n, at, heads in groups(width):
            tile = slice(at, at + LANES)
            dyp = dy_ref[rows, tile]
            dmats = mm_nt(stacked(act_ref[rows, LANES + at : 2 * LANES + at]), dyp)
            mats = []
            for m, h in enumerate(heads):
                decay = jnp.exp(
                    jnp.where(
                        lower,
                        rowa_ref[h : h + 1, rows] - pc[:, h : h + 1],
                        pc[:, nh + h : nh + h + 1] - rowa_ref[nh + h : nh + h + 1, rows],
                    )
                )
                spot = dmats[m * SPAN : (m + 1) * SPAN, :] * decay
                dscore = dscore + spot
                mats.append((score * decay).astype(BF16))
                pull = spot * score
                pull_low = jnp.where(lower, pull, 0.0)
                pull_up = pull - pull_low
                qr = jnp.where(row16 == h, jnp.sum(pull_low, axis=0, keepdims=True), qr)
                qr = jnp.where(row16 == nh + h, jnp.sum(pull_up, axis=0, keepdims=True), qr)
                kc = jnp.where(lane == h, jnp.sum(pull_low, axis=1, keepdims=True), kc)
                kc = jnp.where(lane == nh + h, jnp.sum(pull_up, axis=1, keepdims=True), kc)
            dx_ref[rows, tile] = mm(jnp.concatenate(mats, axis=1), stacked(dyp)).astype(BF16)
        dscore = jnp.where(within, dscore, 0.0).astype(BF16)
        cpad = jnp.where(front_half, cb, 0.0).astype(BF16)
        bpad = jnp.where(front_half, 0.0, cb).astype(BF16)
        dbc_ref[rows, :] = mm(dscore, cpad) + mm_tn(dscore, bpad)
        pulls_ref[rows, :] = kc + exact_tn(qr, eye_ref[...])


def back_kernel(
    nh,
    peers,
    hops,
    own,
    at_ref,
    act_ref,
    slope_ref,
    pack_ref,
    tot_ref,
    dy_ref,
    full_ref,
    dso_ref,
    dro_ref,
    gsuf_ref,
    gpre_ref,
    gates_ref,
    dxin_ref,
    dbc_ref,
    pulls_ref,
    uv_ref,
    uvh_ref,
    halocols_ref,
    taps_ref,
    skip_ref,
    pcol_ref,
    ex_ref,
    ext_ref,
    tril_ref,
    triu_ref,
    normed_ref,
    normh_ref,
    dgate_ref,
    wg_ref,
    wcat_ref,
    gmix_ref,
    gskip_ref,
    *rest,
):
    arrived = rest[: 2 * hops]
    mine_ref, theirs_ref, *chunks = rest[2 * hops : 2 * hops + 2 + peers]
    dbuf, hbuf, dcat, acc, lines, dsent_ref, drent_ref, parts = rest[2 * hops + 2 + peers :]
    i = pl.program_id(0)
    last = pl.num_programs(0) - 1
    tb = act_ref.shape[0]
    width = act_ref.shape[1] - LANES
    model = normed_ref.shape[1]

    @pl.when(i == 0)
    def _():
        dbuf[tb : tb + 8, :] = jnp.zeros((8, LANES + width), F32)
        acc[...] = jnp.zeros_like(acc)
        lines[...] = jnp.zeros_like(lines)
        land_sides(at_ref, hops, arrived, drent_ref, dsent_ref)

    lane = iota((SPAN, LANES), 1)
    forward = lane < nh
    head_lane = lane < 16
    none = jnp.zeros((HDIM, 2 * LANES), BF16)
    for j in reversed(range(tb // SPAN)):
        rows = slice(j * SPAN, (j + 1) * SPAN)
        pack = pack_ref[rows, :]
        tot = tot_ref[j * 8 : j * 8 + 1, :]
        z = pltpu.roll(pack, LANES - 16, 1)
        dt = softplus(z)
        w = jnp.concatenate(
            [
                split(source_weights(pack, tot, dt, lane, nh), 1),
                split(target_weights(pack, tot, lane, nh), 1),
            ],
            axis=0,
        )
        bc = act_ref[rows, :LANES].astype(F32)
        b = bc[:, :HDIM].astype(BF16)
        c = pltpu.roll(bc, HDIM, 1)[:, :HDIM].astype(BF16)
        dbc = dbc_ref[rows, :]
        carried = jnp.zeros((SPAN, LANES), F32)
        leaving = jnp.zeros((SPAN, LANES), F32)
        through = jnp.zeros((8, LANES), F32)
        for n, at, _ in groups(width):
            tile = slice(at, at + LANES)
            wtile = slice(LANES + at, 2 * LANES + at)
            both = slice(2 * at, 2 * at + 2 * LANES)
            first = slice(2 * at, 2 * at + LANES)
            second = slice(2 * at + LANES, 2 * at + 2 * LANES)
            wide = mm(w, ex_ref[:, both])
            x = act_ref[rows, wtile].astype(F32)
            dy = dy_ref[rows, tile].astype(F32)
            x2 = jnp.concatenate([x, x], axis=1)
            dy2 = jnp.concatenate([dy, dy], axis=1)
            held = full_ref[j, :, both]
            dheld = jnp.concatenate(
                [
                    dso_ref[j, :, tile] + gsuf_ref[j, 0:1, first] * dsent_ref[:, tile],
                    dro_ref[j, :, tile] + gpre_ref[j, 0:1, second] * drent_ref[:, tile],
                ],
                axis=1,
            )
            dheld_low = dheld.astype(BF16)
            to_wide = wide[:SPAN]
            fro_wide = wide[SPAN:]
            flow = mm(b, dheld_low) * to_wide
            seen = mm(c, held) * fro_wide
            dbc = dbc + mm_nt((x2 * to_wide).astype(BF16), jnp.concatenate([dheld_low, none], axis=0))
            dbc = dbc + mm_nt((dy2 * fro_wide).astype(BF16), jnp.concatenate([none, held], axis=0))
            ext = ext_ref[both, :]
            carried = carried + mm((dy2 * seen).astype(BF16), ext)
            leaving = leaving + mm((x2 * flow).astype(BF16), ext)
            product = jnp.sum(dheld * held.astype(F32), axis=0, keepdims=True) * gates_ref[j, :, both]
            through = through + mm(product.astype(BF16), ext)
            dx = dxin_ref[rows, tile].astype(F32) + flow[:, :LANES] + flow[:, LANES:]
            dx = dx + skip_ref[0:1, tile] * dy
            dbuf[rows, wtile] = dx * slope_ref[rows, wtile].astype(F32)
        dbuf[rows, :LANES] = dbc * slope_ref[rows, :LANES].astype(F32)
        pulls = pulls_ref[rows, :]
        kc = jnp.where(head_lane, pulls, 0.0)
        moved = jnp.where(head_lane, pltpu.roll(pulls, LANES - 16, 1), 0.0) + carried - kc
        before = mm(tril_ref[:, : 2 * SPAN], split(jnp.where(forward, leaving, moved), 0))
        after = mm(triu_ref[:, : 2 * SPAN], split(jnp.where(forward, moved, leaving), 0))
        dlog = before + after - leaving + through[0:1, :]
        sigz = sigmoid(z)
        rate = pcol_ref[1:2, :]
        dstep = (kc + leaving) * (sigz / jnp.maximum(dt, TINY)) - dlog * rate * sigz
        dstep = jnp.where(head_lane, dstep, 0.0)
        dcat[rows, :LANES] = dstep.astype(BF16)
        lines[7:8, :LANES] += jnp.sum(dstep, axis=0, keepdims=True)
        ends = jnp.where(head_lane, -dlog * dt * rate, 0.0)
        lines[8:9, :LANES] += jnp.sum(ends, axis=0, keepdims=True)
        for at in range(0, LANES + width, LANES):
            tile = slice(at, at + LANES)
            dconv = dbuf[rows, tile]
            uv = uv_ref[rows, tile].astype(F32)
            du = taps_ref[0:1, tile] * dconv
            lines[1:2, tile] += jnp.sum(uv * dconv, axis=0, keepdims=True)
            for k in (1, 2, 3):
                shifted = dbuf[j * SPAN + k : (j + 1) * SPAN + k, tile] * pack[:, 40 + k : 41 + k]
                du = du + taps_ref[k : k + 1, tile] * shifted
                lines[1 + k : 2 + k, tile] += jnp.sum(uv * shifted, axis=0, keepdims=True)
            dcat[rows, LANES + at : 2 * LANES + at] = du.astype(BF16)

    edge = dbuf[0:8, :]
    dbuf[tb : tb + 8, :] = edge
    for at in range(0, model, LANES):
        tile = slice(at, at + LANES)
        part = mm_nt(dgate_ref[...], wg_ref[tile, :]) + mm_nt(dcat[...], wcat_ref[tile, :])
        parts[:, tile] = part.astype(BF16)
        normed = normed_ref[:, tile]
        lines[0:1, tile] += jnp.sum(part * normed.astype(F32), axis=0, keepdims=True)
        acc[tile, :] += mm_tn(normed, dcat[...])
    side = ((last - i) * tb // own ^ at_ref[1]) % 2

    @pl.when(side == 0)
    def _():
        mine_ref[0] = parts[...]

    @pl.when(side == 1)
    def _():
        theirs_ref[0] = parts[...]

    @pl.when(i == last)
    def _():
        taps_at = slice(0, LANES + width)
        hbuf[0:8, :] = jnp.zeros_like(edge)
        hbuf[8:16, :] = edge
        duh = jnp.zeros_like(edge)
        for k in (1, 2, 3):
            shifted = hbuf[k : k + 8, :] * halocols_ref[:, k - 1 : k]
            duh = duh + taps_ref[k : k + 1, :] * shifted
            lines[1 + k : 2 + k, taps_at] += jnp.sum(uvh_ref[...] * shifted, axis=0, keepdims=True)
        duh = duh.astype(BF16)
        normh = normh_ref[...]
        parth = mm_nt(duh, wcat_ref[:, LANES:])
        lines[0:1, :] += jnp.sum(parth * normh.astype(F32), axis=0, keepdims=True)
        skips = jnp.zeros((8, LANES), F32)
        for n, at, _ in groups(width):
            ext = ext_ref[2 * at : 2 * at + LANES, :]
            high = gskip_ref[:, at : at + LANES].astype(BF16)
            low = (gskip_ref[:, at : at + LANES] - high.astype(F32)).astype(BF16)
            skips = skips + mm(high, ext) + mm(low, ext)
        lines[5:6, :LANES] = skips[0:1, :]
        lines[6:7, :width] = gmix_ref[0:1, :]
        acc[:, LANES:] += mm_tn(normh, duh)
        placed = jnp.where(iota((16, LANES), 1) == iota((16, LANES), 0) + 16, 1.0, 0.0)
        acc[:, :LANES] += exact_tn(lines[...], placed)
        row8 = iota((8, LANES), 0)
        taken = iota((8, LANES), 1) == 19 + 3 * at_ref[0] + row8
        taken = taken & (row8 > 4) & (at_ref[0] > 0)
        acc[:, :LANES] += exact_tn(parth, jnp.where(taken, 1.0, 0.0))
        size = model // peers
        for k in range(peers):
            start = pl.multiple_of((at_ref[0] ^ k) * size, 8)
            chunks[k][...] = acc[pl.ds(start, size), :].astype(BF16)


def token_grads(cot, x, s, dn, gain):
    scaled = dn * gain
    inside = jnp.mean(scaled * x, axis=1, keepdims=True)
    return (cot + s * scaled - x * (s * s * s) * inside).astype(BF16)


def finish_kernel(nh, peers, shares, at_ref, *refs):
    chunks = refs[:peers]
    eye_ref, ingain_ref, x_ref, cot_ref, dn_ref = refs[peers : peers + 5]
    gain_ref, value_ref, state_ref, step_ref, bias_ref, decay_ref = refs[peers + 5 : peers + 11]
    convv_ref, convs_ref, skip_ref, mixer_ref, late_ref, extra = refs[peers + 11 :]
    size = chunks[0].shape[0]
    real_width = value_ref.shape[1]
    heads = step_ref.shape[0]
    for k in range(peers):
        rows = pl.ds(pl.multiple_of((at_ref[0] ^ k) * size, 8), size)
        extra[rows, :] = chunks[k][:, :LANES].astype(F32)
        state_ref[rows, :] = chunks[k][:, LANES : 2 * LANES].astype(F32)
        value_ref[rows, :] = chunks[k][:, 2 * LANES : 2 * LANES + real_width].astype(F32)
    found = extra[...].astype(BF16)
    lines = mm_nt(eye_ref[...], found)
    row16 = iota((16, LANES), 0)
    taken = iota((16, LANES), 1) == 27 + 3 * at_ref[0] + row16 - 13
    taken = taken & (row16 > 12) & (at_ref[1] == shares - 1)
    late = mm_nt(jnp.where(taken, 1.0, 0.0).astype(BF16), found)
    x = x_ref[...].astype(F32)
    s = lax.rsqrt(jnp.mean(x * x, axis=1, keepdims=True) + EPSILON)
    cot = cot_ref[...].astype(F32)
    late_ref[...] = token_grads(cot, x, s, dn_ref[...] + late, ingain_ref[...])
    for h in range(heads):
        step_ref[h, 0:1, :] = lines[h : h + 1, :]
        step_ref[h, 1:2, :] = lines[nh + h : nh + h + 1, :]
    gain_ref[...] = lines[16:17, :] / ingain_ref[...]
    convs_ref[...] = lines[17:21, :LANES]
    convv_ref[...] = lines[17:21, LANES : LANES + real_width]
    skip_ref[...] = lines[21:22, :heads]
    mixer_ref[...] = lines[22:23, :real_width]
    bias_ref[0:1, :] = lines[23:24, :heads]
    bias_ref[1:2, :] = lines[23:24, nh : nh + heads]
    decay_ref[...] = lines[24:25, :heads] + lines[24:25, nh : nh + heads]


def whole(shape):
    return pl.BlockSpec(shape, lambda i, *_: (0,) * len(shape))


def row_block(rows, width):
    return pl.BlockSpec((rows, width), lambda i, *_: (i, 0))


def lane_block(rows, width):
    return pl.BlockSpec((rows, width), lambda i, *_: (0, i))


def chunk_block(per, rows, width):
    return pl.BlockSpec((per, rows, width), lambda i, *_: (i, 0, 0))


def sds(shape, dtype):
    return jax.ShapeDtypeStruct(shape, dtype)


def call(kernel, name, grid, ins, outs, scratch, flops, operands, scalars=()):
    return pl.pallas_call(
        kernel,
        name=name,
        grid_spec=pltpu.PrefetchScalarGridSpec(
            num_scalar_prefetch=len(scalars),
            grid=(grid,),
            in_specs=ins,
            out_specs=[spec for spec, _ in outs],
            scratch_shapes=scratch,
        ),
        out_shape=[shape for _, shape in outs],
        compiler_params=pltpu.CompilerParams(
            dimension_semantics=("arbitrary",), vmem_limit_bytes=56 * 1024 * 1024
        ),
        cost_estimate=pl.CostEstimate(
            flops=int(flops), bytes_accessed=1, transcendentals=0
        ),
    )(*scalars, *operands)


def shifted_in(array, axis, by):
    length = lax.axis_size(axis)
    pairs = [(i, i + by) for i in range(length) if 0 <= i + by < length]
    return lax.ppermute(array, axis, pairs)


def exchange_sides(messages, hops):
    size = lax.axis_size("seq")
    arrived = []
    for d in range(1, hops + 1):
        for side in (0, 1):
            pairs = [(i, i + d) for i in range(size - d) if (i // d) % 2 == side]
            both = pairs + [(b, a) for a, b in pairs]
            arrived.append(lax.ppermute(messages[len(arrived)], "seq", both))
    return arrived


def swap(array, axis, k):
    n = lax.axis_size(axis)
    return lax.ppermute(array, axis, [(i, i ^ k) for i in range(n)])


def sum_over(array, axis):
    size = lax.axis_size(axis)
    result = array
    for k in range(1, size):
        result = result + lax.ppermute(array, axis, [(i, i ^ k) for i in range(size)])
    return result


def per_device(
    tokens,
    input_gain,
    proj_gate,
    proj_value,
    proj_state,
    proj_step,
    step_bias,
    decay_log,
    conv_value,
    conv_state,
    skip_gain,
    mixer_gain,
    proj_out,
    doc_lengths,
    pad_mask,
    cotangent,
):
    head_devices = lax.axis_size("head")
    length = pad_mask.shape[0]
    model = tokens.shape[1]
    real_width = proj_gate.shape[1]
    real_heads = proj_step.shape[2]
    inner = real_width * head_devices
    width = -(-real_width // LANES) * LANES
    nh = width // HDIM

    def padded(array, axis, size):
        if array.shape[axis] == size:
            return array
        widths = [(0, 0)] * array.ndim
        widths[axis] = (0, size - array.shape[axis])
        return jnp.pad(array, widths)

    proj_gate = padded(proj_gate, 1, width)
    proj_value = padded(proj_value, 1, width)
    proj_step = padded(proj_step, 2, nh)
    step_bias = padded(step_bias, 1, nh)
    conv_value = padded(conv_value, 1, width)
    skip_gain = padded(skip_gain, 0, nh)
    mixer_gain = padded(mixer_gain, 0, width)
    proj_out = padded(proj_out, 0, width)
    nc = length // SPAN
    tb = BLOCK
    per = tb // SPAN
    grid = length // tb
    wide = LANES + width
    hops = -(-(LONGEST - 1) // length)
    seq_index = lax.axis_index("seq")
    first_place = seq_index * length
    all_tokens = length * lax.axis_size("seq")

    edge_rows = shifted_in(tokens[tokens.shape[0] - 8 :], "seq", 1)
    here = lax.axis_index("head")
    halo = jnp.where(here == head_devices - 1, edge_rows, 0)
    for k in range(1, head_devices):
        halo = halo + jnp.where(here ^ k == head_devices - 1, swap(edge_rows, "head", k), 0)

    offsets = jnp.cumsum(doc_lengths) - doc_lengths
    room = -(-(offsets.shape[0] + 1) // LANES) * LANES - offsets.shape[0]
    fill = jnp.where(jnp.arange(room) == 0, all_tokens, 2 * all_tokens).astype(offsets.dtype)
    offsets = jnp.concatenate([offsets, fill])[None, :]
    live_row = pad_mask[None, :]
    lanes = np.arange(LANES)
    column = np.arange(2 * width)
    head_of = column // (2 * LANES) * 2 + column % LANES // HDIM
    head_of = head_of + np.where(column % (2 * LANES) >= LANES, nh, 0)
    ext = jnp.asarray(head_of[:, None] == lanes[None, :], BF16)
    ex = jnp.asarray(np.tile(head_of[None, :] == lanes[:, None], (2, 1)), BF16)
    at = np.arange(SPAN)
    tril = jnp.asarray(np.tile(at[:, None] >= at[None, :], (1, 3)), BF16)
    triu = at[:, None] <= at[None, :]
    triu_wide = jnp.asarray(np.tile(triu, (1, 2)), BF16)
    triu_tall = jnp.asarray(np.tile(triu, (3, 1)), BF16)
    eye = jnp.asarray(np.arange(16)[:, None] == lanes[None, :], F32)
    eye16 = jnp.asarray(np.arange(16)[:, None] + 16 == lanes[None, :], F32)
    picked = jnp.asarray(np.arange(32)[:, None] == lanes[None, :], BF16)
    peers = lax.axis_size("seq")
    own = length // head_devices
    bits = head_devices.bit_length() - 1
    scalars = [jnp.stack([seq_index, here, first_place]).astype(jnp.int32)]
    size = model // peers

    rate = padded(jnp.exp(decay_log), 0, nh)
    bias_line = jnp.concatenate([step_bias[0], step_bias[1]])
    rate_line = jnp.concatenate([rate, rate])
    pcol = jnp.zeros((8, LANES), F32)
    pcol = pcol.at[0, : 2 * nh].set(bias_line).at[1, : 2 * nh].set(rate_line)
    pcol = pcol.at[0, 16 : 16 + 2 * nh].set(bias_line)
    pad16 = jnp.zeros((16 - 2 * nh,), F32)
    prow = jnp.concatenate(
        [
            jnp.broadcast_to(jnp.concatenate([bias_line, pad16])[:, None], (16, SPAN)),
            jnp.broadcast_to(jnp.concatenate([rate_line, pad16])[:, None], (16, SPAN)),
        ],
        axis=1,
    )
    steps = jnp.concatenate([proj_step[0], proj_step[1]], axis=1)
    wst = jnp.pad(steps, ((0, 0), (0, 16 - 2 * nh)))
    wst = jnp.pad(jnp.tile(wst, (1, 2)), ((0, 0), (0, LANES - 32)))
    wback = jnp.pad(steps, ((0, 0), (0, LANES - 2 * nh)))
    wstr = jnp.pad(steps.T, ((0, 16 - 2 * nh), (0, 0)))
    wsv = jnp.concatenate([proj_state, proj_value], axis=1)
    taps = jnp.pad(jnp.concatenate([conv_state, conv_value], axis=1), ((0, 4), (0, 0)))
    gain = jnp.broadcast_to(input_gain[None, :], (8, model))
    mg = jnp.broadcast_to(mixer_gain[None, :], (8, width))
    skip = jnp.broadcast_to(jnp.repeat(skip_gain, HDIM)[None, :], (8, width))

    wcat = jnp.concatenate([wback, wsv], axis=1)
    pieces_of = {0: tokens}
    for bit in [1 << b for b in range(bits - 1, 0, -1)]:
        pieces_of.update({k | bit: swap(v, "head", bit) for k, v in pieces_of.items()})
    prelims = (halo, offsets, live_row, pcol, prow, wst, wstr, wsv, taps, gain, mg, skip, wcat)
    pieces_of, late, prelims, scalars = lax.optimization_barrier(
        (pieces_of, cotangent, prelims, scalars)
    )
    halo, offsets, live_row, pcol, prow, wst, wstr, wsv, taps, gain, mg, skip, wcat = prelims
    pieces_of.update({k | 1: swap(v, "head", 1) for k, v in pieces_of.items()})
    token_pieces = [pieces_of[k] for k in range(head_devices)]
    cot_all = lax.all_gather(late, "head", axis=0, tiled=True)

    rows = partial(row_block, tb)
    states = sds((nc, HDIM, width), F32)
    gates_of = sds((nc, 8, 2 * width), F32)
    message = sds((HDIM + 8, width), F32)
    state_block = chunk_block(per, HDIM, width)
    gate_block = chunk_block(per, 8, 2 * width)
    tot_block = row_block(per * 8, LANES)
    messages = [(whole(message.shape), message)] * (2 * hops)

    def taller(factor):
        big = tb * factor
        return (
            grid // factor,
            partial(row_block, big),
            partial(lane_block, width=big),
            partial(chunk_block, per * factor),
            row_block(per * factor * 8, LANES),
        )

    def slot_of(j, at):
        place = j ^ at[1]
        return sum(((place >> b) & 1) << (bits - 1 - b) for b in range(bits))

    each = own // tb

    def piece_block(k):
        def index(i, at):
            return jnp.clip(i - (at[1] ^ k) * each, 0, each - 1), 0

        return pl.BlockSpec((tb, model), index)

    def side_block(side):
        def index(i, at):
            row = grid - 1 - i
            j, sub = row // each, row % each
            ours = (j ^ at[1]) % 2 == side
            first = j == head_devices - 1
            j = jnp.where(ours, j, jnp.where(first, j - 1, j + 1))
            sub = jnp.where(ours, sub, jnp.where(first, each - 1, 0))
            return slot_of(j, at) % (head_devices // 2), sub, 0

        return pl.BlockSpec((1, tb, model), index)

    (
        normed,
        normh,
        gate_in,
        acted,
        slope,
        uv,
        uvh,
        pack,
        rowa,
        rowp,
        seg_row,
        halo_cols,
        tot,
        sf,
        rb,
        gates,
        gpre,
        gsuf,
        gtot,
        *ahead,
    ) = call(
        partial(front_kernel, nh, hops, head_devices, own),
        "front",
        grid,
        [piece_block(k) for k in range(head_devices)]
        + [
            whole((8, model)),
            whole((8, model)),
            whole((model, width)),
            whole((model, wide)),
            whole((model, LANES)),
            whole((16, model)),
            whole((8, LANES)),
            whole((16, 2 * SPAN)),
            whole((8, wide)),
            whole(offsets.shape),
            lane_block(1, tb),
            whole(ex.shape),
            whole(tril.shape),
            whole(triu_tall.shape),
        ],
        [
            (rows(model), sds((length, model), BF16)),
            (whole((8, model)), sds((8, model), BF16)),
            (rows(width), sds((length, width), BF16)),
            (rows(wide), sds((length, wide), BF16)),
            (rows(wide), sds((length, wide), BF16)),
            (rows(wide), sds((length, wide), BF16)),
            (whole((8, wide)), sds((8, wide), F32)),
            (rows(LANES), sds((length, LANES), F32)),
            (lane_block(16, tb), sds((16, length), F32)),
            (lane_block(16, tb), sds((16, length), F32)),
            (lane_block(8, tb), sds((8, length), F32)),
            (whole((8, LANES)), sds((8, LANES), F32)),
            (tot_block, sds((nc * 8, LANES), F32)),
            (state_block, states),
            (whole(states.shape), states),
            (whole(gates_of.shape), gates_of),
            (whole(gates_of.shape), gates_of),
            (whole(gates_of.shape), gates_of),
            (whole((8, 2 * width)), sds((8, 2 * width), F32)),
        ]
        + messages,
        [
            pltpu.VMEM((tb + 8, wide), F32),
            pltpu.VMEM((HDIM, width), F32),
            pltpu.VMEM((nc, HDIM, width), F32),
            pltpu.VMEM((tb, LANES), F32),
            pltpu.VMEM((per * 8, LANES), F32),
            pltpu.VMEM((SPAN + 16, LANES), F32),
        ],
        25e9,
        token_pieces
        + [
            halo,
            gain,
            proj_gate,
            wsv,
            wst,
            wstr,
            pcol,
            prow,
            taps,
            offsets,
            live_row,
            ex,
            tril,
            triu_tall,
        ],
        scalars,
    )

    ahead = exchange_sides(ahead, hops)

    big_grid, big_rows, big_lanes, big_chunks, big_tot = taller(2)
    yin, dout = call(
        partial(inner_kernel, nh),
        "inner",
        big_grid,
        [
            big_rows(wide),
            big_rows(LANES),
            big_lanes(8),
            big_lanes(16),
            whole((8, width)),
            big_rows(model),
            whole((width, model)),
        ],
        [
            (big_rows(width), sds((length, width), BF16)),
            (big_rows(width), sds((length, width), BF16)),
        ],
        [],
        6e9,
        [acted, pack, seg_row, rowp, skip, cot_all, proj_out],
    )

    y, stat, full = call(
        partial(merge_kernel, nh, hops),
        "merge",
        big_grid,
        [
            big_rows(LANES),
            big_rows(LANES),
            big_tot,
            big_chunks(HDIM, width),
            big_chunks(HDIM, width),
            big_chunks(8, 2 * width),
            big_chunks(8, 2 * width),
            big_rows(width),
            big_rows(width),
            big_rows(width),
            whole((8, width)),
            whole(ex.shape),
        ]
        + [whole(message.shape)] * (2 * hops),
        [
            (big_rows(width), sds((length, width), BF16)),
            (big_lanes(8), sds((8, length), F32)),
            (big_chunks(HDIM, 2 * width), sds((nc, HDIM, 2 * width), BF16)),
        ],
        [pltpu.VMEM((HDIM, width), F32)] * 2,
        6e9,
        [acted, pack, tot, sf, rb, gpre, gsuf, yin, gate_in, dout, mg, ex] + ahead,
        scalars,
    )

    shares = [stat]
    for k in range(1, head_devices):
        shares.append(lax.ppermute(stat, "head", [(i, i ^ k) for i in range(head_devices)]))

    mixer, dy, dgate, gmix, gskip, gout, ggate, dso, dro, *behind = call(
        partial(turn_kernel, nh, inner, head_devices, hops),
        "turn",
        grid,
        [
            rows(width),
            rows(width),
            rows(width),
            whole((8, width)),
            rows(wide),
            rows(LANES),
            tot_block,
            whole(gates_of.shape),
            whole((8, 2 * width)),
            whole(ex.shape),
            whole((16, LANES)),
            rows(model),
            rows(model),
            whole((width, model)),
        ]
        + [lane_block(8, tb)] * head_devices,
        [
            (rows(model), sds((length, model), BF16)),
            (rows(width), sds((length, width), BF16)),
            (rows(width), sds((length, width), BF16)),
            (whole((8, width)), sds((8, width), F32)),
            (whole((8, width)), sds((8, width), F32)),
            (whole((width, model)), sds((width, model), BF16)),
            (whole((model, width)), sds((model, width), BF16)),
            (whole(states.shape), states),
            (state_block, states),
        ]
        + messages,
        [
            pltpu.VMEM((HDIM, width), F32),
            pltpu.VMEM((nc, HDIM, width), F32),
            pltpu.VMEM((tb, width), BF16),
            pltpu.VMEM((width, model), F32),
            pltpu.VMEM((model, width), F32),
        ],
        24e9,
        [
            y,
            gate_in,
            dout,
            mg,
            acted,
            pack,
            tot,
            gates,
            gtot,
            ex,
            eye,
            normed,
            cot_all,
            proj_out,
        ]
        + shares,
        scalars,
    )

    grad_proj_out, grad_proj_gate = lax.psum((gout, ggate), "seq")
    mixer = lax.psum_scatter(mixer, "head", scatter_dimension=0, tiled=True)
    behind = exchange_sides(behind, hops)

    dxin, dbc, pulls = call(
        partial(mid_kernel, nh),
        "mid",
        grid,
        [
            rows(wide),
            rows(LANES),
            lane_block(8, tb),
            lane_block(16, tb),
            rows(width),
            whole((16, LANES)),
        ],
        [
            (rows(width), sds((length, width), BF16)),
            (rows(LANES), sds((length, LANES), F32)),
            (rows(LANES), sds((length, LANES), F32)),
        ],
        [],
        18e9,
        [acted, pack, seg_row, rowa, dy, eye16],
    )

    back = lambda i: grid - 1 - i

    def rev(spec):
        return pl.BlockSpec(spec.block_shape, lambda i, *_: spec.index_map(back(i)))

    mine, theirs, *chunks = call(
        partial(back_kernel, nh, peers, hops, own),
        "back",
        grid,
        [
            rev(rows(wide)),
            rev(rows(wide)),
            rev(rows(LANES)),
            rev(tot_block),
            rev(rows(width)),
            rev(chunk_block(per, HDIM, 2 * width)),
            rev(state_block),
            rev(state_block),
            rev(gate_block),
            rev(gate_block),
            rev(gate_block),
            rev(rows(width)),
            rev(rows(LANES)),
            rev(rows(LANES)),
            rev(rows(wide)),
            whole((8, wide)),
            whole((8, LANES)),
            whole((8, wide)),
            whole((8, width)),
            whole((8, LANES)),
            whole(ex.shape),
            whole(ext.shape),
            whole(tril.shape),
            whole(triu_wide.shape),
            rev(rows(model)),
            whole((8, model)),
            rev(rows(width)),
            whole((model, width)),
            whole((model, LANES + wide)),
            whole((8, width)),
            whole((8, width)),
        ]
        + [whole(message.shape)] * (2 * hops),
        [
            (side_block(0), sds((head_devices // 2, own, model), BF16)),
            (side_block(1), sds((head_devices // 2, own, model), BF16)),
        ]
        + [(whole((size, LANES + wide)), sds((size, LANES + wide), BF16))] * peers,
        [
            pltpu.VMEM((tb + 8, wide), F32),
            pltpu.VMEM((16, wide), F32),
            pltpu.VMEM((tb, LANES + wide), BF16),
            pltpu.VMEM((model, LANES + wide), F32),
            pltpu.VMEM((16, model), F32),
            pltpu.VMEM((HDIM, width), F32),
            pltpu.VMEM((HDIM, width), F32),
            pltpu.VMEM((tb, model), BF16),
        ],
        33e9,
        [
            acted,
            slope,
            pack,
            tot,
            dy,
            full,
            dso,
            dro,
            gsuf,
            gpre,
            gates,
            dxin,
            dbc,
            pulls,
            uv,
            uvh,
            halo_cols,
            taps,
            skip,
            pcol,
            ex,
            ext,
            tril,
            triu_wide,
            normed,
            normh,
            dgate,
            proj_gate,
            wcat,
            gmix,
            gskip,
        ]
        + behind,
        scalars,
    )

    got = swap(theirs, "head", 1)
    summed = chunks[0].astype(F32)
    for k in range(1, peers):
        summed = summed + swap(chunks[k], "seq", k).astype(F32)
    shared = summed[:, : 2 * LANES]
    row_at = seq_index * size + jnp.arange(size)[:, None]
    lane_at = jnp.arange(2 * LANES)[None, :]
    common = (lane_at == 16) | (lane_at > 26)
    common = common | ((lane_at > 16) & (lane_at < 21) & (row_at < LANES))
    shared = jnp.where(common, sum_over(shared, "head"), shared)

    own_in = mine.astype(F32) + got.astype(F32)
    for b in range(1, bits):
        half = own_in.shape[0] // 2
        own_in = own_in[:half] + swap(own_in[half:].astype(BF16), "head", 1 << b).astype(F32)
    own_in = own_in[0]

    reduced = jnp.concatenate([shared, summed[:, 2 * LANES :]], axis=1).astype(BF16)
    spread_out = [reduced] + [swap(reduced, "seq", k) for k in range(1, peers)]
    layer_out = (tokens.astype(F32) + mixer.astype(F32)).astype(BF16)

    token_values = tokens.astype(F32)
    scale_rows = lax.rsqrt(jnp.mean(token_values * token_values, axis=1, keepdims=True) + EPSILON)
    grad_tokens = token_grads(cotangent.astype(F32), token_values, scale_rows, own_in, input_gain)

    finals = [
        sds((1, model), F32),
        sds((model, real_width), F32),
        sds((model, LANES), F32),
        sds((real_heads, 2, model), F32),
        sds((2, real_heads), F32),
        sds((1, real_heads), F32),
        sds((4, real_width), F32),
        sds((4, LANES), F32),
        sds((1, real_heads), F32),
        sds((1, real_width), F32),
        sds((16, model), BF16),
    ]
    ggain, gvalue, gstate, gstep, gbias, gdecay, gconvv, gconvs, gskips, gmixer, late = call(
        partial(finish_kernel, nh, peers, head_devices),
        "finish",
        1,
        [whole((size, LANES + wide))] * peers
        + [whole((32, LANES)), whole((1, model))]
        + [whole((16, model))] * 3,
        [(whole(f.shape), f) for f in finals],
        [pltpu.VMEM((model, LANES), F32)],
        3e9,
        spread_out
        + [picked, input_gain[None, :]]
        + [tokens[own - 16 :], cotangent[own - 16 :], own_in[own - 16 :]],
        scalars,
    )
    grad_tokens = lax.dynamic_update_slice(grad_tokens, late, (own - 16, 0))
    return (
        layer_out,
        grad_tokens,
        ggain[0],
        grad_proj_gate[:, :real_width].astype(F32),
        gvalue,
        gstate,
        jnp.transpose(gstep, (1, 2, 0)),
        gbias,
        gdecay[0],
        gconvv,
        gconvs,
        gskips[0],
        gmixer[0],
        grad_proj_out[:real_width].astype(F32),
    )


def solution(mesh):
    return jax.shard_map(
        per_device,
        mesh=mesh,
        in_specs=(
            P(("seq", "head"), None),
            P(),
            P(None, "head"),
            P(None, "head"),
            P(),
            P(None, None, "head"),
            P(None, "head"),
            P("head"),
            P(None, "head"),
            P(),
            P("head"),
            P("head"),
            P("head", None),
            P(),
            P("seq"),
            P(("seq", "head"), None),
        ),
        out_specs=(
            P(("seq", "head"), None),
            P(("seq", "head"), None),
            P(),
            P(None, "head"),
            P(None, "head"),
            P(),
            P(None, None, "head"),
            P(None, "head"),
            P("head"),
            P(None, "head"),
            P(),
            P("head"),
            P("head"),
            P("head", None),
        ),
        check_vma=False,
    )
```

time: 328 us -> 299 us (0.912)
  waiting for transfers between devices: 55.2 us -> 34.9 us
  matrix products: 9.9 us -> 0 us
  other arithmetic: 32.5 us -> 24 us
  Pallas kernels: 125 us -> 132 us
    ppermute x10 -> x1, starting transfers between devices: 27.3 us -> 3.41 us  [shifted_in(): return lax.ppermute(array, axis, pairs)]
    all_gather x2 -> x1, waiting for transfers between devices: 23 us -> 0.02 us  [per_device(): cot_all = lax.all_gather(late, 'head', axis=0, tiled=True)]
    ppermute x6 -> x3, waiting for transfers between devices: 1.23 us -> 18.4 us  [sum_over(): lax.ppermute(array, axis, [(i, i ^ k) for i in range(size)])]
    ppermute x0 -> x11, starting transfers between devices: none -> 15.4 us  [the longest x8 13.5 us: exchange_sides(): arrived.append(lax.ppermute(messages[len(arrived)], 'seq', both))]
    ppermute x16 -> x22, starting transfers between devices: 37.7 us -> 50.5 us  [swap(): return lax.ppermute(array, axis, [(i, i ^ k) for i in range(n)])]
    ppermute x10 -> x1, waiting for transfers between devices: 11.5 us -> 0.01 us  [shifted_in(): return lax.ppermute(array, axis, pairs)]
    dot_general x3 -> x0, matrix products: 9.9 us -> none  [the longest x2 6.45 us: weight_grad(): lax.dot_general(a, b, (((0,), (0,)), ((), ())), preferred_element_type=F32)]
    pallas_call x6 -> x7, Pallas kernels: 125 us -> 132 us  [call(): pl.pallas_call(kernel, name=name, grid_spec=pltpu.PrefetchScalarGridSpec(...]
  transfers between devices with their start and end apart: 36 -> 40, of which waited for: 13 -> 10; matrix products, arithmetic and copies ran while one was open for 15% -> 11% of each run, Pallas kernels for 29% -> 33%
where the time goes in v3:
time: 299 us; the launch traced here: 297 us
  Pallas kernels  132 us (44%)
  starting transfers between devices  71.3 us (24%)
  waiting for transfers between devices  34.9 us (12%)
  other arithmetic  24 us (8%)
  local copies, waits for them, and re-layouts  21.1 us (7%)
  between operations  14.4 us (5%)
    pallas_call x7, Pallas kernels, call(): pl.pallas_call(kernel, name=name, grid_spec=pltpu.PrefetchScalarGridSpec(...  132 us
    ppermute x22, starting transfers between devices, swap(): return lax.ppermute(array, axis, [(i, i ^ k) for i in range(n)])  50.5 us
    ppermute x3, waiting for transfers between devices, sum_over(): lax.ppermute(array, axis, [(i, i ^ k) for i in range(size)])  18.4 us
    ppermute x8, starting transfers between devices, exchange_sides(): arrived.append(lax.ppermute(messages[len(arrived)], 'seq', both))  13.5 us
    ppermute x22, waiting for transfers between devices, swap(): return lax.ppermute(array, axis, [(i, i ^ k) for i in range(n)])  12.6 us
    unnamed x72, local copies, waits for them, and re-layouts  6.36 us
  transfers between devices with their start and end apart: 40, of which 10 were waited for; matrix products, arithmetic and copies ran while one was open for 11% of the time, Pallas kernels for 33%

profile of v3, /device:TPU:0, one launch (start us, length us, event | category | flops | bytes accessed | tf_op | source)
XLA Modules:
  0.0 297.5 jit_solution(3500779426520295591)
XLA Ops:
  7.2 3.0 %collective-permute-start = (bf16[512,768]{1,0:T(8,128)(2,1)}, bf16[512,768]{1,0:T(8,128)(2,1)S(1)}, u32[]{:S(2)}, u32[]{:S(2)}) collective-permute-start(bf16[512,768]{1,0:T(8,128)(2,1)} %refs_0_), channel_id=1, source_target_pairs={{0,2},{1,3},{2,0},{3,1},{4,6},{5,7},{6,4},{7,5},{8,10},{9,11},{10,... | collective-permute-start | bytes 2359304 | tf_op jit(solution)/shard_map/ppermute | solution.py:926
  10.3 0.7 slice.98
  11.0 3.4 %collective-permute-start.1 = (bf16[8,768]{1,0:T(8,128)(2,1)S(1)}, bf16[8,768]{1,0:T(8,128)(2,1)S(1)}, u32[]{:S(2)}, u32[]{:S(2)}) collective-permute-start(bf16[8,768]{1,0:T(8,128)(2,1)S(1)} %slice.98), channel_id=1, source_target_pairs={{0,4},{4,8},{8,12},{12,16},{16,20},{20,24},{24,28},{1,5},{5,9},{9,... | collective-permute-start | bytes 36872 | tf_op jit(solution)/shard_map/ppermute | solution.py:910
  14.4 0.7 copy.48
  15.4 0.7 sub.6
  16.1 0.8 slice_bitcast_fusion.2
  16.8 0.7 exp.3
  17.6 1.3 and_reduce_fusion
  19.4 0.8 fusion.10
  21.4 1.3 select_maximum_fusion.refs_12_.taps_ref
  23.3 2.1 pad_maximum_fusion.refs_7_
  25.4 1.1 fusion.8.wcat_ref
  27.3 0.9 collective-permute-start.3
  28.2 1.0 collective-permute-start.2
  29.2 2.0 broadcast_select_fusion
  31.2 1.6 scatter.14.refs_10_.pcol_ref
  32.9 0.7 pad.32.refs_8_
  37.6 1.8 collective-permute-done.5.refs_1_
  39.4 1.1 collective-permute-done.6.refs_3_
  40.5 0.9 copy-done.20
  41.4 31.0 %front.1 = (bf16[2048,768]{1,0:T(8,128)(2,1)}, bf16[8,768]{1,0:T(8,128)(2,1)}, bf16[2048,384]{1,0:T(8,128)(2,1)}, bf16[2048,512]{1,0:T(8,128)(2,1)}, bf16[2048,5...) custom-call(s32[3]{0:T(128)} %pad_add_fusion.at_ref, ...), custom_call_target="tpu_custom_call" | custom-call | flops 24999999488 | bytes 1 | tf_op jit(solution)/shard_map/front/pallas_call | solution.py:887
  72.4 1.6 collective-permute-start.7
  74.6 3.3 %collective-permute-start.9 = (f32[72,384]{1,0:T(8,128)}, f32[72,384]{1,0:T(8,128)S(1)}, u32[]{:S(2)}, u32[]{:S(2)}) collective-permute-start(f32[72,384]{1,0:T(8,128)} %get-tuple-element.162), channel_id=1, source_target_pairs={{0,8},{4,12},{16,24},{20,28},{8,0},{12,4},{24,16},{28,20},{1,9},{5... | collective-permute-start | bytes 331784 | tf_op jit(solution)/shard_map/ppermute | solution.py:920
  77.9 0.7 collective-permute-start.10
  78.6 8.6 %inner.1 = (bf16[2048,384]{1,0:T(8,128)(2,1)}, bf16[2048,384]{1,0:T(8,128)(2,1)}) custom-call(bf16[2048,512]{1,0:T(8,128)(2,1)} %get-tuple-element.145.act_ref.bc_ref, f32[2048,128]{1,0:T(8,128)} %get-tuple-element.146.pack_ref, f32[8,2048]{1,0:T(8,128)} %get-tuple-element.152.segrow_ref, f32[16,2048]{1,0:T(8,128)} %get-tuple-element.153.rowp_ref, ...), custom_call_target="tpu_custom_call" | custom-call | flops 6000000000 | bytes 1 | tf_op jit(solution)/shard_map/inner/pallas_call | solution.py:887
  87.9 9.0 %merge.1 = (bf16[2048,384]{1,0:T(8,128)(2,1)}, f32[8,2048]{1,0:T(8,128)}, bf16[16,64,768]{2,1,0:T(8,128)(2,1)}) custom-call(s32[3]{0:T(128)} %pad_add_fusion.at_ref, bf16[2048,512]{1,0:T(8,128)(2,1)} %get-tuple-element.145.act_ref.bc_ref, f32[2048,128]{1,0:T(8,128)} %get-tuple-element.146.pack_ref, f32[128,128]{1,0:T(8,128)} %get-tuple-element.147.tot_ref, ...), custom_call_target="tpu_custom_call" | custom-call | flops 6000000000 | bytes 1 | tf_op jit(solution)/shard_map/merge/pallas_call | solution.py:887
  97.5 1.4 collective-permute-start.13
  98.9 3.3 %collective-permute-done.12.rest_2_ = f32[8,2048]{1,0:T(8,128)S(1)} collective-permute-done((f32[8,2048]{1,0:T(8,128)}, f32[8,2048]{1,0:T(8,128)S(1)}, u32[]{:S(2)}, u32[]{:S(2)}) %collective-permute-start.12) | collective-permute-done | bytes 65568 | tf_op jit(solution)/shard_map/ppermute | solution.py:1251
  103.3 24.1 %turn.1 = (bf16[2048,768]{1,0:T(8,128)(2,1)}, bf16[2048,384]{1,0:T(8,128)(2,1)}, bf16[2048,384]{1,0:T(8,128)(2,1)}, f32[8,384]{1,0:T(8,128)}, f32[8,384]{1,0:T(8...) custom-call(s32[3]{0:T(128)} %pad_add_fusion.at_ref, ...), custom_call_target="tpu_custom_call" | custom-call | flops 24000000000 | bytes 1 | tf_op jit(solution)/shard_map/turn/pallas_call | solution.py:887
  127.4 2.8 collective-permute-start.14
  130.2 0.7 collective-permute-start.15
  130.9 3.1 %collective-permute-start.16 = (f32[72,384]{1,0:T(8,128)}, f32[72,384]{1,0:T(8,128)S(1)}, u32[]{:S(2)}, u32[]{:S(2)}) collective-permute-start(f32[72,384]{1,0:T(8,128)} %get-tuple-element.189), channel_id=1, source_target_pairs={{0,8},{4,12},{16,24},{20,28},{8,0},{12,4},{24,16},{28,20},{1,9},{5... | collective-permute-start | bytes 331784 | tf_op jit(solution)/shard_map/ppermute | solution.py:920
  133.9 0.8 collective-permute-start.17
  134.8 19.5 %mid.1 = (bf16[2048,384]{1,0:T(8,128)(2,1)}, f32[2048,128]{1,0:T(8,128)}, f32[2048,128]{1,0:T(8,128)}) custom-call(bf16[2048,512]{1,0:T(8,128)(2,1)} %get-tuple-element.145.act_ref.bc_ref, f32[2048,128]{1,0:T(8,128)} %get-tuple-element.146.pack_ref, f32[8,2048]{1,0:T(8,128)} %get-tuple-element.152.segrow_ref, f32[16,2048]{1,0:T(8,128)} %get-tuple-element.175.rowa_ref, ...), custom_call_target="tpu_custom_call" | custom-call | flops 17999998976 | bytes 1 | tf_op jit(solution)/shard_map/mid/pallas_call | solution.py:887
  155.1 36.1 %back.1 = (bf16[2,512,768]{2,1,0:T(8,128)(2,1)}, bf16[2,512,768]{2,1,0:T(8,128)(2,1)}, bf16[96,640]{1,0:T(8,128)(2,1)}, bf16[96,640]{1,0:T(8,128)(2,1)}, bf16[96...) custom-call(s32[3]{0:T(128)} %pad_add_fusion.at_ref, ...), custom_call_target="tpu_custom_call" | custom-call | flops 32999999488 | bytes 1 | tf_op jit(solution)/shard_map/back/pallas_call | solution.py:887
  191.3 2.4 collective-permute-start.26
  193.8 4.4 %collective-permute-start.25 = (bf16[96,640]{1,0:T(8,128)(2,1)}, bf16[96,640]{1,0:T(8,128)(2,1)S(1)}, u32[]{:S(2)}, u32[]{:S(2)}) collective-permute-start(bf16[96,640]{1,0:T(8,128)(2,1)} %get-tuple-element.199), channel_id=1, source_target_pairs={{0,24},{4,28},{8,16},{12,20},{16,8},{20,12},{24,0},{28,4},{1,25},{... | collective-permute-start | bytes 368648 | tf_op jit(solution)/shard_map/ppermute | solution.py:926
  198.8 1.4 slice.109.refs_10_
  200.1 1.4 slice.110.refs_11_
  201.9 1.0 collective-permute-start.23
  202.9 16.8 %collective-permute-start.22 = (bf16[96,640]{1,0:T(8,128)(2,1)}, bf16[96,640]{1,0:T(8,128)(2,1)S(1)}, u32[]{:S(2)}, u32[]{:S(2)}) collective-permute-start(bf16[96,640]{1,0:T(8,128)(2,1)} %get-tuple-element.196), channel_id=1, source_target_pairs={{0,12},{4,8},{8,4},{12,0},{16,28},{20,24},{24,20},{28,16},{1,13},{... | collective-permute-start | bytes 368648 | tf_op jit(solution)/shard_map/ppermute | solution.py:926
  219.7 6.4 %collective-permute-start.21 = (bf16[96,640]{1,0:T(8,128)(2,1)}, bf16[96,640]{1,0:T(8,128)(2,1)S(1)}, u32[]{:S(2)}, u32[]{:S(2)}) collective-permute-start(bf16[96,640]{1,0:T(8,128)(2,1)} %get-tuple-element.195), channel_id=1, source_target_pairs={{0,8},{4,12},{8,0},{12,4},{16,24},{20,28},{24,16},{28,20},{1,9},{5... | collective-permute-start | bytes 368648 | tf_op jit(solution)/shard_map/ppermute | solution.py:926
  226.2 1.2 copy-done.7
  227.3 2.2 convert_add_fusion
  229.6 1.0 slice.125
  231.1 1.3 collective-permute-done.23
  232.4 2.2 collective-permute-done.21
  234.9 1.3 collective-permute-start.28
  236.7 13.4 %collective-permute-done.29 = f32[96,256]{1,0:T(8,128)S(1)} collective-permute-done((f32[96,256]{1,0:T(8,128)S(1)}, f32[96,256]{1,0:T(8,128)S(1)}, u32[]{:S(2)}, u32[]{:S(2)}) %collective-permute-start.29) | collective-permute-done | bytes 98336 | tf_op jit(solution)/shard_map/ppermute | solution.py:933
  250.1 5.0 %collective-permute-done.28 = f32[96,256]{1,0:T(8,128)S(1)} collective-permute-done((f32[96,256]{1,0:T(8,128)S(1)}, f32[96,256]{1,0:T(8,128)S(1)}, u32[]{:S(2)}, u32[]{:S(2)}) %collective-permute-start.28) | collective-permute-done | bytes 98336 | tf_op jit(solution)/shard_map/ppermute | solution.py:933
  255.3 3.6 %collective-permute-start.30 = (bf16[96,640]{1,0:T(8,128)(2,1)S(1)}, bf16[96,640]{1,0:T(8,128)(2,1)S(1)}, u32[]{:S(2)}, u32[]{:S(2)}) collective-permute-start(bf16[96,640]{1,0:T(8,128)(2,1)S(1)} %pad_maximum_fusion.1.refs_0_), channel_id=1, source_target_pairs={{0,4},{4,0},{8,12},{12,8},{16,20},{20,16},{24,28},{28,24},{1,5},{5... | collective-permute-start | bytes 368648 | tf_op jit(solution)/shard_map/ppermute | solution.py:926
  258.9 1.5 collective-permute-start.32
  260.4 2.3 convert_element_type.88
  262.7 1.1 convert_element_type.89
  263.8 4.3 %collective-permute-start.34 = (bf16[96,640]{1,0:T(8,128)(2,1)S(1)}, bf16[96,640]{1,0:T(8,128)(2,1)S(1)}, u32[]{:S(2)}, u32[]{:S(2)}) collective-permute-start(bf16[96,640]{1,0:T(8,128)(2,1)S(1)} %pad_maximum_fusion.1.refs_0_), channel_id=1, source_target_pairs={{0,20},{4,16},{8,28},{12,24},{16,4},{20,0},{24,12},{28,8},{1,21},{... | collective-permute-start | bytes 368648 | tf_op jit(solution)/shard_map/ppermute | solution.py:926
  268.1 1.6 fusion.2
  269.8 3.3 %collective-permute-start.36 = (bf16[96,640]{1,0:T(8,128)(2,1)S(1)}, bf16[96,640]{1,0:T(8,128)(2,1)S(1)}, u32[]{:S(2)}, u32[]{:S(2)}) collective-permute-start(bf16[96,640]{1,0:T(8,128)(2,1)S(1)} %pad_maximum_fusion.1.refs_0_), channel_id=1, source_target_pairs={{0,28},{4,24},{8,20},{12,16},{16,12},{20,8},{24,4},{28,0},{1,29},{... | collective-permute-start | bytes 368648 | tf_op jit(solution)/shard_map/ppermute | solution.py:926
  273.9 6.0 %collective-permute-done.34.refs_5_ = bf16[96,640]{1,0:T(8,128)(2,1)S(1)} collective-permute-done((bf16[96,640]{1,0:T(8,128)(2,1)S(1)}, bf16[96,640]{1,0:T(8,128)(2,1)S(1)}, u32[]{:S(2)}, u32[]{:S(2)}) %collective-permute-start.34) | collective-permute-done | bytes 122912 | tf_op jit(solution)/shard_map/ppermute | solution.py:926
  280.7 0.7 copy-done.24
  281.3 3.5 %finish.1 = (f32[1,768]{1,0:T(1,128)}, f32[768,384]{1,0:T(8,128)}, f32[768,128]{1,0:T(8,128)}, f32[6,2,768]{2,1,0:T(2,128)}, f32[2,6]{1,0:T(2,128)}, /*index=5*/...) custom-call(s32[3]{0:T(128)} %pad_add_fusion.at_ref, ...), custom_call_target="tpu_custom_call" | custom-call | flops 3000000000 | bytes 1 | tf_op jit(solution)/shard_map/finish/pallas_call | solution.py:887
  284.8 1.3 reduce.12
  286.1 1.3 reduce.13
  287.4 2.6 fusion.5
  290.1 0.9 copy-done.8
  (161 shorter events, 15.4 us)
Async XLA Ops:
  7.2 18.2 %copy-start.6 = (bf16[768,384]{1,0:T(8,128)(2,1)S(1)}, bf16[768,384]{1,0:T(8,128)(2,1)}, u32[]{:S(2)}) copy-start(bf16[768,384]{1,0:T(8,128)(2,1)} %param.33) | copy-start | bytes 1769476
  7.2 18.2 %copy-start.9 = (bf16[768,128]{1,0:T(8,128)(2,1)S(1)}, bf16[768,128]{1,0:T(8,128)(2,1)}, u32[]{:S(2)}) copy-start(bf16[768,128]{1,0:T(8,128)(2,1)} %param.34) | copy-start | bytes 589828
  7.2 71.4 %all-gather.2.cloned.1.call-start = ((), (), s32[]{:S(2)}) async-start(), calls=%async_computation.1 | async-start | bytes 3932160 | tf_op jit(solution)/shard_map/all_gather | solution.py:1056
  7.2 27.8 %collective-permute-start = (bf16[512,768]{1,0:T(8,128)(2,1)}, bf16[512,768]{1,0:T(8,128)(2,1)S(1)}, u32[]{:S(2)}, u32[]{:S(2)}) collective-permute-start(bf16[512,768]{1,0:T(8,128)(2,1)} %refs_0_), channel_id=1, source_target_pairs={{0,2},{1,3},{2,0},{3,1},{4,6},{5,7},{6,4},{7,5},{8,10},{9,11},{10,... | collective-permute-start | bytes 2359304 | tf_op jit(solution)/shard_map/ppermute | solution.py:926
  11.0 16.2 %collective-permute-start.1 = (bf16[8,768]{1,0:T(8,128)(2,1)S(1)}, bf16[8,768]{1,0:T(8,128)(2,1)S(1)}, u32[]{:S(2)}, u32[]{:S(2)}) collective-permute-start(bf16[8,768]{1,0:T(8,128)(2,1)S(1)} %slice.98), channel_id=1, source_target_pairs={{0,4},{4,8},{8,12},{12,16},{16,20},{20,24},{24,28},{1,5},{5,9},{9,... | collective-permute-start | bytes 36872 | tf_op jit(solution)/shard_map/ppermute | solution.py:910
  25.4 8.9 %copy-start.17 = (f32[6]{0:T(128)S(1)}, f32[6]{0:T(128)}, u32[]{:S(2)}) copy-start(f32[6]{0:T(128)} %param.40) | copy-start | bytes 76
  25.4 9.7 %copy-start.13 = (f32[768]{0:T(1024)S(1)}, f32[768]{0:T(1024)}, u32[]{:S(2)}) copy-start(f32[768]{0:T(1024)} %param.31) | copy-start | bytes 9220
  25.4 10.4 %copy-start.16 = (f32[384]{0:T(512)S(1)}, f32[384]{0:T(512)}, u32[]{:S(2)}) copy-start(f32[384]{0:T(512)} %param.41) | copy-start | bytes 4612
  25.4 11.6 %copy-start.2 = (bf16[512,768]{1,0:T(8,128)(2,1)S(1)}, bf16[512,768]{1,0:T(8,128)(2,1)}, u32[]{:S(2)}) copy-start(bf16[512,768]{1,0:T(8,128)(2,1)} %refs_0_) | copy-start | bytes 2359300
  27.2 7.2 %collective-permute-start.4 = (bf16[8,768]{1,0:T(8,128)(2,1)S(1)}, bf16[8,768]{1,0:T(8,128)(2,1)S(1)}, u32[]{:S(2)}, u32[]{:S(2)}) collective-permute-start(bf16[8,768]{1,0:T(8,128)(2,1)S(1)} %collective-permute-done.1), channel_id=1, source_target_pairs={{0,3},{1,2},{2,1},{3,0},{4,7},{5,6},{6,5},{7,4},{8,11},{9,10},{10,... | collective-permute-start | bytes 36872 | tf_op jit(solution)/shard_map/ppermute | solution.py:926
  27.3 7.2 %collective-permute-start.3 = (bf16[8,768]{1,0:T(8,128)(2,1)S(1)}, bf16[8,768]{1,0:T(8,128)(2,1)S(1)}, u32[]{:S(2)}, u32[]{:S(2)}) collective-permute-start(bf16[8,768]{1,0:T(8,128)(2,1)S(1)} %collective-permute-done.1), channel_id=1, source_target_pairs={{0,2},{1,3},{2,0},{3,1},{4,6},{5,7},{6,4},{7,5},{8,10},{9,11},{10,... | collective-permute-start | bytes 36872 | tf_op jit(solution)/shard_map/ppermute | solution.py:926
  28.2 6.3 %collective-permute-start.2 = (bf16[8,768]{1,0:T(8,128)(2,1)S(1)}, bf16[8,768]{1,0:T(8,128)(2,1)S(1)}, u32[]{:S(2)}, u32[]{:S(2)}) collective-permute-start(bf16[8,768]{1,0:T(8,128)(2,1)S(1)} %collective-permute-done.1), channel_id=1, source_target_pairs={{0,1},{1,0},{2,3},{3,2},{4,5},{5,4},{6,7},{7,6},{8,9},{9,8},{10,11... | collective-permute-start | bytes 36872 | tf_op jit(solution)/shard_map/ppermute | solution.py:926
  32.7 7.7 %copy-start.15 = (f32[8,128]{1,0:T(8,128)}, f32[8,128]{1,0:T(8,128)S(1)}, u32[]{:S(2)}) copy-start(f32[8,128]{1,0:T(8,128)S(1)} %scatter.14.refs_10_.pcol_ref) | copy-start | bytes 12292
  35.1 5.4 %copy-start.18 = (bf16[512,768]{1,0:T(8,128)(2,1)}, bf16[512,768]{1,0:T(8,128)(2,1)S(1)}, u32[]{:S(2)}) copy-start(bf16[512,768]{1,0:T(8,128)(2,1)S(1)} %collective-permute-done.refs_2_) | copy-start | bytes 2359300
  36.9 223.5 %all-reduce.9.cloned.1.call-start = ((), (), s32[]{:S(2)}) async-start(), calls=%async_computation.3 | async-start | bytes 2359296 | tf_op jit(solution)/shard_map/psum | solution.py:1314
  37.0 2.4 collective-permute-start.5
  37.1 3.4 %collective-permute-start.6 = (bf16[512,768]{1,0:T(8,128)(2,1)S(1)}, bf16[512,768]{1,0:T(8,128)(2,1)S(1)}, u32[]{:S(2)}, u32[]{:S(2)}) collective-permute-start(bf16[512,768]{1,0:T(8,128)(2,1)S(1)} %collective-permute-done.refs_2_), channel_id=1, source_target_pairs={{0,1},{1,0},{2,3},{3,2},{4,5},{5,4},{6,7},{7,6},{8,9},{9,8},{10,11... | collective-permute-start | bytes 2359304 | tf_op jit(solution)/shard_map/ppermute | solution.py:926
  39.4 1.1 copy-start.19
  40.5 0.9 copy-start.20
  72.4 14.8 %collective-permute-start.7 = (f32[72,384]{1,0:T(8,128)}, f32[72,384]{1,0:T(8,128)S(1)}, u32[]{:S(2)}, u32[]{:S(2)}) collective-permute-start(f32[72,384]{1,0:T(8,128)} %get-tuple-element.160), channel_id=1, source_target_pairs={{0,4},{8,12},{16,20},{24,28},{4,0},{12,8},{20,16},{28,24},{1,5},{9... | collective-permute-start | bytes 331784 | tf_op jit(solution)/shard_map/ppermute | solution.py:920
  74.0 13.2 %collective-permute-start.8 = (f32[72,384]{1,0:T(8,128)}, f32[72,384]{1,0:T(8,128)S(1)}, u32[]{:S(2)}, u32[]{:S(2)}) collective-permute-start(f32[72,384]{1,0:T(8,128)} %get-tuple-element.161), channel_id=1, source_target_pairs={{4,8},{12,16},{20,24},{8,4},{16,12},{24,20},{5,9},{13,17},{21,25},... | collective-permute-start | bytes 331784 | tf_op jit(solution)/shard_map/ppermute | solution.py:920
  74.6 12.6 %collective-permute-start.9 = (f32[72,384]{1,0:T(8,128)}, f32[72,384]{1,0:T(8,128)S(1)}, u32[]{:S(2)}, u32[]{:S(2)}) collective-permute-start(f32[72,384]{1,0:T(8,128)} %get-tuple-element.162), channel_id=1, source_target_pairs={{0,8},{4,12},{16,24},{20,28},{8,0},{12,4},{24,16},{28,20},{1,9},{5... | collective-permute-start | bytes 331784 | tf_op jit(solution)/shard_map/ppermute | solution.py:920
  77.9 9.3 %collective-permute-start.10 = (f32[72,384]{1,0:T(8,128)}, f32[72,384]{1,0:T(8,128)S(1)}, u32[]{:S(2)}, u32[]{:S(2)}) collective-permute-start(f32[72,384]{1,0:T(8,128)} %get-tuple-element.163), channel_id=1, source_target_pairs={{8,16},{12,20},{16,8},{20,12},{9,17},{13,21},{17,9},{21,13},{10,18... | collective-permute-start | bytes 331784 | tf_op jit(solution)/shard_map/ppermute | solution.py:920
  96.9 1.9 collective-permute-start.11
  97.0 5.2 %collective-permute-start.12 = (f32[8,2048]{1,0:T(8,128)}, f32[8,2048]{1,0:T(8,128)S(1)}, u32[]{:S(2)}, u32[]{:S(2)}) collective-permute-start(f32[8,2048]{1,0:T(8,128)} %get-tuple-element.168.rest_0_), channel_id=1, source_target_pairs={{0,2},{1,3},{2,0},{3,1},{4,6},{5,7},{6,4},{7,5},{8,10},{9,11},{10,... | collective-permute-start | bytes 196616 | tf_op jit(solution)/shard_map/ppermute | solution.py:1251
  97.5 5.2 %collective-permute-start.13 = (f32[8,2048]{1,0:T(8,128)}, f32[8,2048]{1,0:T(8,128)S(1)}, u32[]{:S(2)}, u32[]{:S(2)}) collective-permute-start(f32[8,2048]{1,0:T(8,128)} %get-tuple-element.168.rest_0_), channel_id=1, source_target_pairs={{0,3},{1,2},{2,1},{3,0},{4,7},{5,6},{6,5},{7,4},{8,11},{9,10},{10,... | collective-permute-start | bytes 196616 | tf_op jit(solution)/shard_map/ppermute | solution.py:1251
  98.8 3.8 %copy-start.33 = (f32[8,2048]{1,0:T(8,128)}, f32[8,2048]{1,0:T(8,128)S(1)}, u32[]{:S(2)}) copy-start(f32[8,2048]{1,0:T(8,128)S(1)} %collective-permute-done.11.rest_1_) | copy-start | bytes 196612
  127.4 160.0 %reduce-scatter.2.cloned.1.call-start = ((), (), s32[]{:S(2)}) async-start(), calls=%async_computation.2 | async-start | bytes 3932160 | tf_op jit(solution)/shard_map/reduce_scatter | solution.py:1315
  127.4 26.9 %collective-permute-start.14 = (f32[72,384]{1,0:T(8,128)}, f32[72,384]{1,0:T(8,128)S(1)}, u32[]{:S(2)}, u32[]{:S(2)}) collective-permute-start(f32[72,384]{1,0:T(8,128)} %get-tuple-element.187), channel_id=1, source_target_pairs={{0,4},{8,12},{16,20},{24,28},{4,0},{12,8},{20,16},{28,24},{1,5},{9... | collective-permute-start | bytes 331784 | tf_op jit(solution)/shard_map/ppermute | solution.py:920
  130.2 24.2 %collective-permute-start.15 = (f32[72,384]{1,0:T(8,128)}, f32[72,384]{1,0:T(8,128)S(1)}, u32[]{:S(2)}, u32[]{:S(2)}) collective-permute-start(f32[72,384]{1,0:T(8,128)} %get-tuple-element.188), channel_id=1, source_target_pairs={{4,8},{12,16},{20,24},{8,4},{16,12},{24,20},{5,9},{13,17},{21,25},... | collective-permute-start | bytes 331784 | tf_op jit(solution)/shard_map/ppermute | solution.py:920
  130.9 23.5 %collective-permute-start.16 = (f32[72,384]{1,0:T(8,128)}, f32[72,384]{1,0:T(8,128)S(1)}, u32[]{:S(2)}, u32[]{:S(2)}) collective-permute-start(f32[72,384]{1,0:T(8,128)} %get-tuple-element.189), channel_id=1, source_target_pairs={{0,8},{4,12},{16,24},{20,28},{8,0},{12,4},{24,16},{28,20},{1,9},{5... | collective-permute-start | bytes 331784 | tf_op jit(solution)/shard_map/ppermute | solution.py:920
  133.9 20.5 %collective-permute-start.17 = (f32[72,384]{1,0:T(8,128)}, f32[72,384]{1,0:T(8,128)S(1)}, u32[]{:S(2)}, u32[]{:S(2)}) collective-permute-start(f32[72,384]{1,0:T(8,128)} %get-tuple-element.190), channel_id=1, source_target_pairs={{8,16},{12,20},{16,8},{20,12},{9,17},{13,21},{17,9},{21,13},{10,18... | collective-permute-start | bytes 331784 | tf_op jit(solution)/shard_map/ppermute | solution.py:920
  154.4 0.7 copy-start.27
  191.3 34.9 %collective-permute-start.18 = (bf16[2,512,768]{2,1,0:T(8,128)(2,1)}, bf16[2,512,768]{2,1,0:T(8,128)(2,1)S(1)}, u32[]{:S(2)}, u32[]{:S(2)}) collective-permute-start(bf16[2,512,768]{2,1,0:T(8,128)(2,1)} %get-tuple-element.192), channel_id=1, source_target_pairs={{0,1},{1,0},{2,3},{3,2},{4,5},{5,4},{6,7},{7,6},{8,9},{9,8},{10,11... | collective-permute-start | bytes 4718600 | tf_op jit(solution)/shard_map/ppermute | solution.py:926
  191.3 11.5 %collective-permute-start.26 = (bf16[96,640]{1,0:T(8,128)(2,1)}, bf16[96,640]{1,0:T(8,128)(2,1)S(1)}, u32[]{:S(2)}, u32[]{:S(2)}) collective-permute-start(bf16[96,640]{1,0:T(8,128)(2,1)} %get-tuple-element.200), channel_id=1, source_target_pairs={{0,28},{4,24},{8,20},{12,16},{16,12},{20,8},{24,4},{28,0},{1,29},{... | collective-permute-start | bytes 368648 | tf_op jit(solution)/shard_map/ppermute | solution.py:926
  193.8 26.0 %collective-permute-start.25 = (bf16[96,640]{1,0:T(8,128)(2,1)}, bf16[96,640]{1,0:T(8,128)(2,1)S(1)}, u32[]{:S(2)}, u32[]{:S(2)}) collective-permute-start(bf16[96,640]{1,0:T(8,128)(2,1)} %get-tuple-element.199), channel_id=1, source_target_pairs={{0,24},{4,28},{8,16},{12,20},{16,8},{20,12},{24,0},{28,4},{1,25},{... | collective-permute-start | bytes 368648 | tf_op jit(solution)/shard_map/ppermute | solution.py:926
  201.5 29.1 %collective-permute-start.24 = (bf16[96,640]{1,0:T(8,128)(2,1)}, bf16[96,640]{1,0:T(8,128)(2,1)S(1)}, u32[]{:S(2)}, u32[]{:S(2)}) collective-permute-start(bf16[96,640]{1,0:T(8,128)(2,1)} %get-tuple-element.198), channel_id=1, source_target_pairs={{0,20},{4,16},{8,28},{12,24},{16,4},{20,0},{24,12},{28,8},{1,21},{... | collective-permute-start | bytes 368648 | tf_op jit(solution)/shard_map/ppermute | solution.py:926
  201.9 30.5 %collective-permute-start.23 = (bf16[96,640]{1,0:T(8,128)(2,1)}, bf16[96,640]{1,0:T(8,128)(2,1)S(1)}, u32[]{:S(2)}, u32[]{:S(2)}) collective-permute-start(bf16[96,640]{1,0:T(8,128)(2,1)} %get-tuple-element.197), channel_id=1, source_target_pairs={{0,16},{4,20},{8,24},{12,28},{16,0},{20,4},{24,8},{28,12},{1,17},{... | collective-permute-start | bytes 368648 | tf_op jit(solution)/shard_map/ppermute | solution.py:926
  202.9 29.5 %collective-permute-start.22 = (bf16[96,640]{1,0:T(8,128)(2,1)}, bf16[96,640]{1,0:T(8,128)(2,1)S(1)}, u32[]{:S(2)}, u32[]{:S(2)}) collective-permute-start(bf16[96,640]{1,0:T(8,128)(2,1)} %get-tuple-element.196), channel_id=1, source_target_pairs={{0,12},{4,8},{8,4},{12,0},{16,28},{20,24},{24,20},{28,16},{1,13},{... | collective-permute-start | bytes 368648 | tf_op jit(solution)/shard_map/ppermute | solution.py:926
  219.7 14.9 %collective-permute-start.21 = (bf16[96,640]{1,0:T(8,128)(2,1)}, bf16[96,640]{1,0:T(8,128)(2,1)S(1)}, u32[]{:S(2)}, u32[]{:S(2)}) collective-permute-start(bf16[96,640]{1,0:T(8,128)(2,1)} %get-tuple-element.195), channel_id=1, source_target_pairs={{0,8},{4,12},{8,0},{12,4},{16,24},{20,28},{24,16},{28,20},{1,9},{5... | collective-permute-start | bytes 368648 | tf_op jit(solution)/shard_map/ppermute | solution.py:926
  226.2 1.2 copy-start.7
  226.2 8.5 %collective-permute-start.20 = (bf16[96,640]{1,0:T(8,128)(2,1)}, bf16[96,640]{1,0:T(8,128)(2,1)S(1)}, u32[]{:S(2)}, u32[]{:S(2)}) collective-permute-start(bf16[96,640]{1,0:T(8,128)(2,1)} %get-tuple-element.194), channel_id=1, source_target_pairs={{0,4},{4,0},{8,12},{12,8},{16,20},{20,16},{24,28},{28,24},{1,5},{5... | collective-permute-start | bytes 368648 | tf_op jit(solution)/shard_map/ppermute | solution.py:926
  229.6 5.1 %copy-start.11 = (bf16[96,640]{1,0:T(8,128)(2,1)S(1)}, bf16[96,640]{1,0:T(8,128)(2,1)}, u32[]{:S(2)}) copy-start(bf16[96,640]{1,0:T(8,128)(2,1)} %get-tuple-element.193) | copy-start | bytes 368644
  230.5 33.3 %collective-permute-start.19 = (bf16[1,512,768]{2,1,0:T(8,128)(2,1)}, bf16[1,512,768]{2,1,0:T(8,128)(2,1)}, u32[]{:S(2)}, u32[]{:S(2)}) collective-permute-start(bf16[1,512,768]{2,1,0:T(8,128)(2,1)} %slice.125), channel_id=1, source_target_pairs={{0,2},{1,3},{2,0},{3,1},{4,6},{5,7},{6,4},{7,5},{8,10},{9,11},{10,... | collective-permute-start | bytes 2359304 | tf_op jit(solution)/shard_map/ppermute | solution.py:926
  234.8 15.3 %collective-permute-start.29 = (f32[96,256]{1,0:T(8,128)S(1)}, f32[96,256]{1,0:T(8,128)S(1)}, u32[]{:S(2)}, u32[]{:S(2)}) collective-permute-start(f32[96,256]{1,0:T(8,128)S(1)} %slice.115), channel_id=1, source_target_pairs={{0,3},{1,2},{2,1},{3,0},{4,7},{5,6},{6,5},{7,4},{8,11},{9,10},{10,... | collective-permute-start | bytes 294920 | tf_op jit(solution)/shard_map/ppermute | solution.py:933
  234.9 20.3 %collective-permute-start.28 = (f32[96,256]{1,0:T(8,128)S(1)}, f32[96,256]{1,0:T(8,128)S(1)}, u32[]{:S(2)}, u32[]{:S(2)}) collective-permute-start(f32[96,256]{1,0:T(8,128)S(1)} %slice.115), channel_id=1, source_target_pairs={{0,2},{1,3},{2,0},{3,1},{4,6},{5,7},{6,4},{7,5},{8,10},{9,11},{10,... | collective-permute-start | bytes 294920 | tf_op jit(solution)/shard_map/ppermute | solution.py:933
  236.1 19.0 %collective-permute-start.27 = (f32[96,256]{1,0:T(8,128)S(1)}, f32[96,256]{1,0:T(8,128)S(1)}, u32[]{:S(2)}, u32[]{:S(2)}) collective-permute-start(f32[96,256]{1,0:T(8,128)S(1)} %slice.115), channel_id=1, source_target_pairs={{0,1},{1,0},{2,3},{3,2},{4,5},{5,4},{6,7},{7,6},{8,9},{9,8},{10,11... | collective-permute-start | bytes 294920 | tf_op jit(solution)/shard_map/ppermute | solution.py:933
  255.3 14.6 %copy-start.12 = (bf16[96,640]{1,0:T(8,128)(2,1)}, bf16[96,640]{1,0:T(8,128)(2,1)S(1)}, u32[]{:S(2)}) copy-start(bf16[96,640]{1,0:T(8,128)(2,1)S(1)} %pad_maximum_fusion.1.refs_0_) | copy-start | bytes 368644
  255.3 14.5 %collective-permute-start.30 = (bf16[96,640]{1,0:T(8,128)(2,1)S(1)}, bf16[96,640]{1,0:T(8,128)(2,1)S(1)}, u32[]{:S(2)}, u32[]{:S(2)}) collective-permute-start(bf16[96,640]{1,0:T(8,128)(2,1)S(1)} %pad_maximum_fusion.1.refs_0_), channel_id=1, source_target_pairs={{0,4},{4,0},{8,12},{12,8},{16,20},{20,16},{24,28},{28,24},{1,5},{5... | collective-permute-start | bytes 368648 | tf_op jit(solution)/shard_map/ppermute | solution.py:926
  258.9 11.0 %collective-permute-start.31 = (bf16[96,640]{1,0:T(8,128)(2,1)S(1)}, bf16[96,640]{1,0:T(8,128)(2,1)}, u32[]{:S(2)}, u32[]{:S(2)}) collective-permute-start(bf16[96,640]{1,0:T(8,128)(2,1)S(1)} %pad_maximum_fusion.1.refs_0_), channel_id=1, source_target_pairs={{0,8},{4,12},{8,0},{12,4},{16,24},{20,28},{24,16},{28,20},{1,9},{5... | collective-permute-start | bytes 368648 | tf_op jit(solution)/shard_map/ppermute | solution.py:926
  258.9 14.9 %collective-permute-start.32 = (bf16[96,640]{1,0:T(8,128)(2,1)S(1)}, bf16[96,640]{1,0:T(8,128)(2,1)}, u32[]{:S(2)}, u32[]{:S(2)}) collective-permute-start(bf16[96,640]{1,0:T(8,128)(2,1)S(1)} %pad_maximum_fusion.1.refs_0_), channel_id=1, source_target_pairs={{0,12},{4,8},{8,4},{12,0},{16,28},{20,24},{24,20},{28,16},{1,13},{... | collective-permute-start | bytes 368648 | tf_op jit(solution)/shard_map/ppermute | solution.py:926
  260.4 13.5 %collective-permute-start.33 = (bf16[96,640]{1,0:T(8,128)(2,1)S(1)}, bf16[96,640]{1,0:T(8,128)(2,1)}, u32[]{:S(2)}, u32[]{:S(2)}) collective-permute-start(bf16[96,640]{1,0:T(8,128)(2,1)S(1)} %pad_maximum_fusion.1.refs_0_), channel_id=1, source_target_pairs={{0,16},{4,20},{8,24},{12,28},{16,0},{20,4},{24,8},{28,12},{1,17},{... | collective-permute-start | bytes 368648 | tf_op jit(solution)/shard_map/ppermute | solution.py:926
  260.4 2.3 copy-start.10
  260.4 7.7 %copy-start.3 = (bf16[512,768]{1,0:T(8,128)(2,1)S(1)}, bf16[512,768]{1,0:T(8,128)(2,1)}, u32[]{:S(2)}) copy-start(bf16[512,768]{1,0:T(8,128)(2,1)} %refs_0_) | copy-start | bytes 2359300
  263.8 16.2 %collective-permute-start.34 = (bf16[96,640]{1,0:T(8,128)(2,1)S(1)}, bf16[96,640]{1,0:T(8,128)(2,1)S(1)}, u32[]{:S(2)}, u32[]{:S(2)}) collective-permute-start(bf16[96,640]{1,0:T(8,128)(2,1)S(1)} %pad_maximum_fusion.1.refs_0_), channel_id=1, source_target_pairs={{0,20},{4,16},{8,28},{12,24},{16,4},{20,0},{24,12},{28,8},{1,21},{... | collective-permute-start | bytes 368648 | tf_op jit(solution)/shard_map/ppermute | solution.py:926
  269.7 3.5 %copy-start = (f32[1,512,768]{2,1,0:T(8,128)}, f32[1,512,768]{2,1,0:T(8,128)S(1)}, u32[]{:S(2)}) copy-start(f32[1,512,768]{2,1,0:T(8,128)S(1)} %get-tuple-element.218) | copy-start | bytes 4718596
  269.7 10.3 %copy-start.21 = (bf16[96,640]{1,0:T(8,128)(2,1)}, bf16[96,640]{1,0:T(8,128)(2,1)S(1)}, u32[]{:S(2)}) copy-start(bf16[96,640]{1,0:T(8,128)(2,1)S(1)} %collective-permute-done.30.refs_1_) | copy-start | bytes 368644
  269.7 10.2 %collective-permute-start.35 = (bf16[96,640]{1,0:T(8,128)(2,1)S(1)}, bf16[96,640]{1,0:T(8,128)(2,1)S(1)}, u32[]{:S(2)}, u32[]{:S(2)}) collective-permute-start(bf16[96,640]{1,0:T(8,128)(2,1)S(1)} %pad_maximum_fusion.1.refs_0_), channel_id=1, source_target_pairs={{0,24},{4,28},{8,16},{12,20},{16,8},{20,12},{24,0},{28,4},{1,25},{... | collective-permute-start | bytes 368648 | tf_op jit(solution)/shard_map/ppermute | solution.py:926
  269.8 10.1 %collective-permute-start.36 = (bf16[96,640]{1,0:T(8,128)(2,1)S(1)}, bf16[96,640]{1,0:T(8,128)(2,1)S(1)}, u32[]{:S(2)}, u32[]{:S(2)}) collective-permute-start(bf16[96,640]{1,0:T(8,128)(2,1)S(1)} %pad_maximum_fusion.1.refs_0_), channel_id=1, source_target_pairs={{0,28},{4,24},{8,20},{12,16},{16,12},{20,8},{24,4},{28,0},{1,29},{... | collective-permute-start | bytes 368648 | tf_op jit(solution)/shard_map/ppermute | solution.py:926
  273.8 13.6 %copy-start.1 = (f32[1,512,768]{2,1,0:T(8,128)S(1)}, f32[1,512,768]{2,1,0:T(8,128)}, u32[]{:S(2)}) copy-start(f32[1,512,768]{2,1,0:T(8,128)} %copy-done) | copy-start | bytes 4718596
  273.8 13.6 %copy-start.4 = (bf16[512,768]{1,0:T(8,128)(2,1)S(1)}, bf16[512,768]{1,0:T(8,128)(2,1)}, u32[]{:S(2)}) copy-start(bf16[512,768]{1,0:T(8,128)(2,1)} %refs_0_) | copy-start | bytes 2359300
  273.8 13.6 %copy-start.5 = (bf16[512,768]{1,0:T(8,128)(2,1)S(1)}, bf16[512,768]{1,0:T(8,128)(2,1)}, u32[]{:S(2)}) copy-start(bf16[512,768]{1,0:T(8,128)(2,1)} %param.45) | copy-start | bytes 2359300
  287.4 2.6 copy-start.14
  290.1 0.9 copy-start.8
  (12 other events, 8.0 us)
Sparse Core Ops, SparseCore 0:
  37.1 27.8 all-gather.1
  127.5 102.3 all-reduce.8
  232.6 37.7 reduce-scatter.1

commit v4 on v3

--- a/solution.py
+++ b/solution.py
@@ -16,7 +16,8 @@
 TINY = 1e-30
 F32 = jnp.float32
 BF16 = jnp.bfloat16
-BLOCK = 256
+BLOCK = 512
+ASIDE = 256
 
 
 def mm(a, b):
@@ -49,6 +50,11 @@
     return jnp.concatenate([high, (v - high.astype(F32)).astype(BF16)], axis=axis)
 
 
+def two_part(v, ex):
+    high = v.astype(BF16)
+    return mm(high, ex) + mm((v - high.astype(F32)).astype(BF16), ex)
+
+
 def sigmoid(v):
     return 1.0 / (1.0 + jnp.exp(-v))
 
@@ -59,6 +65,10 @@
 
 def iota(shape, dim):
     return lax.broadcasted_iota(jnp.int32, shape, dim)
+
+
+def wide_tiles(width):
+    return [slice(at, min(at + 2 * LANES, width)) for at in range(0, width, 2 * LANES)]
 
 
 def groups(width):
@@ -212,9 +222,12 @@
             x = jnp.where(piece == k, x_refs[k][at : at + 64, :], x)
         normed_ref[at : at + 64, :] = norm(x)
     nb = normed_ref[...]
-    for at in range(0, width, LANES):
-        tile = slice(at, at + LANES)
+    for tile in wide_tiles(width):
         gate_ref[:, tile] = mm(nb, wg_ref[:, tile]).astype(BF16)
+    for tile in wide_tiles(LANES + width):
+        uv = mm(nb, wsv_ref[:, tile])
+        ubuf[8 : 8 + tb, tile] = uv
+        uv_ref[:, tile] = uv.astype(BF16)
     zr_all = mm_nt(wstr_ref[...], nb)
     lane = iota((SPAN, LANES), 1)
     forward = lane < nh
@@ -243,9 +256,6 @@
         segrow_ref[:, rows] = jnp.transpose(seg)[:8]
     for at in range(0, LANES + width, LANES):
         tile = slice(at, at + LANES)
-        uv = mm(nb, wsv_ref[:, tile])
-        ubuf[8 : 8 + tb, tile] = uv
-        uv_ref[:, tile] = uv.astype(BF16)
         for j in range(per):
             rows = slice(j * SPAN, (j + 1) * SPAN)
             keep = marks[rows, :]
@@ -345,8 +355,7 @@
     dout_ref,
 ):
     tb, width = y_ref.shape
-    for at in range(0, width, LANES):
-        tile = slice(at, at + LANES)
+    for tile in wide_tiles(width):
         dout_ref[:, tile] = mm_nt(cot_ref[...], wo_ref[tile, :]).astype(BF16)
     t_at = iota((SPAN, SPAN), 0)
     s_at = iota((SPAN, SPAN), 1)
@@ -371,7 +380,7 @@
                 mats.append((score * jnp.exp(gap)).astype(BF16))
             xp = act_ref[rows, LANES + at : 2 * LANES + at]
             y = mm(jnp.concatenate(mats, axis=1), stacked(xp))
-            y_ref[rows, tile] = (y + skip_ref[0:1, tile] * xp.astype(F32)).astype(BF16)
+            y_ref[rows, tile] = y + skip_ref[0:1, tile] * xp.astype(F32)
 
 
 def merge_kernel(
@@ -420,7 +429,7 @@
             held = jnp.concatenate([sfull.astype(BF16), rfull.astype(BF16)], axis=1)
             full_ref[j, :, both] = held
             seen = mm(c, held) * mm(w, ex_ref[:, both])
-            y = (yin_ref[rows, tile].astype(F32) + seen[:, :LANES] + seen[:, LANES:]).astype(BF16)
+            y = (yin_ref[rows, tile] + seen[:, :LANES] + seen[:, LANES:]).astype(BF16)
             y_ref[rows, tile] = y
             gate = gate_ref[rows, tile].astype(F32)
             g = y.astype(F32) * gate * sigmoid(gate)
@@ -432,21 +441,13 @@
 
 
 def turn_kernel(
-    nh,
     inner,
     shares,
-    hops,
-    at_ref,
     y_ref,
     gate_ref,
     dout_ref,
     mg_ref,
     act_ref,
-    pack_ref,
-    tot_ref,
-    gates_ref,
-    gtot_ref,
-    ex_ref,
     eye_ref,
     normed_ref,
     cot_ref,
@@ -455,38 +456,29 @@
 ):
     stats_in = rest[:shares]
     (
-        mixer_ref,
+        aside_ref,
+        outin_ref,
         dy_ref,
         dgate_ref,
         gmix_ref,
         gskip_ref,
         gout_ref,
         ggate_ref,
-        dso_ref,
-        dro_ref,
-        *messages,
-        state,
-        incf,
-        outin,
         gout,
         ggate,
     ) = rest[shares:]
     i = pl.program_id(0)
     tb, width = y_ref.shape
     model = normed_ref.shape[1]
-    per = tb // SPAN
-    nc = dso_ref.shape[0]
-    lane = iota((SPAN, LANES), 1)
 
     @pl.when(i == 0)
     def _():
         gmix_ref[...] = jnp.zeros_like(gmix_ref)
         gskip_ref[...] = jnp.zeros_like(gskip_ref)
-        state[...] = jnp.zeros_like(state)
         gout[...] = jnp.zeros_like(gout)
         ggate[...] = jnp.zeros_like(ggate)
 
-    for j in range(per):
+    for j in range(tb // SPAN):
         rows = slice(j * SPAN, (j + 1) * SPAN)
         stat = stats_in[0][:, rows]
         for more in stats_in[1:]:
@@ -494,14 +486,8 @@
         stat = exact_tn(stat, eye_ref[0:8, :])
         q = lax.rsqrt(stat[:, 0:1] * (1.0 / inner) + EPSILON)
         k3 = q * q * q * stat[:, 1:2] * (1.0 / inner)
-        pack = pack_ref[rows, :]
-        w = split(target_weights(pack, tot_ref[j * 8 : j * 8 + 1, :], lane, nh), 1)
-        ct = jnp.transpose(act_ref[rows, :LANES].astype(F32))[HDIM:].astype(BF16)
-        c = i * per + j
         for n, at, _ in groups(width):
             tile = slice(at, at + LANES)
-            both = slice(2 * at, 2 * at + 2 * LANES)
-            second = slice(2 * at + LANES, 2 * at + 2 * LANES)
             y = y_ref[rows, tile].astype(F32)
             gate = gate_ref[rows, tile].astype(F32)
             sig = sigmoid(gate)
@@ -510,15 +496,71 @@
             gq = g * q
             dout = dout_ref[rows, tile].astype(F32)
             mg = mg_ref[0:1, tile]
-            outin[rows, tile] = (gq * mg).astype(BF16)
+            outin_ref[rows, tile] = (gq * mg).astype(BF16)
             gmix_ref[0:1, tile] += jnp.sum(dout * gq, axis=0, keepdims=True)
             dg = dout * mg * q - g * k3
             dyb = (dg * sg).astype(BF16)
             dy_ref[rows, tile] = dyb
             dgate_ref[rows, tile] = (dg * y * (sig + sg * (1.0 - sig))).astype(BF16)
-            dy = dyb.astype(F32)
             x = act_ref[rows, LANES + at : 2 * LANES + at].astype(F32)
-            gskip_ref[0:1, tile] += jnp.sum(dy * x, axis=0, keepdims=True)
+            gskip_ref[0:1, tile] += jnp.sum(dyb.astype(F32) * x, axis=0, keepdims=True)
+
+    for tile in wide_tiles(model):
+        aside_ref[:, tile] = mm(outin_ref[:ASIDE, :], wo_ref[:, tile]).astype(BF16)
+    for at in range(0, width, LANES):
+        tile = slice(at, at + LANES)
+        gout[tile, :] += mm_tn(outin_ref[:, tile], cot_ref[...])
+    for at in range(0, model, LANES):
+        tile = slice(at, at + LANES)
+        ggate[tile, :] += mm_tn(normed_ref[:, tile], dgate_ref[...])
+
+    @pl.when(i == pl.num_programs(0) - 1)
+    def _():
+        gout_ref[...] = gout[...].astype(BF16)
+        ggate_ref[...] = ggate[...].astype(BF16)
+
+
+def adjoint_kernel(
+    nh,
+    shares,
+    hops,
+    own,
+    at_ref,
+    act_ref,
+    pack_ref,
+    tot_ref,
+    gates_ref,
+    gtot_ref,
+    ex_ref,
+    dy_ref,
+    outin_ref,
+    wo_ref,
+    *rest,
+):
+    pieces_out = rest[:shares]
+    dso_ref, dro_ref, *messages, state, incf = rest[shares:]
+    i = pl.program_id(0)
+    tb, width = dy_ref.shape
+    model = wo_ref.shape[1]
+    per = tb // SPAN
+    nc = dso_ref.shape[0]
+    lane = iota((SPAN, LANES), 1)
+
+    @pl.when(i == 0)
+    def _():
+        state[...] = jnp.zeros_like(state)
+
+    for j in range(per):
+        rows = slice(j * SPAN, (j + 1) * SPAN)
+        pack = pack_ref[rows, :]
+        w = split(target_weights(pack, tot_ref[j * 8 : j * 8 + 1, :], lane, nh), 1)
+        ct = jnp.transpose(act_ref[rows, :].astype(F32))[HDIM:].astype(BF16)
+        c = i * per + j
+        for n, at, _ in groups(width):
+            tile = slice(at, at + LANES)
+            both = slice(2 * at, 2 * at + 2 * LANES)
+            second = slice(2 * at + LANES, 2 * at + 2 * LANES)
+            dy = dy_ref[rows, tile].astype(F32)
             wide = mm(w, ex_ref[:, both])
             fed = jnp.concatenate(
                 [(dy * wide[:, :LANES]).astype(BF16), (dy * wide[:, LANES:]).astype(BF16)], axis=1
@@ -528,20 +570,15 @@
             dro_ref[j, :, tile] = state[:, tile]
             state[:, tile] = state[:, tile] * gates_ref[c, 0:1, second] + inc[:, LANES:]
 
-    for at in range(0, model, 2 * LANES):
-        tile = slice(at, at + 2 * LANES)
-        mixer_ref[:, tile] = mm(outin[...], wo_ref[:, tile]).astype(BF16)
-    for at in range(0, width, LANES):
-        tile = slice(at, at + LANES)
-        gout[tile, :] += mm_tn(outin[:, tile], cot_ref[...])
-    for at in range(0, model, LANES):
-        tile = slice(at, at + LANES)
-        ggate[tile, :] += mm_tn(normed_ref[:, tile], dgate_ref[...])
+    for k in range(shares):
+
+        @pl.when((i * tb // own ^ at_ref[1]) == k)
+        def _():
+            for tile in wide_tiles(model):
+                pieces_out[k][:, tile] = mm(outin_ref[ASIDE:, :], wo_ref[:, tile]).astype(BF16)
 
     @pl.when(i == pl.num_programs(0) - 1)
     def _():
-        gout_ref[...] = gout[...].astype(BF16)
-        ggate_ref[...] = ggate[...].astype(BF16)
         last_state = state[...]
         state[...] = jnp.zeros_like(state)
 
@@ -733,8 +770,8 @@
             dbc = dbc + mm_nt((x2 * to_wide).astype(BF16), jnp.concatenate([dheld_low, none], axis=0))
             dbc = dbc + mm_nt((dy2 * fro_wide).astype(BF16), jnp.concatenate([none, held], axis=0))
             ext = ext_ref[both, :]
-            carried = carried + mm((dy2 * seen).astype(BF16), ext)
-            leaving = leaving + mm((x2 * flow).astype(BF16), ext)
+            carried = carried + two_part(dy2 * seen, ext)
+            leaving = leaving + two_part(x2 * flow, ext)
             product = jnp.sum(dheld * held.astype(F32), axis=0, keepdims=True) * gates_ref[j, :, both]
             through = through + mm(product.astype(BF16), ext)
             dx = dxin_ref[rows, tile].astype(F32) + flow[:, :LANES] + flow[:, LANES:]
@@ -769,8 +806,7 @@
 
     edge = dbuf[0:8, :]
     dbuf[tb : tb + 8, :] = edge
-    for at in range(0, model, LANES):
-        tile = slice(at, at + LANES)
+    for tile in wide_tiles(model):
         part = mm_nt(dgate_ref[...], wg_ref[tile, :]) + mm_nt(dcat[...], wcat_ref[tile, :])
         parts[:, tile] = part.astype(BF16)
         normed = normed_ref[:, tile]
@@ -821,17 +857,11 @@
             chunks[k][...] = acc[pl.ds(start, size), :].astype(BF16)
 
 
-def token_grads(cot, x, s, dn, gain):
-    scaled = dn * gain
-    inside = jnp.mean(scaled * x, axis=1, keepdims=True)
-    return (cot + s * scaled - x * (s * s * s) * inside).astype(BF16)
-
-
 def finish_kernel(nh, peers, shares, at_ref, *refs):
     chunks = refs[:peers]
-    eye_ref, ingain_ref, x_ref, cot_ref, dn_ref = refs[peers : peers + 5]
-    gain_ref, value_ref, state_ref, step_ref, bias_ref, decay_ref = refs[peers + 5 : peers + 11]
-    convv_ref, convs_ref, skip_ref, mixer_ref, late_ref, extra = refs[peers + 11 :]
+    eye_ref, ingain_ref, x_ref, cot_ref, kept_ref, got_ref = refs[peers : peers + 6]
+    gain_ref, value_ref, state_ref, step_ref, bias_ref, decay_ref = refs[peers + 6 : peers + 12]
+    convv_ref, convs_ref, skip_ref, mixer_ref, tokens_ref, extra = refs[peers + 12 :]
     size = chunks[0].shape[0]
     real_width = value_ref.shape[1]
     heads = step_ref.shape[0]
@@ -846,18 +876,28 @@
     taken = iota((16, LANES), 1) == 27 + 3 * at_ref[0] + row16 - 13
     taken = taken & (row16 > 12) & (at_ref[1] == shares - 1)
     late = mm_nt(jnp.where(taken, 1.0, 0.0).astype(BF16), found)
-    x = x_ref[...].astype(F32)
-    s = lax.rsqrt(jnp.mean(x * x, axis=1, keepdims=True) + EPSILON)
-    cot = cot_ref[...].astype(F32)
-    late_ref[...] = token_grads(cot, x, s, dn_ref[...] + late, ingain_ref[...])
+
+    def token_rows(rows, more):
+        x = x_ref[rows, :].astype(F32)
+        s = lax.rsqrt(jnp.mean(x * x, axis=1, keepdims=True) + EPSILON)
+        dn = kept_ref[0, rows, :] + got_ref[0, rows, :].astype(F32) + more
+        scaled = dn * ingain_ref[...]
+        inside = jnp.mean(scaled * x, axis=1, keepdims=True)
+        cot = cot_ref[rows, :].astype(F32)
+        tokens_ref[rows, :] = (cot + s * scaled - x * (s * s * s) * inside).astype(BF16)
+
+    own = x_ref.shape[0]
+    for at in range(0, own, 32):
+        token_rows(slice(at, at + 32), 0.0)
+    token_rows(slice(own - 16, own), late)
     for h in range(heads):
         step_ref[h, 0:1, :] = lines[h : h + 1, :]
         step_ref[h, 1:2, :] = lines[nh + h : nh + h + 1, :]
-    gain_ref[...] = lines[16:17, :] / ingain_ref[...]
+    gain_ref[...] = (lines[16:17, :] / ingain_ref[...])[0]
     convs_ref[...] = lines[17:21, :LANES]
     convv_ref[...] = lines[17:21, LANES : LANES + real_width]
     skip_ref[...] = lines[21:22, :heads]
-    mixer_ref[...] = lines[22:23, :real_width]
+    mixer_ref[...] = lines[22, :real_width]
     bias_ref[0:1, :] = lines[23:24, :heads]
     bias_ref[1:2, :] = lines[23:24, nh : nh + heads]
     decay_ref[...] = lines[24:25, :heads] + lines[24:25, nh : nh + heads]
@@ -1064,14 +1104,13 @@
     tot_block = row_block(per * 8, LANES)
     messages = [(whole(message.shape), message)] * (2 * hops)
 
-    def taller(factor):
-        big = tb * factor
+    def sized(block):
         return (
-            grid // factor,
-            partial(row_block, big),
-            partial(lane_block, width=big),
-            partial(chunk_block, per * factor),
-            row_block(per * factor * 8, LANES),
+            length // block,
+            partial(row_block, block),
+            partial(lane_block, width=block),
+            partial(chunk_block, block // SPAN),
+            row_block(block // SPAN * 8, LANES),
         )
 
     def slot_of(j, at):
@@ -1193,7 +1232,7 @@
 
     ahead = exchange_sides(ahead, hops)
 
-    big_grid, big_rows, big_lanes, big_chunks, big_tot = taller(2)
+    big_grid, big_rows, big_lanes, big_chunks, big_tot = sized(512)
     yin, dout = call(
         partial(inner_kernel, nh),
         "inner",
@@ -1208,7 +1247,7 @@
             whole((width, model)),
         ],
         [
-            (big_rows(width), sds((length, width), BF16)),
+            (big_rows(width), sds((length, width), F32)),
             (big_rows(width), sds((length, width), BF16)),
         ],
         [],
@@ -1250,8 +1289,8 @@
     for k in range(1, head_devices):
         shares.append(lax.ppermute(stat, "head", [(i, i ^ k) for i in range(head_devices)]))
 
-    mixer, dy, dgate, gmix, gskip, gout, ggate, dso, dro, *behind = call(
-        partial(turn_kernel, nh, inner, head_devices, hops),
+    aside, outin, dy, dgate, gmix, gskip, gout, ggate = call(
+        partial(turn_kernel, inner, head_devices),
         "turn",
         grid,
         [
@@ -1260,11 +1299,6 @@
             rows(width),
             whole((8, width)),
             rows(wide),
-            rows(LANES),
-            tot_block,
-            whole(gates_of.shape),
-            whole((8, 2 * width)),
-            whole(ex.shape),
             whole((16, LANES)),
             rows(model),
             rows(model),
@@ -1272,68 +1306,73 @@
         ]
         + [lane_block(8, tb)] * head_devices,
         [
-            (rows(model), sds((length, model), BF16)),
+            (row_block(ASIDE, model), sds((head_devices * ASIDE, model), BF16)),
+            (rows(width), sds((length, width), BF16)),
             (rows(width), sds((length, width), BF16)),
             (rows(width), sds((length, width), BF16)),
             (whole((8, width)), sds((8, width), F32)),
             (whole((8, width)), sds((8, width), F32)),
             (whole((width, model)), sds((width, model), BF16)),
             (whole((model, width)), sds((model, width), BF16)),
+        ],
+        [pltpu.VMEM((width, model), F32), pltpu.VMEM((model, width), F32)],
+        4e9,
+        [y, gate_in, dout, mg, acted, eye, normed, cot_all, proj_out] + shares,
+    )
+    outs = call(
+        partial(adjoint_kernel, nh, head_devices, hops, own),
+        "adjoint",
+        grid,
+        [
+            rows(LANES),
+            rows(LANES),
+            tot_block,
+            whole(gates_of.shape),
+            whole((8, 2 * width)),
+            whole(ex.shape),
+            rows(width),
+            rows(width),
+            whole((width, model)),
+        ],
+        [(whole((own - ASIDE, model)), sds((own - ASIDE, model), BF16))] * head_devices
+        + [
             (whole(states.shape), states),
             (state_block, states),
         ]
         + messages,
-        [
-            pltpu.VMEM((HDIM, width), F32),
-            pltpu.VMEM((nc, HDIM, width), F32),
-            pltpu.VMEM((tb, width), BF16),
-            pltpu.VMEM((width, model), F32),
-            pltpu.VMEM((model, width), F32),
-        ],
-        24e9,
-        [
-            y,
-            gate_in,
-            dout,
-            mg,
-            acted,
-            pack,
-            tot,
-            gates,
-            gtot,
-            ex,
-            eye,
-            normed,
-            cot_all,
-            proj_out,
-        ]
-        + shares,
+        [pltpu.VMEM((HDIM, width), F32), pltpu.VMEM((nc, HDIM, width), F32)],
+        1e8,
+        [acted, pack, tot, gates, gtot, ex, dy, outin, proj_out],
         scalars,
     )
+    mixers = outs[:head_devices]
+    dso, dro, *behind = outs[head_devices:]
 
     grad_proj_out, grad_proj_gate = lax.psum((gout, ggate), "seq")
-    mixer = lax.psum_scatter(mixer, "head", scatter_dimension=0, tiled=True)
+    aside = lax.psum_scatter(aside, "head", scatter_dimension=0, tiled=True)
     behind = exchange_sides(behind, hops)
-
+    mixer_shares = [mixers[0]] + [swap(mixers[k], "head", k) for k in range(1, head_devices)]
+
+    mid_grid, mid_rows, mid_lanes, *_ = sized(256)
     dxin, dbc, pulls = call(
         partial(mid_kernel, nh),
         "mid",
-        grid,
+        mid_grid,
         [
-            rows(wide),
-            rows(LANES),
-            lane_block(8, tb),
-            lane_block(16, tb),
-            rows(width),
+            mid_rows(wide),
+            mid_rows(LANES),
+            mid_lanes(8),
+            mid_lanes(16),
+            mid_rows(width),
             whole((16, LANES)),
         ],
         [
-            (rows(width), sds((length, width), BF16)),
-            (rows(LANES), sds((length, LANES), F32)),
-            (rows(LANES), sds((length, LANES), F32)),
+            (mid_rows(width), sds((length, width), BF16)),
+            (mid_rows(LANES), sds((length, LANES), F32)),
+            (mid_rows(LANES), sds((length, LANES), F32)),
         ],
         [],
-        18e9,
+        1e8,
         [acted, pack, seg_row, rowa, dy, eye16],
     )
 
@@ -1395,7 +1434,7 @@
             pltpu.VMEM((HDIM, width), F32),
             pltpu.VMEM((tb, model), BF16),
         ],
-        33e9,
+        1e8,
         [
             acted,
             slope,
@@ -1433,6 +1472,7 @@
         scalars,
     )
 
+    chunks, theirs, mixer_shares = lax.optimization_barrier((chunks, theirs, mixer_shares))
     got = swap(theirs, "head", 1)
     summed = chunks[0].astype(F32)
     for k in range(1, peers):
@@ -1444,22 +1484,34 @@
     common = common | ((lane_at > 16) & (lane_at < 21) & (row_at < LANES))
     shared = jnp.where(common, sum_over(shared, "head"), shared)
 
-    own_in = mine.astype(F32) + got.astype(F32)
+    half = head_devices // 4
+    own_in = mine[:half].astype(F32) + got[:half].astype(F32)
+    going = (mine[half:].astype(F32) + got[half:].astype(F32)).astype(BF16)
     for b in range(1, bits):
-        half = own_in.shape[0] // 2
-        own_in = own_in[:half] + swap(own_in[half:].astype(BF16), "head", 1 << b).astype(F32)
-    own_in = own_in[0]
+        if b == 1:
+            going, shared = lax.optimization_barrier((going, shared))
+        got = swap(going, "head", 1 << b)
+        if b < bits - 1:
+            half = half // 2
+            going = (own_in[half:] + got[half:].astype(F32)).astype(BF16)
+            own_in = own_in[:half] + got[:half].astype(F32)
 
     reduced = jnp.concatenate([shared, summed[:, 2 * LANES :]], axis=1).astype(BF16)
+    reduced, grad_proj_out, grad_proj_gate, mixer_shares = lax.optimization_barrier(
+        (reduced, grad_proj_out, grad_proj_gate, mixer_shares)
+    )
     spread_out = [reduced] + [swap(reduced, "seq", k) for k in range(1, peers)]
-    layer_out = (tokens.astype(F32) + mixer.astype(F32)).astype(BF16)
-
-    token_values = tokens.astype(F32)
-    scale_rows = lax.rsqrt(jnp.mean(token_values * token_values, axis=1, keepdims=True) + EPSILON)
-    grad_tokens = token_grads(cotangent.astype(F32), token_values, scale_rows, own_in, input_gain)
+    grad_proj_out = grad_proj_out[:real_width].astype(F32)
+    grad_proj_gate = grad_proj_gate[:, :real_width].astype(F32)
+    mixer = sum(share.astype(F32) for share in mixer_shares)
+    mixer = jnp.concatenate([aside.astype(F32), mixer], axis=0)
+    layer_out = (tokens.astype(F32) + mixer).astype(BF16)
+    spread_out, layer_out, grad_proj_out, grad_proj_gate = lax.optimization_barrier(
+        (spread_out, layer_out, grad_proj_out, grad_proj_gate)
+    )
 
     finals = [
-        sds((1, model), F32),
+        sds((model,), F32),
         sds((model, real_width), F32),
         sds((model, LANES), F32),
         sds((real_heads, 2, model), F32),
@@ -1468,30 +1520,30 @@
         sds((4, real_width), F32),
         sds((4, LANES), F32),
         sds((1, real_heads), F32),
-        sds((1, real_width), F32),
-        sds((16, model), BF16),
+        sds((real_width,), F32),
+        sds((own, model), BF16),
     ]
-    ggain, gvalue, gstate, gstep, gbias, gdecay, gconvv, gconvs, gskips, gmixer, late = call(
+    ggain, gvalue, gstate, gstep, gbias, gdecay, gconvv, gconvs, gskips, gmixer, grad_tokens = call(
         partial(finish_kernel, nh, peers, head_devices),
         "finish",
         1,
         [whole((size, LANES + wide))] * peers
         + [whole((32, LANES)), whole((1, model))]
-        + [whole((16, model))] * 3,
+        + [whole((own, model))] * 2
+        + [whole((1, own, model))] * 2,
         [(whole(f.shape), f) for f in finals],
         [pltpu.VMEM((model, LANES), F32)],
         3e9,
         spread_out
         + [picked, input_gain[None, :]]
-        + [tokens[own - 16 :], cotangent[own - 16 :], own_in[own - 16 :]],
+        + [tokens, cotangent, own_in, got],
         scalars,
     )
-    grad_tokens = lax.dynamic_update_slice(grad_tokens, late, (own - 16, 0))
     return (
         layer_out,
         grad_tokens,
-        ggain[0],
-        grad_proj_gate[:, :real_width].astype(F32),
+        ggain,
+        grad_proj_gate,
         gvalue,
         gstate,
         jnp.transpose(gstep, (1, 2, 0)),
@@ -1500,8 +1552,8 @@
         gconvv,
         gconvs,
         gskips[0],
-        gmixer[0],
-        grad_proj_out[:real_width].astype(F32),
+        gmixer,
+        grad_proj_out,
     )
 
 

time: 299 us -> 282 us (0.943)
  local copies, waits for them, and re-layouts: 21.1 us -> 15.3 us
  waiting for transfers between devices: 34.9 us -> 30 us
  other arithmetic: 24 us -> 20.2 us
  starting transfers between devices: 71.3 us -> 68.1 us
    ppermute x3, waiting for transfers between devices: 18.4 us -> 4.01 us  [sum_over(): lax.ppermute(array, axis, [(i, i ^ k) for i in range(size)])]
    ppermute x22 -> x25, waiting for transfers between devices: 12.6 us -> 18.7 us  [swap(): return lax.ppermute(array, axis, [(i, i ^ k) for i in range(n)])]
    slice x4 -> x0, local copies, waits for them, and re-layouts: 4.28 us -> none  [the longest x1 1.35 us: per_device(): tokens[own - 16:]]
    ppermute x22 -> x25, starting transfers between devices: 50.5 us -> 46.4 us  [swap(): return lax.ppermute(array, axis, [(i, i ^ k) for i in range(n)])]
    ppermute x8, waiting for transfers between devices: 0.02 us -> 3.13 us  [exchange_sides(): arrived.append(lax.ppermute(messages[len(arrived)], 'seq', both))]
    pallas_call x7 -> x8, Pallas kernels: 132 us -> 134 us  [call(): pl.pallas_call(kernel, name=name, grid_spec=pltpu.PrefetchScalarGridSpec(...]
    convert_element_type x3 -> x4, other arithmetic: 5.98 us -> 4.29 us  [the longest x1 1.09 us: per_device(): grad_proj_out = grad_proj_out[:real_width].astype(F32)]
    unnamed x72 -> x68, local copies, waits for them, and re-layouts: 6.36 us -> 4.85 us
  transfers between devices with their start and end apart: 40 -> 43, of which waited for: 10 -> 13; matrix products, arithmetic and copies ran while one was open for 11% -> 10% of each run, Pallas kernels for 33% -> 37%
where the time goes in v4:
time: 282 us
  Pallas kernels  134 us (48%)
  starting transfers between devices  68.1 us (24%)
  waiting for transfers between devices  30 us (11%)
  other arithmetic  20.2 us (7%)
  local copies, waits for them, and re-layouts  15.3 us (5%)
  between operations  14.3 us (5%)
    pallas_call x8, Pallas kernels, call(): pl.pallas_call(kernel, name=name, grid_spec=pltpu.PrefetchScalarGridSpec(...  134 us
    ppermute x25, starting transfers between devices, swap(): return lax.ppermute(array, axis, [(i, i ^ k) for i in range(n)])  46.4 us
    ppermute x25, waiting for transfers between devices, swap(): return lax.ppermute(array, axis, [(i, i ^ k) for i in range(n)])  18.7 us
    ppermute x8, starting transfers between devices, exchange_sides(): arrived.append(lax.ppermute(messages[len(arrived)], 'seq', both))  14.1 us
  transfers between devices with their start and end apart: 43, of which 13 were waited for; matrix products, arithmetic and copies ran while one was open for 10% of the time, Pallas kernels for 37%

profile of v4, /device:TPU:0, one launch (start us, length us, event | category | flops | bytes accessed | tf_op | source)
XLA Modules:
  0.0 281.7 jit_solution(3846440068074934278)
XLA Ops:
  7.2 3.0 %collective-permute-start = (bf16[512,768]{1,0:T(8,128)(2,1)}, bf16[512,768]{1,0:T(8,128)(2,1)S(1)}, u32[]{:S(2)}, u32[]{:S(2)}) collective-permute-start(bf16[512,768]{1,0:T(8,128)(2,1)} %refs_10_.1), channel_id=1, source_target_pairs={{0,2},{1,3},{2,0},{3,1},{4,6},{5,7},{6,4},{7,5},{8,10},{9,11},{10,... | collective-permute-start | bytes 2359304 | tf_op jit(solution)/shard_map/ppermute | solution.py:966
  11.0 3.4 %collective-permute-start.1 = (bf16[8,768]{1,0:T(8,128)(2,1)S(1)}, bf16[8,768]{1,0:T(8,128)(2,1)S(1)}, u32[]{:S(2)}, u32[]{:S(2)}) collective-permute-start(bf16[8,768]{1,0:T(8,128)(2,1)S(1)} %slice.91), channel_id=1, source_target_pairs={{0,4},{4,8},{8,12},{12,16},{16,20},{20,24},{24,28},{1,5},{5,9},{9,... | collective-permute-start | bytes 36872 | tf_op jit(solution)/shard_map/ppermute | solution.py:950
  14.4 1.3 and_reduce_fusion
  19.4 0.8 fusion.5
  21.4 1.3 select_maximum_fusion.refs_12_.taps_ref
  23.4 2.1 pad_maximum_fusion.refs_7_
  25.5 1.1 fusion.3.wcat_ref
  27.4 0.9 collective-permute-start.3
  28.3 1.0 collective-permute-start.2
  29.2 2.0 broadcast_select_fusion
  31.2 1.6 scatter.14.refs_10_.pcol_ref
  37.7 1.8 collective-permute-done.5.refs_1_
  39.4 1.1 collective-permute-done.6.refs_3_
  40.6 0.9 copy-done.23
  41.5 27.5 %front.1 = (bf16[2048,768]{1,0:T(8,128)(2,1)}, bf16[8,768]{1,0:T(8,128)(2,1)}, bf16[2048,384]{1,0:T(8,128)(2,1)}, bf16[2048,512]{1,0:T(8,128)(2,1)}, bf16[2048,5...) custom-call(s32[3]{0:T(128)} %pad_add_fusion.at_ref, ...), custom_call_target="tpu_custom_call" | custom-call | flops 24999999488 | bytes 1 | tf_op jit(solution)/shard_map/front/pallas_call | solution.py:927
  69.0 1.6 collective-permute-start.7
  71.3 3.2 %collective-permute-start.9 = (f32[72,384]{1,0:T(8,128)}, f32[72,384]{1,0:T(8,128)S(1)}, u32[]{:S(2)}, u32[]{:S(2)}) collective-permute-start(f32[72,384]{1,0:T(8,128)} %get-tuple-element.201), channel_id=1, source_target_pairs={{0,8},{4,12},{16,24},{20,28},{8,0},{12,4},{24,16},{28,20},{1,9},{5... | collective-permute-start | bytes 331784 | tf_op jit(solution)/shard_map/ppermute | solution.py:960
  74.5 0.8 collective-permute-start.10
  75.4 8.7 %inner.1 = (f32[2048,384]{1,0:T(8,128)}, bf16[2048,384]{1,0:T(8,128)(2,1)}) custom-call(bf16[2048,512]{1,0:T(8,128)(2,1)} %get-tuple-element.183.act_ref.bc_ref, f32[2048,128]{1,0:T(8,128)} %get-tuple-element.185.pack_ref, f32[8,2048]{1,0:T(8,128)} %get-tuple-element.191.segrow_ref, f32[16,2048]{1,0:T(8,128)} %get-tuple-element.192.rowp_ref, ...), custom_call_target="tpu_custom_call" | custom-call | flops 6000000000 | bytes 1 | tf_op jit(solution)/shard_map/inner/pallas_call | solution.py:927
  84.9 9.3 %merge.1 = (bf16[2048,384]{1,0:T(8,128)(2,1)}, f32[8,2048]{1,0:T(8,128)}, bf16[16,64,768]{2,1,0:T(8,128)(2,1)}) custom-call(s32[3]{0:T(128)} %pad_add_fusion.at_ref, bf16[2048,512]{1,0:T(8,128)(2,1)} %get-tuple-element.183.act_ref.bc_ref, f32[2048,128]{1,0:T(8,128)} %get-tuple-element.185.pack_ref, f32[128,128]{1,0:T(8,128)} %get-tuple-element.186.tot_ref, ...), custom_call_target="tpu_custom_call" | custom-call | flops 6000000000 | bytes 1 | tf_op jit(solution)/shard_map/merge/pallas_call | solution.py:927
  94.3 0.9 collective-permute-start.12
  95.2 0.9 collective-permute-start.11
  96.1 2.5 collective-permute-done.13.rest_3_
  100.1 13.4 %turn.1 = (bf16[1024,768]{1,0:T(8,128)(2,1)}, bf16[2048,384]{1,0:T(8,128)(2,1)}, bf16[2048,384]{1,0:T(8,128)(2,1)}, bf16[2048,384]{1,0:T(8,128)(2,1)}, f32[8,384...) custom-call(bf16[2048,384]{1,0:T(8,128)(2,1)} %get-tuple-element.203.y_ref, ...), custom_call_target="tpu_custom_call" | custom-call | flops 4000000000 | bytes 1 | tf_op jit(solution)/shard_map/turn/pallas_call | solution.py:927
  114.3 13.5 %adjoint.1 = (bf16[256,768]{1,0:T(8,128)(2,1)}, bf16[256,768]{1,0:T(8,128)(2,1)}, bf16[256,768]{1,0:T(8,128)(2,1)}, bf16[256,768]{1,0:T(8,128)(2,1)}, f32[16,64,...) custom-call(s32[3]{0:T(128)} %pad_add_fusion.at_ref, ...), custom_call_target="tpu_custom_call" | custom-call | flops 100000000 | bytes 1 | tf_op jit(solution)/shard_map/adjoint/pallas_call | solution.py:927
  127.9 1.2 collective-permute-start.19
  129.7 2.7 collective-permute-start.14
  133.1 3.1 %collective-permute-done.14.rest_0_ = f32[72,384]{1,0:T(8,128)S(1)} collective-permute-done((f32[72,384]{1,0:T(8,128)}, f32[72,384]{1,0:T(8,128)S(1)}, u32[]{:S(2)}, u32[]{:S(2)}) %collective-permute-start.14) | collective-permute-done | bytes 110624 | tf_op jit(solution)/shard_map/ppermute | solution.py:960
  136.2 3.5 %collective-permute-start.16 = (f32[72,384]{1,0:T(8,128)}, f32[72,384]{1,0:T(8,128)S(1)}, u32[]{:S(2)}, u32[]{:S(2)}) collective-permute-start(f32[72,384]{1,0:T(8,128)} %get-tuple-element.227), channel_id=1, source_target_pairs={{0,8},{4,12},{16,24},{20,28},{8,0},{12,4},{24,16},{28,20},{1,9},{5... | collective-permute-start | bytes 331784 | tf_op jit(solution)/shard_map/ppermute | solution.py:960
  139.7 0.9 collective-permute-start.17
  140.6 19.5 %mid.1 = (bf16[2048,384]{1,0:T(8,128)(2,1)}, f32[2048,128]{1,0:T(8,128)}, f32[2048,128]{1,0:T(8,128)}) custom-call(bf16[2048,512]{1,0:T(8,128)(2,1)} %get-tuple-element.183.act_ref.bc_ref, f32[2048,128]{1,0:T(8,128)} %get-tuple-element.185.pack_ref, f32[8,2048]{1,0:T(8,128)} %get-tuple-element.191.segrow_ref, f32[16,2048]{1,0:T(8,128)} %get-tuple-element.213.rowa_ref, ...), custom_call_target="tpu_custom_call" | custom-call | flops 100000000 | bytes 1 | tf_op jit(solution)/shard_map/mid/pallas_call | solution.py:927
  160.8 36.2 %back.1 = (bf16[2,512,768]{2,1,0:T(8,128)(2,1)}, bf16[2,512,768]{2,1,0:T(8,128)(2,1)}, bf16[96,640]{1,0:T(8,128)(2,1)}, bf16[96,640]{1,0:T(8,128)(2,1)}, bf16[96...) custom-call(s32[3]{0:T(128)} %pad_add_fusion.at_ref, ...), custom_call_target="tpu_custom_call" | custom-call | flops 100000000 | bytes 1 | tf_op jit(solution)/shard_map/back/pallas_call | solution.py:927
  198.1 1.6 collective-permute-start.22
  199.7 4.8 %collective-permute-start.23 = (bf16[96,640]{1,0:T(8,128)(2,1)}, bf16[96,640]{1,0:T(8,128)(2,1)S(1)}, u32[]{:S(2)}, u32[]{:S(2)}) collective-permute-start(bf16[96,640]{1,0:T(8,128)(2,1)} %get-tuple-element.246), channel_id=1, source_target_pairs={{0,8},{4,12},{8,0},{12,4},{16,24},{20,28},{24,16},{28,20},{1,9},{5... | collective-permute-start | bytes 368648 | tf_op jit(solution)/shard_map/ppermute | solution.py:966
  204.5 0.8 collective-permute-start.24
  205.3 2.2 collective-permute-start.25
  207.5 3.1 %collective-permute-start.26 = (bf16[96,640]{1,0:T(8,128)(2,1)}, bf16[96,640]{1,0:T(8,128)(2,1)}, u32[]{:S(2)}, u32[]{:S(2)}) collective-permute-start(bf16[96,640]{1,0:T(8,128)(2,1)} %get-tuple-element.249), channel_id=1, source_target_pairs={{0,20},{4,16},{8,28},{12,24},{16,4},{20,0},{24,12},{28,8},{1,21},{... | collective-permute-start | bytes 368648 | tf_op jit(solution)/shard_map/ppermute | solution.py:966
  210.6 4.4 %collective-permute-start.27 = (bf16[96,640]{1,0:T(8,128)(2,1)}, bf16[96,640]{1,0:T(8,128)(2,1)}, u32[]{:S(2)}, u32[]{:S(2)}) collective-permute-start(bf16[96,640]{1,0:T(8,128)(2,1)} %get-tuple-element.250), channel_id=1, source_target_pairs={{0,24},{4,28},{8,16},{12,20},{16,8},{20,12},{24,0},{28,4},{1,25},{... | collective-permute-start | bytes 368648 | tf_op jit(solution)/shard_map/ppermute | solution.py:966
  215.0 0.9 collective-permute-done.24
  215.9 2.3 collective-permute-start.28
  218.2 7.7 %collective-permute-done.26 = bf16[96,640]{1,0:T(8,128)(2,1)} collective-permute-done((bf16[96,640]{1,0:T(8,128)(2,1)}, bf16[96,640]{1,0:T(8,128)(2,1)}, u32[]{:S(2)}, u32[]{:S(2)}) %collective-permute-start.26) | collective-permute-done | bytes 122912 | tf_op jit(solution)/shard_map/ppermute | solution.py:966
  225.9 1.3 convert_add_fusion.2
  227.2 1.2 collective-permute-start.30
  228.4 1.0 collective-permute-start.29
  229.4 3.0 %collective-permute-done.30 = f32[96,256]{1,0:T(8,128)S(1)} collective-permute-done((f32[96,256]{1,0:T(8,128)S(1)}, f32[96,256]{1,0:T(8,128)S(1)}, u32[]{:S(2)}, u32[]{:S(2)}) %collective-permute-start.30) | collective-permute-done | bytes 98336 | tf_op jit(solution)/shard_map/ppermute | solution.py:973
  232.5 1.0 collective-permute-done.31
  233.6 1.7 convert_add_fusion
  235.3 1.0 collective-permute-start.39
  236.9 2.4 collective-permute-start.38
  239.3 2.3 collective-permute-start.37
  241.7 3.9 %collective-permute-start.36 = (bf16[96,640]{1,0:T(8,128)(2,1)S(1)}, bf16[96,640]{1,0:T(8,128)(2,1)}, u32[]{:S(2)}, u32[]{:S(2)}) collective-permute-start(bf16[96,640]{1,0:T(8,128)(2,1)S(1)} %pad_maximum_fusion.1.refs_0_), channel_id=1, source_target_pairs={{0,20},{4,16},{8,28},{12,24},{16,4},{20,0},{24,12},{28,8},{1,21},{... | collective-permute-start | bytes 368648 | tf_op jit(solution)/shard_map/ppermute | solution.py:966
  245.5 1.4 convert_add_fusion.1
  247.0 1.1 convert_element_type.100
  248.1 1.1 convert_element_type.101
  249.2 1.0 convert_element_type.94
  250.2 7.1 %collective-permute-start.34 = (bf16[96,640]{1,0:T(8,128)(2,1)S(1)}, bf16[96,640]{1,0:T(8,128)(2,1)S(1)}, u32[]{:S(2)}, u32[]{:S(2)}) collective-permute-start(bf16[96,640]{1,0:T(8,128)(2,1)S(1)} %pad_maximum_fusion.1.refs_0_), channel_id=1, source_target_pairs={{0,12},{4,8},{8,4},{12,0},{16,28},{20,24},{24,20},{28,16},{1,13},{... | collective-permute-start | bytes 368648 | tf_op jit(solution)/shard_map/ppermute | solution.py:966
  257.3 1.7 collective-permute-start.33
  259.0 2.2 collective-permute-done.36.refs_5_
  261.3 1.4 collective-permute-start.32
  262.7 1.1 fusion.1
  263.8 2.6 collective-permute-done.34.refs_3_
  266.4 1.4 collective-permute-done.33.refs_2_
  267.9 0.8 collective-permute-done.32.refs_1_
  269.6 5.5 %finish.1 = (f32[768]{0:T(1024)}, f32[768,384]{1,0:T(8,128)}, f32[768,128]{1,0:T(8,128)}, f32[6,2,768]{2,1,0:T(2,128)}, f32[2,6]{1,0:T(2,128)}, /*index=5*/f32[1...) custom-call(s32[3]{0:T(128)} %pad_add_fusion.at_ref, ...), custom_call_target="tpu_custom_call" | custom-call | flops 3000000000 | bytes 1 | tf_op jit(solution)/shard_map/finish/pallas_call | solution.py:927
  (156 shorter events, 20.4 us)
Async XLA Ops:
  7.2 18.3 %copy-start.4 = (bf16[768,128]{1,0:T(8,128)(2,1)S(1)}, bf16[768,128]{1,0:T(8,128)(2,1)}, u32[]{:S(2)}) copy-start(bf16[768,128]{1,0:T(8,128)(2,1)} %param.34) | copy-start | bytes 589828
  7.2 18.3 %copy-start = (bf16[768,384]{1,0:T(8,128)(2,1)S(1)}, bf16[768,384]{1,0:T(8,128)(2,1)}, u32[]{:S(2)}) copy-start(bf16[768,384]{1,0:T(8,128)(2,1)} %param.33) | copy-start | bytes 1769476
  7.2 68.2 %all-gather.2.cloned.1.call-start = ((), (), s32[]{:S(2)}) async-start(), calls=%async_computation.1 | async-start | bytes 3932160 | tf_op jit(solution)/shard_map/all_gather | solution.py:1096
  7.2 27.9 %collective-permute-start = (bf16[512,768]{1,0:T(8,128)(2,1)}, bf16[512,768]{1,0:T(8,128)(2,1)S(1)}, u32[]{:S(2)}, u32[]{:S(2)}) collective-permute-start(bf16[512,768]{1,0:T(8,128)(2,1)} %refs_10_.1), channel_id=1, source_target_pairs={{0,2},{1,3},{2,0},{3,1},{4,6},{5,7},{6,4},{7,5},{8,10},{9,11},{10,... | collective-permute-start | bytes 2359304 | tf_op jit(solution)/shard_map/ppermute | solution.py:966
  11.0 16.3 %collective-permute-start.1 = (bf16[8,768]{1,0:T(8,128)(2,1)S(1)}, bf16[8,768]{1,0:T(8,128)(2,1)S(1)}, u32[]{:S(2)}, u32[]{:S(2)}) collective-permute-start(bf16[8,768]{1,0:T(8,128)(2,1)S(1)} %slice.91), channel_id=1, source_target_pairs={{0,4},{4,8},{8,12},{12,16},{16,20},{20,24},{24,28},{1,5},{5,9},{9,... | collective-permute-start | bytes 36872 | tf_op jit(solution)/shard_map/ppermute | solution.py:950
  23.4 9.4 %copy-start.19 = (f32[6]{0:T(128)S(1)}, f32[6]{0:T(128)}, u32[]{:S(2)}) copy-start(f32[6]{0:T(128)} %param.40) | copy-start | bytes 76
  25.4 10.4 %copy-start.18 = (f32[384]{0:T(512)S(1)}, f32[384]{0:T(512)}, u32[]{:S(2)}) copy-start(f32[384]{0:T(512)} %param.41) | copy-start | bytes 4612
  25.5 10.9 %copy-start.17 = (f32[768]{0:T(1024)S(1)}, f32[768]{0:T(1024)}, u32[]{:S(2)}) copy-start(f32[768]{0:T(1024)} %param.31) | copy-start | bytes 9220
  25.5 11.6 %copy-start.2 = (bf16[512,768]{1,0:T(8,128)(2,1)S(1)}, bf16[512,768]{1,0:T(8,128)(2,1)}, u32[]{:S(2)}) copy-start(bf16[512,768]{1,0:T(8,128)(2,1)} %refs_10_.1) | copy-start | bytes 2359300
  27.3 7.2 %collective-permute-start.4 = (bf16[8,768]{1,0:T(8,128)(2,1)S(1)}, bf16[8,768]{1,0:T(8,128)(2,1)S(1)}, u32[]{:S(2)}, u32[]{:S(2)}) collective-permute-start(bf16[8,768]{1,0:T(8,128)(2,1)S(1)} %collective-permute-done.1), channel_id=1, source_target_pairs={{0,3},{1,2},{2,1},{3,0},{4,7},{5,6},{6,5},{7,4},{8,11},{9,10},{10,... | collective-permute-start | bytes 36872 | tf_op jit(solution)/shard_map/ppermute | solution.py:966
  27.4 7.1 %collective-permute-start.3 = (bf16[8,768]{1,0:T(8,128)(2,1)S(1)}, bf16[8,768]{1,0:T(8,128)(2,1)S(1)}, u32[]{:S(2)}, u32[]{:S(2)}) collective-permute-start(bf16[8,768]{1,0:T(8,128)(2,1)S(1)} %collective-permute-done.1), channel_id=1, source_target_pairs={{0,2},{1,3},{2,0},{3,1},{4,6},{5,7},{6,4},{7,5},{8,10},{9,11},{10,... | collective-permute-start | bytes 36872 | tf_op jit(solution)/shard_map/ppermute | solution.py:966
  28.3 6.3 %collective-permute-start.2 = (bf16[8,768]{1,0:T(8,128)(2,1)S(1)}, bf16[8,768]{1,0:T(8,128)(2,1)S(1)}, u32[]{:S(2)}, u32[]{:S(2)}) collective-permute-start(bf16[8,768]{1,0:T(8,128)(2,1)S(1)} %collective-permute-done.1), channel_id=1, source_target_pairs={{0,1},{1,0},{2,3},{3,2},{4,5},{5,4},{6,7},{7,6},{8,9},{9,8},{10,11... | collective-permute-start | bytes 36872 | tf_op jit(solution)/shard_map/ppermute | solution.py:966
  32.8 7.7 %copy-start.16 = (f32[8,128]{1,0:T(8,128)}, f32[8,128]{1,0:T(8,128)S(1)}, u32[]{:S(2)}) copy-start(f32[8,128]{1,0:T(8,128)S(1)} %scatter.14.refs_10_.pcol_ref) | copy-start | bytes 12292
  35.2 5.4 %copy-start.20 = (bf16[512,768]{1,0:T(8,128)(2,1)}, bf16[512,768]{1,0:T(8,128)(2,1)S(1)}, u32[]{:S(2)}) copy-start(bf16[512,768]{1,0:T(8,128)(2,1)S(1)} %collective-permute-done.refs_2_) | copy-start | bytes 2359300
  37.0 199.9 %all-reduce.9.cloned.1.call-start = ((), (), s32[]{:S(2)}) async-start(), calls=%async_computation.3 | async-start | bytes 2359296 | tf_op jit(solution)/shard_map/psum | solution.py:1351
  37.1 2.4 collective-permute-start.5
  37.2 3.4 %collective-permute-start.6 = (bf16[512,768]{1,0:T(8,128)(2,1)S(1)}, bf16[512,768]{1,0:T(8,128)(2,1)S(1)}, u32[]{:S(2)}, u32[]{:S(2)}) collective-permute-start(bf16[512,768]{1,0:T(8,128)(2,1)S(1)} %collective-permute-done.refs_2_), channel_id=1, source_target_pairs={{0,1},{1,0},{2,3},{3,2},{4,5},{5,4},{6,7},{7,6},{8,9},{9,8},{10,11... | collective-permute-start | bytes 2359304 | tf_op jit(solution)/shard_map/ppermute | solution.py:966
  39.4 1.1 copy-start.22
  40.6 0.9 copy-start.23
  69.0 15.1 %collective-permute-start.7 = (f32[72,384]{1,0:T(8,128)}, f32[72,384]{1,0:T(8,128)S(1)}, u32[]{:S(2)}, u32[]{:S(2)}) collective-permute-start(f32[72,384]{1,0:T(8,128)} %get-tuple-element.199), channel_id=1, source_target_pairs={{0,4},{8,12},{16,20},{24,28},{4,0},{12,8},{20,16},{28,24},{1,5},{9... | collective-permute-start | bytes 331784 | tf_op jit(solution)/shard_map/ppermute | solution.py:960
  70.6 13.5 %collective-permute-start.8 = (f32[72,384]{1,0:T(8,128)}, f32[72,384]{1,0:T(8,128)S(1)}, u32[]{:S(2)}, u32[]{:S(2)}) collective-permute-start(f32[72,384]{1,0:T(8,128)} %get-tuple-element.200), channel_id=1, source_target_pairs={{4,8},{12,16},{20,24},{8,4},{16,12},{24,20},{5,9},{13,17},{21,25},... | collective-permute-start | bytes 331784 | tf_op jit(solution)/shard_map/ppermute | solution.py:960
  71.3 12.9 %collective-permute-start.9 = (f32[72,384]{1,0:T(8,128)}, f32[72,384]{1,0:T(8,128)S(1)}, u32[]{:S(2)}, u32[]{:S(2)}) collective-permute-start(f32[72,384]{1,0:T(8,128)} %get-tuple-element.201), channel_id=1, source_target_pairs={{0,8},{4,12},{16,24},{20,28},{8,0},{12,4},{24,16},{28,20},{1,9},{5... | collective-permute-start | bytes 331784 | tf_op jit(solution)/shard_map/ppermute | solution.py:960
  74.5 9.6 %collective-permute-start.10 = (f32[72,384]{1,0:T(8,128)}, f32[72,384]{1,0:T(8,128)S(1)}, u32[]{:S(2)}, u32[]{:S(2)}) collective-permute-start(f32[72,384]{1,0:T(8,128)} %get-tuple-element.202), channel_id=1, source_target_pairs={{8,16},{12,20},{16,8},{20,12},{9,17},{13,21},{17,9},{21,13},{10,18... | collective-permute-start | bytes 331784 | tf_op jit(solution)/shard_map/ppermute | solution.py:960
  94.2 4.5 %collective-permute-start.13 = (f32[8,2048]{1,0:T(8,128)}, f32[8,2048]{1,0:T(8,128)S(1)}, u32[]{:S(2)}, u32[]{:S(2)}) collective-permute-start(f32[8,2048]{1,0:T(8,128)} %get-tuple-element.205.rest_0_), channel_id=1, source_target_pairs={{0,3},{1,2},{2,1},{3,0},{4,7},{5,6},{6,5},{7,4},{8,11},{9,10},{10,... | collective-permute-start | bytes 196616 | tf_op jit(solution)/shard_map/ppermute | solution.py:1290
  94.3 5.2 %collective-permute-start.12 = (f32[8,2048]{1,0:T(8,128)}, f32[8,2048]{1,0:T(8,128)S(1)}, u32[]{:S(2)}, u32[]{:S(2)}) collective-permute-start(f32[8,2048]{1,0:T(8,128)} %get-tuple-element.205.rest_0_), channel_id=1, source_target_pairs={{0,2},{1,3},{2,0},{3,1},{4,6},{5,7},{6,4},{7,5},{8,10},{9,11},{10,... | collective-permute-start | bytes 196616 | tf_op jit(solution)/shard_map/ppermute | solution.py:1290
  95.2 4.3 %collective-permute-start.11 = (f32[8,2048]{1,0:T(8,128)}, f32[8,2048]{1,0:T(8,128)S(1)}, u32[]{:S(2)}, u32[]{:S(2)}) collective-permute-start(f32[8,2048]{1,0:T(8,128)} %get-tuple-element.205.rest_0_), channel_id=1, source_target_pairs={{0,1},{1,0},{2,3},{3,2},{4,5},{5,4},{6,7},{7,6},{8,9},{9,8},{10,11... | collective-permute-start | bytes 196616 | tf_op jit(solution)/shard_map/ppermute | solution.py:1290
  113.5 135.6 %reduce-scatter.2.cloned.1.call-start = ((), (), s32[]{:S(2)}) async-start(), calls=%async_computation.2 | async-start | bytes 1966080 | tf_op jit(solution)/shard_map/reduce_scatter | solution.py:1352
  127.7 69.3 %collective-permute-start.18 = (bf16[256,768]{1,0:T(8,128)(2,1)}, bf16[256,768]{1,0:T(8,128)(2,1)S(1)}, u32[]{:S(2)}, u32[]{:S(2)}) collective-permute-start(bf16[256,768]{1,0:T(8,128)(2,1)} %get-tuple-element.240), channel_id=1, source_target_pairs={{0,1},{1,0},{2,3},{3,2},{4,5},{5,4},{6,7},{7,6},{8,9},{9,8},{10,11... | collective-permute-start | bytes 1179656 | tf_op jit(solution)/shard_map/ppermute | solution.py:966
  127.9 69.2 %collective-permute-start.19 = (bf16[256,768]{1,0:T(8,128)(2,1)}, bf16[256,768]{1,0:T(8,128)(2,1)S(1)}, u32[]{:S(2)}, u32[]{:S(2)}) collective-permute-start(bf16[256,768]{1,0:T(8,128)(2,1)} %get-tuple-element.241), channel_id=1, source_target_pairs={{0,2},{1,3},{2,0},{3,1},{4,6},{5,7},{6,4},{7,5},{8,10},{9,11},{10,... | collective-permute-start | bytes 1179656 | tf_op jit(solution)/shard_map/ppermute | solution.py:966
  129.1 68.0 %collective-permute-start.20 = (bf16[256,768]{1,0:T(8,128)(2,1)}, bf16[256,768]{1,0:T(8,128)(2,1)S(1)}, u32[]{:S(2)}, u32[]{:S(2)}) collective-permute-start(bf16[256,768]{1,0:T(8,128)(2,1)} %get-tuple-element.242), channel_id=1, source_target_pairs={{0,3},{1,2},{2,1},{3,0},{4,7},{5,6},{6,5},{7,4},{8,11},{9,10},{10,... | collective-permute-start | bytes 1179656 | tf_op jit(solution)/shard_map/ppermute | solution.py:966
  129.7 6.5 %collective-permute-start.14 = (f32[72,384]{1,0:T(8,128)}, f32[72,384]{1,0:T(8,128)S(1)}, u32[]{:S(2)}, u32[]{:S(2)}) collective-permute-start(f32[72,384]{1,0:T(8,128)} %get-tuple-element.225), channel_id=1, source_target_pairs={{0,4},{8,12},{16,20},{24,28},{4,0},{12,8},{20,16},{28,24},{1,5},{9... | collective-permute-start | bytes 331784 | tf_op jit(solution)/shard_map/ppermute | solution.py:960
  132.4 7.3 %collective-permute-start.15 = (f32[72,384]{1,0:T(8,128)}, f32[72,384]{1,0:T(8,128)S(1)}, u32[]{:S(2)}, u32[]{:S(2)}) collective-permute-start(f32[72,384]{1,0:T(8,128)} %get-tuple-element.226), channel_id=1, source_target_pairs={{4,8},{12,16},{20,24},{8,4},{16,12},{24,20},{5,9},{13,17},{21,25},... | collective-permute-start | bytes 331784 | tf_op jit(solution)/shard_map/ppermute | solution.py:960
  136.2 24.0 %copy-start.12 = (f32[72,384]{1,0:T(8,128)}, f32[72,384]{1,0:T(8,128)S(1)}, u32[]{:S(2)}) copy-start(f32[72,384]{1,0:T(8,128)S(1)} %collective-permute-done.14.rest_0_) | copy-start | bytes 331780
  136.2 24.0 %collective-permute-start.16 = (f32[72,384]{1,0:T(8,128)}, f32[72,384]{1,0:T(8,128)S(1)}, u32[]{:S(2)}, u32[]{:S(2)}) collective-permute-start(f32[72,384]{1,0:T(8,128)} %get-tuple-element.227), channel_id=1, source_target_pairs={{0,8},{4,12},{16,24},{20,28},{8,0},{12,4},{24,16},{28,20},{1,9},{5... | collective-permute-start | bytes 331784 | tf_op jit(solution)/shard_map/ppermute | solution.py:960
  139.7 20.4 %copy-start.13 = (f32[72,384]{1,0:T(8,128)}, f32[72,384]{1,0:T(8,128)S(1)}, u32[]{:S(2)}) copy-start(f32[72,384]{1,0:T(8,128)S(1)} %collective-permute-done.15.rest_1_) | copy-start | bytes 331780
  139.7 20.5 %collective-permute-start.17 = (f32[72,384]{1,0:T(8,128)}, f32[72,384]{1,0:T(8,128)S(1)}, u32[]{:S(2)}, u32[]{:S(2)}) collective-permute-start(f32[72,384]{1,0:T(8,128)} %get-tuple-element.228), channel_id=1, source_target_pairs={{8,16},{12,20},{16,8},{20,12},{9,17},{13,21},{17,9},{21,13},{10,18... | collective-permute-start | bytes 331784 | tf_op jit(solution)/shard_map/ppermute | solution.py:960
  197.1 36.5 %copy-start.1 = (bf16[2,512,768]{2,1,0:T(8,128)(2,1)S(1)}, bf16[2,512,768]{2,1,0:T(8,128)(2,1)}, u32[]{:S(2)}) copy-start(bf16[2,512,768]{2,1,0:T(8,128)(2,1)} %get-tuple-element.229) | copy-start | bytes 4718596
  197.1 1.0 copy-start.10
  198.0 35.6 %collective-permute-start.21 = (bf16[2,512,768]{2,1,0:T(8,128)(2,1)}, bf16[2,512,768]{2,1,0:T(8,128)(2,1)S(1)}, u32[]{:S(2)}, u32[]{:S(2)}) collective-permute-start(bf16[2,512,768]{2,1,0:T(8,128)(2,1)} %get-tuple-element.243), channel_id=1, source_target_pairs={{0,1},{1,0},{2,3},{3,2},{4,5},{5,4},{6,7},{7,6},{8,9},{9,8},{10,11... | collective-permute-start | bytes 4718600 | tf_op jit(solution)/shard_map/ppermute | solution.py:966
  198.1 9.4 %collective-permute-start.22 = (bf16[96,640]{1,0:T(8,128)(2,1)}, bf16[96,640]{1,0:T(8,128)(2,1)S(1)}, u32[]{:S(2)}, u32[]{:S(2)}) collective-permute-start(bf16[96,640]{1,0:T(8,128)(2,1)} %get-tuple-element.245), channel_id=1, source_target_pairs={{0,4},{4,0},{8,12},{12,8},{16,20},{20,16},{24,28},{28,24},{1,5},{5... | collective-permute-start | bytes 368648 | tf_op jit(solution)/shard_map/ppermute | solution.py:966
  199.7 10.9 %collective-permute-start.23 = (bf16[96,640]{1,0:T(8,128)(2,1)}, bf16[96,640]{1,0:T(8,128)(2,1)S(1)}, u32[]{:S(2)}, u32[]{:S(2)}) collective-permute-start(bf16[96,640]{1,0:T(8,128)(2,1)} %get-tuple-element.246), channel_id=1, source_target_pairs={{0,8},{4,12},{8,0},{12,4},{16,24},{20,28},{24,16},{28,20},{1,9},{5... | collective-permute-start | bytes 368648 | tf_op jit(solution)/shard_map/ppermute | solution.py:966
  204.5 11.4 %collective-permute-start.24 = (bf16[96,640]{1,0:T(8,128)(2,1)}, bf16[96,640]{1,0:T(8,128)(2,1)S(1)}, u32[]{:S(2)}, u32[]{:S(2)}) collective-permute-start(bf16[96,640]{1,0:T(8,128)(2,1)} %get-tuple-element.247), channel_id=1, source_target_pairs={{0,12},{4,8},{8,4},{12,0},{16,28},{20,24},{24,20},{28,16},{1,13},{... | collective-permute-start | bytes 368648 | tf_op jit(solution)/shard_map/ppermute | solution.py:966
  205.3 12.9 %collective-permute-start.25 = (bf16[96,640]{1,0:T(8,128)(2,1)}, bf16[96,640]{1,0:T(8,128)(2,1)}, u32[]{:S(2)}, u32[]{:S(2)}) collective-permute-start(bf16[96,640]{1,0:T(8,128)(2,1)} %get-tuple-element.248), channel_id=1, source_target_pairs={{0,16},{4,20},{8,24},{12,28},{16,0},{20,4},{24,8},{28,12},{1,17},{... | collective-permute-start | bytes 368648 | tf_op jit(solution)/shard_map/ppermute | solution.py:966
  207.5 18.5 %collective-permute-start.26 = (bf16[96,640]{1,0:T(8,128)(2,1)}, bf16[96,640]{1,0:T(8,128)(2,1)}, u32[]{:S(2)}, u32[]{:S(2)}) collective-permute-start(bf16[96,640]{1,0:T(8,128)(2,1)} %get-tuple-element.249), channel_id=1, source_target_pairs={{0,20},{4,16},{8,28},{12,24},{16,4},{20,0},{24,12},{28,8},{1,21},{... | collective-permute-start | bytes 368648 | tf_op jit(solution)/shard_map/ppermute | solution.py:966
  210.6 15.3 %collective-permute-start.27 = (bf16[96,640]{1,0:T(8,128)(2,1)}, bf16[96,640]{1,0:T(8,128)(2,1)}, u32[]{:S(2)}, u32[]{:S(2)}) collective-permute-start(bf16[96,640]{1,0:T(8,128)(2,1)} %get-tuple-element.250), channel_id=1, source_target_pairs={{0,24},{4,28},{8,16},{12,20},{16,8},{20,12},{24,0},{28,4},{1,25},{... | collective-permute-start | bytes 368648 | tf_op jit(solution)/shard_map/ppermute | solution.py:966
  215.9 10.1 %collective-permute-start.28 = (bf16[96,640]{1,0:T(8,128)(2,1)}, bf16[96,640]{1,0:T(8,128)(2,1)}, u32[]{:S(2)}, u32[]{:S(2)}) collective-permute-start(bf16[96,640]{1,0:T(8,128)(2,1)} %get-tuple-element.251), channel_id=1, source_target_pairs={{0,28},{4,24},{8,20},{12,16},{16,12},{20,8},{24,4},{28,0},{1,29},{... | collective-permute-start | bytes 368648 | tf_op jit(solution)/shard_map/ppermute | solution.py:966
  227.2 5.2 %collective-permute-start.30 = (f32[96,256]{1,0:T(8,128)S(1)}, f32[96,256]{1,0:T(8,128)S(1)}, u32[]{:S(2)}, u32[]{:S(2)}) collective-permute-start(f32[96,256]{1,0:T(8,128)S(1)} %slice.105), channel_id=1, source_target_pairs={{0,2},{1,3},{2,0},{3,1},{4,6},{5,7},{6,4},{7,5},{8,10},{9,11},{10,... | collective-permute-start | bytes 294920 | tf_op jit(solution)/shard_map/ppermute | solution.py:973
  228.4 5.0 %collective-permute-start.31 = (f32[96,256]{1,0:T(8,128)S(1)}, f32[96,256]{1,0:T(8,128)S(1)}, u32[]{:S(2)}, u32[]{:S(2)}) collective-permute-start(f32[96,256]{1,0:T(8,128)S(1)} %slice.105), channel_id=1, source_target_pairs={{0,3},{1,2},{2,1},{3,0},{4,7},{5,6},{6,5},{7,4},{8,11},{9,10},{10,... | collective-permute-start | bytes 294920 | tf_op jit(solution)/shard_map/ppermute | solution.py:973
  228.4 5.0 %collective-permute-start.29 = (f32[96,256]{1,0:T(8,128)S(1)}, f32[96,256]{1,0:T(8,128)S(1)}, u32[]{:S(2)}, u32[]{:S(2)}) collective-permute-start(f32[96,256]{1,0:T(8,128)S(1)} %slice.105), channel_id=1, source_target_pairs={{0,1},{1,0},{2,3},{3,2},{4,5},{5,4},{6,7},{7,6},{8,9},{9,8},{10,11... | collective-permute-start | bytes 294920 | tf_op jit(solution)/shard_map/ppermute | solution.py:973
  233.6 12.0 %copy-start.7 = (bf16[256,768]{1,0:T(8,128)(2,1)S(1)}, bf16[256,768]{1,0:T(8,128)(2,1)}, u32[]{:S(2)}) copy-start(bf16[256,768]{1,0:T(8,128)(2,1)} %get-tuple-element.261) | copy-start | bytes 1179652
  235.3 33.4 %collective-permute-start.39 = (bf16[1,512,768]{2,1,0:T(8,128)(2,1)}, bf16[1,512,768]{2,1,0:T(8,128)(2,1)S(1)}, u32[]{:S(2)}, u32[]{:S(2)}) collective-permute-start(bf16[1,512,768]{2,1,0:T(8,128)(2,1)} %get-tuple-element.276), channel_id=1, source_target_pairs={{0,2},{1,3},{2,0},{3,1},{4,6},{5,7},{6,4},{7,5},{8,10},{9,11},{10,... | collective-permute-start | bytes 2359304 | tf_op jit(solution)/shard_map/ppermute | solution.py:966
  236.9 24.4 %copy-start.11 = (bf16[96,640]{1,0:T(8,128)(2,1)}, bf16[96,640]{1,0:T(8,128)(2,1)S(1)}, u32[]{:S(2)}) copy-start(bf16[96,640]{1,0:T(8,128)(2,1)S(1)} %pad_maximum_fusion.1.refs_0_) | copy-start | bytes 368644
  236.9 10.0 %copy-start.6 = (bf16[384,768]{1,0:T(8,128)(2,1)S(1)}, bf16[384,768]{1,0:T(8,128)(2,1)}, u32[]{:S(2)}) copy-start(bf16[384,768]{1,0:T(8,128)(2,1)} %get-tuple-element.265) | copy-start | bytes 1769476
  236.9 11.1 %copy-start.5 = (bf16[768,384]{1,0:T(8,128)(2,1)S(1)}, bf16[768,384]{1,0:T(8,128)(2,1)}, u32[]{:S(2)}) copy-start(bf16[768,384]{1,0:T(8,128)(2,1)} %get-tuple-element.266) | copy-start | bytes 1769476
  236.9 13.3 %collective-permute-start.38 = (bf16[96,640]{1,0:T(8,128)(2,1)S(1)}, bf16[96,640]{1,0:T(8,128)(2,1)}, u32[]{:S(2)}, u32[]{:S(2)}) collective-permute-start(bf16[96,640]{1,0:T(8,128)(2,1)S(1)} %pad_maximum_fusion.1.refs_0_), channel_id=1, source_target_pairs={{0,28},{4,24},{8,20},{12,16},{16,12},{20,8},{24,4},{28,0},{1,29},{... | collective-permute-start | bytes 368648 | tf_op jit(solution)/shard_map/ppermute | solution.py:966
  239.3 18.0 %collective-permute-start.37 = (bf16[96,640]{1,0:T(8,128)(2,1)S(1)}, bf16[96,640]{1,0:T(8,128)(2,1)}, u32[]{:S(2)}, u32[]{:S(2)}) collective-permute-start(bf16[96,640]{1,0:T(8,128)(2,1)S(1)} %pad_maximum_fusion.1.refs_0_), channel_id=1, source_target_pairs={{0,24},{4,28},{8,16},{12,20},{16,8},{20,12},{24,0},{28,4},{1,25},{... | collective-permute-start | bytes 368648 | tf_op jit(solution)/shard_map/ppermute | solution.py:966
  241.7 19.6 %collective-permute-start.36 = (bf16[96,640]{1,0:T(8,128)(2,1)S(1)}, bf16[96,640]{1,0:T(8,128)(2,1)}, u32[]{:S(2)}, u32[]{:S(2)}) collective-permute-start(bf16[96,640]{1,0:T(8,128)(2,1)S(1)} %pad_maximum_fusion.1.refs_0_), channel_id=1, source_target_pairs={{0,20},{4,16},{8,28},{12,24},{16,4},{20,0},{24,12},{28,8},{1,21},{... | collective-permute-start | bytes 368648 | tf_op jit(solution)/shard_map/ppermute | solution.py:966
  245.5 18.2 %collective-permute-start.35 = (bf16[96,640]{1,0:T(8,128)(2,1)S(1)}, bf16[96,640]{1,0:T(8,128)(2,1)}, u32[]{:S(2)}, u32[]{:S(2)}) collective-permute-start(bf16[96,640]{1,0:T(8,128)(2,1)S(1)} %pad_maximum_fusion.1.refs_0_), channel_id=1, source_target_pairs={{0,16},{4,20},{8,24},{12,28},{16,0},{20,4},{24,8},{28,12},{1,17},{... | collective-permute-start | bytes 368648 | tf_op jit(solution)/shard_map/ppermute | solution.py:966
  248.1 14.6 %copy-start.3 = (bf16[512,768]{1,0:T(8,128)(2,1)S(1)}, bf16[512,768]{1,0:T(8,128)(2,1)}, u32[]{:S(2)}) copy-start(bf16[512,768]{1,0:T(8,128)(2,1)} %refs_10_.1) | copy-start | bytes 2359300
  250.2 16.2 %collective-permute-start.34 = (bf16[96,640]{1,0:T(8,128)(2,1)S(1)}, bf16[96,640]{1,0:T(8,128)(2,1)S(1)}, u32[]{:S(2)}, u32[]{:S(2)}) collective-permute-start(bf16[96,640]{1,0:T(8,128)(2,1)S(1)} %pad_maximum_fusion.1.refs_0_), channel_id=1, source_target_pairs={{0,12},{4,8},{8,4},{12,0},{16,28},{20,24},{24,20},{28,16},{1,13},{... | collective-permute-start | bytes 368648 | tf_op jit(solution)/shard_map/ppermute | solution.py:966
  257.3 10.6 %collective-permute-start.33 = (bf16[96,640]{1,0:T(8,128)(2,1)S(1)}, bf16[96,640]{1,0:T(8,128)(2,1)S(1)}, u32[]{:S(2)}, u32[]{:S(2)}) collective-permute-start(bf16[96,640]{1,0:T(8,128)(2,1)S(1)} %pad_maximum_fusion.1.refs_0_), channel_id=1, source_target_pairs={{0,8},{4,12},{8,0},{12,4},{16,24},{20,28},{24,16},{28,20},{1,9},{5... | collective-permute-start | bytes 368648 | tf_op jit(solution)/shard_map/ppermute | solution.py:966
  261.3 7.4 %collective-permute-start.32 = (bf16[96,640]{1,0:T(8,128)(2,1)S(1)}, bf16[96,640]{1,0:T(8,128)(2,1)S(1)}, u32[]{:S(2)}, u32[]{:S(2)}) collective-permute-start(bf16[96,640]{1,0:T(8,128)(2,1)S(1)} %pad_maximum_fusion.1.refs_0_), channel_id=1, source_target_pairs={{0,4},{4,0},{8,12},{12,8},{16,20},{20,16},{24,28},{28,24},{1,5},{5... | collective-permute-start | bytes 368648 | tf_op jit(solution)/shard_map/ppermute | solution.py:966
  266.4 2.3 copy-start.24
  268.7 0.9 copy-start.21
  (13 other events, 9.1 us)
Sparse Core Ops, SparseCore 0:
  37.2 27.9 all-gather.1
  113.7 82.0 all-reduce.8
  198.4 27.3 reduce-scatter.1

commit v5 on v4

--- a/solution.py
+++ b/solution.py
@@ -48,11 +48,6 @@
 def split(v, axis):
     high = v.astype(BF16)
     return jnp.concatenate([high, (v - high.astype(F32)).astype(BF16)], axis=axis)
-
-
-def two_part(v, ex):
-    high = v.astype(BF16)
-    return mm(high, ex) + mm((v - high.astype(F32)).astype(BF16), ex)
 
 
 def sigmoid(v):
@@ -149,7 +144,8 @@
     halo_ref,
     gain_ref,
     wg_ref,
-    wsv_ref,
+    ws_ref,
+    wv_ref,
     wst_ref,
     wstr_ref,
     pcol_ref,
@@ -182,7 +178,7 @@
     *rest,
 ):
     messages = rest[: 2 * hops]
-    ubuf, state, incb, marks, ends, docs = rest[2 * hops :]
+    ubuf, state, incb, marks, ends, docs, wbuf, wides, bts = rest[2 * hops :]
     i = pl.program_id(0)
     tb = normed_ref.shape[0]
     per = tb // SPAN
@@ -199,9 +195,9 @@
     def _():
         edge = norm(halo_ref[...])
         normh_ref[...] = edge
-        before = mm(edge, wsv_ref[...])
-        ubuf[0:8, :] = before
-        uvh_ref[...] = before
+        ubuf[0:8, :LANES] = mm(edge, ws_ref[...])
+        ubuf[0:8, LANES:] = mm(edge, wv_ref[...])
+        uvh_ref[...] = ubuf[0:8, :]
         state[...] = jnp.zeros_like(state)
         place = at_ref[2] - 8 + iota((8, 1), 0)
         here = documents(off_ref, place)
@@ -224,10 +220,14 @@
     nb = normed_ref[...]
     for tile in wide_tiles(width):
         gate_ref[:, tile] = mm(nb, wg_ref[:, tile]).astype(BF16)
-    for tile in wide_tiles(LANES + width):
-        uv = mm(nb, wsv_ref[:, tile])
-        ubuf[8 : 8 + tb, tile] = uv
-        uv_ref[:, tile] = uv.astype(BF16)
+    uv = mm(nb, ws_ref[...])
+    ubuf[8 : 8 + tb, :LANES] = uv
+    uv_ref[:, :LANES] = uv.astype(BF16)
+    for tile in wide_tiles(width):
+        uv = mm(nb, wv_ref[:, tile])
+        at = slice(LANES + tile.start, LANES + tile.stop)
+        ubuf[8 : 8 + tb, at] = uv
+        uv_ref[:, at] = uv.astype(BF16)
     zr_all = mm_nt(wstr_ref[...], nb)
     lane = iota((SPAN, LANES), 1)
     forward = lane < nh
@@ -280,32 +280,41 @@
         pack_ref[rows, :] = pack
         tot8 = jnp.broadcast_to(tot, (8, LANES))
         tot_ref[j * 8 : j * 8 + 8, :] = tot8
-        dtr = softplus(zr_all[:, rows] + prow_ref[:, :SPAN])
-        ar = -dtr * prow_ref[:, SPAN:]
+        dtr = softplus(zr_all[:, rows] + prow_ref[:, 0:1])
+        ar = -dtr * prow_ref[:, 1:2]
         run = mm(jnp.concatenate(pieces(ar), axis=1), triu_ref[...])
         rowa = jnp.where(forward_row, run, run - ar)
         ldt = jnp.log(jnp.maximum(dtr, TINY))
         rowa_ref[:, rows] = rowa
         rowp_ref[:, rows] = jnp.where(forward_row, rowa - ldt, rowa + ldt)
-        gates = split(jnp.exp(tot8) * ends[j * 8 : j * 8 + 8, :], 1)
-        w = split(source_weights(pack, tot, dt, lane, nh), 1)
-        bt = jnp.transpose(act_ref[rows, :LANES].astype(F32))[:HDIM].astype(BF16)
-        c = i * per + j
-        for n, at, _ in groups(width):
-            tile = slice(at, at + LANES)
-            both = slice(2 * at, 2 * at + 2 * LANES)
+        gate8 = jnp.exp(tot8) * ends[j * 8 : j * 8 + 8, :]
+        bts[j * HDIM : (j + 1) * HDIM, :] = jnp.transpose(act_ref[rows, :LANES].astype(F32))[
+            :HDIM
+        ].astype(BF16)
+        wbuf[rows, :] = split(source_weights(pack, tot, dt, lane, nh), 1)
+        wbuf[tb + 16 * j : tb + 16 * j + 16, :] = split(jnp.concatenate([gate8, gate8], axis=0), 1)
+    for n, at, _ in groups(width):
+        tile = slice(at, at + LANES)
+        both = slice(2 * at, 2 * at + 2 * LANES)
+        wides[...] = mm(wbuf[...], ex_ref[:, both])
+        for j in range(per):
+            rows = slice(j * SPAN, (j + 1) * SPAN)
+            c = i * per + j
             x = act_ref[rows, LANES + at : 2 * LANES + at].astype(F32)
-            wide = mm(w, ex_ref[:, both])
             fed = jnp.concatenate(
-                [(x * wide[:, :LANES]).astype(BF16), (x * wide[:, LANES:]).astype(BF16)], axis=1
+                [
+                    (x * wides[rows, :LANES]).astype(BF16),
+                    (x * wides[rows, LANES:]).astype(BF16),
+                ],
+                axis=1,
             )
+            bt = bts[j * HDIM : (j + 1) * HDIM, :]
             inc = mm(bt, fed)
-            gate = mm(gates, ex_ref[:, both])
+            gate = wides[tb + 16 * j : tb + 16 * j + 8, :]
             gates_ref[c, :, both] = gate
             sf_ref[j, :, tile] = state[:, tile]
             state[:, tile] = state[:, tile] * gate[0:1, :LANES] + inc[:, :LANES]
             incb[c, :, tile] = inc[:, LANES:]
-
     @pl.when(i == pl.num_programs(0) - 1)
     def _():
         last_state = state[...]
@@ -538,7 +547,7 @@
     *rest,
 ):
     pieces_out = rest[:shares]
-    dso_ref, dro_ref, *messages, state, incf = rest[shares:]
+    dso_ref, dro_ref, *messages, state, incf, wbuf, wides, cts = rest[shares:]
     i = pl.program_id(0)
     tb, width = dy_ref.shape
     model = wo_ref.shape[1]
@@ -553,19 +562,28 @@
     for j in range(per):
         rows = slice(j * SPAN, (j + 1) * SPAN)
         pack = pack_ref[rows, :]
-        w = split(target_weights(pack, tot_ref[j * 8 : j * 8 + 1, :], lane, nh), 1)
-        ct = jnp.transpose(act_ref[rows, :].astype(F32))[HDIM:].astype(BF16)
-        c = i * per + j
-        for n, at, _ in groups(width):
-            tile = slice(at, at + LANES)
-            both = slice(2 * at, 2 * at + 2 * LANES)
-            second = slice(2 * at + LANES, 2 * at + 2 * LANES)
+        tot = tot_ref[j * 8 : j * 8 + 1, :]
+        wbuf[rows, :] = split(target_weights(pack, tot, lane, nh), 1)
+        cts[j * HDIM : (j + 1) * HDIM, :] = jnp.transpose(act_ref[rows, :].astype(F32))[
+            HDIM:
+        ].astype(BF16)
+    for n, at, _ in groups(width):
+        tile = slice(at, at + LANES)
+        both = slice(2 * at, 2 * at + 2 * LANES)
+        second = slice(2 * at + LANES, 2 * at + 2 * LANES)
+        wides[...] = mm(wbuf[...], ex_ref[:, both])
+        for j in range(per):
+            rows = slice(j * SPAN, (j + 1) * SPAN)
+            c = i * per + j
             dy = dy_ref[rows, tile].astype(F32)
-            wide = mm(w, ex_ref[:, both])
             fed = jnp.concatenate(
-                [(dy * wide[:, :LANES]).astype(BF16), (dy * wide[:, LANES:]).astype(BF16)], axis=1
+                [
+                    (dy * wides[rows, :LANES]).astype(BF16),
+                    (dy * wides[rows, LANES:]).astype(BF16),
+                ],
+                axis=1,
             )
-            inc = mm(ct, fed)
+            inc = mm(cts[j * HDIM : (j + 1) * HDIM, :], fed)
             incf[c, :, tile] = inc[:, :LANES]
             dro_ref[j, :, tile] = state[:, tile]
             state[:, tile] = state[:, tile] * gates_ref[c, 0:1, second] + inc[:, LANES:]
@@ -612,13 +630,24 @@
     dx_ref,
     dbc_ref,
     pulls_ref,
+    qbuf,
+    places,
 ):
     tb, width = dx_ref.shape
+
+    @pl.when(pl.program_id(0) == 0)
+    def _():
+        qbuf[...] = jnp.zeros_like(qbuf)
+        spot_row = iota((4 * SPAN, LANES), 0) < 2 * SPAN
+        spot_lane = iota((4 * SPAN, LANES), 1)
+        for h in range(nh):
+            up = jnp.where(spot_lane == nh + h, jnp.where(spot_row, -1.0, 1.0), 0.0)
+            places[h] = jnp.where(spot_row & (spot_lane == h), 1.0, up).astype(BF16)
+
     s_at = iota((SPAN, SPAN), 0)
     t_at = iota((SPAN, SPAN), 1)
     lower = t_at > s_at
     lane = iota((SPAN, LANES), 1)
-    row16 = iota((16, SPAN), 0)
     front_half = lane < HDIM
     for j in range(tb // SPAN):
         rows = slice(j * SPAN, (j + 1) * SPAN)
@@ -632,7 +661,6 @@
         pc = jnp.where(lane < nh, pack - ldt, pack + ldt)
         dscore = jnp.zeros((SPAN, SPAN), F32)
         kc = jnp.zeros((SPAN, LANES), F32)
-        qr = jnp.zeros((16, SPAN), F32)
         for n, at, heads in groups(width):
             tile = slice(at, at + LANES)
             dyp = dy_ref[rows, tile]
@@ -651,17 +679,17 @@
                 mats.append((score * decay).astype(BF16))
                 pull = spot * score
                 pull_low = jnp.where(lower, pull, 0.0)
-                pull_up = pull - pull_low
-                qr = jnp.where(row16 == h, jnp.sum(pull_low, axis=0, keepdims=True), qr)
-                qr = jnp.where(row16 == nh + h, jnp.sum(pull_up, axis=0, keepdims=True), qr)
-                kc = jnp.where(lane == h, jnp.sum(pull_low, axis=1, keepdims=True), kc)
-                kc = jnp.where(lane == nh + h, jnp.sum(pull_up, axis=1, keepdims=True), kc)
+                down = jnp.sum(pull_low, axis=0, keepdims=True)
+                qbuf[h : h + 1, :] = down
+                qbuf[nh + h : nh + h + 1, :] = jnp.sum(pull, axis=0, keepdims=True) - down
+                both = jnp.concatenate([split(pull_low, 1), split(pull, 1)], axis=1)
+                kc = kc + mm(both, places[h])
             dx_ref[rows, tile] = mm(jnp.concatenate(mats, axis=1), stacked(dyp)).astype(BF16)
         dscore = jnp.where(within, dscore, 0.0).astype(BF16)
         cpad = jnp.where(front_half, cb, 0.0).astype(BF16)
         bpad = jnp.where(front_half, 0.0, cb).astype(BF16)
         dbc_ref[rows, :] = mm(dscore, cpad) + mm_tn(dscore, bpad)
-        pulls_ref[rows, :] = kc + exact_tn(qr, eye_ref[...])
+        pulls_ref[rows, :] = kc + exact_tn(qbuf[...], eye_ref[...])
 
 
 def back_kernel(
@@ -705,7 +733,8 @@
 ):
     arrived = rest[: 2 * hops]
     mine_ref, theirs_ref, *chunks = rest[2 * hops : 2 * hops + 2 + peers]
-    dbuf, hbuf, dcat, acc, lines, dsent_ref, drent_ref, parts = rest[2 * hops + 2 + peers :]
+    scratch = rest[2 * hops + 2 + peers :]
+    dbuf, hbuf, dcat, acc, lines, dsent_ref, drent_ref, parts, wbuf, wides, pbuf, sums = scratch
     i = pl.program_id(0)
     last = pl.num_programs(0) - 1
     tb = act_ref.shape[0]
@@ -723,33 +752,32 @@
     forward = lane < nh
     head_lane = lane < 16
     none = jnp.zeros((HDIM, 2 * LANES), BF16)
-    for j in reversed(range(tb // SPAN)):
+    per = tb // SPAN
+    pair = 2 * LANES
+
+    def part_of(kind, j):
+        return slice((kind * per + j) * SPAN, (kind * per + j + 1) * SPAN)
+
+    for j in range(per):
         rows = slice(j * SPAN, (j + 1) * SPAN)
         pack = pack_ref[rows, :]
         tot = tot_ref[j * 8 : j * 8 + 1, :]
-        z = pltpu.roll(pack, LANES - 16, 1)
-        dt = softplus(z)
-        w = jnp.concatenate(
-            [
-                split(source_weights(pack, tot, dt, lane, nh), 1),
-                split(target_weights(pack, tot, lane, nh), 1),
-            ],
-            axis=0,
-        )
-        bc = act_ref[rows, :LANES].astype(F32)
-        b = bc[:, :HDIM].astype(BF16)
-        c = pltpu.roll(bc, HDIM, 1)[:, :HDIM].astype(BF16)
-        dbc = dbc_ref[rows, :]
-        carried = jnp.zeros((SPAN, LANES), F32)
-        leaving = jnp.zeros((SPAN, LANES), F32)
-        through = jnp.zeros((8, LANES), F32)
-        for n, at, _ in groups(width):
-            tile = slice(at, at + LANES)
-            wtile = slice(LANES + at, 2 * LANES + at)
-            both = slice(2 * at, 2 * at + 2 * LANES)
-            first = slice(2 * at, 2 * at + LANES)
-            second = slice(2 * at + LANES, 2 * at + 2 * LANES)
-            wide = mm(w, ex_ref[:, both])
+        dt = softplus(pltpu.roll(pack, LANES - 16, 1))
+        wbuf[part_of(0, j), :] = split(source_weights(pack, tot, dt, lane, nh), 1)
+        wbuf[part_of(1, j), :] = split(target_weights(pack, tot, lane, nh), 1)
+        dbuf[rows, :LANES] = dbc_ref[rows, :]
+    for n, at, _ in groups(width):
+        tile = slice(at, at + LANES)
+        wtile = slice(LANES + at, 2 * LANES + at)
+        both = slice(2 * at, 2 * at + 2 * LANES)
+        first = slice(2 * at, 2 * at + LANES)
+        second = slice(2 * at + LANES, 2 * at + 2 * LANES)
+        wides[...] = mm(wbuf[...], ex_ref[:, both])
+        for j in range(per):
+            rows = slice(j * SPAN, (j + 1) * SPAN)
+            bc = act_ref[rows, :LANES].astype(F32)
+            b = bc[:, :HDIM].astype(BF16)
+            c = pltpu.roll(bc, HDIM, 1)[:, :HDIM].astype(BF16)
             x = act_ref[rows, wtile].astype(F32)
             dy = dy_ref[rows, tile].astype(F32)
             x2 = jnp.concatenate([x, x], axis=1)
@@ -763,21 +791,37 @@
                 axis=1,
             )
             dheld_low = dheld.astype(BF16)
-            to_wide = wide[:SPAN]
-            fro_wide = wide[SPAN:]
+            to_wide = wides[part_of(0, j), :]
+            fro_wide = wides[part_of(1, j), :]
             flow = mm(b, dheld_low) * to_wide
             seen = mm(c, held) * fro_wide
-            dbc = dbc + mm_nt((x2 * to_wide).astype(BF16), jnp.concatenate([dheld_low, none], axis=0))
+            dbc = mm_nt((x2 * to_wide).astype(BF16), jnp.concatenate([dheld_low, none], axis=0))
             dbc = dbc + mm_nt((dy2 * fro_wide).astype(BF16), jnp.concatenate([none, held], axis=0))
-            ext = ext_ref[both, :]
-            carried = carried + two_part(dy2 * seen, ext)
-            leaving = leaving + two_part(x2 * flow, ext)
+            dbuf[rows, :LANES] += dbc
+            pbuf[part_of(0, j), :] = split(dy2 * seen, 1)
+            pbuf[part_of(1, j), :] = split(x2 * flow, 1)
             product = jnp.sum(dheld * held.astype(F32), axis=0, keepdims=True) * gates_ref[j, :, both]
-            through = through + mm(product.astype(BF16), ext)
+            pbuf[2 * tb + 16 * j : 2 * tb + 16 * j + 16, :] = split(
+                jnp.concatenate([product, product], axis=0), 1
+            )
             dx = dxin_ref[rows, tile].astype(F32) + flow[:, :LANES] + flow[:, LANES:]
             dx = dx + skip_ref[0:1, tile] * dy
             dbuf[rows, wtile] = dx * slope_ref[rows, wtile].astype(F32)
-        dbuf[rows, :LANES] = dbc * slope_ref[rows, :LANES].astype(F32)
+        ext = ext_ref[both, :]
+        found = mm(pbuf[:, :pair], ext) + mm(pbuf[:, pair:], ext)
+        if n == 0:
+            sums[...] = found
+        else:
+            sums[...] += found
+    for j in range(per):
+        rows = slice(j * SPAN, (j + 1) * SPAN)
+        pack = pack_ref[rows, :]
+        z = pltpu.roll(pack, LANES - 16, 1)
+        dt = softplus(z)
+        carried = sums[part_of(0, j), :]
+        leaving = sums[part_of(1, j), :]
+        through = sums[2 * tb + 16 * j : 2 * tb + 16 * j + 8, :]
+        dbuf[rows, :LANES] = dbuf[rows, :LANES] * slope_ref[rows, :LANES].astype(F32)
         pulls = pulls_ref[rows, :]
         kc = jnp.where(head_lane, pulls, 0.0)
         moved = jnp.where(head_lane, pltpu.roll(pulls, LANES - 16, 1), 0.0) + carried - kc
@@ -792,6 +836,9 @@
         lines[7:8, :LANES] += jnp.sum(dstep, axis=0, keepdims=True)
         ends = jnp.where(head_lane, -dlog * dt * rate, 0.0)
         lines[8:9, :LANES] += jnp.sum(ends, axis=0, keepdims=True)
+    for j in range(per):
+        rows = slice(j * SPAN, (j + 1) * SPAN)
+        pack = pack_ref[rows, :]
         for at in range(0, LANES + width, LANES):
             tile = slice(at, at + LANES)
             dconv = dbuf[rows, tile]
@@ -807,7 +854,8 @@
     edge = dbuf[0:8, :]
     dbuf[tb : tb + 8, :] = edge
     for tile in wide_tiles(model):
-        part = mm_nt(dgate_ref[...], wg_ref[tile, :]) + mm_nt(dcat[...], wcat_ref[tile, :])
+        part = mm_nt(dgate_ref[...], wg_ref[tile, :])
+        part = part + mm_nt(dcat[...], wcat_ref[tile, :])
         parts[:, tile] = part.astype(BF16)
         normed = normed_ref[:, tile]
         lines[0:1, tile] += jnp.sum(part * normed.astype(F32), axis=0, keepdims=True)
@@ -1058,39 +1106,29 @@
     size = model // peers
 
     rate = padded(jnp.exp(decay_log), 0, nh)
-    bias_line = jnp.concatenate([step_bias[0], step_bias[1]])
-    rate_line = jnp.concatenate([rate, rate])
-    pcol = jnp.zeros((8, LANES), F32)
-    pcol = pcol.at[0, : 2 * nh].set(bias_line).at[1, : 2 * nh].set(rate_line)
-    pcol = pcol.at[0, 16 : 16 + 2 * nh].set(bias_line)
-    pad16 = jnp.zeros((16 - 2 * nh,), F32)
-    prow = jnp.concatenate(
-        [
-            jnp.broadcast_to(jnp.concatenate([bias_line, pad16])[:, None], (16, SPAN)),
-            jnp.broadcast_to(jnp.concatenate([rate_line, pad16])[:, None], (16, SPAN)),
-        ],
-        axis=1,
-    )
+    gap = 16 - 2 * nh
+    bias16 = jnp.pad(step_bias.reshape(-1), (0, gap))
+    rate16 = jnp.pad(jnp.concatenate([rate, rate]), (0, gap))
+    prow = jnp.stack([bias16, rate16], axis=1)
+    wide_bias = jnp.pad(jnp.concatenate([bias16, bias16]), (0, LANES - 32))
+    pcol = jnp.stack([wide_bias, jnp.pad(rate16, (0, LANES - 16))], axis=0)
     steps = jnp.concatenate([proj_step[0], proj_step[1]], axis=1)
-    wst = jnp.pad(steps, ((0, 0), (0, 16 - 2 * nh)))
-    wst = jnp.pad(jnp.tile(wst, (1, 2)), ((0, 0), (0, LANES - 32)))
-    wback = jnp.pad(steps, ((0, 0), (0, LANES - 2 * nh)))
-    wstr = jnp.pad(steps.T, ((0, 16 - 2 * nh), (0, 0)))
-    wsv = jnp.concatenate([proj_state, proj_value], axis=1)
-    taps = jnp.pad(jnp.concatenate([conv_state, conv_value], axis=1), ((0, 4), (0, 0)))
-    gain = jnp.broadcast_to(input_gain[None, :], (8, model))
-    mg = jnp.broadcast_to(mixer_gain[None, :], (8, width))
-    skip = jnp.broadcast_to(jnp.repeat(skip_gain, HDIM)[None, :], (8, width))
-
-    wcat = jnp.concatenate([wback, wsv], axis=1)
+    steps = jnp.pad(steps, ((0, 0), (0, gap)))
+    wst = jnp.pad(jnp.concatenate([steps, steps], axis=1), ((0, 0), (0, LANES - 32)))
+    wstr = steps.T
+    taps = jnp.concatenate([conv_state, conv_value], axis=1)
+    gain = input_gain[None, :]
+    mg = mixer_gain[None, :]
+    skip = jnp.repeat(skip_gain, HDIM)[None, :]
     pieces_of = {0: tokens}
     for bit in [1 << b for b in range(bits - 1, 0, -1)]:
         pieces_of.update({k | bit: swap(v, "head", bit) for k, v in pieces_of.items()})
-    prelims = (halo, offsets, live_row, pcol, prow, wst, wstr, wsv, taps, gain, mg, skip, wcat)
+    wcat = jnp.concatenate([wst, proj_state, proj_value], axis=1)
+    prelims = (halo, offsets, live_row, pcol, prow, wst, wstr, taps, wcat)
     pieces_of, late, prelims, scalars = lax.optimization_barrier(
         (pieces_of, cotangent, prelims, scalars)
     )
-    halo, offsets, live_row, pcol, prow, wst, wstr, wsv, taps, gain, mg, skip, wcat = prelims
+    halo, offsets, live_row, pcol, prow, wst, wstr, taps, wcat = prelims
     pieces_of.update({k | 1: swap(v, "head", 1) for k, v in pieces_of.items()})
     token_pieces = [pieces_of[k] for k in range(head_devices)]
     cot_all = lax.all_gather(late, "head", axis=0, tiled=True)
@@ -1165,14 +1203,15 @@
         [piece_block(k) for k in range(head_devices)]
         + [
             whole((8, model)),
-            whole((8, model)),
+            whole((1, model)),
             whole((model, width)),
-            whole((model, wide)),
+            whole((model, LANES)),
+            whole((model, width)),
             whole((model, LANES)),
             whole((16, model)),
-            whole((8, LANES)),
-            whole((16, 2 * SPAN)),
-            whole((8, wide)),
+            whole((2, LANES)),
+            whole((16, 2)),
+            whole((4, wide)),
             whole(offsets.shape),
             lane_block(1, tb),
             whole(ex.shape),
@@ -1208,6 +1247,9 @@
             pltpu.VMEM((tb, LANES), F32),
             pltpu.VMEM((per * 8, LANES), F32),
             pltpu.VMEM((SPAN + 16, LANES), F32),
+            pltpu.VMEM((tb + 16 * per, 2 * LANES), BF16),
+            pltpu.VMEM((tb + 16 * per, 2 * LANES), F32),
+            pltpu.VMEM((per * HDIM, LANES), BF16),
         ],
         25e9,
         token_pieces
@@ -1215,7 +1257,8 @@
             halo,
             gain,
             proj_gate,
-            wsv,
+            proj_state,
+            proj_value,
             wst,
             wstr,
             pcol,
@@ -1242,7 +1285,7 @@
             big_rows(LANES),
             big_lanes(8),
             big_lanes(16),
-            whole((8, width)),
+            whole((1, width)),
             big_rows(model),
             whole((width, model)),
         ],
@@ -1270,7 +1313,7 @@
             big_rows(width),
             big_rows(width),
             big_rows(width),
-            whole((8, width)),
+            whole((1, width)),
             whole(ex.shape),
         ]
         + [whole(message.shape)] * (2 * hops),
@@ -1297,7 +1340,7 @@
             rows(width),
             rows(width),
             rows(width),
-            whole((8, width)),
+            whole((1, width)),
             rows(wide),
             whole((16, LANES)),
             rows(model),
@@ -1340,7 +1383,13 @@
             (state_block, states),
         ]
         + messages,
-        [pltpu.VMEM((HDIM, width), F32), pltpu.VMEM((nc, HDIM, width), F32)],
+        [
+            pltpu.VMEM((HDIM, width), F32),
+            pltpu.VMEM((nc, HDIM, width), F32),
+            pltpu.VMEM((tb, 2 * LANES), BF16),
+            pltpu.VMEM((tb, 2 * LANES), F32),
+            pltpu.VMEM((per * HDIM, LANES), BF16),
+        ],
         1e8,
         [acted, pack, tot, gates, gtot, ex, dy, outin, proj_out],
         scalars,
@@ -1371,7 +1420,7 @@
             (mid_rows(LANES), sds((length, LANES), F32)),
             (mid_rows(LANES), sds((length, LANES), F32)),
         ],
-        [],
+        [pltpu.VMEM((16, SPAN), F32), pltpu.VMEM((nh, 4 * SPAN, LANES), BF16)],
         1e8,
         [acted, pack, seg_row, rowa, dy, eye16],
     )
@@ -1403,9 +1452,9 @@
             rev(rows(wide)),
             whole((8, wide)),
             whole((8, LANES)),
-            whole((8, wide)),
-            whole((8, width)),
-            whole((8, LANES)),
+            whole((4, wide)),
+            whole((1, width)),
+            whole((2, LANES)),
             whole(ex.shape),
             whole(ext.shape),
             whole(tril.shape),
@@ -1433,6 +1482,10 @@
             pltpu.VMEM((HDIM, width), F32),
             pltpu.VMEM((HDIM, width), F32),
             pltpu.VMEM((tb, model), BF16),
+            pltpu.VMEM((2 * tb, 2 * LANES), BF16),
+            pltpu.VMEM((2 * tb, 2 * LANES), F32),
+            pltpu.VMEM((2 * tb + 16 * per, 4 * LANES), BF16),
+            pltpu.VMEM((2 * tb + 16 * per, LANES), F32),
         ],
         1e8,
         [

time: 282 us -> 263 us (0.933)
  Pallas kernels: 134 us -> 121 us
  waiting for transfers between devices: 30 us -> 35 us
  local copies, waits for them, and re-layouts: 15.3 us -> 10.9 us
  other arithmetic: 20.2 us -> 16.5 us
  starting transfers between devices: 68.1 us -> 65 us
    pallas_call x8, Pallas kernels: 134 us -> 121 us  [call(): pl.pallas_call(kernel, name=name, grid_spec=pltpu.PrefetchScalarGridSpec(...]
    ppermute x25, starting transfers between devices: 46.4 us -> 43.3 us  [swap(): return lax.ppermute(array, axis, [(i, i ^ k) for i in range(n)])]
  transfers between devices with their start and end apart: 43 -> 43, of which waited for: 13 -> 13; matrix products, arithmetic and copies ran while one was open for 10% -> 9% of each run, Pallas kernels for 37% -> 35%
where the time goes in v5:
time: 263 us; the launch traced here: 262 us
  Pallas kernels  121 us (46%)
  starting transfers between devices  65 us (25%)
  waiting for transfers between devices  35 us (13%)
  other arithmetic  16.5 us (6%)
  between operations  14.2 us (5%)
  local copies, waits for them, and re-layouts  10.9 us (4%)
    pallas_call x8, Pallas kernels, call(): pl.pallas_call(kernel, name=name, grid_spec=pltpu.PrefetchScalarGridSpec(...  121 us
    ppermute x25, starting transfers between devices, swap(): return lax.ppermute(array, axis, [(i, i ^ k) for i in range(n)])  43.3 us
    ppermute x25, waiting for transfers between devices, swap(): return lax.ppermute(array, axis, [(i, i ^ k) for i in range(n)])  21.3 us
    ppermute x8, starting transfers between devices, exchange_sides(): arrived.append(lax.ppermute(messages[len(arrived)], 'seq', both))  13.8 us
    ppermute x3, waiting for transfers between devices, sum_over(): lax.ppermute(array, axis, [(i, i ^ k) for i in range(size)])  5.96 us
  transfers between devices with their start and end apart: 43, of which 13 were waited for; matrix products, arithmetic and copies ran while one was open for 9% of the time, Pallas kernels for 35%

profile of v5, /device:TPU:0, one launch (start us, length us, event | category | flops | bytes accessed | tf_op | source)
XLA Modules:
  0.0 262.5 jit_solution(1025433570471164518)
XLA Ops:
  7.2 3.0 %collective-permute-start = (bf16[512,768]{1,0:T(8,128)(2,1)}, bf16[512,768]{1,0:T(8,128)(2,1)S(1)}, u32[]{:S(2)}, u32[]{:S(2)}) collective-permute-start(bf16[512,768]{1,0:T(8,128)(2,1)} %refs_10_.1), channel_id=1, source_target_pairs={{0,2},{1,3},{2,0},{3,1},{4,6},{5,7},{6,4},{7,5},{8,10},{9,11},{10,... | collective-permute-start | bytes 2359304 | tf_op jit(solution)/shard_map/ppermute | solution.py:1014
  10.2 0.7 slice.28
  11.0 3.4 %collective-permute-start.1 = (bf16[8,768]{1,0:T(8,128)(2,1)S(1)}, bf16[8,768]{1,0:T(8,128)(2,1)S(1)}, u32[]{:S(2)}, u32[]{:S(2)}) collective-permute-start(bf16[8,768]{1,0:T(8,128)(2,1)S(1)} %slice.28), channel_id=1, source_target_pairs={{0,4},{4,8},{8,12},{12,16},{16,20},{20,24},{24,28},{1,5},{5,9},{9,... | collective-permute-start | bytes 36872 | tf_op jit(solution)/shard_map/ppermute | solution.py:998
  14.4 0.7 exp.3
  15.2 0.8 reshape.88
  16.0 0.7 copy.50
  16.9 0.7 sub.3
  17.6 0.8 fusion.8
  20.0 1.4 pad_maximum_fusion.3.refs_13_.taps_ref
  21.4 2.2 pad_maximum_fusion.wcat_ref
  24.1 0.9 collective-permute-start.3
  25.0 1.0 collective-permute-start.2
  26.7 1.0 collective-permute-done.4
  27.6 0.9 collective-permute-done.3
  31.7 0.7 copy.54.refs_12_
  33.2 23.0 %front.1 = (bf16[2048,768]{1,0:T(8,128)(2,1)}, bf16[8,768]{1,0:T(8,128)(2,1)}, bf16[2048,384]{1,0:T(8,128)(2,1)}, bf16[2048,512]{1,0:T(8,128)(2,1)}, bf16[2048,5...) custom-call(s32[3]{0:T(128)} %pad_add_fusion.at_ref, ...), custom_call_target="tpu_custom_call" | custom-call | flops 24999999488 | bytes 1 | tf_op jit(solution)/shard_map/front/pallas_call | solution.py:975
  56.3 1.8 collective-permute-start.7
  58.7 3.1 %collective-permute-start.9 = (f32[72,384]{1,0:T(8,128)}, f32[72,384]{1,0:T(8,128)S(1)}, u32[]{:S(2)}, u32[]{:S(2)}) collective-permute-start(f32[72,384]{1,0:T(8,128)} %get-tuple-element.157), channel_id=1, source_target_pairs={{0,8},{4,12},{16,24},{20,28},{8,0},{12,4},{24,16},{28,20},{1,9},{5... | collective-permute-start | bytes 331784 | tf_op jit(solution)/shard_map/ppermute | solution.py:1008
  62.5 8.7 %inner.1 = (f32[2048,384]{1,0:T(8,128)}, bf16[2048,384]{1,0:T(8,128)(2,1)}) custom-call(bf16[2048,512]{1,0:T(8,128)(2,1)} %get-tuple-element.141.act_ref.bc_ref, f32[2048,128]{1,0:T(8,128)} %get-tuple-element.143.pack_ref, f32[8,2048]{1,0:T(8,128)} %get-tuple-element.149.segrow_ref, f32[16,2048]{1,0:T(8,128)} %get-tuple-element.150.rowp_ref, ...), custom_call_target="tpu_custom_call" | custom-call | flops 6000000000 | bytes 1 | tf_op jit(solution)/shard_map/inner/pallas_call | solution.py:975
  71.9 9.3 %merge.1 = (bf16[2048,384]{1,0:T(8,128)(2,1)}, f32[8,2048]{1,0:T(8,128)}, bf16[16,64,768]{2,1,0:T(8,128)(2,1)}) custom-call(s32[3]{0:T(128)} %pad_add_fusion.at_ref, bf16[2048,512]{1,0:T(8,128)(2,1)} %get-tuple-element.141.act_ref.bc_ref, f32[2048,128]{1,0:T(8,128)} %get-tuple-element.143.pack_ref, f32[128,128]{1,0:T(8,128)} %get-tuple-element.144.tot_ref, ...), custom_call_target="tpu_custom_call" | custom-call | flops 6000000000 | bytes 1 | tf_op jit(solution)/shard_map/merge/pallas_call | solution.py:975
  81.8 1.2 collective-permute-start.12
  83.2 2.4 collective-permute-done.13.rest_3_
  85.6 1.6 collective-permute-done.12.rest_2_
  87.9 13.4 %turn.1 = (bf16[1024,768]{1,0:T(8,128)(2,1)}, bf16[2048,384]{1,0:T(8,128)(2,1)}, bf16[2048,384]{1,0:T(8,128)(2,1)}, bf16[2048,384]{1,0:T(8,128)(2,1)}, f32[8,384...) custom-call(bf16[2048,384]{1,0:T(8,128)(2,1)} %get-tuple-element.159.y_ref, ...), custom_call_target="tpu_custom_call" | custom-call | flops 4000000000 | bytes 1 | tf_op jit(solution)/shard_map/turn/pallas_call | solution.py:975
  102.0 10.5 %adjoint.1 = (bf16[256,768]{1,0:T(8,128)(2,1)}, bf16[256,768]{1,0:T(8,128)(2,1)}, bf16[256,768]{1,0:T(8,128)(2,1)}, bf16[256,768]{1,0:T(8,128)(2,1)}, f32[16,64,...) custom-call(s32[3]{0:T(128)} %pad_add_fusion.at_ref, ...), custom_call_target="tpu_custom_call" | custom-call | flops 100000000 | bytes 1 | tf_op jit(solution)/shard_map/adjoint/pallas_call | solution.py:975
  112.8 0.9 collective-permute-start.19
  113.7 0.8 collective-permute-start.20
  114.5 3.0 %collective-permute-start.14 = (f32[72,384]{1,0:T(8,128)}, f32[72,384]{1,0:T(8,128)S(1)}, u32[]{:S(2)}, u32[]{:S(2)}) collective-permute-start(f32[72,384]{1,0:T(8,128)} %get-tuple-element.181), channel_id=1, source_target_pairs={{0,4},{8,12},{16,20},{24,28},{4,0},{12,8},{20,16},{28,24},{1,5},{9... | collective-permute-start | bytes 331784 | tf_op jit(solution)/shard_map/ppermute | solution.py:1008
  118.2 3.1 %collective-permute-done.14.rest_0_ = f32[72,384]{1,0:T(8,128)S(1)} collective-permute-done((f32[72,384]{1,0:T(8,128)}, f32[72,384]{1,0:T(8,128)S(1)}, u32[]{:S(2)}, u32[]{:S(2)}) %collective-permute-start.14) | collective-permute-done | bytes 110624 | tf_op jit(solution)/shard_map/ppermute | solution.py:1008
  121.3 3.3 %collective-permute-start.16 = (f32[72,384]{1,0:T(8,128)}, f32[72,384]{1,0:T(8,128)S(1)}, u32[]{:S(2)}, u32[]{:S(2)}) collective-permute-start(f32[72,384]{1,0:T(8,128)} %get-tuple-element.183), channel_id=1, source_target_pairs={{0,8},{4,12},{16,24},{20,28},{8,0},{12,4},{24,16},{28,20},{1,9},{5... | collective-permute-start | bytes 331784 | tf_op jit(solution)/shard_map/ppermute | solution.py:1008
  124.7 0.7 collective-permute-start.17
  125.3 17.6 %mid.1 = (bf16[2048,384]{1,0:T(8,128)(2,1)}, f32[2048,128]{1,0:T(8,128)}, f32[2048,128]{1,0:T(8,128)}) custom-call(bf16[2048,512]{1,0:T(8,128)(2,1)} %get-tuple-element.141.act_ref.bc_ref, f32[2048,128]{1,0:T(8,128)} %get-tuple-element.143.pack_ref, f32[8,2048]{1,0:T(8,128)} %get-tuple-element.149.segrow_ref, f32[16,2048]{1,0:T(8,128)} %get-tuple-element.169.rowa_ref, ...), custom_call_target="tpu_custom_call" | custom-call | flops 100000000 | bytes 1 | tf_op jit(solution)/shard_map/mid/pallas_call | solution.py:975
  143.6 32.8 %back.1 = (bf16[2,512,768]{2,1,0:T(8,128)(2,1)}, bf16[2,512,768]{2,1,0:T(8,128)(2,1)}, bf16[96,640]{1,0:T(8,128)(2,1)}, bf16[96,640]{1,0:T(8,128)(2,1)}, bf16[96...) custom-call(s32[3]{0:T(128)} %pad_add_fusion.at_ref, ...), custom_call_target="tpu_custom_call" | custom-call | flops 100000000 | bytes 1 | tf_op jit(solution)/shard_map/back/pallas_call | solution.py:975
  176.5 0.7 copy-done.7
  177.4 3.4 %collective-permute-start.22 = (bf16[96,640]{1,0:T(8,128)(2,1)}, bf16[96,640]{1,0:T(8,128)(2,1)S(1)}, u32[]{:S(2)}, u32[]{:S(2)}) collective-permute-start(bf16[96,640]{1,0:T(8,128)(2,1)} %get-tuple-element.201), channel_id=1, source_target_pairs={{0,4},{4,0},{8,12},{12,8},{16,20},{20,16},{24,28},{28,24},{1,5},{5... | collective-permute-start | bytes 368648 | tf_op jit(solution)/shard_map/ppermute | solution.py:1014
  180.8 3.5 %collective-permute-start.23 = (bf16[96,640]{1,0:T(8,128)(2,1)}, bf16[96,640]{1,0:T(8,128)(2,1)S(1)}, u32[]{:S(2)}, u32[]{:S(2)}) collective-permute-start(bf16[96,640]{1,0:T(8,128)(2,1)} %get-tuple-element.202), channel_id=1, source_target_pairs={{0,8},{4,12},{8,0},{12,4},{16,24},{20,28},{24,16},{28,20},{1,9},{5... | collective-permute-start | bytes 368648 | tf_op jit(solution)/shard_map/ppermute | solution.py:1014
  184.7 3.2 %collective-permute-start.25 = (bf16[96,640]{1,0:T(8,128)(2,1)}, bf16[96,640]{1,0:T(8,128)(2,1)}, u32[]{:S(2)}, u32[]{:S(2)}) collective-permute-start(bf16[96,640]{1,0:T(8,128)(2,1)} %get-tuple-element.204), channel_id=1, source_target_pairs={{0,16},{4,20},{8,24},{12,28},{16,0},{20,4},{24,8},{28,12},{1,17},{... | collective-permute-start | bytes 368648 | tf_op jit(solution)/shard_map/ppermute | solution.py:1014
  188.0 2.0 collective-permute-start.26
  190.0 1.9 collective-permute-start.27
  191.9 3.4 %collective-permute-done.24 = bf16[96,640]{1,0:T(8,128)(2,1)S(1)} collective-permute-done((bf16[96,640]{1,0:T(8,128)(2,1)}, bf16[96,640]{1,0:T(8,128)(2,1)S(1)}, u32[]{:S(2)}, u32[]{:S(2)}) %collective-permute-start.24) | collective-permute-done | bytes 122912 | tf_op jit(solution)/shard_map/ppermute | solution.py:1014
  195.3 1.6 collective-permute-start.28
  197.0 9.5 %collective-permute-done.26 = bf16[96,640]{1,0:T(8,128)(2,1)} collective-permute-done((bf16[96,640]{1,0:T(8,128)(2,1)}, bf16[96,640]{1,0:T(8,128)(2,1)}, u32[]{:S(2)}, u32[]{:S(2)}) %collective-permute-start.26) | collective-permute-done | bytes 122912 | tf_op jit(solution)/shard_map/ppermute | solution.py:1014
  206.5 1.3 convert_add_fusion.2
  207.7 1.0 collective-permute-start.30
  208.8 1.2 collective-permute-start.29
  210.0 5.5 %collective-permute-done.30 = f32[96,256]{1,0:T(8,128)S(1)} collective-permute-done((f32[96,256]{1,0:T(8,128)S(1)}, f32[96,256]{1,0:T(8,128)S(1)}, u32[]{:S(2)}, u32[]{:S(2)}) %collective-permute-start.30) | collective-permute-done | bytes 98336 | tf_op jit(solution)/shard_map/ppermute | solution.py:1021
  216.1 1.7 convert_add_fusion
  217.8 0.9 collective-permute-start.39
  218.7 4.0 %collective-permute-start.38 = (bf16[96,640]{1,0:T(8,128)(2,1)S(1)}, bf16[96,640]{1,0:T(8,128)(2,1)}, u32[]{:S(2)}, u32[]{:S(2)}) collective-permute-start(bf16[96,640]{1,0:T(8,128)(2,1)S(1)} %pad_maximum_fusion.1.refs_0_), channel_id=1, source_target_pairs={{0,28},{4,24},{8,20},{12,16},{16,12},{20,8},{24,4},{28,0},{1,29},{... | collective-permute-start | bytes 368648 | tf_op jit(solution)/shard_map/ppermute | solution.py:1014
  222.8 0.8 collective-permute-start.37
  223.5 1.1 collective-permute-start.36
  224.6 1.9 collective-permute-start.35
  226.5 1.4 convert_add_fusion.1
  227.9 1.1 convert_element_type.101
  229.0 1.1 convert_element_type.102
  230.1 1.0 convert_element_type.95
  231.1 8.2 %collective-permute-start.34 = (bf16[96,640]{1,0:T(8,128)(2,1)S(1)}, bf16[96,640]{1,0:T(8,128)(2,1)S(1)}, u32[]{:S(2)}, u32[]{:S(2)}) collective-permute-start(bf16[96,640]{1,0:T(8,128)(2,1)S(1)} %pad_maximum_fusion.1.refs_0_), channel_id=1, source_target_pairs={{0,12},{4,8},{8,4},{12,0},{16,28},{20,24},{24,20},{28,16},{1,13},{... | collective-permute-start | bytes 368648 | tf_op jit(solution)/shard_map/ppermute | solution.py:1014
  239.4 1.7 collective-permute-start.33
  241.1 2.3 collective-permute-done.36.refs_5_
  243.4 1.3 collective-permute-start.32
  244.7 1.1 fusion
  245.8 2.3 collective-permute-done.34.refs_3_
  248.1 1.4 collective-permute-done.33.refs_2_
  250.4 5.5 %finish.1 = (f32[768]{0:T(1024)}, f32[768,384]{1,0:T(8,128)}, f32[768,128]{1,0:T(8,128)}, f32[6,2,768]{2,1,0:T(2,128)}, f32[2,6]{1,0:T(2,128)}, /*index=5*/f32[1...) custom-call(s32[3]{0:T(128)} %pad_add_fusion.at_ref, ...), custom_call_target="tpu_custom_call" | custom-call | flops 3000000000 | bytes 1 | tf_op jit(solution)/shard_map/finish/pallas_call | solution.py:975
  (138 shorter events, 15.2 us)
Async XLA Ops:
  7.2 55.3 %all-gather.2.cloned.1.call-start = ((), (), s32[]{:S(2)}) async-start(), calls=%async_computation.1 | async-start | bytes 3932160 | tf_op jit(solution)/shard_map/all_gather | solution.py:1134
  7.2 21.9 %collective-permute-start = (bf16[512,768]{1,0:T(8,128)(2,1)}, bf16[512,768]{1,0:T(8,128)(2,1)S(1)}, u32[]{:S(2)}, u32[]{:S(2)}) collective-permute-start(bf16[512,768]{1,0:T(8,128)(2,1)} %refs_10_.1), channel_id=1, source_target_pairs={{0,2},{1,3},{2,0},{3,1},{4,6},{5,7},{6,4},{7,5},{8,10},{9,11},{10,... | collective-permute-start | bytes 2359304 | tf_op jit(solution)/shard_map/ppermute | solution.py:1014
  11.0 13.2 %collective-permute-start.1 = (bf16[8,768]{1,0:T(8,128)(2,1)S(1)}, bf16[8,768]{1,0:T(8,128)(2,1)S(1)}, u32[]{:S(2)}, u32[]{:S(2)}) collective-permute-start(bf16[8,768]{1,0:T(8,128)(2,1)S(1)} %slice.28), channel_id=1, source_target_pairs={{0,4},{4,8},{8,12},{12,16},{16,20},{20,24},{24,28},{1,5},{5,9},{9,... | collective-permute-start | bytes 36872 | tf_op jit(solution)/shard_map/ppermute | solution.py:998
  19.9 9.3 %copy-start.1 = (bf16[512,768]{1,0:T(8,128)(2,1)S(1)}, bf16[512,768]{1,0:T(8,128)(2,1)}, u32[]{:S(2)}) copy-start(bf16[512,768]{1,0:T(8,128)(2,1)} %refs_10_.1) | copy-start | bytes 2359300
  19.9 9.9 %copy-start.16 = (f32[384]{0:T(512)S(1)}, f32[384]{0:T(512)}, u32[]{:S(2)}) copy-start(f32[384]{0:T(512)} %param.35) | copy-start | bytes 4612
  19.9 10.4 %copy-start.15 = (f32[768]{0:T(1024)S(1)}, f32[768]{0:T(1024)}, u32[]{:S(2)}) copy-start(f32[768]{0:T(1024)} %param.25) | copy-start | bytes 9220
  19.9 11.0 %copy-start.17 = (f32[6]{0:T(128)S(1)}, f32[6]{0:T(128)}, u32[]{:S(2)}) copy-start(f32[6]{0:T(128)} %param.34) | copy-start | bytes 76
  20.0 12.9 %copy-start.3 = (bf16[768,128]{1,0:T(8,128)(2,1)}, bf16[768,128]{1,0:T(8,128)(2,1)S(1)}, u32[]{:S(2)}) copy-start(bf16[768,128]{1,0:T(8,128)(2,1)S(1)} %pad.28.refs_9_) | copy-start | bytes 589828
  24.1 3.5 %collective-permute-start.4 = (bf16[8,768]{1,0:T(8,128)(2,1)S(1)}, bf16[8,768]{1,0:T(8,128)(2,1)S(1)}, u32[]{:S(2)}, u32[]{:S(2)}) collective-permute-start(bf16[8,768]{1,0:T(8,128)(2,1)S(1)} %collective-permute-done.1), channel_id=1, source_target_pairs={{0,3},{1,2},{2,1},{3,0},{4,7},{5,6},{6,5},{7,4},{8,11},{9,10},{10,... | collective-permute-start | bytes 36872 | tf_op jit(solution)/shard_map/ppermute | solution.py:1014
  24.1 4.4 %collective-permute-start.3 = (bf16[8,768]{1,0:T(8,128)(2,1)S(1)}, bf16[8,768]{1,0:T(8,128)(2,1)S(1)}, u32[]{:S(2)}, u32[]{:S(2)}) collective-permute-start(bf16[8,768]{1,0:T(8,128)(2,1)S(1)} %collective-permute-done.1), channel_id=1, source_target_pairs={{0,2},{1,3},{2,0},{3,1},{4,6},{5,7},{6,4},{7,5},{8,10},{9,11},{10,... | collective-permute-start | bytes 36872 | tf_op jit(solution)/shard_map/ppermute | solution.py:1014
  25.0 3.5 %collective-permute-start.2 = (bf16[8,768]{1,0:T(8,128)(2,1)S(1)}, bf16[8,768]{1,0:T(8,128)(2,1)S(1)}, u32[]{:S(2)}, u32[]{:S(2)}) collective-permute-start(bf16[8,768]{1,0:T(8,128)(2,1)S(1)} %collective-permute-done.1), channel_id=1, source_target_pairs={{0,1},{1,0},{2,3},{3,2},{4,5},{5,4},{6,7},{7,6},{8,9},{9,8},{10,11... | collective-permute-start | bytes 36872 | tf_op jit(solution)/shard_map/ppermute | solution.py:1014
  29.1 3.7 %copy-start.18 = (bf16[512,768]{1,0:T(8,128)(2,1)}, bf16[512,768]{1,0:T(8,128)(2,1)S(1)}, u32[]{:S(2)}) copy-start(bf16[512,768]{1,0:T(8,128)(2,1)S(1)} %collective-permute-done.refs_2_) | copy-start | bytes 2359300
  29.1 189.6 %all-reduce.9.cloned.1.call-start = ((), (), s32[]{:S(2)}) async-start(), calls=%async_computation.3 | async-start | bytes 2359296 | tf_op jit(solution)/shard_map/psum | solution.py:1400
  29.2 3.1 %collective-permute-start.5 = (bf16[512,768]{1,0:T(8,128)(2,1)S(1)}, bf16[512,768]{1,0:T(8,128)(2,1)S(1)}, u32[]{:S(2)}, u32[]{:S(2)}) collective-permute-start(bf16[512,768]{1,0:T(8,128)(2,1)S(1)} %copy-done.1), channel_id=1, source_target_pairs={{0,1},{1,0},{2,3},{3,2},{4,5},{5,4},{6,7},{7,6},{8,9},{9,8},{10,11... | collective-permute-start | bytes 2359304 | tf_op jit(solution)/shard_map/ppermute | solution.py:1014
  29.3 3.5 %collective-permute-start.6 = (bf16[512,768]{1,0:T(8,128)(2,1)S(1)}, bf16[512,768]{1,0:T(8,128)(2,1)}, u32[]{:S(2)}, u32[]{:S(2)}) collective-permute-start(bf16[512,768]{1,0:T(8,128)(2,1)S(1)} %collective-permute-done.refs_2_), channel_id=1, source_target_pairs={{0,1},{1,0},{2,3},{3,2},{4,5},{5,4},{6,7},{7,6},{8,9},{9,8},{10,11... | collective-permute-start | bytes 2359304 | tf_op jit(solution)/shard_map/ppermute | solution.py:1014
  32.3 0.9 copy-start.20
  56.3 14.9 %collective-permute-start.7 = (f32[72,384]{1,0:T(8,128)}, f32[72,384]{1,0:T(8,128)S(1)}, u32[]{:S(2)}, u32[]{:S(2)}) collective-permute-start(f32[72,384]{1,0:T(8,128)} %get-tuple-element.155), channel_id=1, source_target_pairs={{0,4},{8,12},{16,20},{24,28},{4,0},{12,8},{20,16},{28,24},{1,5},{9... | collective-permute-start | bytes 331784 | tf_op jit(solution)/shard_map/ppermute | solution.py:1008
  58.1 13.1 %collective-permute-start.8 = (f32[72,384]{1,0:T(8,128)}, f32[72,384]{1,0:T(8,128)S(1)}, u32[]{:S(2)}, u32[]{:S(2)}) collective-permute-start(f32[72,384]{1,0:T(8,128)} %get-tuple-element.156), channel_id=1, source_target_pairs={{4,8},{12,16},{20,24},{8,4},{16,12},{24,20},{5,9},{13,17},{21,25},... | collective-permute-start | bytes 331784 | tf_op jit(solution)/shard_map/ppermute | solution.py:1008
  58.7 12.4 %collective-permute-start.9 = (f32[72,384]{1,0:T(8,128)}, f32[72,384]{1,0:T(8,128)S(1)}, u32[]{:S(2)}, u32[]{:S(2)}) collective-permute-start(f32[72,384]{1,0:T(8,128)} %get-tuple-element.157), channel_id=1, source_target_pairs={{0,8},{4,12},{16,24},{20,28},{8,0},{12,4},{24,16},{28,20},{1,9},{5... | collective-permute-start | bytes 331784 | tf_op jit(solution)/shard_map/ppermute | solution.py:1008
  61.8 9.4 %collective-permute-start.10 = (f32[72,384]{1,0:T(8,128)}, f32[72,384]{1,0:T(8,128)S(1)}, u32[]{:S(2)}, u32[]{:S(2)}) collective-permute-start(f32[72,384]{1,0:T(8,128)} %get-tuple-element.158), channel_id=1, source_target_pairs={{8,16},{12,20},{16,8},{20,12},{9,17},{13,21},{17,9},{21,13},{10,18... | collective-permute-start | bytes 331784 | tf_op jit(solution)/shard_map/ppermute | solution.py:1008
  81.2 4.4 %collective-permute-start.13 = (f32[8,2048]{1,0:T(8,128)}, f32[8,2048]{1,0:T(8,128)S(1)}, u32[]{:S(2)}, u32[]{:S(2)}) collective-permute-start(f32[8,2048]{1,0:T(8,128)} %get-tuple-element.161.rest_0_), channel_id=1, source_target_pairs={{0,3},{1,2},{2,1},{3,0},{4,7},{5,6},{6,5},{7,4},{8,11},{9,10},{10,... | collective-permute-start | bytes 196616 | tf_op jit(solution)/shard_map/ppermute | solution.py:1333
  81.8 5.4 %collective-permute-start.12 = (f32[8,2048]{1,0:T(8,128)}, f32[8,2048]{1,0:T(8,128)S(1)}, u32[]{:S(2)}, u32[]{:S(2)}) collective-permute-start(f32[8,2048]{1,0:T(8,128)} %get-tuple-element.161.rest_0_), channel_id=1, source_target_pairs={{0,2},{1,3},{2,0},{3,1},{4,6},{5,7},{6,4},{7,5},{8,10},{9,11},{10,... | collective-permute-start | bytes 196616 | tf_op jit(solution)/shard_map/ppermute | solution.py:1333
  83.1 4.1 %collective-permute-start.11 = (f32[8,2048]{1,0:T(8,128)}, f32[8,2048]{1,0:T(8,128)S(1)}, u32[]{:S(2)}, u32[]{:S(2)}) collective-permute-start(f32[8,2048]{1,0:T(8,128)} %get-tuple-element.161.rest_0_), channel_id=1, source_target_pairs={{0,1},{1,0},{2,3},{3,2},{4,5},{5,4},{6,7},{7,6},{8,9},{9,8},{10,11... | collective-permute-start | bytes 196616 | tf_op jit(solution)/shard_map/ppermute | solution.py:1333
  85.6 1.6 copy-start.28
  101.3 128.8 %reduce-scatter.2.cloned.1.call-start = ((), (), s32[]{:S(2)}) async-start(), calls=%async_computation.2 | async-start | bytes 1966080 | tf_op jit(solution)/shard_map/reduce_scatter | solution.py:1401
  112.6 63.8 %collective-permute-start.18 = (bf16[256,768]{1,0:T(8,128)(2,1)}, bf16[256,768]{1,0:T(8,128)(2,1)S(1)}, u32[]{:S(2)}, u32[]{:S(2)}) collective-permute-start(bf16[256,768]{1,0:T(8,128)(2,1)} %get-tuple-element.196), channel_id=1, source_target_pairs={{0,1},{1,0},{2,3},{3,2},{4,5},{5,4},{6,7},{7,6},{8,9},{9,8},{10,11... | collective-permute-start | bytes 1179656 | tf_op jit(solution)/shard_map/ppermute | solution.py:1014
  112.8 63.6 %collective-permute-start.19 = (bf16[256,768]{1,0:T(8,128)(2,1)}, bf16[256,768]{1,0:T(8,128)(2,1)S(1)}, u32[]{:S(2)}, u32[]{:S(2)}) collective-permute-start(bf16[256,768]{1,0:T(8,128)(2,1)} %get-tuple-element.197), channel_id=1, source_target_pairs={{0,2},{1,3},{2,0},{3,1},{4,6},{5,7},{6,4},{7,5},{8,10},{9,11},{10,... | collective-permute-start | bytes 1179656 | tf_op jit(solution)/shard_map/ppermute | solution.py:1014
  113.7 62.8 %collective-permute-start.20 = (bf16[256,768]{1,0:T(8,128)(2,1)}, bf16[256,768]{1,0:T(8,128)(2,1)S(1)}, u32[]{:S(2)}, u32[]{:S(2)}) collective-permute-start(bf16[256,768]{1,0:T(8,128)(2,1)} %get-tuple-element.198), channel_id=1, source_target_pairs={{0,3},{1,2},{2,1},{3,0},{4,7},{5,6},{6,5},{7,4},{8,11},{9,10},{10,... | collective-permute-start | bytes 1179656 | tf_op jit(solution)/shard_map/ppermute | solution.py:1014
  114.5 6.8 %collective-permute-start.14 = (f32[72,384]{1,0:T(8,128)}, f32[72,384]{1,0:T(8,128)S(1)}, u32[]{:S(2)}, u32[]{:S(2)}) collective-permute-start(f32[72,384]{1,0:T(8,128)} %get-tuple-element.181), channel_id=1, source_target_pairs={{0,4},{8,12},{16,20},{24,28},{4,0},{12,8},{20,16},{28,24},{1,5},{9... | collective-permute-start | bytes 331784 | tf_op jit(solution)/shard_map/ppermute | solution.py:1008
  117.6 7.1 %collective-permute-start.15 = (f32[72,384]{1,0:T(8,128)}, f32[72,384]{1,0:T(8,128)S(1)}, u32[]{:S(2)}, u32[]{:S(2)}) collective-permute-start(f32[72,384]{1,0:T(8,128)} %get-tuple-element.182), channel_id=1, source_target_pairs={{4,8},{12,16},{20,24},{8,4},{16,12},{24,20},{5,9},{13,17},{21,25},... | collective-permute-start | bytes 331784 | tf_op jit(solution)/shard_map/ppermute | solution.py:1008
  121.3 21.5 %copy-start.11 = (f32[72,384]{1,0:T(8,128)}, f32[72,384]{1,0:T(8,128)S(1)}, u32[]{:S(2)}) copy-start(f32[72,384]{1,0:T(8,128)S(1)} %collective-permute-done.14.rest_0_) | copy-start | bytes 331780
  121.3 21.6 %collective-permute-start.16 = (f32[72,384]{1,0:T(8,128)}, f32[72,384]{1,0:T(8,128)S(1)}, u32[]{:S(2)}, u32[]{:S(2)}) collective-permute-start(f32[72,384]{1,0:T(8,128)} %get-tuple-element.183), channel_id=1, source_target_pairs={{0,8},{4,12},{16,24},{20,28},{8,0},{12,4},{24,16},{28,20},{1,9},{5... | collective-permute-start | bytes 331784 | tf_op jit(solution)/shard_map/ppermute | solution.py:1008
  124.7 18.2 %copy-start.12 = (f32[72,384]{1,0:T(8,128)}, f32[72,384]{1,0:T(8,128)S(1)}, u32[]{:S(2)}) copy-start(f32[72,384]{1,0:T(8,128)S(1)} %collective-permute-done.15.rest_1_) | copy-start | bytes 331780
  124.7 18.2 %collective-permute-start.17 = (f32[72,384]{1,0:T(8,128)}, f32[72,384]{1,0:T(8,128)S(1)}, u32[]{:S(2)}, u32[]{:S(2)}) collective-permute-start(f32[72,384]{1,0:T(8,128)} %get-tuple-element.184), channel_id=1, source_target_pairs={{8,16},{12,20},{16,8},{20,12},{9,17},{13,21},{17,9},{21,13},{10,18... | collective-permute-start | bytes 331784 | tf_op jit(solution)/shard_map/ppermute | solution.py:1008
  176.4 39.6 %copy-start = (bf16[2,512,768]{2,1,0:T(8,128)(2,1)S(1)}, bf16[2,512,768]{2,1,0:T(8,128)(2,1)}, u32[]{:S(2)}) copy-start(bf16[2,512,768]{2,1,0:T(8,128)(2,1)} %get-tuple-element.185) | copy-start | bytes 4718596
  176.4 0.7 copy-start.7
  176.4 0.9 copy-start.8
  176.5 1.0 copy-start.9
  177.3 38.7 %collective-permute-start.21 = (bf16[2,512,768]{2,1,0:T(8,128)(2,1)}, bf16[2,512,768]{2,1,0:T(8,128)(2,1)S(1)}, u32[]{:S(2)}, u32[]{:S(2)}) collective-permute-start(bf16[2,512,768]{2,1,0:T(8,128)(2,1)} %get-tuple-element.199), channel_id=1, source_target_pairs={{0,1},{1,0},{2,3},{3,2},{4,5},{5,4},{6,7},{7,6},{8,9},{9,8},{10,11... | collective-permute-start | bytes 4718600 | tf_op jit(solution)/shard_map/ppermute | solution.py:1014
  177.4 10.6 %collective-permute-start.22 = (bf16[96,640]{1,0:T(8,128)(2,1)}, bf16[96,640]{1,0:T(8,128)(2,1)S(1)}, u32[]{:S(2)}, u32[]{:S(2)}) collective-permute-start(bf16[96,640]{1,0:T(8,128)(2,1)} %get-tuple-element.201), channel_id=1, source_target_pairs={{0,4},{4,0},{8,12},{12,8},{16,20},{20,16},{24,28},{28,24},{1,5},{5... | collective-permute-start | bytes 368648 | tf_op jit(solution)/shard_map/ppermute | solution.py:1014
  180.8 9.2 %collective-permute-start.23 = (bf16[96,640]{1,0:T(8,128)(2,1)}, bf16[96,640]{1,0:T(8,128)(2,1)S(1)}, u32[]{:S(2)}, u32[]{:S(2)}) collective-permute-start(bf16[96,640]{1,0:T(8,128)(2,1)} %get-tuple-element.202), channel_id=1, source_target_pairs={{0,8},{4,12},{8,0},{12,4},{16,24},{20,28},{24,16},{28,20},{1,9},{5... | collective-permute-start | bytes 368648 | tf_op jit(solution)/shard_map/ppermute | solution.py:1014
  184.3 11.0 %collective-permute-start.24 = (bf16[96,640]{1,0:T(8,128)(2,1)}, bf16[96,640]{1,0:T(8,128)(2,1)S(1)}, u32[]{:S(2)}, u32[]{:S(2)}) collective-permute-start(bf16[96,640]{1,0:T(8,128)(2,1)} %get-tuple-element.203), channel_id=1, source_target_pairs={{0,12},{4,8},{8,4},{12,0},{16,28},{20,24},{24,20},{28,16},{1,13},{... | collective-permute-start | bytes 368648 | tf_op jit(solution)/shard_map/ppermute | solution.py:1014
  184.7 12.2 %collective-permute-start.25 = (bf16[96,640]{1,0:T(8,128)(2,1)}, bf16[96,640]{1,0:T(8,128)(2,1)}, u32[]{:S(2)}, u32[]{:S(2)}) collective-permute-start(bf16[96,640]{1,0:T(8,128)(2,1)} %get-tuple-element.204), channel_id=1, source_target_pairs={{0,16},{4,20},{8,24},{12,28},{16,0},{20,4},{24,8},{28,12},{1,17},{... | collective-permute-start | bytes 368648 | tf_op jit(solution)/shard_map/ppermute | solution.py:1014
  188.0 18.5 %collective-permute-start.26 = (bf16[96,640]{1,0:T(8,128)(2,1)}, bf16[96,640]{1,0:T(8,128)(2,1)}, u32[]{:S(2)}, u32[]{:S(2)}) collective-permute-start(bf16[96,640]{1,0:T(8,128)(2,1)} %get-tuple-element.205), channel_id=1, source_target_pairs={{0,20},{4,16},{8,28},{12,24},{16,4},{20,0},{24,12},{28,8},{1,21},{... | collective-permute-start | bytes 368648 | tf_op jit(solution)/shard_map/ppermute | solution.py:1014
  190.0 16.4 %collective-permute-start.27 = (bf16[96,640]{1,0:T(8,128)(2,1)}, bf16[96,640]{1,0:T(8,128)(2,1)}, u32[]{:S(2)}, u32[]{:S(2)}) collective-permute-start(bf16[96,640]{1,0:T(8,128)(2,1)} %get-tuple-element.206), channel_id=1, source_target_pairs={{0,24},{4,28},{8,16},{12,20},{16,8},{20,12},{24,0},{28,4},{1,25},{... | collective-permute-start | bytes 368648 | tf_op jit(solution)/shard_map/ppermute | solution.py:1014
  195.3 11.1 %collective-permute-start.28 = (bf16[96,640]{1,0:T(8,128)(2,1)}, bf16[96,640]{1,0:T(8,128)(2,1)}, u32[]{:S(2)}, u32[]{:S(2)}) collective-permute-start(bf16[96,640]{1,0:T(8,128)(2,1)} %get-tuple-element.207), channel_id=1, source_target_pairs={{0,28},{4,24},{8,20},{12,16},{16,12},{20,8},{24,4},{28,0},{1,29},{... | collective-permute-start | bytes 368648 | tf_op jit(solution)/shard_map/ppermute | solution.py:1014
  207.7 7.7 %collective-permute-start.30 = (f32[96,256]{1,0:T(8,128)S(1)}, f32[96,256]{1,0:T(8,128)S(1)}, u32[]{:S(2)}, u32[]{:S(2)}) collective-permute-start(f32[96,256]{1,0:T(8,128)S(1)} %slice.38), channel_id=1, source_target_pairs={{0,2},{1,3},{2,0},{3,1},{4,6},{5,7},{6,4},{7,5},{8,10},{9,11},{10,... | collective-permute-start | bytes 294920 | tf_op jit(solution)/shard_map/ppermute | solution.py:1021
  208.8 7.2 %collective-permute-start.31 = (f32[96,256]{1,0:T(8,128)S(1)}, f32[96,256]{1,0:T(8,128)S(1)}, u32[]{:S(2)}, u32[]{:S(2)}) collective-permute-start(f32[96,256]{1,0:T(8,128)S(1)} %slice.38), channel_id=1, source_target_pairs={{0,3},{1,2},{2,1},{3,0},{4,7},{5,6},{6,5},{7,4},{8,11},{9,10},{10,... | collective-permute-start | bytes 294920 | tf_op jit(solution)/shard_map/ppermute | solution.py:1021
  208.8 7.2 %collective-permute-start.29 = (f32[96,256]{1,0:T(8,128)S(1)}, f32[96,256]{1,0:T(8,128)S(1)}, u32[]{:S(2)}, u32[]{:S(2)}) collective-permute-start(f32[96,256]{1,0:T(8,128)S(1)} %slice.38), channel_id=1, source_target_pairs={{0,1},{1,0},{2,3},{3,2},{4,5},{5,4},{6,7},{7,6},{8,9},{9,8},{10,11... | collective-permute-start | bytes 294920 | tf_op jit(solution)/shard_map/ppermute | solution.py:1021
  216.0 10.4 %copy-start.6 = (bf16[256,768]{1,0:T(8,128)(2,1)S(1)}, bf16[256,768]{1,0:T(8,128)(2,1)}, u32[]{:S(2)}) copy-start(bf16[256,768]{1,0:T(8,128)(2,1)} %get-tuple-element.217) | copy-start | bytes 1179652
  217.8 31.7 %collective-permute-start.39 = (bf16[1,512,768]{2,1,0:T(8,128)(2,1)}, bf16[1,512,768]{2,1,0:T(8,128)(2,1)S(1)}, u32[]{:S(2)}, u32[]{:S(2)}) collective-permute-start(bf16[1,512,768]{2,1,0:T(8,128)(2,1)} %get-tuple-element.232), channel_id=1, source_target_pairs={{0,2},{1,3},{2,0},{3,1},{4,6},{5,7},{6,4},{7,5},{8,10},{9,11},{10,... | collective-permute-start | bytes 2359304 | tf_op jit(solution)/shard_map/ppermute | solution.py:1014
  218.7 24.8 %copy-start.10 = (bf16[96,640]{1,0:T(8,128)(2,1)}, bf16[96,640]{1,0:T(8,128)(2,1)S(1)}, u32[]{:S(2)}) copy-start(bf16[96,640]{1,0:T(8,128)(2,1)S(1)} %pad_maximum_fusion.1.refs_0_) | copy-start | bytes 368644
  218.7 9.2 %copy-start.5 = (bf16[384,768]{1,0:T(8,128)(2,1)S(1)}, bf16[384,768]{1,0:T(8,128)(2,1)}, u32[]{:S(2)}) copy-start(bf16[384,768]{1,0:T(8,128)(2,1)} %get-tuple-element.221) | copy-start | bytes 1769476
  218.7 10.2 %copy-start.4 = (bf16[768,384]{1,0:T(8,128)(2,1)S(1)}, bf16[768,384]{1,0:T(8,128)(2,1)}, u32[]{:S(2)}) copy-start(bf16[768,384]{1,0:T(8,128)(2,1)} %get-tuple-element.222) | copy-start | bytes 1769476
  218.7 12.4 %collective-permute-start.38 = (bf16[96,640]{1,0:T(8,128)(2,1)S(1)}, bf16[96,640]{1,0:T(8,128)(2,1)}, u32[]{:S(2)}, u32[]{:S(2)}) collective-permute-start(bf16[96,640]{1,0:T(8,128)(2,1)S(1)} %pad_maximum_fusion.1.refs_0_), channel_id=1, source_target_pairs={{0,28},{4,24},{8,20},{12,16},{16,12},{20,8},{24,4},{28,0},{1,29},{... | collective-permute-start | bytes 368648 | tf_op jit(solution)/shard_map/ppermute | solution.py:1014
  222.8 16.6 %collective-permute-start.37 = (bf16[96,640]{1,0:T(8,128)(2,1)S(1)}, bf16[96,640]{1,0:T(8,128)(2,1)}, u32[]{:S(2)}, u32[]{:S(2)}) collective-permute-start(bf16[96,640]{1,0:T(8,128)(2,1)S(1)} %pad_maximum_fusion.1.refs_0_), channel_id=1, source_target_pairs={{0,24},{4,28},{8,16},{12,20},{16,8},{20,12},{24,0},{28,4},{1,25},{... | collective-permute-start | bytes 368648 | tf_op jit(solution)/shard_map/ppermute | solution.py:1014
  223.5 19.9 %collective-permute-start.36 = (bf16[96,640]{1,0:T(8,128)(2,1)S(1)}, bf16[96,640]{1,0:T(8,128)(2,1)}, u32[]{:S(2)}, u32[]{:S(2)}) collective-permute-start(bf16[96,640]{1,0:T(8,128)(2,1)S(1)} %pad_maximum_fusion.1.refs_0_), channel_id=1, source_target_pairs={{0,20},{4,16},{8,28},{12,24},{16,4},{20,0},{24,12},{28,8},{1,21},{... | collective-permute-start | bytes 368648 | tf_op jit(solution)/shard_map/ppermute | solution.py:1014
  224.6 21.2 %collective-permute-start.35 = (bf16[96,640]{1,0:T(8,128)(2,1)S(1)}, bf16[96,640]{1,0:T(8,128)(2,1)}, u32[]{:S(2)}, u32[]{:S(2)}) collective-permute-start(bf16[96,640]{1,0:T(8,128)(2,1)S(1)} %pad_maximum_fusion.1.refs_0_), channel_id=1, source_target_pairs={{0,16},{4,20},{8,24},{12,28},{16,0},{20,4},{24,8},{28,12},{1,17},{... | collective-permute-start | bytes 368648 | tf_op jit(solution)/shard_map/ppermute | solution.py:1014
  229.0 15.8 %copy-start.2 = (bf16[512,768]{1,0:T(8,128)(2,1)S(1)}, bf16[512,768]{1,0:T(8,128)(2,1)}, u32[]{:S(2)}) copy-start(bf16[512,768]{1,0:T(8,128)(2,1)} %refs_10_.1) | copy-start | bytes 2359300
  231.1 17.0 %collective-permute-start.34 = (bf16[96,640]{1,0:T(8,128)(2,1)S(1)}, bf16[96,640]{1,0:T(8,128)(2,1)S(1)}, u32[]{:S(2)}, u32[]{:S(2)}) collective-permute-start(bf16[96,640]{1,0:T(8,128)(2,1)S(1)} %pad_maximum_fusion.1.refs_0_), channel_id=1, source_target_pairs={{0,12},{4,8},{8,4},{12,0},{16,28},{20,24},{24,20},{28,16},{1,13},{... | collective-permute-start | bytes 368648 | tf_op jit(solution)/shard_map/ppermute | solution.py:1014
  239.4 10.1 %collective-permute-start.33 = (bf16[96,640]{1,0:T(8,128)(2,1)S(1)}, bf16[96,640]{1,0:T(8,128)(2,1)S(1)}, u32[]{:S(2)}, u32[]{:S(2)}) collective-permute-start(bf16[96,640]{1,0:T(8,128)(2,1)S(1)} %pad_maximum_fusion.1.refs_0_), channel_id=1, source_target_pairs={{0,8},{4,12},{8,0},{12,4},{16,24},{20,28},{24,16},{28,20},{1,9},{5... | collective-permute-start | bytes 368648 | tf_op jit(solution)/shard_map/ppermute | solution.py:1014
  243.4 6.0 %collective-permute-start.32 = (bf16[96,640]{1,0:T(8,128)(2,1)S(1)}, bf16[96,640]{1,0:T(8,128)(2,1)S(1)}, u32[]{:S(2)}, u32[]{:S(2)}) collective-permute-start(bf16[96,640]{1,0:T(8,128)(2,1)S(1)} %pad_maximum_fusion.1.refs_0_), channel_id=1, source_target_pairs={{0,4},{4,0},{8,12},{12,8},{16,20},{20,16},{24,28},{28,24},{1,5},{5... | collective-permute-start | bytes 368648 | tf_op jit(solution)/shard_map/ppermute | solution.py:1014
  248.1 1.4 copy-start.21
  249.5 0.9 copy-start.19
  (10 other events, 6.6 us)
Sparse Core Ops, SparseCore 0:
  29.3 30.0 all-gather.1
  101.4 82.5 all-reduce.8
  186.7 30.9 reduce-scatter.1

commit v6 on v5

--- a/solution.py
+++ b/solution.py
@@ -1550,10 +1550,10 @@
             own_in = own_in[:half] + got[:half].astype(F32)
 
     reduced = jnp.concatenate([shared, summed[:, 2 * LANES :]], axis=1).astype(BF16)
-    reduced, grad_proj_out, grad_proj_gate, mixer_shares = lax.optimization_barrier(
-        (reduced, grad_proj_out, grad_proj_gate, mixer_shares)
+    spread_out = [reduced] + [swap(reduced, "seq", k) for k in range(1, peers)]
+    spread_out[2], grad_proj_out, grad_proj_gate, mixer_shares = lax.optimization_barrier(
+        (spread_out[2], grad_proj_out, grad_proj_gate, mixer_shares)
     )
-    spread_out = [reduced] + [swap(reduced, "seq", k) for k in range(1, peers)]
     grad_proj_out = grad_proj_out[:real_width].astype(F32)
     grad_proj_gate = grad_proj_gate[:, :real_width].astype(F32)
     mixer = sum(share.astype(F32) for share in mixer_shares)

time: 263 us -> 261 us (level)
  transfers between devices with their start and end apart: 43 -> 43, of which waited for: 13 -> 13; matrix products, arithmetic and copies ran while one was open for 9% -> 9% of each run, Pallas kernels for 35% -> 36%
where the time goes in v6:
time: 261 us; the launch traced here: 260 us
  Pallas kernels  121 us (46%)
  starting transfers between devices  62.5 us (24%)
  waiting for transfers between devices  34.6 us (13%)
  other arithmetic  16.6 us (6%)
  between operations  14.2 us (5%)
  local copies, waits for them, and re-layouts  11.5 us (4%)
    pallas_call x8, Pallas kernels, call(): pl.pallas_call(kernel, name=name, grid_spec=pltpu.PrefetchScalarGridSpec(...  121 us
    ppermute x25, starting transfers between devices, swap(): return lax.ppermute(array, axis, [(i, i ^ k) for i in range(n)])  40.8 us
    ppermute x25, waiting for transfers between devices, swap(): return lax.ppermute(array, axis, [(i, i ^ k) for i in range(n)])  20.8 us
    ppermute x8, starting transfers between devices, exchange_sides(): arrived.append(lax.ppermute(messages[len(arrived)], 'seq', both))  13.8 us
    ppermute x3, waiting for transfers between devices, sum_over(): lax.ppermute(array, axis, [(i, i ^ k) for i in range(size)])  5.95 us
  transfers between devices with their start and end apart: 43, of which 13 were waited for; matrix products, arithmetic and copies ran while one was open for 9% of the time, Pallas kernels for 36%

profile of v6, /device:TPU:0, one launch (start us, length us, event | category | flops | bytes accessed | tf_op | source)
XLA Modules:
  0.0 260.2 jit_solution(8176021107849057139)
XLA Ops:
  7.2 3.0 %collective-permute-start = (bf16[512,768]{1,0:T(8,128)(2,1)}, bf16[512,768]{1,0:T(8,128)(2,1)S(1)}, u32[]{:S(2)}, u32[]{:S(2)}) collective-permute-start(bf16[512,768]{1,0:T(8,128)(2,1)} %refs_10_.1), channel_id=1, source_target_pairs={{0,2},{1,3},{2,0},{3,1},{4,6},{5,7},{6,4},{7,5},{8,10},{9,11},{10,... | collective-permute-start | bytes 2359304 | tf_op jit(solution)/shard_map/ppermute | solution.py:1014
  10.2 0.7 slice.28
  11.0 3.4 %collective-permute-start.1 = (bf16[8,768]{1,0:T(8,128)(2,1)S(1)}, bf16[8,768]{1,0:T(8,128)(2,1)S(1)}, u32[]{:S(2)}, u32[]{:S(2)}) collective-permute-start(bf16[8,768]{1,0:T(8,128)(2,1)S(1)} %slice.28), channel_id=1, source_target_pairs={{0,4},{4,8},{8,12},{12,16},{16,20},{20,24},{24,28},{1,5},{5,9},{9,... | collective-permute-start | bytes 36872 | tf_op jit(solution)/shard_map/ppermute | solution.py:998
  14.4 0.7 exp.3
  15.2 0.8 reshape.88
  16.0 0.7 copy.50
  16.9 0.7 sub.3
  17.6 0.8 fusion.8
  20.0 1.4 pad_maximum_fusion.3.refs_13_.taps_ref
  21.4 2.2 pad_maximum_fusion.wcat_ref
  24.1 0.9 collective-permute-start.3
  25.0 1.0 collective-permute-start.2
  26.7 1.0 collective-permute-done.4
  27.6 0.9 collective-permute-done.3
  31.7 0.7 copy.54.refs_12_
  33.2 23.0 %front.1 = (bf16[2048,768]{1,0:T(8,128)(2,1)}, bf16[8,768]{1,0:T(8,128)(2,1)}, bf16[2048,384]{1,0:T(8,128)(2,1)}, bf16[2048,512]{1,0:T(8,128)(2,1)}, bf16[2048,5...) custom-call(s32[3]{0:T(128)} %pad_add_fusion.at_ref, ...), custom_call_target="tpu_custom_call" | custom-call | flops 24999999488 | bytes 1 | tf_op jit(solution)/shard_map/front/pallas_call | solution.py:975
  56.3 1.8 collective-permute-start.7
  58.1 0.7 collective-permute-start.8
  58.7 3.1 %collective-permute-start.9 = (f32[72,384]{1,0:T(8,128)}, f32[72,384]{1,0:T(8,128)S(1)}, u32[]{:S(2)}, u32[]{:S(2)}) collective-permute-start(f32[72,384]{1,0:T(8,128)} %get-tuple-element.157), channel_id=1, source_target_pairs={{0,8},{4,12},{16,24},{20,28},{8,0},{12,4},{24,16},{28,20},{1,9},{5... | collective-permute-start | bytes 331784 | tf_op jit(solution)/shard_map/ppermute | solution.py:1008
  62.5 8.7 %inner.1 = (f32[2048,384]{1,0:T(8,128)}, bf16[2048,384]{1,0:T(8,128)(2,1)}) custom-call(bf16[2048,512]{1,0:T(8,128)(2,1)} %get-tuple-element.141.act_ref.bc_ref, f32[2048,128]{1,0:T(8,128)} %get-tuple-element.143.pack_ref, f32[8,2048]{1,0:T(8,128)} %get-tuple-element.149.segrow_ref, f32[16,2048]{1,0:T(8,128)} %get-tuple-element.150.rowp_ref, ...), custom_call_target="tpu_custom_call" | custom-call | flops 6000000000 | bytes 1 | tf_op jit(solution)/shard_map/inner/pallas_call | solution.py:975
  71.9 9.3 %merge.1 = (bf16[2048,384]{1,0:T(8,128)(2,1)}, f32[8,2048]{1,0:T(8,128)}, bf16[16,64,768]{2,1,0:T(8,128)(2,1)}) custom-call(s32[3]{0:T(128)} %pad_add_fusion.at_ref, bf16[2048,512]{1,0:T(8,128)(2,1)} %get-tuple-element.141.act_ref.bc_ref, f32[2048,128]{1,0:T(8,128)} %get-tuple-element.143.pack_ref, f32[128,128]{1,0:T(8,128)} %get-tuple-element.144.tot_ref, ...), custom_call_target="tpu_custom_call" | custom-call | flops 6000000000 | bytes 1 | tf_op jit(solution)/shard_map/merge/pallas_call | solution.py:975
  81.8 1.2 collective-permute-start.12
  83.2 2.4 collective-permute-done.13.rest_3_
  85.6 1.6 collective-permute-done.12.rest_2_
  87.9 13.4 %turn.1 = (bf16[1024,768]{1,0:T(8,128)(2,1)}, bf16[2048,384]{1,0:T(8,128)(2,1)}, bf16[2048,384]{1,0:T(8,128)(2,1)}, bf16[2048,384]{1,0:T(8,128)(2,1)}, f32[8,384...) custom-call(bf16[2048,384]{1,0:T(8,128)(2,1)} %get-tuple-element.159.y_ref, ...), custom_call_target="tpu_custom_call" | custom-call | flops 4000000000 | bytes 1 | tf_op jit(solution)/shard_map/turn/pallas_call | solution.py:975
  102.0 10.5 %adjoint.1 = (bf16[256,768]{1,0:T(8,128)(2,1)}, bf16[256,768]{1,0:T(8,128)(2,1)}, bf16[256,768]{1,0:T(8,128)(2,1)}, bf16[256,768]{1,0:T(8,128)(2,1)}, f32[16,64,...) custom-call(s32[3]{0:T(128)} %pad_add_fusion.at_ref, ...), custom_call_target="tpu_custom_call" | custom-call | flops 100000000 | bytes 1 | tf_op jit(solution)/shard_map/adjoint/pallas_call | solution.py:975
  112.8 0.9 collective-permute-start.19
  113.7 0.8 collective-permute-start.20
  114.5 3.0 %collective-permute-start.14 = (f32[72,384]{1,0:T(8,128)}, f32[72,384]{1,0:T(8,128)S(1)}, u32[]{:S(2)}, u32[]{:S(2)}) collective-permute-start(f32[72,384]{1,0:T(8,128)} %get-tuple-element.181), channel_id=1, source_target_pairs={{0,4},{8,12},{16,20},{24,28},{4,0},{12,8},{20,16},{28,24},{1,5},{9... | collective-permute-start | bytes 331784 | tf_op jit(solution)/shard_map/ppermute | solution.py:1008
  118.2 3.1 %collective-permute-done.14.rest_0_ = f32[72,384]{1,0:T(8,128)S(1)} collective-permute-done((f32[72,384]{1,0:T(8,128)}, f32[72,384]{1,0:T(8,128)S(1)}, u32[]{:S(2)}, u32[]{:S(2)}) %collective-permute-start.14) | collective-permute-done | bytes 110624 | tf_op jit(solution)/shard_map/ppermute | solution.py:1008
  121.3 3.3 %collective-permute-start.16 = (f32[72,384]{1,0:T(8,128)}, f32[72,384]{1,0:T(8,128)S(1)}, u32[]{:S(2)}, u32[]{:S(2)}) collective-permute-start(f32[72,384]{1,0:T(8,128)} %get-tuple-element.183), channel_id=1, source_target_pairs={{0,8},{4,12},{16,24},{20,28},{8,0},{12,4},{24,16},{28,20},{1,9},{5... | collective-permute-start | bytes 331784 | tf_op jit(solution)/shard_map/ppermute | solution.py:1008
  124.7 0.7 collective-permute-start.17
  125.3 17.6 %mid.1 = (bf16[2048,384]{1,0:T(8,128)(2,1)}, f32[2048,128]{1,0:T(8,128)}, f32[2048,128]{1,0:T(8,128)}) custom-call(bf16[2048,512]{1,0:T(8,128)(2,1)} %get-tuple-element.141.act_ref.bc_ref, f32[2048,128]{1,0:T(8,128)} %get-tuple-element.143.pack_ref, f32[8,2048]{1,0:T(8,128)} %get-tuple-element.149.segrow_ref, f32[16,2048]{1,0:T(8,128)} %get-tuple-element.169.rowa_ref, ...), custom_call_target="tpu_custom_call" | custom-call | flops 100000000 | bytes 1 | tf_op jit(solution)/shard_map/mid/pallas_call | solution.py:975
  143.6 32.8 %back.1 = (bf16[2,512,768]{2,1,0:T(8,128)(2,1)}, bf16[2,512,768]{2,1,0:T(8,128)(2,1)}, bf16[96,640]{1,0:T(8,128)(2,1)}, bf16[96,640]{1,0:T(8,128)(2,1)}, bf16[96...) custom-call(s32[3]{0:T(128)} %pad_add_fusion.at_ref, ...), custom_call_target="tpu_custom_call" | custom-call | flops 100000000 | bytes 1 | tf_op jit(solution)/shard_map/back/pallas_call | solution.py:975
  176.5 0.7 copy-done.7
  177.4 3.4 %collective-permute-start.22 = (bf16[96,640]{1,0:T(8,128)(2,1)}, bf16[96,640]{1,0:T(8,128)(2,1)S(1)}, u32[]{:S(2)}, u32[]{:S(2)}) collective-permute-start(bf16[96,640]{1,0:T(8,128)(2,1)} %get-tuple-element.201), channel_id=1, source_target_pairs={{0,4},{4,0},{8,12},{12,8},{16,20},{20,16},{24,28},{28,24},{1,5},{5... | collective-permute-start | bytes 368648 | tf_op jit(solution)/shard_map/ppermute | solution.py:1014
  180.8 3.5 %collective-permute-start.23 = (bf16[96,640]{1,0:T(8,128)(2,1)}, bf16[96,640]{1,0:T(8,128)(2,1)S(1)}, u32[]{:S(2)}, u32[]{:S(2)}) collective-permute-start(bf16[96,640]{1,0:T(8,128)(2,1)} %get-tuple-element.202), channel_id=1, source_target_pairs={{0,8},{4,12},{8,0},{12,4},{16,24},{20,28},{24,16},{28,20},{1,9},{5... | collective-permute-start | bytes 368648 | tf_op jit(solution)/shard_map/ppermute | solution.py:1014
  184.7 3.2 %collective-permute-start.25 = (bf16[96,640]{1,0:T(8,128)(2,1)}, bf16[96,640]{1,0:T(8,128)(2,1)}, u32[]{:S(2)}, u32[]{:S(2)}) collective-permute-start(bf16[96,640]{1,0:T(8,128)(2,1)} %get-tuple-element.204), channel_id=1, source_target_pairs={{0,16},{4,20},{8,24},{12,28},{16,0},{20,4},{24,8},{28,12},{1,17},{... | collective-permute-start | bytes 368648 | tf_op jit(solution)/shard_map/ppermute | solution.py:1014
  188.0 2.0 collective-permute-start.26
  190.0 1.9 collective-permute-start.27
  191.9 3.4 %collective-permute-done.24 = bf16[96,640]{1,0:T(8,128)(2,1)S(1)} collective-permute-done((bf16[96,640]{1,0:T(8,128)(2,1)}, bf16[96,640]{1,0:T(8,128)(2,1)S(1)}, u32[]{:S(2)}, u32[]{:S(2)}) %collective-permute-start.24) | collective-permute-done | bytes 122912 | tf_op jit(solution)/shard_map/ppermute | solution.py:1014
  195.3 1.6 collective-permute-start.28
  197.0 9.5 %collective-permute-done.26 = bf16[96,640]{1,0:T(8,128)(2,1)} collective-permute-done((bf16[96,640]{1,0:T(8,128)(2,1)}, bf16[96,640]{1,0:T(8,128)(2,1)}, u32[]{:S(2)}, u32[]{:S(2)}) %collective-permute-start.26) | collective-permute-done | bytes 122912 | tf_op jit(solution)/shard_map/ppermute | solution.py:1014
  206.5 1.3 convert_add_fusion.2
  207.7 1.0 collective-permute-start.30
  208.8 1.2 collective-permute-start.29
  210.0 5.5 %collective-permute-done.30 = f32[96,256]{1,0:T(8,128)S(1)} collective-permute-done((f32[96,256]{1,0:T(8,128)S(1)}, f32[96,256]{1,0:T(8,128)S(1)}, u32[]{:S(2)}, u32[]{:S(2)}) %collective-permute-start.30) | collective-permute-done | bytes 98336 | tf_op jit(solution)/shard_map/ppermute | solution.py:1021
  216.1 1.7 convert_add_fusion
  217.8 0.9 collective-permute-start.39
  218.7 2.6 %collective-permute-start.33 = (bf16[96,640]{1,0:T(8,128)(2,1)S(1)}, bf16[96,640]{1,0:T(8,128)(2,1)S(1)}, u32[]{:S(2)}, u32[]{:S(2)}) collective-permute-start(bf16[96,640]{1,0:T(8,128)(2,1)S(1)} %pad_maximum_fusion.1.refs_0_), channel_id=1, source_target_pairs={{0,8},{4,12},{8,0},{12,4},{16,24},{20,28},{24,16},{28,20},{1,9},{5... | collective-permute-start | bytes 368648 | tf_op jit(solution)/shard_map/ppermute | solution.py:1014
  221.3 2.7 %collective-permute-start.38 = (bf16[96,640]{1,0:T(8,128)(2,1)S(1)}, bf16[96,640]{1,0:T(8,128)(2,1)}, u32[]{:S(2)}, u32[]{:S(2)}) collective-permute-start(bf16[96,640]{1,0:T(8,128)(2,1)S(1)} %pad_maximum_fusion.1.refs_0_), channel_id=1, source_target_pairs={{0,28},{4,24},{8,20},{12,16},{16,12},{20,8},{24,4},{28,0},{1,29},{... | collective-permute-start | bytes 368648 | tf_op jit(solution)/shard_map/ppermute | solution.py:1014
  224.0 1.5 collective-permute-start.37
  226.1 3.5 %collective-permute-start.35 = (bf16[96,640]{1,0:T(8,128)(2,1)S(1)}, bf16[96,640]{1,0:T(8,128)(2,1)}, u32[]{:S(2)}, u32[]{:S(2)}) collective-permute-start(bf16[96,640]{1,0:T(8,128)(2,1)S(1)} %pad_maximum_fusion.1.refs_0_), channel_id=1, source_target_pairs={{0,16},{4,20},{8,24},{12,28},{16,0},{20,4},{24,8},{28,12},{1,17},{... | collective-permute-start | bytes 368648 | tf_op jit(solution)/shard_map/ppermute | solution.py:1014
  229.6 1.5 convert_add_fusion.1
  231.1 1.1 convert_element_type.101
  232.2 1.1 convert_element_type.102
  233.3 1.0 convert_element_type.95
  234.4 4.9 %collective-permute-start.34 = (bf16[96,640]{1,0:T(8,128)(2,1)S(1)}, bf16[96,640]{1,0:T(8,128)(2,1)S(1)}, u32[]{:S(2)}, u32[]{:S(2)}) collective-permute-start(bf16[96,640]{1,0:T(8,128)(2,1)S(1)} %pad_maximum_fusion.1.refs_0_), channel_id=1, source_target_pairs={{0,12},{4,8},{8,4},{12,0},{16,28},{20,24},{24,20},{28,16},{1,13},{... | collective-permute-start | bytes 368648 | tf_op jit(solution)/shard_map/ppermute | solution.py:1014
  239.3 1.3 collective-permute-start.32
  240.6 1.1 fusion
  241.6 2.3 collective-permute-done.36.refs_5_
  244.0 1.4 collective-permute-done.35.refs_4_
  245.4 1.9 collective-permute-done.34.refs_3_
  248.2 5.5 %finish.1 = (f32[768]{0:T(1024)}, f32[768,384]{1,0:T(8,128)}, f32[768,128]{1,0:T(8,128)}, f32[6,2,768]{2,1,0:T(2,128)}, f32[2,6]{1,0:T(2,128)}, /*index=5*/f32[1...) custom-call(s32[3]{0:T(128)} %pad_add_fusion.at_ref, ...), custom_call_target="tpu_custom_call" | custom-call | flops 3000000000 | bytes 1 | tf_op jit(solution)/shard_map/finish/pallas_call | solution.py:975
  (138 shorter events, 15.1 us)
Async XLA Ops:
  7.2 55.3 %all-gather.2.cloned.1.call-start = ((), (), s32[]{:S(2)}) async-start(), calls=%async_computation.1 | async-start | bytes 3932160 | tf_op jit(solution)/shard_map/all_gather | solution.py:1134
  7.2 21.9 %collective-permute-start = (bf16[512,768]{1,0:T(8,128)(2,1)}, bf16[512,768]{1,0:T(8,128)(2,1)S(1)}, u32[]{:S(2)}, u32[]{:S(2)}) collective-permute-start(bf16[512,768]{1,0:T(8,128)(2,1)} %refs_10_.1), channel_id=1, source_target_pairs={{0,2},{1,3},{2,0},{3,1},{4,6},{5,7},{6,4},{7,5},{8,10},{9,11},{10,... | collective-permute-start | bytes 2359304 | tf_op jit(solution)/shard_map/ppermute | solution.py:1014
  11.0 13.2 %collective-permute-start.1 = (bf16[8,768]{1,0:T(8,128)(2,1)S(1)}, bf16[8,768]{1,0:T(8,128)(2,1)S(1)}, u32[]{:S(2)}, u32[]{:S(2)}) collective-permute-start(bf16[8,768]{1,0:T(8,128)(2,1)S(1)} %slice.28), channel_id=1, source_target_pairs={{0,4},{4,8},{8,12},{12,16},{16,20},{20,24},{24,28},{1,5},{5,9},{9,... | collective-permute-start | bytes 36872 | tf_op jit(solution)/shard_map/ppermute | solution.py:998
  19.9 9.3 %copy-start.1 = (bf16[512,768]{1,0:T(8,128)(2,1)S(1)}, bf16[512,768]{1,0:T(8,128)(2,1)}, u32[]{:S(2)}) copy-start(bf16[512,768]{1,0:T(8,128)(2,1)} %refs_10_.1) | copy-start | bytes 2359300
  19.9 9.9 %copy-start.16 = (f32[384]{0:T(512)S(1)}, f32[384]{0:T(512)}, u32[]{:S(2)}) copy-start(f32[384]{0:T(512)} %param.35) | copy-start | bytes 4612
  19.9 10.4 %copy-start.15 = (f32[768]{0:T(1024)S(1)}, f32[768]{0:T(1024)}, u32[]{:S(2)}) copy-start(f32[768]{0:T(1024)} %param.25) | copy-start | bytes 9220
  19.9 11.0 %copy-start.17 = (f32[6]{0:T(128)S(1)}, f32[6]{0:T(128)}, u32[]{:S(2)}) copy-start(f32[6]{0:T(128)} %param.34) | copy-start | bytes 76
  20.0 12.9 %copy-start.3 = (bf16[768,128]{1,0:T(8,128)(2,1)}, bf16[768,128]{1,0:T(8,128)(2,1)S(1)}, u32[]{:S(2)}) copy-start(bf16[768,128]{1,0:T(8,128)(2,1)S(1)} %pad.28.refs_9_) | copy-start | bytes 589828
  24.1 3.5 %collective-permute-start.4 = (bf16[8,768]{1,0:T(8,128)(2,1)S(1)}, bf16[8,768]{1,0:T(8,128)(2,1)S(1)}, u32[]{:S(2)}, u32[]{:S(2)}) collective-permute-start(bf16[8,768]{1,0:T(8,128)(2,1)S(1)} %collective-permute-done.1), channel_id=1, source_target_pairs={{0,3},{1,2},{2,1},{3,0},{4,7},{5,6},{6,5},{7,4},{8,11},{9,10},{10,... | collective-permute-start | bytes 36872 | tf_op jit(solution)/shard_map/ppermute | solution.py:1014
  24.1 4.4 %collective-permute-start.3 = (bf16[8,768]{1,0:T(8,128)(2,1)S(1)}, bf16[8,768]{1,0:T(8,128)(2,1)S(1)}, u32[]{:S(2)}, u32[]{:S(2)}) collective-permute-start(bf16[8,768]{1,0:T(8,128)(2,1)S(1)} %collective-permute-done.1), channel_id=1, source_target_pairs={{0,2},{1,3},{2,0},{3,1},{4,6},{5,7},{6,4},{7,5},{8,10},{9,11},{10,... | collective-permute-start | bytes 36872 | tf_op jit(solution)/shard_map/ppermute | solution.py:1014
  25.0 3.5 %collective-permute-start.2 = (bf16[8,768]{1,0:T(8,128)(2,1)S(1)}, bf16[8,768]{1,0:T(8,128)(2,1)S(1)}, u32[]{:S(2)}, u32[]{:S(2)}) collective-permute-start(bf16[8,768]{1,0:T(8,128)(2,1)S(1)} %collective-permute-done.1), channel_id=1, source_target_pairs={{0,1},{1,0},{2,3},{3,2},{4,5},{5,4},{6,7},{7,6},{8,9},{9,8},{10,11... | collective-permute-start | bytes 36872 | tf_op jit(solution)/shard_map/ppermute | solution.py:1014
  29.1 3.7 %copy-start.18 = (bf16[512,768]{1,0:T(8,128)(2,1)}, bf16[512,768]{1,0:T(8,128)(2,1)S(1)}, u32[]{:S(2)}) copy-start(bf16[512,768]{1,0:T(8,128)(2,1)S(1)} %collective-permute-done.refs_2_) | copy-start | bytes 2359300
  29.1 200.4 %all-reduce.9.cloned.1.call-start = ((), (), s32[]{:S(2)}) async-start(), calls=%async_computation.3 | async-start | bytes 2359296 | tf_op jit(solution)/shard_map/psum | solution.py:1400
  29.2 3.1 %collective-permute-start.5 = (bf16[512,768]{1,0:T(8,128)(2,1)S(1)}, bf16[512,768]{1,0:T(8,128)(2,1)S(1)}, u32[]{:S(2)}, u32[]{:S(2)}) collective-permute-start(bf16[512,768]{1,0:T(8,128)(2,1)S(1)} %copy-done.1), channel_id=1, source_target_pairs={{0,1},{1,0},{2,3},{3,2},{4,5},{5,4},{6,7},{7,6},{8,9},{9,8},{10,11... | collective-permute-start | bytes 2359304 | tf_op jit(solution)/shard_map/ppermute | solution.py:1014
  29.3 3.5 %collective-permute-start.6 = (bf16[512,768]{1,0:T(8,128)(2,1)S(1)}, bf16[512,768]{1,0:T(8,128)(2,1)}, u32[]{:S(2)}, u32[]{:S(2)}) collective-permute-start(bf16[512,768]{1,0:T(8,128)(2,1)S(1)} %collective-permute-done.refs_2_), channel_id=1, source_target_pairs={{0,1},{1,0},{2,3},{3,2},{4,5},{5,4},{6,7},{7,6},{8,9},{9,8},{10,11... | collective-permute-start | bytes 2359304 | tf_op jit(solution)/shard_map/ppermute | solution.py:1014
  32.3 0.9 copy-start.20
  56.3 14.9 %collective-permute-start.7 = (f32[72,384]{1,0:T(8,128)}, f32[72,384]{1,0:T(8,128)S(1)}, u32[]{:S(2)}, u32[]{:S(2)}) collective-permute-start(f32[72,384]{1,0:T(8,128)} %get-tuple-element.155), channel_id=1, source_target_pairs={{0,4},{8,12},{16,20},{24,28},{4,0},{12,8},{20,16},{28,24},{1,5},{9... | collective-permute-start | bytes 331784 | tf_op jit(solution)/shard_map/ppermute | solution.py:1008
  58.1 13.1 %collective-permute-start.8 = (f32[72,384]{1,0:T(8,128)}, f32[72,384]{1,0:T(8,128)S(1)}, u32[]{:S(2)}, u32[]{:S(2)}) collective-permute-start(f32[72,384]{1,0:T(8,128)} %get-tuple-element.156), channel_id=1, source_target_pairs={{4,8},{12,16},{20,24},{8,4},{16,12},{24,20},{5,9},{13,17},{21,25},... | collective-permute-start | bytes 331784 | tf_op jit(solution)/shard_map/ppermute | solution.py:1008
  58.7 12.4 %collective-permute-start.9 = (f32[72,384]{1,0:T(8,128)}, f32[72,384]{1,0:T(8,128)S(1)}, u32[]{:S(2)}, u32[]{:S(2)}) collective-permute-start(f32[72,384]{1,0:T(8,128)} %get-tuple-element.157), channel_id=1, source_target_pairs={{0,8},{4,12},{16,24},{20,28},{8,0},{12,4},{24,16},{28,20},{1,9},{5... | collective-permute-start | bytes 331784 | tf_op jit(solution)/shard_map/ppermute | solution.py:1008
  61.8 9.4 %collective-permute-start.10 = (f32[72,384]{1,0:T(8,128)}, f32[72,384]{1,0:T(8,128)S(1)}, u32[]{:S(2)}, u32[]{:S(2)}) collective-permute-start(f32[72,384]{1,0:T(8,128)} %get-tuple-element.158), channel_id=1, source_target_pairs={{8,16},{12,20},{16,8},{20,12},{9,17},{13,21},{17,9},{21,13},{10,18... | collective-permute-start | bytes 331784 | tf_op jit(solution)/shard_map/ppermute | solution.py:1008
  81.2 4.4 %collective-permute-start.13 = (f32[8,2048]{1,0:T(8,128)}, f32[8,2048]{1,0:T(8,128)S(1)}, u32[]{:S(2)}, u32[]{:S(2)}) collective-permute-start(f32[8,2048]{1,0:T(8,128)} %get-tuple-element.161.rest_0_), channel_id=1, source_target_pairs={{0,3},{1,2},{2,1},{3,0},{4,7},{5,6},{6,5},{7,4},{8,11},{9,10},{10,... | collective-permute-start | bytes 196616 | tf_op jit(solution)/shard_map/ppermute | solution.py:1333
  81.8 5.4 %collective-permute-start.12 = (f32[8,2048]{1,0:T(8,128)}, f32[8,2048]{1,0:T(8,128)S(1)}, u32[]{:S(2)}, u32[]{:S(2)}) collective-permute-start(f32[8,2048]{1,0:T(8,128)} %get-tuple-element.161.rest_0_), channel_id=1, source_target_pairs={{0,2},{1,3},{2,0},{3,1},{4,6},{5,7},{6,4},{7,5},{8,10},{9,11},{10,... | collective-permute-start | bytes 196616 | tf_op jit(solution)/shard_map/ppermute | solution.py:1333
  83.1 4.1 %collective-permute-start.11 = (f32[8,2048]{1,0:T(8,128)}, f32[8,2048]{1,0:T(8,128)S(1)}, u32[]{:S(2)}, u32[]{:S(2)}) collective-permute-start(f32[8,2048]{1,0:T(8,128)} %get-tuple-element.161.rest_0_), channel_id=1, source_target_pairs={{0,1},{1,0},{2,3},{3,2},{4,5},{5,4},{6,7},{7,6},{8,9},{9,8},{10,11... | collective-permute-start | bytes 196616 | tf_op jit(solution)/shard_map/ppermute | solution.py:1333
  85.6 1.6 copy-start.28
  101.3 132.0 %reduce-scatter.2.cloned.1.call-start = ((), (), s32[]{:S(2)}) async-start(), calls=%async_computation.2 | async-start | bytes 1966080 | tf_op jit(solution)/shard_map/reduce_scatter | solution.py:1401
  112.6 63.8 %collective-permute-start.18 = (bf16[256,768]{1,0:T(8,128)(2,1)}, bf16[256,768]{1,0:T(8,128)(2,1)S(1)}, u32[]{:S(2)}, u32[]{:S(2)}) collective-permute-start(bf16[256,768]{1,0:T(8,128)(2,1)} %get-tuple-element.196), channel_id=1, source_target_pairs={{0,1},{1,0},{2,3},{3,2},{4,5},{5,4},{6,7},{7,6},{8,9},{9,8},{10,11... | collective-permute-start | bytes 1179656 | tf_op jit(solution)/shard_map/ppermute | solution.py:1014
  112.8 63.6 %collective-permute-start.19 = (bf16[256,768]{1,0:T(8,128)(2,1)}, bf16[256,768]{1,0:T(8,128)(2,1)S(1)}, u32[]{:S(2)}, u32[]{:S(2)}) collective-permute-start(bf16[256,768]{1,0:T(8,128)(2,1)} %get-tuple-element.197), channel_id=1, source_target_pairs={{0,2},{1,3},{2,0},{3,1},{4,6},{5,7},{6,4},{7,5},{8,10},{9,11},{10,... | collective-permute-start | bytes 1179656 | tf_op jit(solution)/shard_map/ppermute | solution.py:1014
  113.7 62.8 %collective-permute-start.20 = (bf16[256,768]{1,0:T(8,128)(2,1)}, bf16[256,768]{1,0:T(8,128)(2,1)S(1)}, u32[]{:S(2)}, u32[]{:S(2)}) collective-permute-start(bf16[256,768]{1,0:T(8,128)(2,1)} %get-tuple-element.198), channel_id=1, source_target_pairs={{0,3},{1,2},{2,1},{3,0},{4,7},{5,6},{6,5},{7,4},{8,11},{9,10},{10,... | collective-permute-start | bytes 1179656 | tf_op jit(solution)/shard_map/ppermute | solution.py:1014
  114.5 6.8 %collective-permute-start.14 = (f32[72,384]{1,0:T(8,128)}, f32[72,384]{1,0:T(8,128)S(1)}, u32[]{:S(2)}, u32[]{:S(2)}) collective-permute-start(f32[72,384]{1,0:T(8,128)} %get-tuple-element.181), channel_id=1, source_target_pairs={{0,4},{8,12},{16,20},{24,28},{4,0},{12,8},{20,16},{28,24},{1,5},{9... | collective-permute-start | bytes 331784 | tf_op jit(solution)/shard_map/ppermute | solution.py:1008
  117.6 7.1 %collective-permute-start.15 = (f32[72,384]{1,0:T(8,128)}, f32[72,384]{1,0:T(8,128)S(1)}, u32[]{:S(2)}, u32[]{:S(2)}) collective-permute-start(f32[72,384]{1,0:T(8,128)} %get-tuple-element.182), channel_id=1, source_target_pairs={{4,8},{12,16},{20,24},{8,4},{16,12},{24,20},{5,9},{13,17},{21,25},... | collective-permute-start | bytes 331784 | tf_op jit(solution)/shard_map/ppermute | solution.py:1008
  121.3 21.5 %copy-start.11 = (f32[72,384]{1,0:T(8,128)}, f32[72,384]{1,0:T(8,128)S(1)}, u32[]{:S(2)}) copy-start(f32[72,384]{1,0:T(8,128)S(1)} %collective-permute-done.14.rest_0_) | copy-start | bytes 331780
  121.3 21.6 %collective-permute-start.16 = (f32[72,384]{1,0:T(8,128)}, f32[72,384]{1,0:T(8,128)S(1)}, u32[]{:S(2)}, u32[]{:S(2)}) collective-permute-start(f32[72,384]{1,0:T(8,128)} %get-tuple-element.183), channel_id=1, source_target_pairs={{0,8},{4,12},{16,24},{20,28},{8,0},{12,4},{24,16},{28,20},{1,9},{5... | collective-permute-start | bytes 331784 | tf_op jit(solution)/shard_map/ppermute | solution.py:1008
  124.7 18.2 %copy-start.12 = (f32[72,384]{1,0:T(8,128)}, f32[72,384]{1,0:T(8,128)S(1)}, u32[]{:S(2)}) copy-start(f32[72,384]{1,0:T(8,128)S(1)} %collective-permute-done.15.rest_1_) | copy-start | bytes 331780
  124.7 18.2 %collective-permute-start.17 = (f32[72,384]{1,0:T(8,128)}, f32[72,384]{1,0:T(8,128)S(1)}, u32[]{:S(2)}, u32[]{:S(2)}) collective-permute-start(f32[72,384]{1,0:T(8,128)} %get-tuple-element.184), channel_id=1, source_target_pairs={{8,16},{12,20},{16,8},{20,12},{9,17},{13,21},{17,9},{21,13},{10,18... | collective-permute-start | bytes 331784 | tf_op jit(solution)/shard_map/ppermute | solution.py:1008
  176.4 39.6 %copy-start = (bf16[2,512,768]{2,1,0:T(8,128)(2,1)S(1)}, bf16[2,512,768]{2,1,0:T(8,128)(2,1)}, u32[]{:S(2)}) copy-start(bf16[2,512,768]{2,1,0:T(8,128)(2,1)} %get-tuple-element.185) | copy-start | bytes 4718596
  176.4 0.7 copy-start.7
  176.4 0.9 copy-start.8
  176.5 1.0 copy-start.9
  177.3 38.7 %collective-permute-start.21 = (bf16[2,512,768]{2,1,0:T(8,128)(2,1)}, bf16[2,512,768]{2,1,0:T(8,128)(2,1)S(1)}, u32[]{:S(2)}, u32[]{:S(2)}) collective-permute-start(bf16[2,512,768]{2,1,0:T(8,128)(2,1)} %get-tuple-element.199), channel_id=1, source_target_pairs={{0,1},{1,0},{2,3},{3,2},{4,5},{5,4},{6,7},{7,6},{8,9},{9,8},{10,11... | collective-permute-start | bytes 4718600 | tf_op jit(solution)/shard_map/ppermute | solution.py:1014
  177.4 10.6 %collective-permute-start.22 = (bf16[96,640]{1,0:T(8,128)(2,1)}, bf16[96,640]{1,0:T(8,128)(2,1)S(1)}, u32[]{:S(2)}, u32[]{:S(2)}) collective-permute-start(bf16[96,640]{1,0:T(8,128)(2,1)} %get-tuple-element.201), channel_id=1, source_target_pairs={{0,4},{4,0},{8,12},{12,8},{16,20},{20,16},{24,28},{28,24},{1,5},{5... | collective-permute-start | bytes 368648 | tf_op jit(solution)/shard_map/ppermute | solution.py:1014
  180.8 9.2 %collective-permute-start.23 = (bf16[96,640]{1,0:T(8,128)(2,1)}, bf16[96,640]{1,0:T(8,128)(2,1)S(1)}, u32[]{:S(2)}, u32[]{:S(2)}) collective-permute-start(bf16[96,640]{1,0:T(8,128)(2,1)} %get-tuple-element.202), channel_id=1, source_target_pairs={{0,8},{4,12},{8,0},{12,4},{16,24},{20,28},{24,16},{28,20},{1,9},{5... | collective-permute-start | bytes 368648 | tf_op jit(solution)/shard_map/ppermute | solution.py:1014
  184.3 11.0 %collective-permute-start.24 = (bf16[96,640]{1,0:T(8,128)(2,1)}, bf16[96,640]{1,0:T(8,128)(2,1)S(1)}, u32[]{:S(2)}, u32[]{:S(2)}) collective-permute-start(bf16[96,640]{1,0:T(8,128)(2,1)} %get-tuple-element.203), channel_id=1, source_target_pairs={{0,12},{4,8},{8,4},{12,0},{16,28},{20,24},{24,20},{28,16},{1,13},{... | collective-permute-start | bytes 368648 | tf_op jit(solution)/shard_map/ppermute | solution.py:1014
  184.7 12.2 %collective-permute-start.25 = (bf16[96,640]{1,0:T(8,128)(2,1)}, bf16[96,640]{1,0:T(8,128)(2,1)}, u32[]{:S(2)}, u32[]{:S(2)}) collective-permute-start(bf16[96,640]{1,0:T(8,128)(2,1)} %get-tuple-element.204), channel_id=1, source_target_pairs={{0,16},{4,20},{8,24},{12,28},{16,0},{20,4},{24,8},{28,12},{1,17},{... | collective-permute-start | bytes 368648 | tf_op jit(solution)/shard_map/ppermute | solution.py:1014
  188.0 18.5 %collective-permute-start.26 = (bf16[96,640]{1,0:T(8,128)(2,1)}, bf16[96,640]{1,0:T(8,128)(2,1)}, u32[]{:S(2)}, u32[]{:S(2)}) collective-permute-start(bf16[96,640]{1,0:T(8,128)(2,1)} %get-tuple-element.205), channel_id=1, source_target_pairs={{0,20},{4,16},{8,28},{12,24},{16,4},{20,0},{24,12},{28,8},{1,21},{... | collective-permute-start | bytes 368648 | tf_op jit(solution)/shard_map/ppermute | solution.py:1014
  190.0 16.4 %collective-permute-start.27 = (bf16[96,640]{1,0:T(8,128)(2,1)}, bf16[96,640]{1,0:T(8,128)(2,1)}, u32[]{:S(2)}, u32[]{:S(2)}) collective-permute-start(bf16[96,640]{1,0:T(8,128)(2,1)} %get-tuple-element.206), channel_id=1, source_target_pairs={{0,24},{4,28},{8,16},{12,20},{16,8},{20,12},{24,0},{28,4},{1,25},{... | collective-permute-start | bytes 368648 | tf_op jit(solution)/shard_map/ppermute | solution.py:1014
  195.3 11.1 %collective-permute-start.28 = (bf16[96,640]{1,0:T(8,128)(2,1)}, bf16[96,640]{1,0:T(8,128)(2,1)}, u32[]{:S(2)}, u32[]{:S(2)}) collective-permute-start(bf16[96,640]{1,0:T(8,128)(2,1)} %get-tuple-element.207), channel_id=1, source_target_pairs={{0,28},{4,24},{8,20},{12,16},{16,12},{20,8},{24,4},{28,0},{1,29},{... | collective-permute-start | bytes 368648 | tf_op jit(solution)/shard_map/ppermute | solution.py:1014
  207.7 7.7 %collective-permute-start.30 = (f32[96,256]{1,0:T(8,128)S(1)}, f32[96,256]{1,0:T(8,128)S(1)}, u32[]{:S(2)}, u32[]{:S(2)}) collective-permute-start(f32[96,256]{1,0:T(8,128)S(1)} %slice.38), channel_id=1, source_target_pairs={{0,2},{1,3},{2,0},{3,1},{4,6},{5,7},{6,4},{7,5},{8,10},{9,11},{10,... | collective-permute-start | bytes 294920 | tf_op jit(solution)/shard_map/ppermute | solution.py:1021
  208.8 7.2 %collective-permute-start.31 = (f32[96,256]{1,0:T(8,128)S(1)}, f32[96,256]{1,0:T(8,128)S(1)}, u32[]{:S(2)}, u32[]{:S(2)}) collective-permute-start(f32[96,256]{1,0:T(8,128)S(1)} %slice.38), channel_id=1, source_target_pairs={{0,3},{1,2},{2,1},{3,0},{4,7},{5,6},{6,5},{7,4},{8,11},{9,10},{10,... | collective-permute-start | bytes 294920 | tf_op jit(solution)/shard_map/ppermute | solution.py:1021
  208.8 7.2 %collective-permute-start.29 = (f32[96,256]{1,0:T(8,128)S(1)}, f32[96,256]{1,0:T(8,128)S(1)}, u32[]{:S(2)}, u32[]{:S(2)}) collective-permute-start(f32[96,256]{1,0:T(8,128)S(1)} %slice.38), channel_id=1, source_target_pairs={{0,1},{1,0},{2,3},{3,2},{4,5},{5,4},{6,7},{7,6},{8,9},{9,8},{10,11... | collective-permute-start | bytes 294920 | tf_op jit(solution)/shard_map/ppermute | solution.py:1021
  216.0 13.6 %copy-start.6 = (bf16[256,768]{1,0:T(8,128)(2,1)S(1)}, bf16[256,768]{1,0:T(8,128)(2,1)}, u32[]{:S(2)}) copy-start(bf16[256,768]{1,0:T(8,128)(2,1)} %get-tuple-element.217) | copy-start | bytes 1179652
  217.8 29.5 %collective-permute-start.39 = (bf16[1,512,768]{2,1,0:T(8,128)(2,1)}, bf16[1,512,768]{2,1,0:T(8,128)(2,1)S(1)}, u32[]{:S(2)}, u32[]{:S(2)}) collective-permute-start(bf16[1,512,768]{2,1,0:T(8,128)(2,1)} %get-tuple-element.232), channel_id=1, source_target_pairs={{0,2},{1,3},{2,0},{3,1},{4,6},{5,7},{6,4},{7,5},{8,10},{9,11},{10,... | collective-permute-start | bytes 2359304 | tf_op jit(solution)/shard_map/ppermute | solution.py:1014
  218.7 20.6 %copy-start.10 = (bf16[96,640]{1,0:T(8,128)(2,1)}, bf16[96,640]{1,0:T(8,128)(2,1)S(1)}, u32[]{:S(2)}) copy-start(bf16[96,640]{1,0:T(8,128)(2,1)S(1)} %pad_maximum_fusion.1.refs_0_) | copy-start | bytes 368644
  218.7 6.8 %collective-permute-start.33 = (bf16[96,640]{1,0:T(8,128)(2,1)S(1)}, bf16[96,640]{1,0:T(8,128)(2,1)S(1)}, u32[]{:S(2)}, u32[]{:S(2)}) collective-permute-start(bf16[96,640]{1,0:T(8,128)(2,1)S(1)} %pad_maximum_fusion.1.refs_0_), channel_id=1, source_target_pairs={{0,8},{4,12},{8,0},{12,4},{16,24},{20,28},{24,16},{28,20},{1,9},{5... | collective-permute-start | bytes 368648 | tf_op jit(solution)/shard_map/ppermute | solution.py:1014
  221.3 13.1 %collective-permute-start.38 = (bf16[96,640]{1,0:T(8,128)(2,1)S(1)}, bf16[96,640]{1,0:T(8,128)(2,1)}, u32[]{:S(2)}, u32[]{:S(2)}) collective-permute-start(bf16[96,640]{1,0:T(8,128)(2,1)S(1)} %pad_maximum_fusion.1.refs_0_), channel_id=1, source_target_pairs={{0,28},{4,24},{8,20},{12,16},{16,12},{20,8},{24,4},{28,0},{1,29},{... | collective-permute-start | bytes 368648 | tf_op jit(solution)/shard_map/ppermute | solution.py:1014
  224.0 15.3 %collective-permute-start.37 = (bf16[96,640]{1,0:T(8,128)(2,1)S(1)}, bf16[96,640]{1,0:T(8,128)(2,1)}, u32[]{:S(2)}, u32[]{:S(2)}) collective-permute-start(bf16[96,640]{1,0:T(8,128)(2,1)S(1)} %pad_maximum_fusion.1.refs_0_), channel_id=1, source_target_pairs={{0,24},{4,28},{8,16},{12,20},{16,8},{20,12},{24,0},{28,4},{1,25},{... | collective-permute-start | bytes 368648 | tf_op jit(solution)/shard_map/ppermute | solution.py:1014
  225.4 18.5 %collective-permute-start.36 = (bf16[96,640]{1,0:T(8,128)(2,1)S(1)}, bf16[96,640]{1,0:T(8,128)(2,1)}, u32[]{:S(2)}, u32[]{:S(2)}) collective-permute-start(bf16[96,640]{1,0:T(8,128)(2,1)S(1)} %pad_maximum_fusion.1.refs_0_), channel_id=1, source_target_pairs={{0,20},{4,16},{8,28},{12,24},{16,4},{20,0},{24,12},{28,8},{1,21},{... | collective-permute-start | bytes 368648 | tf_op jit(solution)/shard_map/ppermute | solution.py:1014
  226.1 19.3 %collective-permute-start.35 = (bf16[96,640]{1,0:T(8,128)(2,1)S(1)}, bf16[96,640]{1,0:T(8,128)(2,1)}, u32[]{:S(2)}, u32[]{:S(2)}) collective-permute-start(bf16[96,640]{1,0:T(8,128)(2,1)S(1)} %pad_maximum_fusion.1.refs_0_), channel_id=1, source_target_pairs={{0,16},{4,20},{8,24},{12,28},{16,0},{20,4},{24,8},{28,12},{1,17},{... | collective-permute-start | bytes 368648 | tf_op jit(solution)/shard_map/ppermute | solution.py:1014
  229.6 1.5 copy-start.5
  229.6 2.6 %copy-start.4 = (bf16[768,384]{1,0:T(8,128)(2,1)S(1)}, bf16[768,384]{1,0:T(8,128)(2,1)}, u32[]{:S(2)}) copy-start(bf16[768,384]{1,0:T(8,128)(2,1)} %get-tuple-element.222) | copy-start | bytes 1769476
  232.2 8.4 %copy-start.2 = (bf16[512,768]{1,0:T(8,128)(2,1)S(1)}, bf16[512,768]{1,0:T(8,128)(2,1)}, u32[]{:S(2)}) copy-start(bf16[512,768]{1,0:T(8,128)(2,1)} %refs_10_.1) | copy-start | bytes 2359300
  234.4 12.9 %collective-permute-start.34 = (bf16[96,640]{1,0:T(8,128)(2,1)S(1)}, bf16[96,640]{1,0:T(8,128)(2,1)S(1)}, u32[]{:S(2)}, u32[]{:S(2)}) collective-permute-start(bf16[96,640]{1,0:T(8,128)(2,1)S(1)} %pad_maximum_fusion.1.refs_0_), channel_id=1, source_target_pairs={{0,12},{4,8},{8,4},{12,0},{16,28},{20,24},{24,20},{28,16},{1,13},{... | collective-permute-start | bytes 368648 | tf_op jit(solution)/shard_map/ppermute | solution.py:1014
  239.3 8.0 %collective-permute-start.32 = (bf16[96,640]{1,0:T(8,128)(2,1)S(1)}, bf16[96,640]{1,0:T(8,128)(2,1)S(1)}, u32[]{:S(2)}, u32[]{:S(2)}) collective-permute-start(bf16[96,640]{1,0:T(8,128)(2,1)S(1)} %pad_maximum_fusion.1.refs_0_), channel_id=1, source_target_pairs={{0,4},{4,0},{8,12},{12,8},{16,20},{20,16},{24,28},{28,24},{1,5},{5... | collective-permute-start | bytes 368648 | tf_op jit(solution)/shard_map/ppermute | solution.py:1014
  247.2 0.7 copy-start.23
  247.2 1.0 copy-start.19
  (10 other events, 6.5 us)
Sparse Core Ops, SparseCore 0:
  29.3 30.0 all-gather.1
  101.4 82.5 all-reduce.8
  186.7 30.9 reduce-scatter.1

commit v7 on v6

--- a/solution.py
+++ b/solution.py
@@ -1015,11 +1015,14 @@
 
 
 def sum_over(array, axis):
-    size = lax.axis_size(axis)
-    result = array
-    for k in range(1, size):
-        result = result + lax.ppermute(array, axis, [(i, i ^ k) for i in range(size)])
-    return result
+    rounded = lax.reduce_precision(array, 8, 7)
+    message = rounded.astype(BF16)
+    terms = [rounded]
+    for k in range(1, lax.axis_size(axis)):
+        terms.append(swap(message, axis, k).astype(F32))
+    while len(terms) > 1:
+        terms = [a + b for a, b in zip(terms[::2], terms[1::2])]
+    return terms[0]
 
 
 def per_device(

time: 261 us -> 259 us (level)
    ppermute x3 -> x0, waiting for transfers between devices: 5.95 us -> none  [sum_over(): lax.ppermute(array, axis, [(i, i ^ k) for i in range(size)])]
    ppermute x25 -> x28, waiting for transfers between devices: 20.8 us -> 24.7 us  [swap(): return lax.ppermute(array, axis, [(i, i ^ k) for i in range(n)])]
    ppermute x25 -> x28, starting transfers between devices: 40.8 us -> 42.9 us  [swap(): return lax.ppermute(array, axis, [(i, i ^ k) for i in range(n)])]
where the time goes in v7:
time: 259 us; the launch traced here: 258 us
  Pallas kernels  121 us (47%)
  starting transfers between devices  62.4 us (24%)
  waiting for transfers between devices  32.5 us (13%)
  other arithmetic  16.6 us (6%)
  between operations  14.2 us (5%)
  local copies, waits for them, and re-layouts  11.5 us (4%)
    pallas_call x8, Pallas kernels, call(): pl.pallas_call(kernel, name=name, grid_spec=pltpu.PrefetchScalarGridSpec(...  121 us
    ppermute x28, starting transfers between devices, swap(): return lax.ppermute(array, axis, [(i, i ^ k) for i in range(n)])  42.9 us
    ppermute x28, waiting for transfers between devices, swap(): return lax.ppermute(array, axis, [(i, i ^ k) for i in range(n)])  24.7 us
    ppermute x8, starting transfers between devices, exchange_sides(): arrived.append(lax.ppermute(messages[len(arrived)], 'seq', both))  13.8 us
  transfers between devices with their start and end apart: 43, of which 13 were waited for; matrix products, arithmetic and copies ran while one was open for 9% of the time, Pallas kernels for 36%

profile of v7, /device:TPU:0, one launch (start us, length us, event | category | flops | bytes accessed | tf_op | source)
XLA Modules:
  0.0 258.0 jit_solution(11079707735554485954)
XLA Ops:
  7.2 3.0 %collective-permute-start = (bf16[512,768]{1,0:T(8,128)(2,1)}, bf16[512,768]{1,0:T(8,128)(2,1)S(1)}, u32[]{:S(2)}, u32[]{:S(2)}) collective-permute-start(bf16[512,768]{1,0:T(8,128)(2,1)} %refs_10_.1), channel_id=1, source_target_pairs={{0,2},{1,3},{2,0},{3,1},{4,6},{5,7},{6,4},{7,5},{8,10},{9,11},{10,... | collective-permute-start | bytes 2359304 | tf_op jit(solution)/shard_map/ppermute | solution.py:1014
  10.2 0.7 slice.28
  11.0 3.4 %collective-permute-start.1 = (bf16[8,768]{1,0:T(8,128)(2,1)S(1)}, bf16[8,768]{1,0:T(8,128)(2,1)S(1)}, u32[]{:S(2)}, u32[]{:S(2)}) collective-permute-start(bf16[8,768]{1,0:T(8,128)(2,1)S(1)} %slice.28), channel_id=1, source_target_pairs={{0,4},{4,8},{8,12},{12,16},{16,20},{20,24},{24,28},{1,5},{5,9},{9,... | collective-permute-start | bytes 36872 | tf_op jit(solution)/shard_map/ppermute | solution.py:998
  14.4 0.7 exp.3
  15.2 0.8 reshape.88
  16.0 0.7 copy.50
  16.9 0.7 sub.3
  17.6 0.8 fusion.9
  20.0 1.4 pad_maximum_fusion.3.refs_13_.taps_ref
  21.4 2.2 pad_maximum_fusion.wcat_ref
  24.1 0.9 collective-permute-start.3
  25.0 1.0 collective-permute-start.2
  26.7 1.0 collective-permute-done.4
  27.6 0.9 collective-permute-done.3
  31.7 0.7 copy.54.refs_12_
  33.2 23.0 %front.1 = (bf16[2048,768]{1,0:T(8,128)(2,1)}, bf16[8,768]{1,0:T(8,128)(2,1)}, bf16[2048,384]{1,0:T(8,128)(2,1)}, bf16[2048,512]{1,0:T(8,128)(2,1)}, bf16[2048,5...) custom-call(s32[3]{0:T(128)} %pad_add_fusion.at_ref, ...), custom_call_target="tpu_custom_call" | custom-call | flops 24999999488 | bytes 1 | tf_op jit(solution)/shard_map/front/pallas_call | solution.py:975
  56.3 1.8 collective-permute-start.7
  58.7 3.1 %collective-permute-start.9 = (f32[72,384]{1,0:T(8,128)}, f32[72,384]{1,0:T(8,128)S(1)}, u32[]{:S(2)}, u32[]{:S(2)}) collective-permute-start(f32[72,384]{1,0:T(8,128)} %get-tuple-element.157), channel_id=1, source_target_pairs={{0,8},{4,12},{16,24},{20,28},{8,0},{12,4},{24,16},{28,20},{1,9},{5... | collective-permute-start | bytes 331784 | tf_op jit(solution)/shard_map/ppermute | solution.py:1008
  62.5 8.7 %inner.1 = (f32[2048,384]{1,0:T(8,128)}, bf16[2048,384]{1,0:T(8,128)(2,1)}) custom-call(bf16[2048,512]{1,0:T(8,128)(2,1)} %get-tuple-element.141.act_ref.bc_ref, f32[2048,128]{1,0:T(8,128)} %get-tuple-element.143.pack_ref, f32[8,2048]{1,0:T(8,128)} %get-tuple-element.149.segrow_ref, f32[16,2048]{1,0:T(8,128)} %get-tuple-element.150.rowp_ref, ...), custom_call_target="tpu_custom_call" | custom-call | flops 6000000000 | bytes 1 | tf_op jit(solution)/shard_map/inner/pallas_call | solution.py:975
  71.9 9.3 %merge.1 = (bf16[2048,384]{1,0:T(8,128)(2,1)}, f32[8,2048]{1,0:T(8,128)}, bf16[16,64,768]{2,1,0:T(8,128)(2,1)}) custom-call(s32[3]{0:T(128)} %pad_add_fusion.at_ref, bf16[2048,512]{1,0:T(8,128)(2,1)} %get-tuple-element.141.act_ref.bc_ref, f32[2048,128]{1,0:T(8,128)} %get-tuple-element.143.pack_ref, f32[128,128]{1,0:T(8,128)} %get-tuple-element.144.tot_ref, ...), custom_call_target="tpu_custom_call" | custom-call | flops 6000000000 | bytes 1 | tf_op jit(solution)/shard_map/merge/pallas_call | solution.py:975
  81.8 1.2 collective-permute-start.12
  83.2 2.4 collective-permute-done.13.rest_3_
  85.6 1.6 collective-permute-done.12.rest_2_
  87.9 13.4 %turn.1 = (bf16[1024,768]{1,0:T(8,128)(2,1)}, bf16[2048,384]{1,0:T(8,128)(2,1)}, bf16[2048,384]{1,0:T(8,128)(2,1)}, bf16[2048,384]{1,0:T(8,128)(2,1)}, f32[8,384...) custom-call(bf16[2048,384]{1,0:T(8,128)(2,1)} %get-tuple-element.159.y_ref, ...), custom_call_target="tpu_custom_call" | custom-call | flops 4000000000 | bytes 1 | tf_op jit(solution)/shard_map/turn/pallas_call | solution.py:975
  102.0 10.5 %adjoint.1 = (bf16[256,768]{1,0:T(8,128)(2,1)}, bf16[256,768]{1,0:T(8,128)(2,1)}, bf16[256,768]{1,0:T(8,128)(2,1)}, bf16[256,768]{1,0:T(8,128)(2,1)}, f32[16,64,...) custom-call(s32[3]{0:T(128)} %pad_add_fusion.at_ref, ...), custom_call_target="tpu_custom_call" | custom-call | flops 100000000 | bytes 1 | tf_op jit(solution)/shard_map/adjoint/pallas_call | solution.py:975
  112.8 0.9 collective-permute-start.19
  113.7 0.8 collective-permute-start.20
  114.5 3.0 %collective-permute-start.14 = (f32[72,384]{1,0:T(8,128)}, f32[72,384]{1,0:T(8,128)S(1)}, u32[]{:S(2)}, u32[]{:S(2)}) collective-permute-start(f32[72,384]{1,0:T(8,128)} %get-tuple-element.181), channel_id=1, source_target_pairs={{0,4},{8,12},{16,20},{24,28},{4,0},{12,8},{20,16},{28,24},{1,5},{9... | collective-permute-start | bytes 331784 | tf_op jit(solution)/shard_map/ppermute | solution.py:1008
  118.2 3.1 %collective-permute-done.14.rest_0_ = f32[72,384]{1,0:T(8,128)S(1)} collective-permute-done((f32[72,384]{1,0:T(8,128)}, f32[72,384]{1,0:T(8,128)S(1)}, u32[]{:S(2)}, u32[]{:S(2)}) %collective-permute-start.14) | collective-permute-done | bytes 110624 | tf_op jit(solution)/shard_map/ppermute | solution.py:1008
  121.3 3.3 %collective-permute-start.16 = (f32[72,384]{1,0:T(8,128)}, f32[72,384]{1,0:T(8,128)S(1)}, u32[]{:S(2)}, u32[]{:S(2)}) collective-permute-start(f32[72,384]{1,0:T(8,128)} %get-tuple-element.183), channel_id=1, source_target_pairs={{0,8},{4,12},{16,24},{20,28},{8,0},{12,4},{24,16},{28,20},{1,9},{5... | collective-permute-start | bytes 331784 | tf_op jit(solution)/shard_map/ppermute | solution.py:1008
  124.7 0.7 collective-permute-start.17
  125.3 17.6 %mid.1 = (bf16[2048,384]{1,0:T(8,128)(2,1)}, f32[2048,128]{1,0:T(8,128)}, f32[2048,128]{1,0:T(8,128)}) custom-call(bf16[2048,512]{1,0:T(8,128)(2,1)} %get-tuple-element.141.act_ref.bc_ref, f32[2048,128]{1,0:T(8,128)} %get-tuple-element.143.pack_ref, f32[8,2048]{1,0:T(8,128)} %get-tuple-element.149.segrow_ref, f32[16,2048]{1,0:T(8,128)} %get-tuple-element.169.rowa_ref, ...), custom_call_target="tpu_custom_call" | custom-call | flops 100000000 | bytes 1 | tf_op jit(solution)/shard_map/mid/pallas_call | solution.py:975
  143.6 32.8 %back.1 = (bf16[2,512,768]{2,1,0:T(8,128)(2,1)}, bf16[2,512,768]{2,1,0:T(8,128)(2,1)}, bf16[96,640]{1,0:T(8,128)(2,1)}, bf16[96,640]{1,0:T(8,128)(2,1)}, bf16[96...) custom-call(s32[3]{0:T(128)} %pad_add_fusion.at_ref, ...), custom_call_target="tpu_custom_call" | custom-call | flops 100000000 | bytes 1 | tf_op jit(solution)/shard_map/back/pallas_call | solution.py:975
  176.5 0.7 copy-done.7
  177.4 3.4 %collective-permute-start.22 = (bf16[96,640]{1,0:T(8,128)(2,1)}, bf16[96,640]{1,0:T(8,128)(2,1)S(1)}, u32[]{:S(2)}, u32[]{:S(2)}) collective-permute-start(bf16[96,640]{1,0:T(8,128)(2,1)} %get-tuple-element.201), channel_id=1, source_target_pairs={{0,4},{4,0},{8,12},{12,8},{16,20},{20,16},{24,28},{28,24},{1,5},{5... | collective-permute-start | bytes 368648 | tf_op jit(solution)/shard_map/ppermute | solution.py:1014
  180.8 3.5 %collective-permute-start.23 = (bf16[96,640]{1,0:T(8,128)(2,1)}, bf16[96,640]{1,0:T(8,128)(2,1)S(1)}, u32[]{:S(2)}, u32[]{:S(2)}) collective-permute-start(bf16[96,640]{1,0:T(8,128)(2,1)} %get-tuple-element.202), channel_id=1, source_target_pairs={{0,8},{4,12},{8,0},{12,4},{16,24},{20,28},{24,16},{28,20},{1,9},{5... | collective-permute-start | bytes 368648 | tf_op jit(solution)/shard_map/ppermute | solution.py:1014
  184.7 3.2 %collective-permute-start.25 = (bf16[96,640]{1,0:T(8,128)(2,1)}, bf16[96,640]{1,0:T(8,128)(2,1)}, u32[]{:S(2)}, u32[]{:S(2)}) collective-permute-start(bf16[96,640]{1,0:T(8,128)(2,1)} %get-tuple-element.204), channel_id=1, source_target_pairs={{0,16},{4,20},{8,24},{12,28},{16,0},{20,4},{24,8},{28,12},{1,17},{... | collective-permute-start | bytes 368648 | tf_op jit(solution)/shard_map/ppermute | solution.py:1014
  188.0 2.0 collective-permute-start.26
  190.0 1.9 collective-permute-start.27
  191.9 3.4 %collective-permute-done.24 = bf16[96,640]{1,0:T(8,128)(2,1)S(1)} collective-permute-done((bf16[96,640]{1,0:T(8,128)(2,1)}, bf16[96,640]{1,0:T(8,128)(2,1)S(1)}, u32[]{:S(2)}, u32[]{:S(2)}) %collective-permute-start.24) | collective-permute-done | bytes 122912 | tf_op jit(solution)/shard_map/ppermute | solution.py:1014
  195.3 1.6 collective-permute-start.28
  197.0 9.5 %collective-permute-done.26 = bf16[96,640]{1,0:T(8,128)(2,1)} collective-permute-done((bf16[96,640]{1,0:T(8,128)(2,1)}, bf16[96,640]{1,0:T(8,128)(2,1)}, u32[]{:S(2)}, u32[]{:S(2)}) %collective-permute-start.26) | collective-permute-done | bytes 122912 | tf_op jit(solution)/shard_map/ppermute | solution.py:1014
  206.5 1.3 convert_add_fusion.2
  207.8 1.0 collective-permute-start.30
  208.9 0.8 collective-permute-start.29
  209.7 3.2 %collective-permute-done.31 = bf16[96,256]{1,0:T(8,128)(2,1)S(1)} collective-permute-done((bf16[96,256]{1,0:T(8,128)(2,1)S(1)}, bf16[96,256]{1,0:T(8,128)(2,1)S(1)}, u32[]{:S(2)}, u32[]{:S(2)}) %collective-permute-start.31) | collective-permute-done | bytes 49184 | tf_op jit(solution)/shard_map/ppermute | solution.py:1014
  212.9 1.5 collective-permute-done.30
  214.5 1.7 convert_add_fusion
  216.2 1.0 collective-permute-start.39
  217.2 2.6 %collective-permute-start.33 = (bf16[96,640]{1,0:T(8,128)(2,1)S(1)}, bf16[96,640]{1,0:T(8,128)(2,1)S(1)}, u32[]{:S(2)}, u32[]{:S(2)}) collective-permute-start(bf16[96,640]{1,0:T(8,128)(2,1)S(1)} %pad_maximum_fusion.1.refs_0_), channel_id=1, source_target_pairs={{0,8},{4,12},{8,0},{12,4},{16,24},{20,28},{24,16},{28,20},{1,9},{5... | collective-permute-start | bytes 368648 | tf_op jit(solution)/shard_map/ppermute | solution.py:1014
  219.8 2.7 %collective-permute-start.38 = (bf16[96,640]{1,0:T(8,128)(2,1)S(1)}, bf16[96,640]{1,0:T(8,128)(2,1)}, u32[]{:S(2)}, u32[]{:S(2)}) collective-permute-start(bf16[96,640]{1,0:T(8,128)(2,1)S(1)} %pad_maximum_fusion.1.refs_0_), channel_id=1, source_target_pairs={{0,28},{4,24},{8,20},{12,16},{16,12},{20,8},{24,4},{28,0},{1,29},{... | collective-permute-start | bytes 368648 | tf_op jit(solution)/shard_map/ppermute | solution.py:1014
  222.5 1.5 collective-permute-start.37
  224.6 3.5 %collective-permute-start.35 = (bf16[96,640]{1,0:T(8,128)(2,1)S(1)}, bf16[96,640]{1,0:T(8,128)(2,1)}, u32[]{:S(2)}, u32[]{:S(2)}) collective-permute-start(bf16[96,640]{1,0:T(8,128)(2,1)S(1)} %pad_maximum_fusion.1.refs_0_), channel_id=1, source_target_pairs={{0,16},{4,20},{8,24},{12,28},{16,0},{20,4},{24,8},{28,12},{1,17},{... | collective-permute-start | bytes 368648 | tf_op jit(solution)/shard_map/ppermute | solution.py:1014
  228.1 1.5 convert_add_fusion.1
  229.6 1.1 convert_element_type.117
  230.7 1.1 convert_element_type.118
  231.8 1.0 convert_element_type.111
  232.9 5.1 %collective-permute-start.34 = (bf16[96,640]{1,0:T(8,128)(2,1)S(1)}, bf16[96,640]{1,0:T(8,128)(2,1)S(1)}, u32[]{:S(2)}, u32[]{:S(2)}) collective-permute-start(bf16[96,640]{1,0:T(8,128)(2,1)S(1)} %pad_maximum_fusion.1.refs_0_), channel_id=1, source_target_pairs={{0,12},{4,8},{8,4},{12,0},{16,28},{20,24},{24,20},{28,16},{1,13},{... | collective-permute-start | bytes 368648 | tf_op jit(solution)/shard_map/ppermute | solution.py:1014
  238.0 1.1 collective-permute-start.32
  239.1 1.1 fusion
  240.2 2.3 collective-permute-done.36.refs_5_
  242.4 0.9 collective-permute-done.35.refs_4_
  243.3 1.7 collective-permute-done.34.refs_3_
  246.0 5.5 %finish.1 = (f32[768]{0:T(1024)}, f32[768,384]{1,0:T(8,128)}, f32[768,128]{1,0:T(8,128)}, f32[6,2,768]{2,1,0:T(2,128)}, f32[2,6]{1,0:T(2,128)}, /*index=5*/f32[1...) custom-call(s32[3]{0:T(128)} %pad_add_fusion.at_ref, ...), custom_call_target="tpu_custom_call" | custom-call | flops 3000000000 | bytes 1 | tf_op jit(solution)/shard_map/finish/pallas_call | solution.py:975
  (138 shorter events, 15.4 us)
Async XLA Ops:
  7.2 55.3 %all-gather.2.cloned.1.call-start = ((), (), s32[]{:S(2)}) async-start(), calls=%async_computation.1 | async-start | bytes 3932160 | tf_op jit(solution)/shard_map/all_gather | solution.py:1137
  7.2 21.9 %collective-permute-start = (bf16[512,768]{1,0:T(8,128)(2,1)}, bf16[512,768]{1,0:T(8,128)(2,1)S(1)}, u32[]{:S(2)}, u32[]{:S(2)}) collective-permute-start(bf16[512,768]{1,0:T(8,128)(2,1)} %refs_10_.1), channel_id=1, source_target_pairs={{0,2},{1,3},{2,0},{3,1},{4,6},{5,7},{6,4},{7,5},{8,10},{9,11},{10,... | collective-permute-start | bytes 2359304 | tf_op jit(solution)/shard_map/ppermute | solution.py:1014
  11.0 13.2 %collective-permute-start.1 = (bf16[8,768]{1,0:T(8,128)(2,1)S(1)}, bf16[8,768]{1,0:T(8,128)(2,1)S(1)}, u32[]{:S(2)}, u32[]{:S(2)}) collective-permute-start(bf16[8,768]{1,0:T(8,128)(2,1)S(1)} %slice.28), channel_id=1, source_target_pairs={{0,4},{4,8},{8,12},{12,16},{16,20},{20,24},{24,28},{1,5},{5,9},{9,... | collective-permute-start | bytes 36872 | tf_op jit(solution)/shard_map/ppermute | solution.py:998
  19.9 9.3 %copy-start.1 = (bf16[512,768]{1,0:T(8,128)(2,1)S(1)}, bf16[512,768]{1,0:T(8,128)(2,1)}, u32[]{:S(2)}) copy-start(bf16[512,768]{1,0:T(8,128)(2,1)} %refs_10_.1) | copy-start | bytes 2359300
  19.9 9.9 %copy-start.16 = (f32[384]{0:T(512)S(1)}, f32[384]{0:T(512)}, u32[]{:S(2)}) copy-start(f32[384]{0:T(512)} %param.35) | copy-start | bytes 4612
  19.9 10.4 %copy-start.15 = (f32[768]{0:T(1024)S(1)}, f32[768]{0:T(1024)}, u32[]{:S(2)}) copy-start(f32[768]{0:T(1024)} %param.25) | copy-start | bytes 9220
  19.9 11.0 %copy-start.17 = (f32[6]{0:T(128)S(1)}, f32[6]{0:T(128)}, u32[]{:S(2)}) copy-start(f32[6]{0:T(128)} %param.34) | copy-start | bytes 76
  20.0 12.9 %copy-start.3 = (bf16[768,128]{1,0:T(8,128)(2,1)}, bf16[768,128]{1,0:T(8,128)(2,1)S(1)}, u32[]{:S(2)}) copy-start(bf16[768,128]{1,0:T(8,128)(2,1)S(1)} %pad.28.refs_9_) | copy-start | bytes 589828
  24.1 3.5 %collective-permute-start.4 = (bf16[8,768]{1,0:T(8,128)(2,1)S(1)}, bf16[8,768]{1,0:T(8,128)(2,1)S(1)}, u32[]{:S(2)}, u32[]{:S(2)}) collective-permute-start(bf16[8,768]{1,0:T(8,128)(2,1)S(1)} %collective-permute-done.1), channel_id=1, source_target_pairs={{0,3},{1,2},{2,1},{3,0},{4,7},{5,6},{6,5},{7,4},{8,11},{9,10},{10,... | collective-permute-start | bytes 36872 | tf_op jit(solution)/shard_map/ppermute | solution.py:1014
  24.1 4.4 %collective-permute-start.3 = (bf16[8,768]{1,0:T(8,128)(2,1)S(1)}, bf16[8,768]{1,0:T(8,128)(2,1)S(1)}, u32[]{:S(2)}, u32[]{:S(2)}) collective-permute-start(bf16[8,768]{1,0:T(8,128)(2,1)S(1)} %collective-permute-done.1), channel_id=1, source_target_pairs={{0,2},{1,3},{2,0},{3,1},{4,6},{5,7},{6,4},{7,5},{8,10},{9,11},{10,... | collective-permute-start | bytes 36872 | tf_op jit(solution)/shard_map/ppermute | solution.py:1014
  25.0 3.5 %collective-permute-start.2 = (bf16[8,768]{1,0:T(8,128)(2,1)S(1)}, bf16[8,768]{1,0:T(8,128)(2,1)S(1)}, u32[]{:S(2)}, u32[]{:S(2)}) collective-permute-start(bf16[8,768]{1,0:T(8,128)(2,1)S(1)} %collective-permute-done.1), channel_id=1, source_target_pairs={{0,1},{1,0},{2,3},{3,2},{4,5},{5,4},{6,7},{7,6},{8,9},{9,8},{10,11... | collective-permute-start | bytes 36872 | tf_op jit(solution)/shard_map/ppermute | solution.py:1014
  29.1 3.7 %copy-start.18 = (bf16[512,768]{1,0:T(8,128)(2,1)}, bf16[512,768]{1,0:T(8,128)(2,1)S(1)}, u32[]{:S(2)}) copy-start(bf16[512,768]{1,0:T(8,128)(2,1)S(1)} %collective-permute-done.refs_2_) | copy-start | bytes 2359300
  29.1 199.0 %all-reduce.9.cloned.1.call-start = ((), (), s32[]{:S(2)}) async-start(), calls=%async_computation.3 | async-start | bytes 2359296 | tf_op jit(solution)/shard_map/psum | solution.py:1403
  29.2 3.1 %collective-permute-start.5 = (bf16[512,768]{1,0:T(8,128)(2,1)S(1)}, bf16[512,768]{1,0:T(8,128)(2,1)S(1)}, u32[]{:S(2)}, u32[]{:S(2)}) collective-permute-start(bf16[512,768]{1,0:T(8,128)(2,1)S(1)} %copy-done.1), channel_id=1, source_target_pairs={{0,1},{1,0},{2,3},{3,2},{4,5},{5,4},{6,7},{7,6},{8,9},{9,8},{10,11... | collective-permute-start | bytes 2359304 | tf_op jit(solution)/shard_map/ppermute | solution.py:1014
  29.3 3.5 %collective-permute-start.6 = (bf16[512,768]{1,0:T(8,128)(2,1)S(1)}, bf16[512,768]{1,0:T(8,128)(2,1)}, u32[]{:S(2)}, u32[]{:S(2)}) collective-permute-start(bf16[512,768]{1,0:T(8,128)(2,1)S(1)} %collective-permute-done.refs_2_), channel_id=1, source_target_pairs={{0,1},{1,0},{2,3},{3,2},{4,5},{5,4},{6,7},{7,6},{8,9},{9,8},{10,11... | collective-permute-start | bytes 2359304 | tf_op jit(solution)/shard_map/ppermute | solution.py:1014
  32.3 0.9 copy-start.20
  56.3 14.9 %collective-permute-start.7 = (f32[72,384]{1,0:T(8,128)}, f32[72,384]{1,0:T(8,128)S(1)}, u32[]{:S(2)}, u32[]{:S(2)}) collective-permute-start(f32[72,384]{1,0:T(8,128)} %get-tuple-element.155), channel_id=1, source_target_pairs={{0,4},{8,12},{16,20},{24,28},{4,0},{12,8},{20,16},{28,24},{1,5},{9... | collective-permute-start | bytes 331784 | tf_op jit(solution)/shard_map/ppermute | solution.py:1008
  58.1 13.1 %collective-permute-start.8 = (f32[72,384]{1,0:T(8,128)}, f32[72,384]{1,0:T(8,128)S(1)}, u32[]{:S(2)}, u32[]{:S(2)}) collective-permute-start(f32[72,384]{1,0:T(8,128)} %get-tuple-element.156), channel_id=1, source_target_pairs={{4,8},{12,16},{20,24},{8,4},{16,12},{24,20},{5,9},{13,17},{21,25},... | collective-permute-start | bytes 331784 | tf_op jit(solution)/shard_map/ppermute | solution.py:1008
  58.7 12.4 %collective-permute-start.9 = (f32[72,384]{1,0:T(8,128)}, f32[72,384]{1,0:T(8,128)S(1)}, u32[]{:S(2)}, u32[]{:S(2)}) collective-permute-start(f32[72,384]{1,0:T(8,128)} %get-tuple-element.157), channel_id=1, source_target_pairs={{0,8},{4,12},{16,24},{20,28},{8,0},{12,4},{24,16},{28,20},{1,9},{5... | collective-permute-start | bytes 331784 | tf_op jit(solution)/shard_map/ppermute | solution.py:1008
  61.8 9.4 %collective-permute-start.10 = (f32[72,384]{1,0:T(8,128)}, f32[72,384]{1,0:T(8,128)S(1)}, u32[]{:S(2)}, u32[]{:S(2)}) collective-permute-start(f32[72,384]{1,0:T(8,128)} %get-tuple-element.158), channel_id=1, source_target_pairs={{8,16},{12,20},{16,8},{20,12},{9,17},{13,21},{17,9},{21,13},{10,18... | collective-permute-start | bytes 331784 | tf_op jit(solution)/shard_map/ppermute | solution.py:1008
  81.2 4.4 %collective-permute-start.13 = (f32[8,2048]{1,0:T(8,128)}, f32[8,2048]{1,0:T(8,128)S(1)}, u32[]{:S(2)}, u32[]{:S(2)}) collective-permute-start(f32[8,2048]{1,0:T(8,128)} %get-tuple-element.161.rest_0_), channel_id=1, source_target_pairs={{0,3},{1,2},{2,1},{3,0},{4,7},{5,6},{6,5},{7,4},{8,11},{9,10},{10,... | collective-permute-start | bytes 196616 | tf_op jit(solution)/shard_map/ppermute | solution.py:1336
  81.8 5.4 %collective-permute-start.12 = (f32[8,2048]{1,0:T(8,128)}, f32[8,2048]{1,0:T(8,128)S(1)}, u32[]{:S(2)}, u32[]{:S(2)}) collective-permute-start(f32[8,2048]{1,0:T(8,128)} %get-tuple-element.161.rest_0_), channel_id=1, source_target_pairs={{0,2},{1,3},{2,0},{3,1},{4,6},{5,7},{6,4},{7,5},{8,10},{9,11},{10,... | collective-permute-start | bytes 196616 | tf_op jit(solution)/shard_map/ppermute | solution.py:1336
  83.1 4.1 %collective-permute-start.11 = (f32[8,2048]{1,0:T(8,128)}, f32[8,2048]{1,0:T(8,128)S(1)}, u32[]{:S(2)}, u32[]{:S(2)}) collective-permute-start(f32[8,2048]{1,0:T(8,128)} %get-tuple-element.161.rest_0_), channel_id=1, source_target_pairs={{0,1},{1,0},{2,3},{3,2},{4,5},{5,4},{6,7},{7,6},{8,9},{9,8},{10,11... | collective-permute-start | bytes 196616 | tf_op jit(solution)/shard_map/ppermute | solution.py:1336
  85.6 1.6 copy-start.28
  101.3 130.5 %reduce-scatter.2.cloned.1.call-start = ((), (), s32[]{:S(2)}) async-start(), calls=%async_computation.2 | async-start | bytes 1966080 | tf_op jit(solution)/shard_map/reduce_scatter | solution.py:1404
  112.6 63.8 %collective-permute-start.18 = (bf16[256,768]{1,0:T(8,128)(2,1)}, bf16[256,768]{1,0:T(8,128)(2,1)S(1)}, u32[]{:S(2)}, u32[]{:S(2)}) collective-permute-start(bf16[256,768]{1,0:T(8,128)(2,1)} %get-tuple-element.196), channel_id=1, source_target_pairs={{0,1},{1,0},{2,3},{3,2},{4,5},{5,4},{6,7},{7,6},{8,9},{9,8},{10,11... | collective-permute-start | bytes 1179656 | tf_op jit(solution)/shard_map/ppermute | solution.py:1014
  112.8 63.6 %collective-permute-start.19 = (bf16[256,768]{1,0:T(8,128)(2,1)}, bf16[256,768]{1,0:T(8,128)(2,1)S(1)}, u32[]{:S(2)}, u32[]{:S(2)}) collective-permute-start(bf16[256,768]{1,0:T(8,128)(2,1)} %get-tuple-element.197), channel_id=1, source_target_pairs={{0,2},{1,3},{2,0},{3,1},{4,6},{5,7},{6,4},{7,5},{8,10},{9,11},{10,... | collective-permute-start | bytes 1179656 | tf_op jit(solution)/shard_map/ppermute | solution.py:1014
  113.7 62.8 %collective-permute-start.20 = (bf16[256,768]{1,0:T(8,128)(2,1)}, bf16[256,768]{1,0:T(8,128)(2,1)S(1)}, u32[]{:S(2)}, u32[]{:S(2)}) collective-permute-start(bf16[256,768]{1,0:T(8,128)(2,1)} %get-tuple-element.198), channel_id=1, source_target_pairs={{0,3},{1,2},{2,1},{3,0},{4,7},{5,6},{6,5},{7,4},{8,11},{9,10},{10,... | collective-permute-start | bytes 1179656 | tf_op jit(solution)/shard_map/ppermute | solution.py:1014
  114.5 6.8 %collective-permute-start.14 = (f32[72,384]{1,0:T(8,128)}, f32[72,384]{1,0:T(8,128)S(1)}, u32[]{:S(2)}, u32[]{:S(2)}) collective-permute-start(f32[72,384]{1,0:T(8,128)} %get-tuple-element.181), channel_id=1, source_target_pairs={{0,4},{8,12},{16,20},{24,28},{4,0},{12,8},{20,16},{28,24},{1,5},{9... | collective-permute-start | bytes 331784 | tf_op jit(solution)/shard_map/ppermute | solution.py:1008
  117.6 7.1 %collective-permute-start.15 = (f32[72,384]{1,0:T(8,128)}, f32[72,384]{1,0:T(8,128)S(1)}, u32[]{:S(2)}, u32[]{:S(2)}) collective-permute-start(f32[72,384]{1,0:T(8,128)} %get-tuple-element.182), channel_id=1, source_target_pairs={{4,8},{12,16},{20,24},{8,4},{16,12},{24,20},{5,9},{13,17},{21,25},... | collective-permute-start | bytes 331784 | tf_op jit(solution)/shard_map/ppermute | solution.py:1008
  121.3 21.5 %copy-start.11 = (f32[72,384]{1,0:T(8,128)}, f32[72,384]{1,0:T(8,128)S(1)}, u32[]{:S(2)}) copy-start(f32[72,384]{1,0:T(8,128)S(1)} %collective-permute-done.14.rest_0_) | copy-start | bytes 331780
  121.3 21.6 %collective-permute-start.16 = (f32[72,384]{1,0:T(8,128)}, f32[72,384]{1,0:T(8,128)S(1)}, u32[]{:S(2)}, u32[]{:S(2)}) collective-permute-start(f32[72,384]{1,0:T(8,128)} %get-tuple-element.183), channel_id=1, source_target_pairs={{0,8},{4,12},{16,24},{20,28},{8,0},{12,4},{24,16},{28,20},{1,9},{5... | collective-permute-start | bytes 331784 | tf_op jit(solution)/shard_map/ppermute | solution.py:1008
  124.7 18.2 %copy-start.12 = (f32[72,384]{1,0:T(8,128)}, f32[72,384]{1,0:T(8,128)S(1)}, u32[]{:S(2)}) copy-start(f32[72,384]{1,0:T(8,128)S(1)} %collective-permute-done.15.rest_1_) | copy-start | bytes 331780
  124.7 18.2 %collective-permute-start.17 = (f32[72,384]{1,0:T(8,128)}, f32[72,384]{1,0:T(8,128)S(1)}, u32[]{:S(2)}, u32[]{:S(2)}) collective-permute-start(f32[72,384]{1,0:T(8,128)} %get-tuple-element.184), channel_id=1, source_target_pairs={{8,16},{12,20},{16,8},{20,12},{9,17},{13,21},{17,9},{21,13},{10,18... | collective-permute-start | bytes 331784 | tf_op jit(solution)/shard_map/ppermute | solution.py:1008
  176.4 38.1 %copy-start = (bf16[2,512,768]{2,1,0:T(8,128)(2,1)S(1)}, bf16[2,512,768]{2,1,0:T(8,128)(2,1)}, u32[]{:S(2)}) copy-start(bf16[2,512,768]{2,1,0:T(8,128)(2,1)} %get-tuple-element.185) | copy-start | bytes 4718596
  176.4 0.7 copy-start.7
  176.4 0.9 copy-start.8
  176.5 1.0 copy-start.9
  177.3 37.1 %collective-permute-start.21 = (bf16[2,512,768]{2,1,0:T(8,128)(2,1)}, bf16[2,512,768]{2,1,0:T(8,128)(2,1)S(1)}, u32[]{:S(2)}, u32[]{:S(2)}) collective-permute-start(bf16[2,512,768]{2,1,0:T(8,128)(2,1)} %get-tuple-element.199), channel_id=1, source_target_pairs={{0,1},{1,0},{2,3},{3,2},{4,5},{5,4},{6,7},{7,6},{8,9},{9,8},{10,11... | collective-permute-start | bytes 4718600 | tf_op jit(solution)/shard_map/ppermute | solution.py:1014
  177.4 10.6 %collective-permute-start.22 = (bf16[96,640]{1,0:T(8,128)(2,1)}, bf16[96,640]{1,0:T(8,128)(2,1)S(1)}, u32[]{:S(2)}, u32[]{:S(2)}) collective-permute-start(bf16[96,640]{1,0:T(8,128)(2,1)} %get-tuple-element.201), channel_id=1, source_target_pairs={{0,4},{4,0},{8,12},{12,8},{16,20},{20,16},{24,28},{28,24},{1,5},{5... | collective-permute-start | bytes 368648 | tf_op jit(solution)/shard_map/ppermute | solution.py:1014
  180.8 9.2 %collective-permute-start.23 = (bf16[96,640]{1,0:T(8,128)(2,1)}, bf16[96,640]{1,0:T(8,128)(2,1)S(1)}, u32[]{:S(2)}, u32[]{:S(2)}) collective-permute-start(bf16[96,640]{1,0:T(8,128)(2,1)} %get-tuple-element.202), channel_id=1, source_target_pairs={{0,8},{4,12},{8,0},{12,4},{16,24},{20,28},{24,16},{28,20},{1,9},{5... | collective-permute-start | bytes 368648 | tf_op jit(solution)/shard_map/ppermute | solution.py:1014
  184.3 11.0 %collective-permute-start.24 = (bf16[96,640]{1,0:T(8,128)(2,1)}, bf16[96,640]{1,0:T(8,128)(2,1)S(1)}, u32[]{:S(2)}, u32[]{:S(2)}) collective-permute-start(bf16[96,640]{1,0:T(8,128)(2,1)} %get-tuple-element.203), channel_id=1, source_target_pairs={{0,12},{4,8},{8,4},{12,0},{16,28},{20,24},{24,20},{28,16},{1,13},{... | collective-permute-start | bytes 368648 | tf_op jit(solution)/shard_map/ppermute | solution.py:1014
  184.7 12.2 %collective-permute-start.25 = (bf16[96,640]{1,0:T(8,128)(2,1)}, bf16[96,640]{1,0:T(8,128)(2,1)}, u32[]{:S(2)}, u32[]{:S(2)}) collective-permute-start(bf16[96,640]{1,0:T(8,128)(2,1)} %get-tuple-element.204), channel_id=1, source_target_pairs={{0,16},{4,20},{8,24},{12,28},{16,0},{20,4},{24,8},{28,12},{1,17},{... | collective-permute-start | bytes 368648 | tf_op jit(solution)/shard_map/ppermute | solution.py:1014
  188.0 18.5 %collective-permute-start.26 = (bf16[96,640]{1,0:T(8,128)(2,1)}, bf16[96,640]{1,0:T(8,128)(2,1)}, u32[]{:S(2)}, u32[]{:S(2)}) collective-permute-start(bf16[96,640]{1,0:T(8,128)(2,1)} %get-tuple-element.205), channel_id=1, source_target_pairs={{0,20},{4,16},{8,28},{12,24},{16,4},{20,0},{24,12},{28,8},{1,21},{... | collective-permute-start | bytes 368648 | tf_op jit(solution)/shard_map/ppermute | solution.py:1014
  190.0 16.4 %collective-permute-start.27 = (bf16[96,640]{1,0:T(8,128)(2,1)}, bf16[96,640]{1,0:T(8,128)(2,1)}, u32[]{:S(2)}, u32[]{:S(2)}) collective-permute-start(bf16[96,640]{1,0:T(8,128)(2,1)} %get-tuple-element.206), channel_id=1, source_target_pairs={{0,24},{4,28},{8,16},{12,20},{16,8},{20,12},{24,0},{28,4},{1,25},{... | collective-permute-start | bytes 368648 | tf_op jit(solution)/shard_map/ppermute | solution.py:1014
  195.3 11.1 %collective-permute-start.28 = (bf16[96,640]{1,0:T(8,128)(2,1)}, bf16[96,640]{1,0:T(8,128)(2,1)}, u32[]{:S(2)}, u32[]{:S(2)}) collective-permute-start(bf16[96,640]{1,0:T(8,128)(2,1)} %get-tuple-element.207), channel_id=1, source_target_pairs={{0,28},{4,24},{8,20},{12,16},{16,12},{20,8},{24,4},{28,0},{1,29},{... | collective-permute-start | bytes 368648 | tf_op jit(solution)/shard_map/ppermute | solution.py:1014
  207.7 5.1 %collective-permute-start.31 = (bf16[96,256]{1,0:T(8,128)(2,1)S(1)}, bf16[96,256]{1,0:T(8,128)(2,1)S(1)}, u32[]{:S(2)}, u32[]{:S(2)}) collective-permute-start(bf16[96,256]{1,0:T(8,128)(2,1)S(1)} %fusion.1), channel_id=1, source_target_pairs={{0,3},{1,2},{2,1},{3,0},{4,7},{5,6},{6,5},{7,4},{8,11},{9,10},{10,... | collective-permute-start | bytes 147464 | tf_op jit(solution)/shard_map/ppermute | solution.py:1014
  207.8 6.5 %collective-permute-start.30 = (bf16[96,256]{1,0:T(8,128)(2,1)S(1)}, bf16[96,256]{1,0:T(8,128)(2,1)S(1)}, u32[]{:S(2)}, u32[]{:S(2)}) collective-permute-start(bf16[96,256]{1,0:T(8,128)(2,1)S(1)} %fusion.1), channel_id=1, source_target_pairs={{0,2},{1,3},{2,0},{3,1},{4,6},{5,7},{6,4},{7,5},{8,10},{9,11},{10,... | collective-permute-start | bytes 147464 | tf_op jit(solution)/shard_map/ppermute | solution.py:1014
  208.9 5.5 %collective-permute-start.29 = (bf16[96,256]{1,0:T(8,128)(2,1)S(1)}, bf16[96,256]{1,0:T(8,128)(2,1)S(1)}, u32[]{:S(2)}, u32[]{:S(2)}) collective-permute-start(bf16[96,256]{1,0:T(8,128)(2,1)S(1)} %fusion.1), channel_id=1, source_target_pairs={{0,1},{1,0},{2,3},{3,2},{4,5},{5,4},{6,7},{7,6},{8,9},{9,8},{10,11... | collective-permute-start | bytes 147464 | tf_op jit(solution)/shard_map/ppermute | solution.py:1014
  214.5 13.7 %copy-start.6 = (bf16[256,768]{1,0:T(8,128)(2,1)S(1)}, bf16[256,768]{1,0:T(8,128)(2,1)}, u32[]{:S(2)}) copy-start(bf16[256,768]{1,0:T(8,128)(2,1)} %get-tuple-element.217) | copy-start | bytes 1179652
  216.2 28.8 %collective-permute-start.39 = (bf16[1,512,768]{2,1,0:T(8,128)(2,1)}, bf16[1,512,768]{2,1,0:T(8,128)(2,1)S(1)}, u32[]{:S(2)}, u32[]{:S(2)}) collective-permute-start(bf16[1,512,768]{2,1,0:T(8,128)(2,1)} %get-tuple-element.232), channel_id=1, source_target_pairs={{0,2},{1,3},{2,0},{3,1},{4,6},{5,7},{6,4},{7,5},{8,10},{9,11},{10,... | collective-permute-start | bytes 2359304 | tf_op jit(solution)/shard_map/ppermute | solution.py:1014
  217.2 20.8 %copy-start.10 = (bf16[96,640]{1,0:T(8,128)(2,1)}, bf16[96,640]{1,0:T(8,128)(2,1)S(1)}, u32[]{:S(2)}) copy-start(bf16[96,640]{1,0:T(8,128)(2,1)S(1)} %pad_maximum_fusion.1.refs_0_) | copy-start | bytes 368644
  217.2 6.7 %collective-permute-start.33 = (bf16[96,640]{1,0:T(8,128)(2,1)S(1)}, bf16[96,640]{1,0:T(8,128)(2,1)S(1)}, u32[]{:S(2)}, u32[]{:S(2)}) collective-permute-start(bf16[96,640]{1,0:T(8,128)(2,1)S(1)} %pad_maximum_fusion.1.refs_0_), channel_id=1, source_target_pairs={{0,8},{4,12},{8,0},{12,4},{16,24},{20,28},{24,16},{28,20},{1,9},{5... | collective-permute-start | bytes 368648 | tf_op jit(solution)/shard_map/ppermute | solution.py:1014
  219.8 13.1 %collective-permute-start.38 = (bf16[96,640]{1,0:T(8,128)(2,1)S(1)}, bf16[96,640]{1,0:T(8,128)(2,1)}, u32[]{:S(2)}, u32[]{:S(2)}) collective-permute-start(bf16[96,640]{1,0:T(8,128)(2,1)S(1)} %pad_maximum_fusion.1.refs_0_), channel_id=1, source_target_pairs={{0,28},{4,24},{8,20},{12,16},{16,12},{20,8},{24,4},{28,0},{1,29},{... | collective-permute-start | bytes 368648 | tf_op jit(solution)/shard_map/ppermute | solution.py:1014
  222.5 15.6 %collective-permute-start.37 = (bf16[96,640]{1,0:T(8,128)(2,1)S(1)}, bf16[96,640]{1,0:T(8,128)(2,1)}, u32[]{:S(2)}, u32[]{:S(2)}) collective-permute-start(bf16[96,640]{1,0:T(8,128)(2,1)S(1)} %pad_maximum_fusion.1.refs_0_), channel_id=1, source_target_pairs={{0,24},{4,28},{8,16},{12,20},{16,8},{20,12},{24,0},{28,4},{1,25},{... | collective-permute-start | bytes 368648 | tf_op jit(solution)/shard_map/ppermute | solution.py:1014
  223.9 18.5 %collective-permute-start.36 = (bf16[96,640]{1,0:T(8,128)(2,1)S(1)}, bf16[96,640]{1,0:T(8,128)(2,1)}, u32[]{:S(2)}, u32[]{:S(2)}) collective-permute-start(bf16[96,640]{1,0:T(8,128)(2,1)S(1)} %pad_maximum_fusion.1.refs_0_), channel_id=1, source_target_pairs={{0,20},{4,16},{8,28},{12,24},{16,4},{20,0},{24,12},{28,8},{1,21},{... | collective-permute-start | bytes 368648 | tf_op jit(solution)/shard_map/ppermute | solution.py:1014
  224.6 18.7 %collective-permute-start.35 = (bf16[96,640]{1,0:T(8,128)(2,1)S(1)}, bf16[96,640]{1,0:T(8,128)(2,1)}, u32[]{:S(2)}, u32[]{:S(2)}) collective-permute-start(bf16[96,640]{1,0:T(8,128)(2,1)S(1)} %pad_maximum_fusion.1.refs_0_), channel_id=1, source_target_pairs={{0,16},{4,20},{8,24},{12,28},{16,0},{20,4},{24,8},{28,12},{1,17},{... | collective-permute-start | bytes 368648 | tf_op jit(solution)/shard_map/ppermute | solution.py:1014
  228.1 1.5 copy-start.5
  228.1 2.6 %copy-start.4 = (bf16[768,384]{1,0:T(8,128)(2,1)S(1)}, bf16[768,384]{1,0:T(8,128)(2,1)}, u32[]{:S(2)}) copy-start(bf16[768,384]{1,0:T(8,128)(2,1)} %get-tuple-element.222) | copy-start | bytes 1769476
  230.7 8.4 %copy-start.2 = (bf16[512,768]{1,0:T(8,128)(2,1)S(1)}, bf16[512,768]{1,0:T(8,128)(2,1)}, u32[]{:S(2)}) copy-start(bf16[512,768]{1,0:T(8,128)(2,1)} %refs_10_.1) | copy-start | bytes 2359300
  232.9 12.1 %collective-permute-start.34 = (bf16[96,640]{1,0:T(8,128)(2,1)S(1)}, bf16[96,640]{1,0:T(8,128)(2,1)S(1)}, u32[]{:S(2)}, u32[]{:S(2)}) collective-permute-start(bf16[96,640]{1,0:T(8,128)(2,1)S(1)} %pad_maximum_fusion.1.refs_0_), channel_id=1, source_target_pairs={{0,12},{4,8},{8,4},{12,0},{16,28},{20,24},{24,20},{28,16},{1,13},{... | collective-permute-start | bytes 368648 | tf_op jit(solution)/shard_map/ppermute | solution.py:1014
  238.0 7.0 %collective-permute-start.32 = (bf16[96,640]{1,0:T(8,128)(2,1)S(1)}, bf16[96,640]{1,0:T(8,128)(2,1)S(1)}, u32[]{:S(2)}, u32[]{:S(2)}) collective-permute-start(bf16[96,640]{1,0:T(8,128)(2,1)S(1)} %pad_maximum_fusion.1.refs_0_), channel_id=1, source_target_pairs={{0,4},{4,0},{8,12},{12,8},{16,20},{20,16},{24,28},{28,24},{1,5},{5... | collective-permute-start | bytes 368648 | tf_op jit(solution)/shard_map/ppermute | solution.py:1014
  245.0 0.7 copy-start.23
  245.0 1.0 copy-start.19
  (10 other events, 6.5 us)
Sparse Core Ops, SparseCore 0:
  29.3 30.0 all-gather.1
  101.4 82.5 all-reduce.8
  186.7 29.4 reduce-scatter.1
